TPU v7x, 32 devices: a whole 2x2x4 slice. The times are simulated.
32 devices in a mesh: dp: 16 (over z, x, core), tensor: 2 (over y).
Axes of the slice: x: 2, y: 2, z: 4, core: 2. Of those that a mesh axis runs over, the one named last changes fastest.
Arguments:
- hidden_in: bfloat16 [16384, 768], P(('dp', 'tensor')), may hold values from -6 to 6
- segment_ids: int32 [16384], P('dp'), may hold values from 0 to 6, as said below
- norm_gain: bfloat16 [768], P('dp'), may hold values from 0.5 to 1.5
- proj_inner: bfloat16 [768, 2, 1536], P('dp', None, 'tensor'), may hold values from -0.21875 to 0.21875
- proj_shared: bfloat16 [768, 2, 128], P('dp'), may hold values from -0.21875 to 0.21875
- proj_step: bfloat16 [768, 24], P('dp', 'tensor'), may hold values from -0.21875 to 0.21875
- conv_inner: bfloat16 [4, 1536], P(None, 'tensor'), may hold values from -3 to 3
- conv_shared: bfloat16 [4, 2, 128], P(None, None, 'dp'), may hold values from -3 to 3
- step_bias: float32 [24], P('tensor'), may hold values from -6 to -3
- log_decay: float32 [24], P('tensor'), may hold values from 0 to 2
- skip_gain: float32 [24], P('tensor'), may hold values from 0.5 to 1.5
- gate_gain: bfloat16 [1536], P('tensor'), may hold values from 0.5 to 1.5
- proj_out: bfloat16 [1536, 768], P('tensor', 'dp'), may hold values from -0.15625 to 0.15625
- out_grad: bfloat16 [16384, 768], P(('dp', 'tensor')), may hold values from -6 to 6
Outputs:
- hidden_out: bfloat16 [16384, 768], P(('dp', 'tensor'))
- hidden_grad: float32 [16384, 768], P(('dp', 'tensor'))
- norm_grad: float32 [768], P('dp')
- inner_grad: float32 [768, 2, 1536], P('dp', None, 'tensor')
- shared_grad: float32 [768, 2, 128], P('dp')
- step_grad: float32 [768, 24], P('dp', 'tensor')
- conv_inner_grad: float32 [4, 1536], P(None, 'tensor')
- conv_shared_grad: float32 [4, 2, 128], P(None, None, 'dp')
- bias_grad: float32 [24], P('tensor')
- decay_grad: float32 [24], P('tensor')
- skip_grad: float32 [24], P('tensor')
- gate_grad: float32 [1536], P('tensor')
- out_proj_grad: float32 [1536, 768], P('tensor', 'dp')
Inputs may be any that keep to these rules, and one draw needn't show every extreme that they name: `segment_ids`: in each sequence of 1024 tokens, 6 documents of one token or more carry ids 1 to 6 in rising order, followed by one run of padding with id 0 that ends the sequence.
All inputs are finite; a program needn't handle non-finite values.
Results may differ from a plain program's by a relative error of at most 0.019.
Values may be sent and summed in bfloat16 or wider, within the bound.
No kernel may reach another device: no remote copies, remote signals or barrier semaphores. Data moves between devices by JAX's collectives and lax.ppermute only.
A program may use at most 192 MiB of HBM per device.

v0:
```python
from functools import partial

import jax
import jax.numpy as jnp
from jax import lax
from jax.sharding import PartitionSpec as P

HEAD_DIM = 64
BLOCK = 256


epsilon = 1e-05
highest = lax.Precision.HIGHEST


def causal_conv(values, kernel, segment):
    kernel_len = kernel.shape[0]
    length = values.shape[0]
    summed = kernel[kernel_len - 1] * values
    for offset in range(1, kernel_len):
        shifted = jnp.concatenate(
            [jnp.zeros((offset, values.shape[1]), values.dtype), values[: length - offset]], axis=0
        )
        earlier = jnp.concatenate([jnp.full((offset,), -1, jnp.int32), segment[: length - offset]])
        matching = (earlier == segment).astype(values.dtype)
        summed = summed + kernel[kernel_len - 1 - offset] * shifted * matching[:, None]
    return summed


def ssd_core(inputs, b_rows, c_rows, step_size, decay_rate, segment, block_len):
    length, head_count, head_size = inputs.shape
    block_count = length // block_len
    x_blocks = inputs.reshape(block_count, block_len, head_count, head_size)
    b_blocks = b_rows.reshape(block_count, block_len, b_rows.shape[1])
    c_blocks = c_rows.reshape(block_count, block_len, c_rows.shape[1])
    step_blocks = step_size.reshape(block_count, block_len, head_count)
    seg_blocks = segment.reshape(block_count, block_len)
    decay_sum = jnp.cumsum(step_blocks * decay_rate, axis=1)
    last_seg = seg_blocks[:, block_len - 1]
    prior_seg = jnp.concatenate([jnp.full((1,), -1, jnp.int32), last_seg[: block_count - 1]])
    causal = jnp.arange(block_len)[:, None] >= jnp.arange(block_len)[None, :]
    inside = ((seg_blocks[:, :, None] == seg_blocks[:, None, :]) & causal[None])[..., None]
    gap_decay = jnp.where(inside, decay_sum[:, :, None, :] - decay_sum[:, None, :, :], 0.0)
    within = jnp.where(inside, jnp.exp(gap_decay), 0.0)
    scores = jnp.einsum("ctn,csn->cts", c_blocks, b_blocks, precision=highest)
    mixing = scores[..., None] * within * step_blocks[:, None, :, :]
    in_block = jnp.einsum("ctsh,cshp->cthp", mixing, x_blocks, precision=highest)
    block_decay = decay_sum[:, block_len - 1, :]
    keeps_end = (seg_blocks == last_seg[:, None]).astype(inputs.dtype)
    to_end = jnp.exp(block_decay[:, None, :] - decay_sum) * keeps_end[..., None] * step_blocks
    block_state = jnp.einsum(
        "cshp,csn->chpn", to_end[..., None] * x_blocks, b_blocks, precision=highest
    )
    block_index = jnp.arange(block_count)
    between = (
        (block_index[None, None, :] > block_index[None, :, None])
        & (block_index[None, None, :] < block_index[:, None, None])
    ).astype(inputs.dtype)
    span_decay = jnp.einsum("dek,kh->deh", between, block_decay, precision=highest)
    linked = (
        (block_index[None, :] < block_index[:, None]) & (prior_seg[:, None] == last_seg[None, :])
    )[..., None]
    carried = jnp.where(linked, jnp.exp(jnp.where(linked, span_decay, 0.0)), 0.0)
    entry_state = jnp.einsum("deh,ehpn->dhpn", carried, block_state, precision=highest)
    entry_gate = (
        jnp.exp(decay_sum) * (seg_blocks == prior_seg[:, None]).astype(inputs.dtype)[..., None]
    )
    from_past = (
        jnp.einsum("ctn,chpn->cthp", c_blocks, entry_state, precision=highest)
        * entry_gate[..., None]
    )
    return (in_block + from_past).reshape(length, head_count, head_size)


def mixer_local(
    gate_in,
    conv_in,
    shared_in,
    step_raw,
    taps_inner,
    taps_shared,
    step_bias,
    log_decay,
    skip_gain,
    segment,
    block_len,
    head_size,
):
    length = gate_in.shape[0]
    head_count = step_raw.shape[1]
    state_size = shared_in.shape[1] // 2
    live_mask = (segment != 0).astype(gate_in.dtype)
    conv_out = jax.nn.silu(causal_conv(conv_in, taps_inner, segment))
    shared_out = jax.nn.silu(causal_conv(shared_in, taps_shared, segment))
    step_size = jax.nn.softplus(step_raw + step_bias) * live_mask[:, None]
    decay_rate = -jnp.exp(log_decay)
    heads_view = conv_out.reshape(length, head_count, head_size)
    mixed = ssd_core(
        heads_view,
        shared_out[:, :state_size],
        shared_out[:, state_size:],
        step_size,
        decay_rate,
        segment,
        block_len,
    )
    mixed = mixed + skip_gain[:, None] * heads_view
    mixed = mixed.reshape(length, head_count * head_size) * live_mask[:, None]
    return mixed * jax.nn.silu(gate_in)


def contract_rows(left, right):
    return lax.dot_general(
        left, right, (((0,), (0,)), ((), ())), preferred_element_type=jnp.float32
    )


def contract_cols(left, right):
    return lax.dot_general(
        left, right, (((1,), (1,)), ((), ())), preferred_element_type=jnp.float32
    )


def body(
    hidden_in,
    segment_ids,
    norm_gain,
    proj_inner,
    proj_shared,
    proj_step,
    conv_inner,
    conv_shared,
    step_bias,
    log_decay,
    skip_gain,
    gate_gain,
    proj_out,
    out_grad,
):
    tensor_count = lax.axis_size("tensor")
    model_dim = hidden_in.shape[1]
    local_inner = proj_inner.shape[2]
    state_size = proj_shared.shape[2]
    kernel_len = conv_inner.shape[0]
    full_inner = local_inner * tensor_count
    norm_full, inner_full, shared_full, step_full, taps_full, out_full = (
        lax.all_gather(norm_gain, "dp", axis=0, tiled=True),
        lax.all_gather(proj_inner, "dp", axis=0, tiled=True),
        lax.all_gather(proj_shared, "dp", axis=0, tiled=True),
        lax.all_gather(proj_step, "dp", axis=0, tiled=True),
        lax.all_gather(conv_shared, "dp", axis=2, tiled=True),
        lax.all_gather(proj_out, "dp", axis=1, tiled=True),
    )
    hidden = hidden_in.astype(jnp.float32)
    inv_norm = lax.rsqrt(jnp.mean(hidden * hidden, axis=-1, keepdims=True) + epsilon)
    unit_in = hidden * inv_norm
    norm_scale = norm_full.astype(jnp.float32)
    normed_own = (unit_in * norm_scale).astype(jnp.bfloat16)
    normed = lax.all_gather(normed_own, "tensor", axis=0, tiled=True)
    shared_mat = shared_full.reshape(model_dim, 2 * state_size)
    head_mat = jnp.concatenate([inner_full[:, 0, :], inner_full[:, 1, :], step_full], axis=1)
    head_proj = jnp.dot(normed, head_mat, preferred_element_type=jnp.float32)
    shared_proj = jnp.dot(normed, shared_mat, preferred_element_type=jnp.float32)
    gate_in = head_proj[:, :local_inner]
    conv_in = head_proj[:, local_inner : 2 * local_inner]
    step_raw = head_proj[:, 2 * local_inner :]
    local_fn = partial(mixer_local, segment=segment_ids, block_len=BLOCK, head_size=HEAD_DIM)
    gated, mixer_pull = jax.vjp(
        local_fn,
        gate_in,
        conv_in,
        shared_proj,
        step_raw,
        conv_inner.astype(jnp.float32),
        taps_full.reshape(kernel_len, 2 * state_size).astype(jnp.float32),
        step_bias,
        log_decay,
        skip_gain,
    )
    squares = lax.psum(jnp.sum(gated * gated, axis=1), "tensor")
    inv_gate = lax.rsqrt(squares / full_inner + epsilon)[:, None]
    unit_gate = gated * inv_gate
    gain_scale = gate_gain.astype(jnp.float32)
    normed_out = (unit_gate * gain_scale).astype(jnp.bfloat16)
    out_rows = lax.psum_scatter(
        jnp.dot(normed_out, out_full, preferred_element_type=jnp.float32).astype(jnp.bfloat16),
        "tensor",
        scatter_dimension=0,
        tiled=True,
    ).astype(jnp.float32)
    hidden_out = (hidden + out_rows).astype(jnp.bfloat16)
    grad_full = lax.all_gather(out_grad, "tensor", axis=0, tiled=True)
    normed_out_grad = contract_cols(grad_full, out_full)
    out_wgrad = contract_rows(normed_out, grad_full)
    gate_wgrad = jnp.sum(normed_out_grad * unit_gate, axis=0)
    scaled_gate = normed_out_grad * gain_scale
    inner_prod = lax.psum(jnp.sum(scaled_gate * unit_gate, axis=1), "tensor")
    gated_grad = inv_gate * (scaled_gate - unit_gate * (inner_prod / full_inner)[:, None])
    (
        grad_gate,
        grad_conv,
        grad_shared,
        grad_step,
        grad_taps_inner,
        grad_taps_shared,
        grad_bias,
        grad_decay,
        grad_skip,
    ) = mixer_pull(gated_grad)
    head_grad = jnp.concatenate([grad_gate, grad_conv, grad_step], axis=1).astype(jnp.bfloat16)
    own_terms = lax.psum_scatter(
        jnp.concatenate([contract_cols(head_grad, head_mat), grad_shared], axis=1),
        "tensor",
        scatter_dimension=0,
        tiled=True,
    )
    shared_own = own_terms[:, model_dim:].astype(jnp.bfloat16)
    normed_grad = own_terms[:, :model_dim] + contract_cols(shared_own, shared_mat)
    head_wgrad = contract_rows(normed, head_grad)
    inner_wgrad = jnp.stack(
        [head_wgrad[:, :local_inner], head_wgrad[:, local_inner : 2 * local_inner]], axis=1
    )
    step_wgrad = head_wgrad[:, 2 * local_inner :]
    shared_wgrad = contract_rows(normed_own, shared_own).reshape(model_dim, 2, state_size)
    norm_wgrad = jnp.sum(normed_grad * unit_in, axis=0)
    scaled_in = normed_grad * norm_scale
    hidden_grad = inv_norm * (
        scaled_in - unit_in * jnp.mean(scaled_in * unit_in, axis=-1, keepdims=True)
    ) + out_grad.astype(jnp.float32)
    taps_wgrad = grad_taps_shared.reshape(kernel_len, 2, state_size)
    inner_sum, step_sum, out_sum, shared_sum, norm_sum, taps_sum = (
        lax.psum_scatter(
            inner_wgrad.astype(jnp.bfloat16), "dp", scatter_dimension=0, tiled=True
        ).astype(jnp.float32),
        lax.psum_scatter(
            step_wgrad.astype(jnp.bfloat16), "dp", scatter_dimension=0, tiled=True
        ).astype(jnp.float32),
        lax.psum_scatter(
            out_wgrad.astype(jnp.bfloat16), "dp", scatter_dimension=1, tiled=True
        ).astype(jnp.float32),
        lax.psum_scatter(
            shared_wgrad.astype(jnp.bfloat16), "dp", scatter_dimension=0, tiled=True
        ).astype(jnp.float32),
        lax.psum_scatter(
            norm_wgrad.astype(jnp.bfloat16), "dp", scatter_dimension=0, tiled=True
        ).astype(jnp.float32),
        lax.psum_scatter(
            taps_wgrad.astype(jnp.bfloat16), "dp", scatter_dimension=2, tiled=True
        ).astype(jnp.float32),
    )
    shared_total, norm_total, taps_total = lax.psum((shared_sum, norm_sum, taps_sum), "tensor")
    conv_total, bias_total, decay_total, skip_total, gain_total = lax.psum(
        (grad_taps_inner, grad_bias, grad_decay, grad_skip, gate_wgrad), "dp"
    )
    return (
        hidden_out,
        hidden_grad,
        norm_total,
        inner_sum,
        shared_total,
        step_sum,
        conv_total,
        taps_total,
        bias_total,
        decay_total,
        skip_total,
        gain_total,
        out_sum,
    )


def solution(mesh):
    in_specs = (
        P(("dp", "tensor"), None),
        P("dp"),
        P("dp"),
        P("dp", None, "tensor"),
        P("dp", None, None),
        P("dp", "tensor"),
        P(None, "tensor"),
        P(None, None, "dp"),
        P("tensor"),
        P("tensor"),
        P("tensor"),
        P("tensor"),
        P("tensor", "dp"),
        P(("dp", "tensor"), None),
    )
    out_specs = (
        P(("dp", "tensor"), None),
        P(("dp", "tensor"), None),
        P("dp"),
        P("dp", None, "tensor"),
        P("dp", None, None),
        P("dp", "tensor"),
        P(None, "tensor"),
        P(None, None, "dp"),
        P("tensor"),
        P("tensor"),
        P("tensor"),
        P("tensor"),
        P("tensor", "dp"),
    )
    return jax.shard_map(body, mesh=mesh, in_specs=in_specs, out_specs=out_specs, check_vma=False)
```

profile of v0, /device:TPU:0, one launch (start us, length us, event | category | flops | bytes accessed | tf_op | source)
XLA Modules:
  0.0 669.5 jit_solution(2769528606647185569)
XLA Ops:
  11.6 34.9 %all-reduce.25 = bf16[768]{0:T(1024)(128)(2,1)S(1)} all-reduce(bf16[768]{0:T(1024)(128)(2,1)S(1)} %dynamic-update-slice), channel_id=1, replica_groups=mesh['dp'=16,'tensor'=2] {'dp'}, use_global_device_ids=true, to_apply=%add.25 | all-reduce | flops 768 | bytes 3072
  52.0 17.3 %all_gather.28 = bf16[4,2,128]{0,1,2:T(2,128)(2,1)S(1)} all-gather(bf16[4,2,8]{0,1,2:T(2,128)(2,1)S(1)} %copy.258), channel_id=1, replica_groups=mesh['dp'=16,'tensor'=2] {'dp'}, dimensions={2}, use_global_device_ids=true | all-gather | bytes 2176 | tf_op jit(solution)/shard_map/all_gather | solution.py:151
  69.3 19.3 %all-gather = bf16[16,48,12]{1,2,0:T(8,128)(2,1)S(1)} all-gather(bf16[1,48,12]{1,2,0:T(8,128)(2,1)S(1)} %bitcast.226), channel_id=1, replica_groups=mesh['dp'=16,'tensor'=2] {'dp'}, dimensions={0}, use_global_device_ids=true | all-gather | bytes 19584 | tf_op jit(solution)/shard_map/all_gather | solution.py:150
  89.8 19.1 %all_gather.29 = bf16[768,2,128]{2,1,0:T(2,128)(2,1)S(1)} all-gather(bf16[48,2,128]{2,1,0:T(2,128)(2,1)S(1)} %copy-done.57), channel_id=1, replica_groups=mesh['dp'=16,'tensor'=2] {'dp'}, dimensions={0}, use_global_device_ids=true | all-gather | bytes 417792 | tf_op jit(solution)/shard_map/all_gather | solution.py:149
  133.3 8.1 %fusion.31 = (f32[1024,768]{0,1:T(8,128)}, f32[1024,768]{0,1:T(8,128)}) fusion(f32[1024]{0:T(1024)S(1)} %get-tuple-element.129, f32[1021,768]{0,1:T(8,128)} %slice.175, f32[768]{0:T(1024)S(1)} %get-tuple-element.61, f32[1024]{0:T(1024)S(1)} %get-tuple-element.130, f32[1022,768]{0,1:T(8,128)} %slice.173, f32[768]{0:T(1024)S(1)} %get-tuple-element.62, ...), kind=kLoop, calls=%fused_computation.61 | loop fusion | flops 11010048 | bytes 18880512 | tf_op jit(solution)/shard_map/jvp(jit(silu))/mul | solution.py:93
  141.4 5.3 reshape.337
  146.8 5.0 fusion.38
  159.6 15.6 %bitcast_add_fusion.1 = f32[4,256,12,64]{1,3,2,0:T(8,128)S(1)} fusion(f32[4,256,12,64]{1,3,2,0:T(8,128)S(1)} %fusion.79, f32[4,256,12]{1,2,0:T(8,128)S(1)} %get-tuple-element.125, f32[4,256,12]{1,2,0:T(8,128)S(1)} %bitcast.199, f32[4,256,256]{2,1,0:T(8,128)S(1)} %copy-done.42, pred[4,256,256]{2,1,0:T(8,128)(4,1)S(1)} %copy-done.45, ...), kind=kOutput, calls=%fused_computation.42 | convolution fusion | flops 2433220608 | bytes 10895360 | tf_op jit(solution)/shard_map/jvp(ctsh,cshp->cthp)/dot_general | solution.py:47
  179.5 4.9 multiply_reduce_fusion.10
  184.4 4.9 psum.70
  189.4 6.9 %multiply_reduce_fusion.1 = (f32[768]{0:T(1024)}, f32[1024]{0:T(1024)S(1)}, f32[1024,768]{0,1:T(8,128)}) fusion(f32[1024,768]{0,1:T(8,128)} %get-tuple-element.95, f32[1024]{0:T(1024)S(1)} %add_rsqrt_fusion, f32[768]{0:T(1024)S(1)} %convert_element_type.115, bf16[1024,768]{1,0:T(8,128)(2,1)} %all-gather.12.cloned.1.call-done, ...), kind=kOutput, calls=%fused_computation.43 | convolution fusion | flops 1212676352 | bytes 9058304 | tf_op jit(solution)/shard_map/dot_general | solution.py:119
  196.3 4.9 psum.71
  201.2 9.7 %multiply_reduce_fusion.2 = (f32[768]{0:T(1024)}, f32[1024,768]{0,1:T(8,128)}, bf16[1024,768]{0,1:T(8,128)(2,1)}) fusion(f32[1024,768]{0,1:T(8,128)} %get-tuple-element.97, f32[1024]{0:T(1024)S(1)} %get-tuple-element.131, f32[1024,1548]{0,1:T(8,128)} %copy-done, f32[1024]{0:T(1024)S(1)} %broadcast_multiply_fusion.6, f32[1024,768]{0,1:T(8,128)} %get-tuple-element.95, ...), kind=kLoop, calls=%fused_computation.44 | loop fusion | flops 22019328 | bytes 20468736 | tf_op jit(solution)/shard_map/transpose(jvp())/reduce_sum | solution.py:107
  210.9 5.1 reshape.345
  220.2 6.0 fusion.92
  226.3 21.9 %fusion.9 = (f32[4,256,12]{1,2,0:T(8,128)}, f32[4,256,12]{1,2,0:T(8,128)}, f32[4,256,12]{1,2,0:T(8,128)}, f32[4,256,256]{2,1,0:T(8,128)}) fusion(f32[4,256,12]{1,2,0:T(8,128)S(1)} %copy-done.53, f32[4,256,12]{1,2,0:T(8,128)S(1)} %bitcast.200, f32[4,256,256]{2,1,0:T(8,128)S(1)} %copy-done.43, pred[4,256,256]{2,1,0:T(8,128)(4,1)S(1)} %copy-done.46, ...), kind=kOutput, calls=%fused_computation.12 | convolution fusion | flops 2462806016 | bytes 8896512 | tf_op jit(solution)/shard_map/transpose(jvp(ctsh,cshp->cthp))/dot_general | solution.py:47
  251.4 9.9 %fusion.97 = f32[12,4,4]{2,1,0:T(4,128)S(1)} fusion(f32[4,12,64,128]{3,2,1,0:T(8,128)S(1)} %fusion.38, f32[12,64,128,4]{2,1,0,3:T(8,128)S(1)} %fusion.72), kind=kOutput, calls=%fused_computation.131 | convolution fusion | flops 18874368 | bytes 3146496 | tf_op jit(solution)/shard_map/transpose(jvp(deh,ehpn->dhpn))/dot_general | solution.py:64
  261.2 4.1 convolution_bitcast_fusion
  265.4 6.0 fusion.87
  271.4 4.8 multiply_reduce_fusion.8
  283.3 12.9 %bitcast_add_fusion = f32[4,256,12,64]{1,3,2,0:T(8,128)S(1)} fusion(f32[4,256,12,64]{1,3,2,0:T(8,128)} %get-tuple-element.136, f32[4,256,12]{1,2,0:T(8,128)S(1)} %copy-done.54, f32[4,256,12]{1,2,0:T(8,128)S(1)} %bitcast.201, f32[4,256,256]{2,1,0:T(8,128)S(1)} %copy-done.44, pred[4,256,256]{2,1,0:T(8,128)(4,1)S(1)} %copy-done.47, ...), kind=kOutput, calls=%fused_computation.38 | convolution fusion | flops 2433220608 | bytes 10895360 | tf_op jit(solution)/shard_map/transpose(jvp(ctsh,cshp->cthp))/dot_general | solution.py:47
  301.1 4.3 multiply_reduce_fusion.6
  305.6 5.4 multiply_reduce_fusion.5
  312.5 10.1 %reduce-window.16 = f32[4,12,2,128]{3,1,2,0:T(8,128)S(1)} reduce-window(f32[4,12,2,128]{3,1,2,0:T(8,128)S(1)} %copy.296, f32[]{:T(128)} %constant.19.clone.1), window={size=1x1x1x128 pad=0_0x0_0x0_0x0_127}, to_apply=%region_14.15 | reduce-window | flops 1560576 | bytes 98308 | tf_op jit(solution)/shard_map/reduce-window.2
  346.0 5.1 convolution_convert_fusion
  366.6 4.7 copy.306
  372.2 27.3 %reduce-scatter.10.cloned.1.call-done = f32[512,1024]{1,0:T(8,128)} async-done(((f32[1024,1024]{1,0:T(8,128)}), f32[512,1024]{1,0:T(8,128)}) %reduce-scatter.10.cloned.1.call-update) | async-done | bytes 2097168 | tf_op jit(solution)/shard_map/reduce_scatter | solution.py:211
  402.4 61.1 %all-reduce.30 = (f32[4,768]{1,0:T(4,128)}, f32[12]{0:T(128)}, f32[12]{0:T(128)}, f32[12]{0:T(128)}, f32[768]{0:T(1024)}) all-reduce(f32[4,768]{1,0:T(4,128)S(1)} %pad_add_fusion, f32[12]{0:T(128)S(1)} %copy-done.86, f32[12]{0:T(128)S(1)} %negate_multiply_fusion, ...), channel_id=1, replica_groups=mesh['dp'=16,'tensor'=2] {'dp'}, use_global_device_ids=true, to_apply=%region_30.31 | all-reduce | flops 3876 | bytes 31008 | tf_op jit(solution)/shard_map/psum | solution.py:252
  464.9 52.7 %reduce-scatter.12.cloned.1.call-done = bf16[768,48]{0,1:T(8,128)(2,1)} async-done(((bf16[768,768]{0,1:T(8,128)(2,1)}), bf16[768,48]{0,1:T(8,128)(2,1)}) %reduce-scatter.12.cloned.1.call-update) | async-done | bytes 73744 | tf_op jit(solution)/shard_map/reduce_scatter | solution.py:238
  522.0 29.7 %all-reduce.32 = (bf16[768]{0:T(1024)(128)(2,1)S(1)}, bf16[4,2,128]{2,1,0:T(2,128)(2,1)S(1)}) all-reduce(bf16[768]{0:T(1024)(128)(2,1)} %get-tuple-element.58, bf16[4,2,128]{2,1,0:T(2,128)(2,1)S(1)} %convert_element_type.129), channel_id=4, replica_groups=mesh['dp'=16,'tensor'=2] {'dp'}, use_global_device_ids=true, to_apply=%region_20.21.clone | all-reduce | flops 1792 | bytes 7168
  555.0 95.9 %all-reduce.36.cloned.1.call-done = (bf16[768,2,128]{2,1,0:T(2,128)(2,1)}, bf16[768,2,768]{2,1,0:T(2,128)(2,1)}) async-done(((bf16[768,2,128]{2,1,0:T(2,128)(2,1)}, bf16[768,2,768]{2,1,0:T(2,128)(2,1)}), (bf16[768,2,128]{2,1,0:T(2,128)(2,1)}, bf16[768,2,768]{2,1,0:T(2,128)(2,1)})) %all-reduce.36.cloned.1.call-update) | async-done | bytes 2752528
  653.3 9.3 %all-reduce.31 = (f32[48]{0:T(128)}, f32[48,2,128]{2,1,0:T(2,128)}, f32[4,2,8]{2,1,0:T(2,128)}) all-reduce(f32[48]{0:T(128)S(1)} %dynamic-slice_convert_fusion.3, f32[48,2,128]{2,1,0:T(2,128)S(1)} %dynamic-slice_convert_fusion.1, f32[4,2,8]{2,1,0:T(2,128)S(1)} %dynamic-slice_convert_fusion.2), channel_id=1, replica_groups=mesh['dp'=16,'tensor'=2] {'tensor'}, use_global_device_ids=true, to_apply=%region_21.22 | all-reduce | flops 12400 | bytes 99200 | tf_op jit(solution)/shard_map/psum | solution.py:251
  (352 shorter events, 119.7 us)
Async XLA Ops:
  7.2 41.7 %copy-start.50 = (bf16[48,2,768]{2,1,0:T(2,128)(2,1)S(1)}, bf16[48,2,768]{2,1,0:T(2,128)(2,1)}, u32[]{:S(2)}) copy-start(bf16[48,2,768]{2,1,0:T(2,128)(2,1)} %param.17) | copy-start | bytes 442372
  7.2 43.8 %copy-start.51 = (s32[1024]{0:T(1024)S(1)}, s32[1024]{0:T(1024)}, u32[]{:S(2)}) copy-start(s32[1024]{0:T(1024)} %param.15) | copy-start | bytes 12292
  7.2 44.5 %copy-start.95 = (f32[12]{0:T(128)S(1)}, f32[12]{0:T(128)}, u32[]{:S(2)}) copy-start(f32[12]{0:T(128)} %param.23) | copy-start | bytes 148
  7.2 44.5 %copy-start.87 = (bf16[768]{0:T(1024)(128)(2,1)S(1)}, bf16[768]{0:T(1024)(128)(2,1)}, u32[]{:S(2)}) copy-start(bf16[768]{0:T(1024)(128)(2,1)} %param.25) | copy-start | bytes 4612
  7.2 44.5 %copy-start.88 = (bf16[4,2,8]{2,1,0:T(2,128)(2,1)S(1)}, bf16[4,2,8]{2,1,0:T(2,128)(2,1)}, u32[]{:S(2)}) copy-start(bf16[4,2,8]{2,1,0:T(2,128)(2,1)} %param.21) | copy-start | bytes 388
  7.2 44.6 %copy-start.92 = (f32[12]{0:T(128)S(1)}, f32[12]{0:T(128)}, u32[]{:S(2)}) copy-start(f32[12]{0:T(128)} %param.24) | copy-start | bytes 148
  7.2 44.7 %copy-start.77 = (bf16[4,768]{1,0:T(4,128)(2,1)S(1)}, bf16[4,768]{1,0:T(4,128)(2,1)}, u32[]{:S(2)}) copy-start(bf16[4,768]{1,0:T(4,128)(2,1)} %param.20) | copy-start | bytes 18436
  7.3 62.1 %copy-start.82 = (bf16[48,12]{0,1:T(8,128)(2,1)S(1)}, bf16[48,12]{0,1:T(8,128)(2,1)}, u32[]{:S(2)}) copy-start(bf16[48,12]{0,1:T(8,128)(2,1)} %param.19) | copy-start | bytes 3460
  7.3 82.6 %copy-start.57 = (bf16[48,2,128]{2,1,0:T(2,128)(2,1)S(1)}, bf16[48,2,128]{2,1,0:T(2,128)(2,1)}, u32[]{:S(2)}) copy-start(bf16[48,2,128]{2,1,0:T(2,128)(2,1)} %param.18) | copy-start | bytes 73732
  7.3 102.4 %all-gather.6.cloned.1.call-start = ((), (), s32[]{:S(2)}) async-start(), calls=%async_computation.4 | async-start | bytes 2359296 | tf_op jit(solution)/shard_map/all_gather | solution.py:159
  8.8 42.2 %copy-start.58 = (f32[512]{0:T(512)}, f32[512]{0:T(512)S(1)}, u32[]{:S(2)}) copy-start(f32[512]{0:T(512)S(1)} %add_rsqrt_fusion.1) | copy-start | bytes 6148
  48.8 69.8 %all-gather.8.cloned.1.call-start = ((), (), s32[]{:S(2)}) async-start(), calls=%async_computation.5 | async-start | bytes 2506752 | tf_op jit(solution)/shard_map/all_gather | solution.py:148
  49.6 139.7 %all-gather.12.cloned.1.call-start = ((), (), s32[]{:S(2)}) async-start(), calls=%async_computation.8 | async-start | bytes 2359296 | tf_op jit(solution)/shard_map/all_gather | solution.py:192
  50.3 139.0 %all-gather.10.cloned.1.call-start = ((), (), s32[]{:S(2)}) async-start(), calls=%async_computation.6 | async-start | bytes 1253376 | tf_op jit(solution)/shard_map/all_gather | solution.py:152
  50.9 348.6 %reduce-scatter.10.cloned.1.call-start = ((), (), s32[]{:S(2)}) async-start(), calls=%async_computation.9 | async-start | bytes 6291456 | tf_op jit(solution)/shard_map/reduce_scatter | solution.py:211
  51.0 81.8 %copy-start.97 = (pred[4,4]{0,1:T(4,128)(4,1)}, pred[4,4]{0,1:T(4,128)(4,1)S(1)}, u32[]{:S(2)}) copy-start(pred[4,4]{0,1:T(4,128)(4,1)S(1)} %iota_compare_fusion.1) | copy-start | bytes 52
  51.5 81.3 %copy-start.93 = (pred[4,4]{1,0:T(4,128)(4,1)}, pred[4,4]{1,0:T(4,128)(4,1)S(1)}, u32[]{:S(2)}) copy-start(pred[4,4]{1,0:T(4,128)(4,1)S(1)} %get-tuple-element.138) | copy-start | bytes 52
  51.5 81.6 %copy-start.89 = (pred[4,4]{1,0:T(4,128)(4,1)}, pred[4,4]{1,0:T(4,128)(4,1)S(1)}, u32[]{:S(2)}) copy-start(pred[4,4]{1,0:T(4,128)(4,1)S(1)} %get-tuple-element.139) | copy-start | bytes 52
  51.7 78.1 %copy-start.85 = (f32[12]{0:T(128)}, f32[12]{0:T(128)S(1)}, u32[]{:S(2)}) copy-start(f32[12]{0:T(128)S(1)} %exponential_negate_fusion) | copy-start | bytes 148
  51.7 149.5 %copy-start.63 = (f32[768]{0:T(1024)}, f32[768]{0:T(1024)S(1)}, u32[]{:S(2)}) copy-start(f32[768]{0:T(1024)S(1)} %convert_element_type.115) | copy-start | bytes 9220
  52.0 81.3 %copy-start.55 = (f32[768]{0:T(1024)}, f32[768]{0:T(1024)S(1)}, u32[]{:S(2)}) copy-start(f32[768]{0:T(1024)S(1)} %get-tuple-element.60) | copy-start | bytes 9220
  88.9 31.6 %copy-start.48 = (bf16[16,48,12]{2,1,0:T(8,128)(2,1)}, bf16[16,48,12]{2,1,0:T(8,128)(2,1)S(1)}, u32[]{:S(2)}) copy-start(bf16[16,48,12]{2,1,0:T(8,128)(2,1)S(1)} %copy.319) | copy-start | bytes 55300
  346.0 117.5 %reduce-scatter.14.cloned.1.call-start = ((), (), s32[]{:S(2)}) async-start(), calls=%async_computation.11 | async-start | bytes 208896
  353.4 164.2 %reduce-scatter.12.cloned.1.call-start = ((), (), s32[]{:S(2)}) async-start(), calls=%async_computation.10 | async-start | bytes 1253376 | tf_op jit(solution)/shard_map/reduce_scatter | solution.py:238
  357.9 194.0 %reduce-scatter.8.cloned.1.call-start = ((), (), s32[]{:S(2)}) async-start(), calls=%async_computation.7 | async-start | bytes 2359296 | tf_op jit(solution)/shard_map/reduce_scatter | solution.py:185
  362.0 288.8 %all-reduce.36.cloned.1.call-start = ((), (), s32[]{:S(2)}) async-start(), calls=%async_computation.12 | async-start | bytes 5505024
  366.6 32.9 %copy-start.26 = (bf16[512,768]{1,0:T(8,128)(2,1)S(1)}, bf16[512,768]{1,0:T(8,128)(2,1)}, u32[]{:S(2)}) copy-start(bf16[512,768]{1,0:T(8,128)(2,1)} %fusion.60) | copy-start | bytes 2359300
  371.3 31.1 %copy-start.83 = (f32[768]{0:T(1024)S(1)}, f32[768]{0:T(1024)}, u32[]{:S(2)}) copy-start(f32[768]{0:T(1024)} %get-tuple-element.56) | copy-start | bytes 9220
  371.3 147.9 %copy-start.25 = (bf16[512,768]{1,0:T(8,128)(2,1)S(1)}, bf16[512,768]{1,0:T(8,128)(2,1)}, u32[]{:S(2)}) copy-start(bf16[512,768]{1,0:T(8,128)(2,1)} %param.14) | copy-start | bytes 2359300
  371.3 147.9 %copy-start.35 = (bf16[768,2,128]{2,1,0:T(2,128)(2,1)S(1)}, bf16[768,2,128]{2,1,0:T(2,128)(2,1)}, u32[]{:S(2)}) copy-start(bf16[768,2,128]{2,1,0:T(2,128)(2,1)} %copy-done.34) | copy-start | bytes 1179652
  371.3 147.8 %copy-start.59 = (f32[512]{0:T(512)S(1)}, f32[512]{0:T(512)}, u32[]{:S(2)}) copy-start(f32[512]{0:T(512)} %copy-done.58) | copy-start | bytes 6148
  402.1 149.8 %copy-start.29 = (bf16[512,768]{1,0:T(8,128)(2,1)S(1)}, bf16[512,768]{1,0:T(8,128)(2,1)}, u32[]{:S(2)}) copy-start(bf16[512,768]{1,0:T(8,128)(2,1)} %param.27) | copy-start | bytes 2359300
  (76 other events, 634.2 us)
Sparse Core Ops, SparseCore 0:
  49.0 24.5 all-gather.5
  76.4 42.2 all-gather.7
  120.2 26.1 all-gather.11
  148.6 38.3 all-gather.9
  346.1 53.3 reduce-scatter.9
  403.4 53.3 reduce-scatter.13
  460.4 57.1 reduce-scatter.11
  520.4 25.0 reduce-scatter.7
  549.3 101.4 all-reduce.35
where the time goes:
time: 679 us; the launch traced here: 670 us
  blocking collectives  201 us (30%)
  waiting for transfers between devices  179 us (26%)
  matrix products  138 us (20%)
  other arithmetic  81.7 us (12%)
  local copies, waits for them, and re-layouts  52.2 us (8%)
  between operations  17.7 us (3%)
    unnamed x11, waiting for transfers between devices  97.2 us
    unnamed x2, blocking collectives  64.6 us
    psum x1, blocking collectives, body(): lax.psum((grad_taps_inner, grad_bias, grad_decay, grad_skip, gate_wgrad),...  61.1 us
    reduce_scatter x1, waiting for transfers between devices, body(): lax.psum_scatter(out_wgrad.astype(jnp.bfloat16), 'dp', scatter_dimension=...  52.7 us
    dot_general x3, matrix products, ssd_core(): jnp.einsum('ctsh,cshp->cthp', mixing, x_blocks, precision=highest)  50.4 us
    reduce_scatter x1, waiting for transfers between devices, body(): lax.psum_scatter(jnp.concatenate([contract_cols(head_grad, head_mat), gra...  27.3 us
    all_gather x1, blocking collectives, body(): lax.all_gather(proj_step, 'dp', axis=0, tiled=True)  19.3 us
    all_gather x1, blocking collectives, body(): lax.all_gather(proj_shared, 'dp', axis=0, tiled=True)  19.1 us
  transfers between devices with their start and end apart: 9, of which 4 were waited for; matrix products, arithmetic and copies ran while one was open for 16% of the time, Pallas kernels for 0%

commit v1 on v0

v1 whole, which is shorter than its diff:
```python
from functools import partial

import jax
import jax.numpy as jnp
from jax import lax
from jax.experimental import pallas as pl
from jax.experimental.pallas import tpu as pltpu
from jax.sharding import PartitionSpec as P

HEAD_DIM = 64
CHUNK = 128
LANES = 128
epsilon = 1e-05
f32 = jnp.float32
bf16 = jnp.bfloat16
highest = lax.Precision.HIGHEST


def dot_nn(a, b):
    return lax.dot_general(a, b, (((1,), (0,)), ((), ())), preferred_element_type=f32)


def dot_nt(a, b):
    return lax.dot_general(a, b, (((1,), (1,)), ((), ())), preferred_element_type=f32)


def dot_tn(a, b):
    return lax.dot_general(a, b, (((0,), (0,)), ((), ())), preferred_element_type=f32)


def dot_exact(a, b):
    return lax.dot_general(
        a, b, (((1,), (0,)), ((), ())), preferred_element_type=f32, precision=highest
    )


def dot_split(a, b):
    high = a.astype(bf16)
    rest = (a - high.astype(f32)).astype(bf16)
    return dot_nn(high, b) + dot_nn(rest, b)


def sigmoid(v):
    return 1.0 / (1.0 + jnp.exp(-v))


def softplus(v):
    return jnp.maximum(v, 0.0) + jnp.log1p(jnp.exp(-jnp.abs(v)))


def halves(lane_low, values, head):
    return jnp.where(lane_low, values[:, head : head + 1], values[:, head + 1 : head + 2])


def back_shift(window, offset):
    return pltpu.roll(window, offset, 0)[8:, :]


def ahead_shift(window, offset):
    rows = window.shape[0]
    return pltpu.roll(window, rows - offset, 0)[: rows - 8, :]


def conv_rows(window, taps, aux):
    total = taps[3:4, :] * window[8:, :]
    for offset in range(1, 4):
        total = total + taps[3 - offset : 4 - offset, :] * (
            back_shift(window, offset) * aux[:, offset : offset + 1]
        )
    return total


def forward_kernel(
    proj_ref,
    tapi_ref,
    taps_ref,
    bias_ref,
    rate_ref,
    skip_ref,
    aux_ref,
    segr_ref,
    mixed_ref,
    u_ref,
    su_ref,
    entry_ref,
    sums_ref,
    state_ref,
    carry_ref,
    scarry_ref,
    xw_ref,
):
    length, width = mixed_ref.shape
    chunks = length // CHUNK
    pairs = width // LANES
    shared_size = su_ref.shape[1]
    state_size = shared_size // 2
    shared_cols = slice(2 * width, 2 * width + shared_size)
    step_cols = slice(2 * width + shared_size, 2 * width + shared_size + LANES)
    state_ref[...] = jnp.zeros_like(state_ref)
    carry_ref[...] = jnp.zeros_like(carry_ref)
    scarry_ref[...] = jnp.zeros_like(scarry_ref)
    rows = lax.broadcasted_iota(jnp.int32, (CHUNK, CHUNK), 0)
    cols = lax.broadcasted_iota(jnp.int32, (CHUNK, CHUNK), 1)
    lower = rows >= cols
    summing = lower.astype(f32)
    lane_low = lax.broadcasted_iota(jnp.int32, (CHUNK, LANES), 1) < HEAD_DIM

    def chunk_step(chunk, _):
        start = pl.multiple_of(chunk * CHUNK, CHUNK)
        here = pl.ds(start, CHUNK)
        aux = aux_ref[here, :]
        live = aux[:, 7:8]
        same = lower & (aux[:, 0:1] == segr_ref[pl.ds(chunk, 1), :])
        shared_now = proj_ref[here, shared_cols]
        su = conv_rows(jnp.concatenate([scarry_ref[...], shared_now], axis=0), taps_ref[...], aux)
        scarry_ref[...] = shared_now[CHUNK - 8 :, :]
        su_ref[here, :] = su
        shared = (su * sigmoid(su)).astype(bf16)
        b_rows = shared[:, :state_size]
        c_rows = shared[:, state_size:]
        scores = jnp.where(same, dot_nt(c_rows, b_rows), 0.0)
        step = softplus(proj_ref[here, step_cols] + bias_ref[...]) * live
        decay = dot_exact(summing, step * rate_ref[...])
        decay_t = decay.T
        last = decay[CHUNK - 1 :, :]
        entry_scale = jnp.exp(decay) * aux[:, 8:9]
        end_scale = jnp.exp(last - decay) * aux[:, 9:10]
        keep = jnp.exp(last) * aux[:1, 10:11]
        state = state_ref[...]
        state_low = state.astype(bf16)
        entry_ref[pl.ds(chunk, 1)] = state_low[None]
        past = dot_nn(c_rows, state_low)
        square = jnp.zeros((CHUNK, LANES), f32)
        for pair in range(pairs):
            lanes = slice(pair * LANES, (pair + 1) * LANES)
            head = 2 * pair
            now = proj_ref[here, width + pair * LANES : width + (pair + 1) * LANES]
            window = jnp.concatenate([carry_ref[:, lanes], now], axis=0)
            carry_ref[:, lanes] = now[CHUNK - 8 :, :]
            u = conv_rows(window, tapi_ref[:, lanes], aux)
            u_ref[here, lanes] = u
            x = u * sigmoid(u)
            scaled = x * halves(lane_low, step, head)
            mixing = jnp.concatenate(
                [
                    (
                        scores
                        * jnp.exp(
                            jnp.minimum(decay[:, h : h + 1] - decay_t[h : h + 1, :], 0.0)
                        )
                    ).astype(bf16)
                    for h in (head, head + 1)
                ],
                axis=1,
            )
            stacked = jnp.concatenate(
                [jnp.where(lane_low, scaled, 0.0), jnp.where(lane_low, 0.0, scaled)], axis=0
            ).astype(bf16)
            inside = dot_nn(mixing, stacked)
            xw_ref[:, lanes] = (scaled * halves(lane_low, end_scale, head)).astype(bf16)
            mixed = (
                inside
                + past[:, lanes] * halves(lane_low, entry_scale, head)
                + skip_ref[:, lanes] * x
            ) * live
            mixed_ref[here, lanes] = mixed
            state_ref[:, lanes] = state[:, lanes] * halves(
                lane_low[:1], keep, head
            )
            gate = proj_ref[here, lanes]
            gated = mixed * gate * sigmoid(gate)
            square = square + gated * gated
        state_ref[...] += dot_tn(b_rows, xw_ref[...])
        sums_ref[here, :] = jnp.sum(square, axis=1, keepdims=True)
        return 0

    lax.fori_loop(0, chunks, chunk_step, 0)


def silu_slope(v, s):
    return s * (1.0 + v * (1.0 - s))


def backward_kernel(
    proj_ref,
    mixed_ref,
    u_ref,
    su_ref,
    entry_ref,
    nog_ref,
    sums_ref,
    tapi_ref,
    taps_ref,
    bias_ref,
    rate_ref,
    skip_ref,
    gain_ref,
    aux_ref,
    segr_ref,
    place_ref,
    dproj_ref,
    wide_ref,
    shared_ref,
    state_ref,
    ahead_ref,
    sahead_ref,
    xw_ref,
    ge_ref,
    row_ref,
    proda_ref,
    prodb_ref,
    *,
    full_inner,
):
    length, width = mixed_ref.shape
    chunks = length // CHUNK
    pairs = width // LANES
    shared_size = su_ref.shape[1]
    state_size = shared_size // 2
    shared_cols = slice(2 * width, 2 * width + shared_size)
    step_cols = slice(2 * width + shared_size, 2 * width + shared_size + LANES)
    for ref in (state_ref, ahead_ref, sahead_ref, row_ref, wide_ref, shared_ref):
        ref[...] = jnp.zeros_like(ref)
    rows = lax.broadcasted_iota(jnp.int32, (CHUNK, CHUNK), 0)
    cols = lax.broadcasted_iota(jnp.int32, (CHUNK, CHUNK), 1)
    upper = rows <= cols
    summing = (rows >= cols).astype(f32)
    unsumming = upper.astype(f32)
    last_row = (lax.broadcasted_iota(jnp.int32, (CHUNK, LANES), 0) == CHUNK - 1).astype(f32)
    lane_ids = lax.broadcasted_iota(jnp.int32, (CHUNK, LANES), 1)
    lane_low = lane_ids < HEAD_DIM

    def chunk_step(step_index, _):
        chunk = chunks - 1 - step_index
        start = pl.multiple_of(chunk * CHUNK, CHUNK)
        here = pl.ds(start, CHUNK)
        aux = aux_ref[here, :]
        live = aux[:, 7:8]
        same = upper & (aux[:, 0:1] == segr_ref[pl.ds(chunk, 1), :])
        sums = sums_ref[here, :]
        inv = lax.rsqrt(sums[:, 0:1] / full_inner + epsilon)
        mean = inv * sums[:, 1:2] / full_inner
        su = su_ref[here, :]
        su_sig = sigmoid(su)
        shared = (su * su_sig).astype(bf16)
        b_rows = shared[:, :state_size]
        c_rows = shared[:, state_size:]
        scores = jnp.where(same, dot_nt(b_rows, c_rows), 0.0)
        pre = proj_ref[here, step_cols] + bias_ref[...]
        step = softplus(pre) * live
        rate = rate_ref[...]
        decay = dot_exact(summing, step * rate)
        decay_t = decay.T
        last = decay[CHUNK - 1 :, :]
        entry_scale = jnp.exp(decay) * aux[:, 8:9]
        end_scale = jnp.exp(last - decay) * aux[:, 9:10]
        keep = jnp.exp(last) * aux[:1, 10:11]
        entry = entry_ref[pl.ds(chunk, 1)][0]
        dstate = state_ref[...]
        dstate_low = dstate.astype(bf16)
        past = dot_nn(c_rows, entry)
        bds = dot_nn(b_rows, dstate_low)
        score_grad = jnp.zeros((CHUNK, CHUNK), f32)
        col_part = jnp.zeros((CHUNK, LANES), f32)
        for pair in range(pairs):
            lanes = slice(pair * LANES, (pair + 1) * LANES)
            head = 2 * pair
            inner_lanes = slice(width + pair * LANES, width + (pair + 1) * LANES)
            gate = proj_ref[here, lanes]
            gate_sig = sigmoid(gate)
            gate_silu = gate * gate_sig
            mixed = mixed_ref[here, lanes]
            unit = mixed * gate_silu * inv
            nog = nog_ref[here, lanes]
            gg = inv * (nog * gain_ref[:, lanes] - unit * mean)
            dproj_ref[here, lanes] = (gg * mixed * silu_slope(gate, gate_sig)).astype(bf16)
            g = gg * gate_silu * live
            u = u_ref[here, lanes]
            u_sig = sigmoid(u)
            x = u * u_sig
            step_c = halves(lane_low, step, head)
            scaled = x * step_c
            stacked = jnp.concatenate(
                [jnp.where(lane_low, scaled, 0.0), jnp.where(lane_low, 0.0, scaled)], axis=0
            ).astype(bf16)
            g_low = g.astype(bf16)
            dmix = dot_nt(stacked, g_low)
            mixing = []
            for k, h in enumerate((head, head + 1)):
                decays = jnp.exp(jnp.minimum(decay_t[h : h + 1, :] - decay[:, h : h + 1], 0.0))
                dmix_h = dmix[k * CHUNK : (k + 1) * CHUNK, :]
                score_grad = score_grad + dmix_h * decays
                mixing_h = scores * decays
                mixing.append(mixing_h.astype(bf16))
                both = mixing_h * dmix_h
                col_part = jnp.where(lane_ids == h, jnp.sum(both, axis=1, keepdims=True), col_part)
                row_ref[h : h + 1, :] = jnp.sum(both, axis=0, keepdims=True)
            g_stacked = jnp.concatenate(
                [jnp.where(lane_low, g, 0.0), jnp.where(lane_low, 0.0, g)], axis=0
            ).astype(bf16)
            end_c = halves(lane_low, end_scale, head)
            entry_c = halves(lane_low, entry_scale, head)
            keep_c = halves(lane_low[:1], keep, head)
            from_state = end_c * bds[:, lanes]
            dscaled = dot_nn(jnp.concatenate(mixing, axis=1), g_stacked) + from_state
            xw_ref[:, lanes] = (scaled * end_c).astype(bf16)
            q = scaled * from_state
            ge = g * entry_c
            ge_ref[:, lanes] = ge.astype(bf16)
            dstate_p = dstate[:, lanes]
            tail = jnp.sum(q, axis=0, keepdims=True) + keep_c * jnp.sum(
                dstate_p * entry[:, lanes].astype(f32), axis=0, keepdims=True
            )
            proda_ref[:, lanes] = x * dscaled
            prodb_ref[:, lanes] = ge * past[:, lanes] - q + last_row * tail
            state_ref[:, lanes] = dstate_p * keep_c
            dx = step_c * dscaled + skip_ref[:, lanes] * g
            du = dx * silu_slope(u, u_sig)
            window = jnp.concatenate([du, ahead_ref[:, lanes]], axis=0)
            ahead_ref[:, lanes] = du[:8, :]
            cin = proj_ref[here, inner_lanes]
            taps = tapi_ref[:, lanes]
            dcin = taps[3:4, :] * du
            wide_ref[3:4, lanes] += jnp.sum(cin * du, axis=0, keepdims=True)
            for offset in range(1, 4):
                moved = ahead_shift(window, offset) * aux[:, 3 + offset : 4 + offset]
                dcin = dcin + taps[3 - offset : 4 - offset, :] * moved
                wide_ref[3 - offset : 4 - offset, lanes] += jnp.sum(
                    cin * moved, axis=0, keepdims=True
                )
            dproj_ref[here, inner_lanes] = dcin.astype(bf16)
            wide_ref[4:5, lanes] += jnp.sum(nog * unit, axis=0, keepdims=True)
            wide_ref[5:6, lanes] += jnp.sum(g * x, axis=0, keepdims=True)
        score_low = jnp.where(same, score_grad, 0.0).astype(bf16)
        ge_all = ge_ref[...]
        db = dot_nn(score_low, c_rows) + dot_nt(xw_ref[...], dstate_low)
        dc = dot_tn(score_low, b_rows) + dot_nt(ge_all, entry)
        state_ref[...] += dot_tn(c_rows, ge_all)
        ds = jnp.concatenate([db, dc], axis=1) * silu_slope(su, su_sig)
        window = jnp.concatenate([ds, sahead_ref[...]], axis=0)
        sahead_ref[...] = ds[:8, :]
        taps = taps_ref[...]
        sin = proj_ref[here, shared_cols]
        dsin = taps[3:4, :] * ds
        shared_ref[3:4, :] += jnp.sum(sin * ds, axis=0, keepdims=True)
        for offset in range(1, 4):
            moved = ahead_shift(window, offset) * aux[:, 3 + offset : 4 + offset]
            dsin = dsin + taps[3 - offset : 4 - offset, :] * moved
            shared_ref[3 - offset : 4 - offset, :] += jnp.sum(sin * moved, axis=0, keepdims=True)
        dproj_ref[here, shared_cols] = dsin.astype(bf16)
        place = place_ref[...]
        ddecay = row_ref[...].T - col_part + dot_split(prodb_ref[...], place)
        dlog = dot_exact(unsumming, ddecay)
        dstep = (dot_split(proda_ref[...], place) + rate * dlog) * live * sigmoid(pre)
        dproj_ref[here, step_cols] = dstep.astype(bf16)
        wide_ref[6:7, :LANES] += jnp.sum(dstep, axis=0, keepdims=True)
        wide_ref[6:7, LANES : 2 * LANES] += jnp.sum(step * dlog, axis=0, keepdims=True) * rate
        return 0

    lax.fori_loop(0, chunks, chunk_step, 0)


def token_facts(segments):
    length = segments.shape[0]
    chunks = length // CHUNK
    columns = [segments]
    for offset in range(1, 4):
        earlier = jnp.concatenate([jnp.full((offset,), -1, jnp.int32), segments[: length - offset]])
        columns.append(earlier == segments)
    for offset in range(1, 4):
        later = jnp.concatenate([segments[offset:], jnp.full((offset,), -1, jnp.int32)])
        columns.append(later == segments)
    columns.append(segments != 0)
    blocks = segments.reshape(chunks, CHUNK)
    last = blocks[:, CHUNK - 1 :]
    prior = jnp.concatenate([jnp.full((1, 1), -1, jnp.int32), last[: chunks - 1]], axis=0)
    columns.append((blocks == prior).reshape(length))
    columns.append((blocks == last).reshape(length))
    columns.append(jnp.broadcast_to(last == prior, blocks.shape).reshape(length))
    columns += [jnp.zeros_like(segments)] * 5
    aux = jnp.stack([c.astype(f32) for c in columns], axis=1)
    return aux, blocks.astype(f32)


def run_forward(proj, tapi, taps, bias, rate, skip, aux, segr):
    length = proj.shape[0]
    width = tapi.shape[1]
    shared_size = taps.shape[1]
    chunks = length // CHUNK
    sds = jax.ShapeDtypeStruct
    return pl.pallas_call(
        forward_kernel,
        out_shape=(
            sds((length, width), f32),
            sds((length, width), f32),
            sds((length, shared_size), f32),
            sds((chunks, shared_size // 2, width), bf16),
            sds((length, 1), f32),
        ),
        scratch_shapes=[
            pltpu.VMEM((shared_size // 2, width), f32),
            pltpu.VMEM((8, width), f32),
            pltpu.VMEM((8, shared_size), f32),
            pltpu.VMEM((CHUNK, width), bf16),
        ],
        name="scan_forward",
    )(proj, tapi, taps, bias, rate, skip, aux, segr)


def run_backward(
    proj, mixed, u, su, entry, nog, sums, tapi, taps, bias, rate, skip, gain, aux, segr, place, full_inner
):
    length, width = mixed.shape
    shared_size = su.shape[1]
    sds = jax.ShapeDtypeStruct
    return pl.pallas_call(
        partial(backward_kernel, full_inner=float(full_inner)),
        out_shape=(
            sds(proj.shape, bf16),
            sds((8, width), f32),
            sds((8, shared_size), f32),
        ),
        scratch_shapes=[
            pltpu.VMEM((shared_size // 2, width), f32),
            pltpu.VMEM((8, width), f32),
            pltpu.VMEM((8, shared_size), f32),
            pltpu.VMEM((CHUNK, width), bf16),
            pltpu.VMEM((CHUNK, width), bf16),
            pltpu.VMEM((LANES, CHUNK), f32),
            pltpu.VMEM((CHUNK, width), f32),
            pltpu.VMEM((CHUNK, width), f32),
        ],
        name="scan_backward",
    )(proj, mixed, u, su, entry, nog, sums, tapi, taps, bias, rate, skip, gain, aux, segr, place)


def gather_rows(shard):
    count = lax.axis_size("dp")
    index = lax.axis_index("dp")
    whole = shard[None]
    bit = count // 2
    while bit:
        other = lax.ppermute(whole, "dp", [(i, i ^ bit) for i in range(count)])
        mine = (index & bit) == 0
        first = jnp.where(mine, whole, other)
        second = jnp.where(mine, other, whole)
        whole = jnp.stack([first, second], axis=1)
        whole = whole.reshape((-1,) + shard.shape)
        bit //= 2
    return whole.reshape((-1,) + shard.shape[1:])


def scatter_rows(partial_sum):
    count = lax.axis_size("dp")
    index = lax.axis_index("dp")
    rows = partial_sum.shape[0] // count
    total = partial_sum.reshape((count, rows) + partial_sum.shape[1:])
    bit = 1
    while bit < count:
        total = total.reshape((-1, 2) + total.shape[1:])
        side = jnp.where((index & bit) == 0, 0, 1)
        keep = lax.dynamic_index_in_dim(total, side, 1, keepdims=False)
        send = lax.dynamic_index_in_dim(total, 1 - side, 1, keepdims=False)
        got = lax.ppermute(send.astype(bf16), "dp", [(i, i ^ bit) for i in range(count)])
        total = keep.astype(f32) + got.astype(f32)
        bit *= 2
    return total[0]


def total_over_dp(values):
    count = lax.axis_size("dp")
    bit = 1
    while bit < count:
        values = values + lax.ppermute(values, "dp", [(i, i ^ bit) for i in range(count)])
        bit *= 2
    return values


def swap(values):
    return lax.ppermute(values, "tensor", [(0, 1), (1, 0)])


def total_over_tensor(values):
    if lax.axis_size("tensor") == 2:
        return values + swap(values)
    return lax.psum(values, "tensor")


def gather_tokens(own):
    if lax.axis_size("tensor") == 2:
        other = swap(own)
        mine = lax.axis_index("tensor") == 0
        return jnp.concatenate([jnp.where(mine, own, other), jnp.where(mine, other, own)], axis=0)
    return lax.all_gather(own, "tensor", axis=0, tiled=True)


def scatter_tokens(whole):
    if lax.axis_size("tensor") == 2:
        half = whole.shape[0] // 2
        index = lax.axis_index("tensor")
        keep = lax.dynamic_slice_in_dim(whole, index * half, half)
        send = lax.dynamic_slice_in_dim(whole, (1 - index) * half, half)
        return keep.astype(f32) + swap(send).astype(f32)
    return lax.psum_scatter(whole, "tensor", scatter_dimension=0, tiled=True).astype(f32)


def pad_to(values, axis, size):
    pads = [(0, 0)] * values.ndim
    pads[axis] = (0, size - values.shape[axis])
    return jnp.pad(values, pads)


def body(
    hidden_in,
    segment_ids,
    norm_gain,
    proj_inner,
    proj_shared,
    proj_step,
    conv_inner,
    conv_shared,
    step_bias,
    log_decay,
    skip_gain,
    gate_gain,
    proj_out,
    out_grad,
):
    dp_count = lax.axis_size("dp")
    rows = proj_inner.shape[0]
    model_dim = hidden_in.shape[1]
    local_inner = proj_inner.shape[2]
    heads = proj_step.shape[1]
    state_size = proj_shared.shape[2]
    kernel_len = conv_inner.shape[0]
    shared_size = 2 * state_size
    full_inner = local_inner * lax.axis_size("tensor")
    width = -(-local_inner // (2 * LANES)) * 2 * LANES
    tap_block = conv_shared.shape[2]
    tap_count = kernel_len * 2 * tap_block
    tap_cols = -(-tap_count // rows)
    shared_at = 2 * width
    step_at = shared_at + shared_size

    hidden = gather_tokens(hidden_in).astype(f32)
    extra = pad_to(conv_shared.reshape(-1), 0, rows * tap_cols).reshape(rows, tap_cols)
    packed = jnp.concatenate(
        [
            pad_to(proj_inner[:, 0, :], 1, width),
            pad_to(proj_inner[:, 1, :], 1, width),
            proj_shared.reshape(rows, shared_size),
            pad_to(jnp.concatenate([proj_step, norm_gain[:, None], extra], axis=1), 1, LANES),
        ],
        axis=1,
    )
    weights = gather_rows(packed)
    gain_col = weights[:, step_at + heads]
    extra = weights[:, step_at + heads + 1 : step_at + heads + 1 + tap_cols]
    extra = extra.reshape(dp_count, rows * tap_cols)[:, :tap_count]
    taps = (
        extra.reshape(dp_count, kernel_len, 2, tap_block)
        .transpose(1, 2, 0, 3)
        .reshape(kernel_len, shared_size)
        .astype(f32)
    )
    out_rows = gather_rows(pad_to(proj_out.T, 1, width))
    grad_full = gather_tokens(out_grad)

    norm_scale = gain_col.astype(f32)
    inv_norm = lax.rsqrt(jnp.mean(hidden * hidden, axis=-1, keepdims=True) + epsilon)
    unit_in = hidden * inv_norm
    normed = (unit_in * norm_scale).astype(bf16)
    proj = dot_nn(normed, weights)

    aux, segr = token_facts(segment_ids)
    tapi = pad_to(pad_to(conv_inner.astype(f32), 1, width), 0, 8)
    taps = pad_to(taps, 0, 8)
    bias = pad_to(step_bias[None], 1, LANES)
    rate = pad_to(-jnp.exp(log_decay)[None], 1, LANES)
    skip = pad_to(jnp.repeat(skip_gain, HEAD_DIM)[None], 1, width)
    gain = pad_to(gate_gain.astype(f32)[None], 1, width)
    mixed, u, su, entry, squares = run_forward(proj, tapi, taps, bias, rate, skip, aux, segr)

    nog = dot_nn(grad_full, out_rows)
    gate = proj[:, :width]
    gated = mixed * gate * jax.nn.sigmoid(gate)
    products = jnp.sum(nog * gain * gated, axis=1, keepdims=True)
    sums = total_over_tensor(jnp.concatenate([squares, products], axis=1))
    inv_gate = lax.rsqrt(sums[:, :1] / full_inner + epsilon)
    normed_out = (gated * inv_gate * gain).astype(bf16)
    hidden_out = (
        hidden_in.astype(f32) + scatter_tokens(dot_nt(normed_out, out_rows).astype(bf16))
    ).astype(bf16)
    out_sum = scatter_rows(dot_tn(grad_full, normed_out)).T[:local_inner]

    lane = jnp.arange(width)[:, None] // HEAD_DIM
    place = (lane == jnp.arange(LANES)[None]).astype(bf16)
    dproj, wide, dtaps = run_backward(
        proj, mixed, u, su, entry, nog, sums, tapi, taps, bias, rate, skip, gain, aux, segr, place, full_inner
    )
    normed_grad = dot_nt(dproj, weights)
    norm_wgrad = jnp.sum(normed_grad * unit_in, axis=0)
    own_grad = scatter_tokens(normed_grad.astype(bf16))
    wgrad = dot_tn(normed, dproj)
    dtaps = (
        dtaps[:kernel_len]
        .reshape(kernel_len, 2, dp_count, tap_block)
        .transpose(2, 0, 1, 3)
        .reshape(dp_count, tap_count)
    )
    dtaps = pad_to(dtaps, 1, rows * tap_cols).reshape(model_dim, tap_cols)
    wgrad = jnp.concatenate(
        [
            wgrad[:, : step_at + heads],
            pad_to(jnp.concatenate([norm_wgrad[:, None], dtaps], axis=1), 1, LANES - heads),
        ],
        axis=1,
    )
    wsum = scatter_rows(wgrad)
    both = total_over_tensor(wsum[:, shared_at:])
    inner_sum = jnp.stack([wsum[:, :local_inner], wsum[:, width : width + local_inner]], axis=1)
    step_sum = wsum[:, step_at : step_at + heads]
    shared_total = both[:, :shared_size].reshape(rows, 2, state_size)
    norm_total = both[:, shared_size + heads]
    taps_total = both[:, shared_size + heads + 1 : shared_size + heads + 1 + tap_cols]
    taps_total = taps_total.reshape(-1)[:tap_count].reshape(kernel_len, 2, tap_block)
    wide = total_over_dp(wide)
    conv_total = wide[:kernel_len, :local_inner]
    gain_total = wide[4, :local_inner]
    skip_total = jnp.sum(wide[5].reshape(-1, HEAD_DIM), axis=1)[:heads]
    bias_total = wide[6, :heads]
    decay_total = wide[6, LANES : LANES + heads]

    own = hidden_in.astype(f32)
    own_inv = lax.rsqrt(jnp.mean(own * own, axis=-1, keepdims=True) + epsilon)
    own_unit = own * own_inv
    scaled_in = own_grad * norm_scale
    hidden_grad = own_inv * (
        scaled_in - own_unit * jnp.mean(scaled_in * own_unit, axis=-1, keepdims=True)
    ) + out_grad.astype(f32)
    return (
        hidden_out,
        hidden_grad,
        norm_total,
        inner_sum,
        shared_total,
        step_sum,
        conv_total,
        taps_total,
        bias_total,
        decay_total,
        skip_total,
        gain_total,
        out_sum,
    )


def solution(mesh):
    in_specs = (
        P(("dp", "tensor"), None),
        P("dp"),
        P("dp"),
        P("dp", None, "tensor"),
        P("dp", None, None),
        P("dp", "tensor"),
        P(None, "tensor"),
        P(None, None, "dp"),
        P("tensor"),
        P("tensor"),
        P("tensor"),
        P("tensor"),
        P("tensor", "dp"),
        P(("dp", "tensor"), None),
    )
    out_specs = (
        P(("dp", "tensor"), None),
        P(("dp", "tensor"), None),
        P("dp"),
        P("dp", None, "tensor"),
        P("dp", None, None),
        P("dp", "tensor"),
        P(None, "tensor"),
        P(None, None, "dp"),
        P("tensor"),
        P("tensor"),
        P("tensor"),
        P("tensor"),
        P("tensor", "dp"),
    )
    return jax.shard_map(body, mesh=mesh, in_specs=in_specs, out_specs=out_specs, check_vma=False)
```

time: 679 us -> 264 us (0.39); the launches traced: 670 us -> 263 us
  blocking collectives: 201 us -> 0 us
  waiting for transfers between devices: 179 us -> 68 us
  matrix products: 138 us -> 33.9 us
  Pallas kernels: 0 us -> 59.5 us
  other arithmetic: 81.7 us -> 31 us
  starting transfers between devices: 0.62 us -> 33.5 us
  between operations: 17.7 us -> 1.34 us
  local copies, waits for them, and re-layouts: 52.2 us -> 36.1 us
    dot_general x26 -> x6, matrix products: 138 us -> 33.9 us  [the longest x2 16.4 us: dot_nn(): lax.dot_general(a, b, (((1,), (0,)), ((), ())), preferred_element_type=f32)]
    unnamed x11 -> x0, waiting for transfers between devices: 97.2 us -> none
    psum x4 -> x0, blocking collectives: 80.2 us -> none  [the longest x1 61.1 us: body(): lax.psum((grad_taps_inner, grad_bias, grad_decay, grad_skip, gate_wgrad),...]
    reduce_scatter x3 -> x0, waiting for transfers between devices: 80 us -> none  [the longest x1 52.7 us: body(): lax.psum_scatter(out_wgrad.astype(jnp.bfloat16), 'dp', scatter_dimension=...]
    ppermute x0 -> x26, waiting for transfers between devices: none -> 68 us  [the longest x6 33.3 us: swap(): return lax.ppermute(values, 'tensor', [(0, 1), (1, 0)])]
    unnamed x2 -> x0, blocking collectives: 64.6 us -> none
    pallas_call x0 -> x2, Pallas kernels: none -> 59.5 us  [the longest x1 38.3 us: run_backward(): pl.pallas_call(partial(backward_kernel, full_inner=float(full_inner)), ou...]
    all_gather x3 -> x0, blocking collectives: 55.7 us -> none  [the longest x1 19.3 us: body(): lax.all_gather(proj_step, 'dp', axis=0, tiled=True)]
  transfers between devices with their start and end apart: 9 -> 26, of which waited for: 4 -> 9; matrix products, arithmetic and copies ran while one was open for 16% -> 24% of each run, Pallas kernels for 0% -> 0%
where the time goes in v1:
time: 264 us; the launch traced here: 263 us
  waiting for transfers between devices  68 us (26%)
  Pallas kernels  59.5 us (23%)
  local copies, waits for them, and re-layouts  36.1 us (14%)
  matrix products  33.9 us (13%)
  starting transfers between devices  33.5 us (13%)
  other arithmetic  31 us (12%)
    pallas_call x1, Pallas kernels, run_backward(): pl.pallas_call(partial(backward_kernel, full_inner=float(full_inner)), ou...  38.3 us
    ppermute x6, waiting for transfers between devices, swap(): return lax.ppermute(values, 'tensor', [(0, 1), (1, 0)])  33.3 us
    ppermute x8, waiting for transfers between devices, gather_rows(): other = lax.ppermute(whole, 'dp', [(i, i ^ bit) for i in range(count)])  23.4 us
    pallas_call x1, Pallas kernels, run_forward(): pl.pallas_call(forward_kernel, out_shape=(sds((length, width), f32), sds(...  21.2 us
    dot_general x2, matrix products, dot_nn(): lax.dot_general(a, b, (((1,), (0,)), ((), ())), preferred_element_type=f32)  16.4 us
    dot_general x2, matrix products, dot_tn(): lax.dot_general(a, b, (((0,), (0,)), ((), ())), preferred_element_type=f32)  11.6 us
    ppermute x8, starting transfers between devices, scatter_rows(): lax.ppermute(send.astype(bf16), 'dp', [(i, i ^ bit) for i in range(count)])  10.6 us
    ppermute x8, starting transfers between devices, gather_rows(): other = lax.ppermute(whole, 'dp', [(i, i ^ bit) for i in range(count)])  9.89 us
  transfers between devices with their start and end apart: 26, of which 9 were waited for; matrix products, arithmetic and copies ran while one was open for 24% of the time, Pallas kernels for 0%

profile of v1, /device:TPU:0, one launch (start us, length us, event | category | flops | bytes accessed | tf_op | source)
XLA Modules:
  0.0 263.2 jit_solution(10235061189436586720)
XLA Ops:
  0.7 4.1 %collective-permute-start.6 = (bf16[1,48,768]{2,1,0:T(8,128)(2,1)}, bf16[1,48,768]{2,1,0:T(8,128)(2,1)S(1)}, u32[]{:S(2)}, u32[]{:S(2)}) collective-permute-start(bf16[1,48,768]{2,1,0:T(8,128)(2,1)} %bitcast.199), channel_id=1, source_target_pairs={{0,16},{2,18},{4,20},{6,22},{8,24},{10,26},{12,28},{14,30},{16,0},... | collective-permute-start | bytes 221192 | tf_op jit(solution)/shard_map/ppermute | solution.py:443
  9.5 1.8 collective-permute-start
  21.3 1.9 collective-permute-start.2
  26.7 5.8 %collective-permute-done.2 = bf16[2,48,1920]{2,1,0:T(8,128)(2,1)S(1)} collective-permute-done((bf16[2,48,1920]{2,1,0:T(8,128)(2,1)S(1)}, bf16[2,48,1920]{2,1,0:T(8,128)(2,1)S(1)}, u32[]{:S(2)}, u32[]{:S(2)}) %collective-permute-start.2) | collective-permute-done | bytes 368672 | tf_op jit(solution)/shard_map/ppermute | solution.py:443
  32.7 1.6 collective-permute-start.3
  36.5 17.6 %collective-permute-done.8 = bf16[4,48,768]{2,1,0:T(8,128)(2,1)S(1)} collective-permute-done((bf16[4,48,768]{2,1,0:T(8,128)(2,1)S(1)}, bf16[4,48,768]{2,1,0:T(8,128)(2,1)S(1)}, u32[]{:S(2)}, u32[]{:S(2)}) %collective-permute-start.8) | collective-permute-done | bytes 294944 | tf_op jit(solution)/shard_map/ppermute | solution.py:443
  57.4 2.5 broadcast_select_fusion.1
  65.1 8.3 %fusion.47.proj_ref = f32[1024,1920]{1,0:T(8,128)} fusion(bf16[768,1920]{1,0:T(8,128)(2,1)} %bitcast.179, f32[768]{0:T(1024)S(1)} %convert_reduce_fusion, f32[1024]{0:T(1024)S(1)} %add_rsqrt_fusion, bf16[512,768]{1,0:T(8,128)(2,1)S(1)} %get-tuple-element.103, bf16[512,768]{1,0:T(8,128)(2,1)S(1)} %get-tuple-element.102), kind=kOutput, calls=%fused_computation.148 | convolution fusion | flops 3025403904 | bytes 12393472 | tf_op jit(solution)/shard_map/dot_general | solution.py:20
  73.4 21.2 %scan_forward.1 = (f32[1024,768]{1,0:T(8,128)}, f32[1024,768]{1,0:T(8,128)}, f32[1024,256]{1,0:T(8,128)}, bf16[8,128,768]{2,1,0:T(8,128)(2,1)}, f32[1024,1]{1,0:T(8,128)}) custom-call(f32[1024,1920]{1,0:T(8,128)} %fusion.47.proj_ref, f32[8,768]{1,0:T(8,128)} %pad_convert_fusion.tapi_ref, f32[8,256]{1,0:T(8,128)} %pad_convert_fusion.1.taps_ref, ...), custom_call_target="tpu_custom_call" | custom-call | tf_op jit(solution)/shard_map/scan_forward/pallas_call | solution.py:391
  95.8 8.1 %multiply_reduce_fusion = (f32[1024]{0:T(1024)S(1)}, f32[1024,768]{1,0:T(8,128)}, f32[1024,768]{1,0:T(8,128)}) fusion(f32[768]{0:T(1024)S(1)} %convert_element_type.194, f32[1024,768]{1,0:T(8,128)} %get-tuple-element.21.mixed_ref, f32[1024,1920]{1,0:T(8,128)} %fusion.47.proj_ref, bf16[768,768]{1,0:T(8,128)(2,1)} %bitcast.189, ...), kind=kOutput, calls=%fused_computation.11 | convolution fusion | flops 1217395712 | bytes 15342592 | tf_op jit(solution)/shard_map/dot_general | solution.py:20
  106.1 11.9 %collective-permute-done.10 = f32[1024,2]{1,0:T(8,128)} collective-permute-done((f32[1024,2]{1,0:T(8,128)S(1)}, f32[1024,2]{1,0:T(8,128)}, u32[]{:S(2)}, u32[]{:S(2)}) %collective-permute-start.10) | collective-permute-done | bytes 8224 | tf_op jit(solution)/shard_map/ppermute | solution.py:480
  120.1 38.3 %scan_backward.1 = (bf16[1024,1920]{1,0:T(8,128)(2,1)}, f32[8,768]{1,0:T(8,128)}, f32[8,256]{1,0:T(8,128)}) custom-call(f32[1024,1920]{1,0:T(8,128)} %fusion.47.proj_ref, f32[1024,768]{1,0:T(8,128)} %get-tuple-element.21.mixed_ref, f32[1024,768]{1,0:T(8,128)} %get-tuple-element.23.u_ref, f32[1024,256]{1,0:T(8,128)} %get-tuple-element.24.su_ref, ...), custom_call_target="tpu_custom_call" | custom-call | tf_op jit(solution)/shard_map/scan_backward/pallas_call | solution.py:416
  158.4 7.9 %fusion = f32[768,1804]{0,1:T(8,128)} fusion(bf16[1024,1920]{1,0:T(8,128)(2,1)} %get-tuple-element.26, f32[768]{0:T(1024)S(1)} %convert_reduce_fusion, f32[1024]{0:T(1024)S(1)} %add_rsqrt_fusion, bf16[512,768]{1,0:T(8,128)(2,1)S(1)} %get-tuple-element.103, bf16[512,768]{1,0:T(8,128)(2,1)S(1)} %get-tuple-element.102), kind=kOutput, calls=%fused_computation.1 | convolution fusion | flops 2842951680 | bytes 11054080 | tf_op jit(solution)/shard_map/dot_general | solution.py:28
  166.3 4.4 %fusion.5 = (f32[768]{0:T(1024)S(1)}, bf16[1024,768]{1,0:T(8,128)(2,1)S(1)}) fusion(f32[1024]{0:T(1024)S(1)} %add_rsqrt_fusion, bf16[512,768]{1,0:T(8,128)(2,1)} %copy-done.4, bf16[512,768]{1,0:T(8,128)(2,1)S(1)} %get-tuple-element.102, bf16[1024,1920]{1,0:T(8,128)(2,1)S(1)} %copy-done.20, bf16[768,1920]{1,0:T(8,128)(2,1)S(1)} %bitcast.180), kind=kOutput, calls=%fused_computation.8 | convolution fusion | flops 3026189568 | bytes 10034176 | tf_op jit(solution)/shard_map/dot_general | solution.py:24
  171.5 5.5 %pad_maximum_fusion = f32[768,1920]{0,1:T(8,128)} fusion(f32[768,116]{0,1:T(8,128)S(1)} %select_maximum_fusion, f32[768,1804]{0,1:T(8,128)} %fusion), kind=kLoop, calls=%fused_computation | loop fusion | flops 1474560 | bytes 11796480 | tf_op jit(solution)/shard_map/concatenate | solution.py:612
  177.0 6.5 %copy.152 = f32[768,1920]{1,0:T(8,128)} copy(f32[768,1920]{0,1:T(8,128)} %pad_maximum_fusion) | data formatting | bytes 11796480 | tf_op jit(solution)/shard_map/concatenate | solution.py:612
  183.5 3.2 %fusion.15 = bf16[8,48,1920]{2,1,0:T(8,128)(2,1)} fusion(f32[8,2,48,1920]{3,2,1,0:T(8,128)} %bitcast.170, s32[]{:T(128)S(6)} %select_n.216), kind=kLoop, calls=%fused_computation.31 | loop fusion | bytes 2949124 | tf_op jit(solution)/shard_map/convert_element_type | solution.py:464
  187.2 3.7 %fusion.16 = f32[768,768]{1,0:T(8,128)S(1)} fusion(bf16[512,768]{1,0:T(8,128)(2,1)S(1)} %copy-done.13, bf16[512,768]{1,0:T(8,128)(2,1)S(1)} %copy-done.12, f32[1024,768]{1,0:T(8,128)} %get-tuple-element.97, f32[1024]{0:T(1024)S(1)} %fusion.22, f32[768]{0:T(1024)S(1)} %convert_element_type.194), kind=kOutput, calls=%fused_computation.40 | convolution fusion | flops 1213464576 | bytes 7085056 | tf_op jit(solution)/shard_map/dot_general | solution.py:28
  194.7 1.7 collective-permute-done.19
  198.6 1.5 collective-permute-start.11
  200.2 2.6 collective-permute-start.21
  207.4 1.6 bitcast_add_fusion.2
  209.0 1.6 collective-permute-start.23
  210.6 2.5 bitcast_add_fusion
  213.8 20.2 %collective-permute-done.12 = bf16[512,768]{1,0:T(8,128)(2,1)S(1)} collective-permute-done((bf16[512,768]{1,0:T(8,128)(2,1)}, bf16[512,768]{1,0:T(8,128)(2,1)S(1)}, u32[]{:S(2)}, u32[]{:S(2)}) %collective-permute-start.12) | collective-permute-done | bytes 786464 | tf_op jit(solution)/shard_map/ppermute | solution.py:480
  235.4 1.6 collective-permute-start.15
  237.1 3.4 %fusion.12 = (f32[512,768]{1,0:T(8,128)}, bf16[512,768]{1,0:T(8,128)(2,1)}) fusion(bf16[512,768]{1,0:T(8,128)(2,1)S(1)} %copy-done, bf16[512,768]{1,0:T(8,128)(2,1)S(1)} %copy-done.6, bf16[512,768]{1,0:T(8,128)(2,1)S(1)} %collective-permute-done.12, f32[512]{0:T(512)S(1)} %broadcast_multiply_fusion, f32[768]{0:T(1024)S(1)} %convert_reduce_fusion, ...), kind=kLoop, calls=%fused_computation.25 | loop fusion | flops 6291456 | bytes 7085060 | tf_op jit(solution)/shard_map/add | solution.py:638
  241.5 2.6 collective-permute-start.25
  244.1 3.9 %collective-permute-done.15 = bf16[2,48,1920]{2,1,0:T(8,128)(2,1)S(1)} collective-permute-done((bf16[2,48,1920]{2,1,0:T(8,128)(2,1)S(1)}, bf16[2,48,1920]{2,1,0:T(8,128)(2,1)S(1)}, u32[]{:S(2)}, u32[]{:S(2)}) %collective-permute-start.15) | collective-permute-done | bytes 368672 | tf_op jit(solution)/shard_map/ppermute | solution.py:464
  248.1 3.2 %collective-permute-start.16 = (bf16[1,48,1920]{2,1,0:T(8,128)(2,1)S(1)}, bf16[1,48,1920]{2,1,0:T(8,128)(2,1)S(1)}, u32[]{:S(2)}, u32[]{:S(2)}) collective-permute-start(bf16[1,48,1920]{2,1,0:T(8,128)(2,1)S(1)} %dynamic-slice_convert_fusion.3), channel_id=1, source_target_pairs={{0,16},{2,18},{4,20},{6,22},{8,24},{10,26},{12,28},{14,30},{16,0},... | collective-permute-start | bytes 552968 | tf_op jit(solution)/shard_map/ppermute | solution.py:464
  251.9 4.7 %collective-permute-done.16 = bf16[1,48,1920]{2,1,0:T(8,128)(2,1)S(1)} collective-permute-done((bf16[1,48,1920]{2,1,0:T(8,128)(2,1)S(1)}, bf16[1,48,1920]{2,1,0:T(8,128)(2,1)S(1)}, u32[]{:S(2)}, u32[]{:S(2)}) %collective-permute-start.16) | collective-permute-done | bytes 184352 | tf_op jit(solution)/shard_map/ppermute | solution.py:464
  256.7 1.6 collective-permute-start.17
  (199 shorter events, 55.0 us)
Async XLA Ops:
  0.6 22.6 %copy-start.14 = (s32[1024]{0:T(1024)S(1)}, s32[1024]{0:T(1024)}, u32[]{:S(2)}) copy-start(s32[1024]{0:T(1024)} %param.15) | copy-start | bytes 12292
  0.7 23.9 %copy-start.19 = (f32[12]{0:T(128)S(1)}, f32[12]{0:T(128)}, u32[]{:S(2)}) copy-start(f32[12]{0:T(128)} %param.24) | copy-start | bytes 148
  0.7 25.2 %copy-start.21 = (f32[12]{0:T(128)S(1)}, f32[12]{0:T(128)}, u32[]{:S(2)}) copy-start(f32[12]{0:T(128)} %param.22) | copy-start | bytes 148
  0.7 25.7 %copy-start.17 = (bf16[768]{0:T(1024)(128)(2,1)S(1)}, bf16[768]{0:T(1024)(128)(2,1)}, u32[]{:S(2)}) copy-start(bf16[768]{0:T(1024)(128)(2,1)} %param.25) | copy-start | bytes 4612
  0.7 25.7 %copy-start.15 = (bf16[768,48]{0,1:T(8,128)(2,1)S(1)}, bf16[768,48]{0,1:T(8,128)(2,1)}, u32[]{:S(2)}) copy-start(bf16[768,48]{0,1:T(8,128)(2,1)} %param.26) | copy-start | bytes 221188
  0.7 25.7 %collective-permute-start.6 = (bf16[1,48,768]{2,1,0:T(8,128)(2,1)}, bf16[1,48,768]{2,1,0:T(8,128)(2,1)S(1)}, u32[]{:S(2)}, u32[]{:S(2)}) collective-permute-start(bf16[1,48,768]{2,1,0:T(8,128)(2,1)} %bitcast.199), channel_id=1, source_target_pairs={{0,16},{2,18},{4,20},{6,22},{8,24},{10,26},{12,28},{14,30},{16,0},... | collective-permute-start | bytes 221192 | tf_op jit(solution)/shard_map/ppermute | solution.py:443
  9.4 11.8 %collective-permute-start.1 = (bf16[1,48,1920]{2,1,0:T(8,128)(2,1)S(1)}, bf16[1,48,1920]{2,1,0:T(8,128)(2,1)S(1)}, u32[]{:S(2)}, u32[]{:S(2)}) collective-permute-start(bf16[1,48,1920]{2,1,0:T(8,128)(2,1)S(1)} %maximum_bitcast_fusion.1), channel_id=1, source_target_pairs={{0,16},{2,18},{4,20},{6,22},{8,24},{10,26},{12,28},{14,30},{16,0},... | collective-permute-start | bytes 552968 | tf_op jit(solution)/shard_map/ppermute | solution.py:443
  9.5 46.0 %collective-permute-start = (bf16[512,768]{1,0:T(8,128)(2,1)}, bf16[512,768]{1,0:T(8,128)(2,1)}, u32[]{:S(2)}, u32[]{:S(2)}) collective-permute-start(bf16[512,768]{1,0:T(8,128)(2,1)} %param.14), channel_id=1, source_target_pairs={{0,1},{1,0},{2,3},{3,2},{4,5},{5,4},{6,7},{7,6},{8,9},{9,8},{10,11... | collective-permute-start | bytes 2359304 | tf_op jit(solution)/shard_map/ppermute | solution.py:480
  11.3 46.0 %collective-permute-start.5 = (bf16[512,768]{1,0:T(8,128)(2,1)}, bf16[512,768]{1,0:T(8,128)(2,1)}, u32[]{:S(2)}, u32[]{:S(2)}) collective-permute-start(bf16[512,768]{1,0:T(8,128)(2,1)} %param.27), channel_id=1, source_target_pairs={{0,1},{1,0},{2,3},{3,2},{4,5},{5,4},{6,7},{7,6},{8,9},{9,8},{10,11... | collective-permute-start | bytes 2359304 | tf_op jit(solution)/shard_map/ppermute | solution.py:480
  21.3 11.1 %collective-permute-start.2 = (bf16[2,48,1920]{2,1,0:T(8,128)(2,1)S(1)}, bf16[2,48,1920]{2,1,0:T(8,128)(2,1)S(1)}, u32[]{:S(2)}, u32[]{:S(2)}) collective-permute-start(bf16[2,48,1920]{2,1,0:T(8,128)(2,1)S(1)} %maximum_bitcast_fusion), channel_id=1, source_target_pairs={{0,8},{2,10},{4,12},{6,14},{8,0},{10,2},{12,4},{14,6},{16,24},{18,... | collective-permute-start | bytes 1105928 | tf_op jit(solution)/shard_map/ppermute | solution.py:443
  26.4 7.8 %collective-permute-start.7 = (bf16[2,48,768]{2,1,0:T(8,128)(2,1)S(1)}, bf16[2,48,768]{2,1,0:T(8,128)(2,1)S(1)}, u32[]{:S(2)}, u32[]{:S(2)}) collective-permute-start(bf16[2,48,768]{2,1,0:T(8,128)(2,1)S(1)} %maximum_bitcast_fusion.2), channel_id=1, source_target_pairs={{0,8},{2,10},{4,12},{6,14},{8,0},{10,2},{12,4},{14,6},{16,24},{18,... | collective-permute-start | bytes 442376 | tf_op jit(solution)/shard_map/ppermute | solution.py:443
  32.7 21.5 %collective-permute-start.3 = (bf16[4,48,1920]{2,1,0:T(8,128)(2,1)S(1)}, bf16[4,48,1920]{2,1,0:T(8,128)(2,1)S(1)}, u32[]{:S(2)}, u32[]{:S(2)}) collective-permute-start(bf16[4,48,1920]{2,1,0:T(8,128)(2,1)S(1)} %bitcast.183), channel_id=1, source_target_pairs={{0,4},{2,6},{4,0},{6,2},{8,12},{10,14},{12,8},{14,10},{16,20},{18,... | collective-permute-start | bytes 2211848 | tf_op jit(solution)/shard_map/ppermute | solution.py:443
  34.3 19.8 %collective-permute-start.8 = (bf16[4,48,768]{2,1,0:T(8,128)(2,1)S(1)}, bf16[4,48,768]{2,1,0:T(8,128)(2,1)S(1)}, u32[]{:S(2)}, u32[]{:S(2)}) collective-permute-start(bf16[4,48,768]{2,1,0:T(8,128)(2,1)S(1)} %bitcast.191), channel_id=1, source_target_pairs={{0,4},{2,6},{4,0},{6,2},{8,12},{10,14},{12,8},{14,10},{16,20},{18,... | collective-permute-start | bytes 884744 | tf_op jit(solution)/shard_map/ppermute | solution.py:443
  54.7 6.5 %collective-permute-start.4 = (bf16[8,48,1920]{2,1,0:T(8,128)(2,1)S(1)}, bf16[8,48,1920]{2,1,0:T(8,128)(2,1)S(1)}, u32[]{:S(2)}, u32[]{:S(2)}) collective-permute-start(bf16[8,48,1920]{2,1,0:T(8,128)(2,1)S(1)} %bitcast.174), channel_id=1, source_target_pairs={{0,2},{2,0},{4,6},{6,4},{8,10},{10,8},{12,14},{14,12},{16,18},{18,... | collective-permute-start | bytes 4423688 | tf_op jit(solution)/shard_map/ppermute | solution.py:443
  54.9 5.0 %collective-permute-start.9 = (bf16[8,48,768]{2,1,0:T(8,128)(2,1)S(1)}, bf16[8,48,768]{2,1,0:T(8,128)(2,1)S(1)}, u32[]{:S(2)}, u32[]{:S(2)}) collective-permute-start(bf16[8,48,768]{2,1,0:T(8,128)(2,1)S(1)} %bitcast.184), channel_id=1, source_target_pairs={{0,2},{2,0},{4,6},{6,4},{8,10},{10,8},{12,14},{14,12},{16,18},{18,... | collective-permute-start | bytes 1769480 | tf_op jit(solution)/shard_map/ppermute | solution.py:443
  57.0 101.4 %copy-start.4 = (bf16[512,768]{1,0:T(8,128)(2,1)}, bf16[512,768]{1,0:T(8,128)(2,1)S(1)}, u32[]{:S(2)}) copy-start(bf16[512,768]{1,0:T(8,128)(2,1)S(1)} %get-tuple-element.103) | copy-start | bytes 2359300
  104.2 13.8 %collective-permute-start.10 = (f32[1024,2]{1,0:T(8,128)S(1)}, f32[1024,2]{1,0:T(8,128)}, u32[]{:S(2)}, u32[]{:S(2)}) collective-permute-start(f32[1024,2]{1,0:T(8,128)S(1)} %copy.146), channel_id=1, source_target_pairs={{0,1},{1,0},{2,3},{3,2},{4,5},{5,4},{6,7},{7,6},{8,9},{9,8},{10,11... | collective-permute-start | bytes 24584 | tf_op jit(solution)/shard_map/ppermute | solution.py:480
  170.8 21.6 %collective-permute-start.18 = (f32[8,768]{1,0:T(8,128)S(1)}, f32[8,768]{1,0:T(8,128)S(1)}, u32[]{:S(2)}, u32[]{:S(2)}) collective-permute-start(f32[8,768]{1,0:T(8,128)S(1)} %copy-done.16), channel_id=1, source_target_pairs={{0,2},{2,0},{4,6},{6,4},{8,10},{10,8},{12,14},{14,12},{16,18},{18,... | collective-permute-start | bytes 73736 | tf_op jit(solution)/shard_map/ppermute | solution.py:474
  186.7 23.8 %collective-permute-start.13 = (bf16[8,48,1920]{2,1,0:T(8,128)(2,1)}, bf16[8,48,1920]{2,1,0:T(8,128)(2,1)}, u32[]{:S(2)}, u32[]{:S(2)}) collective-permute-start(bf16[8,48,1920]{2,1,0:T(8,128)(2,1)} %fusion.15), channel_id=1, source_target_pairs={{0,2},{2,0},{4,6},{6,4},{8,10},{10,8},{12,14},{14,12},{16,18},{18,... | collective-permute-start | bytes 4423688 | tf_op jit(solution)/shard_map/ppermute | solution.py:464
  192.5 3.9 %collective-permute-start.19 = (f32[8,768]{1,0:T(8,128)S(1)}, f32[8,768]{1,0:T(8,128)S(1)}, u32[]{:S(2)}, u32[]{:S(2)}) collective-permute-start(f32[8,768]{1,0:T(8,128)S(1)} %add.174), channel_id=1, source_target_pairs={{0,4},{2,6},{4,0},{6,2},{8,12},{10,14},{12,8},{14,10},{16,20},{18,... | collective-permute-start | bytes 73736 | tf_op jit(solution)/shard_map/ppermute | solution.py:474
  194.7 12.7 %collective-permute-start.22 = (bf16[8,48,768]{2,1,0:T(8,128)(2,1)}, bf16[8,48,768]{2,1,0:T(8,128)(2,1)}, u32[]{:S(2)}, u32[]{:S(2)}) collective-permute-start(bf16[8,48,768]{2,1,0:T(8,128)(2,1)} %fusion.19), channel_id=1, source_target_pairs={{0,2},{2,0},{4,6},{6,4},{8,10},{10,8},{12,14},{14,12},{16,18},{18,... | collective-permute-start | bytes 1769480 | tf_op jit(solution)/shard_map/ppermute | solution.py:464
  196.4 3.8 %collective-permute-start.20 = (f32[8,768]{1,0:T(8,128)S(1)}, f32[8,768]{1,0:T(8,128)S(1)}, u32[]{:S(2)}, u32[]{:S(2)}) collective-permute-start(f32[8,768]{1,0:T(8,128)S(1)} %add.175), channel_id=1, source_target_pairs={{0,8},{2,10},{4,12},{6,14},{8,0},{10,2},{12,4},{14,6},{16,24},{18,... | collective-permute-start | bytes 73736 | tf_op jit(solution)/shard_map/ppermute | solution.py:474
  198.6 38.4 %collective-permute-start.11 = (bf16[512,768]{1,0:T(8,128)(2,1)}, bf16[512,768]{1,0:T(8,128)(2,1)}, u32[]{:S(2)}, u32[]{:S(2)}) collective-permute-start(bf16[512,768]{1,0:T(8,128)(2,1)} %constant_dynamic-slice_fusion.1), channel_id=1, source_target_pairs={{0,1},{1,0},{2,3},{3,2},{4,5},{5,4},{6,7},{7,6},{8,9},{9,8},{10,11... | collective-permute-start | bytes 2359304 | tf_op jit(solution)/shard_map/ppermute | solution.py:480
  200.2 4.8 %collective-permute-start.21 = (f32[8,768]{1,0:T(8,128)S(1)}, f32[8,768]{1,0:T(8,128)S(1)}, u32[]{:S(2)}, u32[]{:S(2)}) collective-permute-start(f32[8,768]{1,0:T(8,128)S(1)} %add.176), channel_id=1, source_target_pairs={{0,16},{2,18},{4,20},{6,22},{8,24},{10,26},{12,28},{14,30},{16,0},... | collective-permute-start | bytes 73736 | tf_op jit(solution)/shard_map/ppermute | solution.py:474
  203.7 30.3 %collective-permute-start.12 = (bf16[512,768]{1,0:T(8,128)(2,1)}, bf16[512,768]{1,0:T(8,128)(2,1)S(1)}, u32[]{:S(2)}, u32[]{:S(2)}) collective-permute-start(bf16[512,768]{1,0:T(8,128)(2,1)} %constant_dynamic-slice_fusion), channel_id=1, source_target_pairs={{0,1},{1,0},{2,3},{3,2},{4,5},{5,4},{6,7},{7,6},{8,9},{9,8},{10,11... | collective-permute-start | bytes 2359304 | tf_op jit(solution)/shard_map/ppermute | solution.py:480
  209.0 25.5 %collective-permute-start.23 = (bf16[4,48,768]{2,1,0:T(8,128)(2,1)S(1)}, bf16[4,48,768]{2,1,0:T(8,128)(2,1)S(1)}, u32[]{:S(2)}, u32[]{:S(2)}) collective-permute-start(bf16[4,48,768]{2,1,0:T(8,128)(2,1)S(1)} %fusion.25), channel_id=1, source_target_pairs={{0,4},{2,6},{4,0},{6,2},{8,12},{10,14},{12,8},{14,10},{16,20},{18,... | collective-permute-start | bytes 884744 | tf_op jit(solution)/shard_map/ppermute | solution.py:464
  213.2 22.0 %collective-permute-start.14 = (bf16[4,48,1920]{2,1,0:T(8,128)(2,1)S(1)}, bf16[4,48,1920]{2,1,0:T(8,128)(2,1)S(1)}, u32[]{:S(2)}, u32[]{:S(2)}) collective-permute-start(bf16[4,48,1920]{2,1,0:T(8,128)(2,1)S(1)} %fusion.18), channel_id=1, source_target_pairs={{0,4},{2,6},{4,0},{6,2},{8,12},{10,14},{12,8},{14,10},{16,20},{18,... | collective-permute-start | bytes 2211848 | tf_op jit(solution)/shard_map/ppermute | solution.py:464
  234.7 6.8 %collective-permute-start.24 = (bf16[2,48,768]{2,1,0:T(8,128)(2,1)S(1)}, bf16[2,48,768]{2,1,0:T(8,128)(2,1)S(1)}, u32[]{:S(2)}, u32[]{:S(2)}) collective-permute-start(bf16[2,48,768]{2,1,0:T(8,128)(2,1)S(1)} %fusion.26), channel_id=1, source_target_pairs={{0,8},{2,10},{4,12},{6,14},{8,0},{10,2},{12,4},{14,6},{16,24},{18,... | collective-permute-start | bytes 442376 | tf_op jit(solution)/shard_map/ppermute | solution.py:464
  235.4 12.6 %collective-permute-start.15 = (bf16[2,48,1920]{2,1,0:T(8,128)(2,1)S(1)}, bf16[2,48,1920]{2,1,0:T(8,128)(2,1)S(1)}, u32[]{:S(2)}, u32[]{:S(2)}) collective-permute-start(bf16[2,48,1920]{2,1,0:T(8,128)(2,1)S(1)} %fusion.24), channel_id=1, source_target_pairs={{0,8},{2,10},{4,12},{6,14},{8,0},{10,2},{12,4},{14,6},{16,24},{18,... | collective-permute-start | bytes 1105928 | tf_op jit(solution)/shard_map/ppermute | solution.py:464
  241.5 9.7 %collective-permute-start.25 = (bf16[1,48,768]{2,1,0:T(8,128)(2,1)S(1)}, bf16[1,48,768]{2,1,0:T(8,128)(2,1)S(1)}, u32[]{:S(2)}, u32[]{:S(2)}) collective-permute-start(bf16[1,48,768]{2,1,0:T(8,128)(2,1)S(1)} %dynamic-slice_convert_fusion.5), channel_id=1, source_target_pairs={{0,16},{2,18},{4,20},{6,22},{8,24},{10,26},{12,28},{14,30},{16,0},... | collective-permute-start | bytes 221192 | tf_op jit(solution)/shard_map/ppermute | solution.py:464
  248.1 8.5 %collective-permute-start.16 = (bf16[1,48,1920]{2,1,0:T(8,128)(2,1)S(1)}, bf16[1,48,1920]{2,1,0:T(8,128)(2,1)S(1)}, u32[]{:S(2)}, u32[]{:S(2)}) collective-permute-start(bf16[1,48,1920]{2,1,0:T(8,128)(2,1)S(1)} %dynamic-slice_convert_fusion.3), channel_id=1, source_target_pairs={{0,16},{2,18},{4,20},{6,22},{8,24},{10,26},{12,28},{14,30},{16,0},... | collective-permute-start | bytes 552968 | tf_op jit(solution)/shard_map/ppermute | solution.py:464
  256.7 4.4 %collective-permute-start.17 = (f32[48,384]{1,0:T(8,128)S(1)}, f32[48,384]{1,0:T(8,128)S(1)}, u32[]{:S(2)}, u32[]{:S(2)}) collective-permute-start(f32[48,384]{1,0:T(8,128)S(1)} %slice.126), channel_id=1, source_target_pairs={{0,1},{1,0},{2,3},{3,2},{4,5},{5,4},{6,7},{7,6},{8,9},{9,8},{10,11... | collective-permute-start | bytes 221192 | tf_op jit(solution)/shard_map/ppermute | solution.py:480
  (17 other events, 65.8 us)

commit v2 on v1

v2 whole, which is shorter than its diff:
```python
from functools import partial

import jax
import jax.numpy as jnp
import numpy as np
from jax import lax
from jax.experimental import pallas as pl
from jax.experimental.pallas import tpu as pltpu
from jax.sharding import PartitionSpec as P

HEAD_DIM = 64
CHUNK = 128
LANES = 128
TOKEN_BLOCK = 256
epsilon = 1e-05
f32 = jnp.float32
bf16 = jnp.bfloat16
highest = lax.Precision.HIGHEST


def dot_nn(a, b):
    return lax.dot_general(a, b, (((1,), (0,)), ((), ())), preferred_element_type=f32)


def dot_nt(a, b):
    return lax.dot_general(a, b, (((1,), (1,)), ((), ())), preferred_element_type=f32)


def dot_tn(a, b):
    return lax.dot_general(a, b, (((0,), (0,)), ((), ())), preferred_element_type=f32)


def dot_exact(a, b):
    return lax.dot_general(
        a, b, (((1,), (0,)), ((), ())), preferred_element_type=f32, precision=highest
    )


def dot_split(a, b):
    high = a.astype(bf16)
    rest = (a - high.astype(f32)).astype(bf16)
    return dot_nn(high, b) + dot_nn(rest, b)


def sigmoid(v):
    return 1.0 / (1.0 + jnp.exp(-v))


def softplus(v):
    return jnp.maximum(v, 0.0) + jnp.log1p(jnp.exp(-jnp.abs(v)))


def halves(lane_low, values, head):
    return jnp.where(lane_low, values[:, head : head + 1], values[:, head + 1 : head + 2])


def back_shift(window, offset):
    return pltpu.roll(window, offset, 0)[8:, :]


def ahead_shift(window, offset):
    rows = window.shape[0]
    return pltpu.roll(window, rows - offset, 0)[: rows - 8, :]


def conv_rows(window, taps, aux):
    total = taps[3:4, :] * window[8:, :]
    for offset in range(1, 4):
        total = total + taps[3 - offset : 4 - offset, :] * (
            back_shift(window, offset) * aux[:, offset : offset + 1]
        )
    return total


def forward_kernel(
    proj_ref,
    step_ref,
    tapi_ref,
    taps_ref,
    heads_ref,
    aux_ref,
    segr_ref,
    mixed_ref,
    u_ref,
    su_ref,
    entry_ref,
    state_ref,
    carry_ref,
    scarry_ref,
    xw_ref,
):
    width = mixed_ref.shape[1]
    pairs = width // LANES
    shared_size = su_ref.shape[1]
    state_size = shared_size // 2
    chunk = pl.program_id(0)

    @pl.when(chunk == 0)
    def _():
        for ref in (state_ref, carry_ref, scarry_ref):
            ref[...] = jnp.zeros_like(ref)

    rows = lax.broadcasted_iota(jnp.int32, (CHUNK, CHUNK), 0)
    cols = lax.broadcasted_iota(jnp.int32, (CHUNK, CHUNK), 1)
    lower = rows >= cols
    summing = lower.astype(f32)
    lane_low = lax.broadcasted_iota(jnp.int32, (CHUNK, LANES), 1) < HEAD_DIM
    bias = heads_ref[0:1, :]
    rate = -jnp.exp(heads_ref[1:2, :])
    skips = heads_ref[2:3, :]
    aux = aux_ref[...]
    live = aux[:, 7:8]
    same = lower & (aux[:, 0:1] == segr_ref[pl.ds(chunk, 1), :])
    shared_now = proj_ref[:, width:].astype(f32)
    su = conv_rows(jnp.concatenate([scarry_ref[...], shared_now], axis=0), taps_ref[...], aux)
    scarry_ref[...] = shared_now[CHUNK - 8 :, :]
    su_ref[...] = su
    shared = (su * sigmoid(su)).astype(bf16)
    b_rows = shared[:, :state_size]
    c_rows = shared[:, state_size:]
    scores = jnp.where(same, dot_nt(c_rows, b_rows), 0.0)
    step = softplus(step_ref[...] + bias) * live
    decay = dot_exact(summing, step * rate)
    decay_t = decay.T
    last = decay[CHUNK - 1 :, :]
    entry_scale = jnp.exp(decay) * aux[:, 8:9]
    end_scale = jnp.exp(last - decay) * aux[:, 9:10]
    keep = jnp.exp(last) * aux[:1, 10:11]
    state = state_ref[...]
    state_low = state.astype(bf16)
    entry_ref[...] = state_low[None]
    past = dot_nn(c_rows, state_low)
    for pair in range(pairs):
        lanes = slice(pair * LANES, (pair + 1) * LANES)
        head = 2 * pair
        now = proj_ref[:, lanes].astype(f32)
        window = jnp.concatenate([carry_ref[:, lanes], now], axis=0)
        carry_ref[:, lanes] = now[CHUNK - 8 :, :]
        u = conv_rows(window, tapi_ref[:, lanes].astype(f32), aux)
        u_ref[:, lanes] = u.astype(bf16)
        x = u * sigmoid(u)
        scaled = x * halves(lane_low, step, head)
        mixing = jnp.concatenate(
            [
                (
                    scores
                    * jnp.exp(jnp.minimum(decay[:, h : h + 1] - decay_t[h : h + 1, :], 0.0))
                ).astype(bf16)
                for h in (head, head + 1)
            ],
            axis=1,
        )
        stacked = jnp.concatenate(
            [jnp.where(lane_low, scaled, 0.0), jnp.where(lane_low, 0.0, scaled)], axis=0
        ).astype(bf16)
        inside = dot_nn(mixing, stacked)
        xw_ref[:, lanes] = (scaled * halves(lane_low, end_scale, head)).astype(bf16)
        mixed = (
            inside
            + past[:, lanes] * halves(lane_low, entry_scale, head)
            + halves(lane_low[:1], skips, head) * x
        ) * live
        mixed_ref[:, lanes] = mixed.astype(bf16)
        state_ref[:, lanes] = state[:, lanes] * halves(lane_low[:1], keep, head)
    state_ref[...] += dot_tn(b_rows, xw_ref[...])


def token_scales(sums, full_inner):
    columns = sums.T
    inv = lax.rsqrt(columns[:, 0:1] / full_inner + epsilon)
    return inv, inv * columns[:, 1:2] / full_inner


def silu_slope(v, s):
    return s * (1.0 + v * (1.0 - s))


def backward_kernel(
    proj_ref,
    praw_ref,
    u_ref,
    su_ref,
    entry_ref,
    grad_ref,
    tapi_ref,
    taps_ref,
    heads_ref,
    aux_ref,
    segr_ref,
    dproj_ref,
    wide_ref,
    shared_ref,
    state_ref,
    ahead_ref,
    sahead_ref,
    xw_ref,
    ge_ref,
    row_ref,
    proda_ref,
    prodb_ref,
):
    width = u_ref.shape[1]
    chunks = pl.num_programs(0)
    pairs = width // LANES
    shared_size = su_ref.shape[1]
    state_size = shared_size // 2
    shared_cols = slice(width, width + shared_size)
    step_cols = slice(width + shared_size, width + shared_size + LANES)
    chunk = chunks - 1 - pl.program_id(0)

    @pl.when(pl.program_id(0) == 0)
    def _():
        for ref in (state_ref, ahead_ref, sahead_ref, row_ref, wide_ref, shared_ref):
            ref[...] = jnp.zeros_like(ref)

    rows = lax.broadcasted_iota(jnp.int32, (CHUNK, CHUNK), 0)
    cols = lax.broadcasted_iota(jnp.int32, (CHUNK, CHUNK), 1)
    upper = rows <= cols
    summing = (rows >= cols).astype(f32)
    unsumming = upper.astype(f32)
    last_row = (lax.broadcasted_iota(jnp.int32, (CHUNK, LANES), 0) == CHUNK - 1).astype(f32)
    lane_ids = lax.broadcasted_iota(jnp.int32, (CHUNK, LANES), 1)
    lane_low = lane_ids < HEAD_DIM
    bias = heads_ref[0:1, :]
    rate = -jnp.exp(heads_ref[1:2, :])
    skips = heads_ref[2:3, :]
    place = (
        lax.broadcasted_iota(jnp.int32, (width, LANES), 0) // HEAD_DIM
        == lax.broadcasted_iota(jnp.int32, (width, LANES), 1)
    ).astype(bf16)

    aux = aux_ref[...]
    live = aux[:, 7:8]
    same = upper & (aux[:, 0:1] == segr_ref[pl.ds(chunk, 1), :])
    su = su_ref[...]
    su_sig = sigmoid(su)
    shared = (su * su_sig).astype(bf16)
    b_rows = shared[:, :state_size]
    c_rows = shared[:, state_size:]
    scores = jnp.where(same, dot_nt(b_rows, c_rows), 0.0)
    pre = praw_ref[...] + bias
    step = softplus(pre) * live
    decay = dot_exact(summing, step * rate)
    decay_t = decay.T
    last = decay[CHUNK - 1 :, :]
    entry_scale = jnp.exp(decay) * aux[:, 8:9]
    end_scale = jnp.exp(last - decay) * aux[:, 9:10]
    keep = jnp.exp(last) * aux[:1, 10:11]
    entry = entry_ref[0]
    dstate = state_ref[...]
    dstate_low = dstate.astype(bf16)
    past = dot_nn(c_rows, entry)
    bds = dot_nn(b_rows, dstate_low)
    score_grad = jnp.zeros((CHUNK, CHUNK), f32)
    col_part = jnp.zeros((CHUNK, LANES), f32)
    for pair in range(pairs):
        lanes = slice(pair * LANES, (pair + 1) * LANES)
        head = 2 * pair
        g_low = grad_ref[:, lanes]
        g = g_low.astype(f32)
        u = u_ref[:, lanes].astype(f32)
        u_sig = sigmoid(u)
        x = u * u_sig
        step_c = halves(lane_low, step, head)
        scaled = x * step_c
        stacked = jnp.concatenate(
            [jnp.where(lane_low, scaled, 0.0), jnp.where(lane_low, 0.0, scaled)], axis=0
        ).astype(bf16)
        dmix = dot_nt(stacked, g_low)
        mixing = []
        for k, h in enumerate((head, head + 1)):
            decays = jnp.exp(jnp.minimum(decay_t[h : h + 1, :] - decay[:, h : h + 1], 0.0))
            dmix_h = dmix[k * CHUNK : (k + 1) * CHUNK, :]
            score_grad = score_grad + dmix_h * decays
            mixing_h = scores * decays
            mixing.append(mixing_h.astype(bf16))
            both = mixing_h * dmix_h
            col_part = jnp.where(lane_ids == h, jnp.sum(both, axis=1, keepdims=True), col_part)
            row_ref[h : h + 1, :] = jnp.sum(both, axis=0, keepdims=True)
        g_stacked = jnp.concatenate(
            [jnp.where(lane_low, g, 0.0), jnp.where(lane_low, 0.0, g)], axis=0
        ).astype(bf16)
        end_c = halves(lane_low, end_scale, head)
        entry_c = halves(lane_low, entry_scale, head)
        keep_c = halves(lane_low[:1], keep, head)
        from_state = end_c * bds[:, lanes]
        dscaled = dot_nn(jnp.concatenate(mixing, axis=1), g_stacked) + from_state
        xw_ref[:, lanes] = (scaled * end_c).astype(bf16)
        q = scaled * from_state
        ge = g * entry_c
        ge_ref[:, lanes] = ge.astype(bf16)
        dstate_p = dstate[:, lanes]
        tail = jnp.sum(q, axis=0, keepdims=True) + keep_c * jnp.sum(
            dstate_p * entry[:, lanes].astype(f32), axis=0, keepdims=True
        )
        proda_ref[:, lanes] = x * dscaled
        prodb_ref[:, lanes] = ge * past[:, lanes] - q + last_row * tail
        state_ref[:, lanes] = dstate_p * keep_c
        dx = step_c * dscaled + halves(lane_low[:1], skips, head) * g
        du = dx * silu_slope(u, u_sig)
        window = jnp.concatenate([du, ahead_ref[:, lanes]], axis=0)
        ahead_ref[:, lanes] = du[:8, :]
        cin = proj_ref[:, lanes].astype(f32)
        taps = tapi_ref[:, lanes].astype(f32)
        dcin = taps[3:4, :] * du
        wide_ref[3:4, lanes] += jnp.sum(cin * du, axis=0, keepdims=True)
        for offset in range(1, 4):
            moved = ahead_shift(window, offset) * aux[:, 3 + offset : 4 + offset]
            dcin = dcin + taps[3 - offset : 4 - offset, :] * moved
            wide_ref[3 - offset : 4 - offset, lanes] += jnp.sum(
                cin * moved, axis=0, keepdims=True
            )
        dproj_ref[:, lanes] = dcin.astype(bf16)
        wide_ref[5:6, lanes] += jnp.sum(g * x, axis=0, keepdims=True)
    score_low = jnp.where(same, score_grad, 0.0).astype(bf16)
    ge_all = ge_ref[...]
    db = dot_nn(score_low, c_rows) + dot_nt(xw_ref[...], dstate_low)
    dc = dot_tn(score_low, b_rows) + dot_nt(ge_all, entry)
    state_ref[...] += dot_tn(c_rows, ge_all)
    ds = jnp.concatenate([db, dc], axis=1) * silu_slope(su, su_sig)
    window = jnp.concatenate([ds, sahead_ref[...]], axis=0)
    sahead_ref[...] = ds[:8, :]
    taps = taps_ref[...]
    sin = proj_ref[:, shared_cols].astype(f32)
    dsin = taps[3:4, :] * ds
    shared_ref[3:4, :] += jnp.sum(sin * ds, axis=0, keepdims=True)
    for offset in range(1, 4):
        moved = ahead_shift(window, offset) * aux[:, 3 + offset : 4 + offset]
        dsin = dsin + taps[3 - offset : 4 - offset, :] * moved
        shared_ref[3 - offset : 4 - offset, :] += jnp.sum(sin * moved, axis=0, keepdims=True)
    dproj_ref[:, shared_cols] = dsin.astype(bf16)
    ddecay = row_ref[...].T - col_part + dot_split(prodb_ref[...], place)
    dlog = dot_exact(unsumming, ddecay)
    dstep = (dot_split(proda_ref[...], place) + rate * dlog) * live * sigmoid(pre)
    dproj_ref[:, step_cols] = dstep.astype(bf16)
    wide_ref[6:7, :LANES] += jnp.sum(dstep, axis=0, keepdims=True)
    wide_ref[6:7, LANES : 2 * LANES] += jnp.sum(step * dlog, axis=0, keepdims=True) * rate


def token_facts(segments):
    length = segments.shape[0]
    chunks = length // CHUNK
    columns = [segments]
    for offset in range(1, 4):
        earlier = jnp.concatenate([jnp.full((offset,), -1, jnp.int32), segments[: length - offset]])
        columns.append(earlier == segments)
    for offset in range(1, 4):
        later = jnp.concatenate([segments[offset:], jnp.full((offset,), -1, jnp.int32)])
        columns.append(later == segments)
    columns.append(segments != 0)
    blocks = segments.reshape(chunks, CHUNK)
    last = blocks[:, CHUNK - 1 :]
    prior = jnp.concatenate([jnp.full((1, 1), -1, jnp.int32), last[: chunks - 1]], axis=0)
    columns.append((blocks == prior).reshape(length))
    columns.append((blocks == last).reshape(length))
    columns.append(jnp.broadcast_to(last == prior, blocks.shape).reshape(length))
    columns += [jnp.zeros_like(segments)] * 5
    aux = jnp.stack([c.astype(f32) for c in columns], axis=1)
    return aux, blocks.astype(f32)


def chunk_spec(columns, last):
    if last is None:
        return pl.BlockSpec((CHUNK, columns), lambda i: (i, 0))
    return pl.BlockSpec((CHUNK, columns), lambda i: (last - i, 0))


def fixed_spec(values):
    zeros = (0,) * values.ndim
    return pl.BlockSpec(values.shape, lambda i: zeros)


def run_forward(proj, praw, tapi, taps, heads, aux, segr):
    length = proj.shape[0]
    width = tapi.shape[1]
    shared_size = taps.shape[1]
    state_size = shared_size // 2
    chunks = length // CHUNK
    sds = jax.ShapeDtypeStruct
    return pl.pallas_call(
        forward_kernel,
        grid=(chunks,),
        in_specs=[
            chunk_spec(proj.shape[1], None),
            chunk_spec(LANES, None),
            fixed_spec(tapi),
            fixed_spec(taps),
            fixed_spec(heads),
            chunk_spec(aux.shape[1], None),
            fixed_spec(segr),
        ],
        out_specs=[
            chunk_spec(width, None),
            chunk_spec(width, None),
            chunk_spec(shared_size, None),
            pl.BlockSpec((1, state_size, width), lambda i: (i, 0, 0)),
        ],
        out_shape=(
            sds((length, width), bf16),
            sds((length, width), bf16),
            sds((length, shared_size), f32),
            sds((chunks, state_size, width), bf16),
        ),
        scratch_shapes=[
            pltpu.VMEM((state_size, width), f32),
            pltpu.VMEM((8, width), f32),
            pltpu.VMEM((8, shared_size), f32),
            pltpu.VMEM((CHUNK, width), bf16),
        ],
        name="scan_forward",
        cost_estimate=cost(18),
    )(proj, praw, tapi, taps, heads, aux, segr)


def run_backward(proj, praw, u, su, entry, grad, tapi, taps, heads, aux, segr):
    length, width = u.shape
    shared_size = su.shape[1]
    state_size = shared_size // 2
    chunks = length // CHUNK
    last = chunks - 1
    columns = width + shared_size + LANES
    sds = jax.ShapeDtypeStruct
    return pl.pallas_call(
        backward_kernel,
        grid=(chunks,),
        in_specs=[
            chunk_spec(proj.shape[1], last),
            chunk_spec(LANES, last),
            chunk_spec(width, last),
            chunk_spec(shared_size, last),
            pl.BlockSpec((1, state_size, width), lambda i: (last - i, 0, 0)),
            chunk_spec(width, last),
            fixed_spec(tapi),
            fixed_spec(taps),
            fixed_spec(heads),
            chunk_spec(aux.shape[1], last),
            fixed_spec(segr),
        ],
        out_specs=[
            chunk_spec(columns, last),
            pl.BlockSpec((8, width), lambda i: (0, 0)),
            pl.BlockSpec((8, shared_size), lambda i: (0, 0)),
        ],
        out_shape=(
            sds((length, columns), bf16),
            sds((8, width), f32),
            sds((8, shared_size), f32),
        ),
        scratch_shapes=[
            pltpu.VMEM((state_size, width), f32),
            pltpu.VMEM((8, width), f32),
            pltpu.VMEM((8, shared_size), f32),
            pltpu.VMEM((CHUNK, width), bf16),
            pltpu.VMEM((CHUNK, width), bf16),
            pltpu.VMEM((LANES, CHUNK), f32),
            pltpu.VMEM((CHUNK, width), f32),
            pltpu.VMEM((CHUNK, width), f32),
        ],
        name="scan_backward",
        cost_estimate=cost(32),
    )(proj, praw, u, su, entry, grad, tapi, taps, heads, aux, segr)


def block_plan():
    count = lax.axis_size("dp")
    bits = []
    bit = count // 2
    while bit > 1:
        bits.append(bit)
        bit //= 2
    mixed = bits[:-2] + bits[-2:][::-1]
    by_core = (bits, mixed)
    stages = []
    for stage in range(len(bits)):
        stages.append([(i, i ^ by_core[i % 2][stage]) for i in range(count)])
    core = [(i, i ^ 1) for i in range(count)]
    device = np.zeros((count, count), np.int32)
    for own in range(count):
        for spot in range(count):
            other = own ^ 1 if spot >= count // 2 else own
            for stage, bit in enumerate(by_core[other % 2]):
                if (spot >> stage) & 1:
                    other ^= bit
            device[own, spot] = other
    table = jnp.asarray(device)[lax.axis_index("dp")]
    return stages, core, table


def core_groups():
    count = lax.axis_size("dp")
    groups = [list(range(side, count, 2)) for side in range(2)]
    return groups, jnp.asarray(
        [groups[0] + groups[1], groups[1] + groups[0]], jnp.int32
    )[lax.axis_index("dp") % 2]


def exchange(blocks, groups):
    return lax.all_to_all(
        blocks, "dp", 0, 0, axis_index_groups=groups, tiled=True
    )


def sum_blocks(blocks, rows):
    return jnp.sum(blocks.reshape(-1, rows, blocks.shape[1]).astype(f32), axis=0)


def total_over_dp(values):
    count = lax.axis_size("dp")
    bit = 1
    while bit < count:
        values = values + lax.ppermute(values, "dp", [(i, i ^ bit) for i in range(count)])
        bit *= 2
    return values


def swap(values):
    return lax.ppermute(values, "tensor", [(0, 1), (1, 0)])


def total_over_tensor(values):
    if lax.axis_size("tensor") == 2:
        return values + swap(values)
    return lax.psum(values, "tensor")


def both_halves(own):
    if lax.axis_size("tensor") == 2:
        return own, swap(own)
    whole = lax.all_gather(own, "tensor", axis=0, tiled=True)
    return whole, whole


def token_starts(blocks):
    if lax.axis_size("tensor") == 2:
        index = lax.axis_index("tensor")
        return jnp.stack([index * (blocks // 2), (1 - index) * (blocks // 2)]).astype(jnp.int32)
    return jnp.zeros((2,), jnp.int32)


def add_halves(send, keep):
    if lax.axis_size("tensor") == 2:
        return keep.astype(f32) + swap(send).astype(f32)
    whole = jnp.concatenate([send.astype(bf16), keep.astype(bf16)], axis=0)
    return lax.psum_scatter(whole, "tensor", scatter_dimension=0, tiled=True).astype(f32)


def own_block(step, starts, own_blocks):
    return jnp.clip(step - starts[0], 0, own_blocks - 1)


def other_block(step, starts, own_blocks):
    return jnp.clip(step - starts[1], 0, own_blocks - 1)


def place_blocks(table_ref, low_ref, high_ref, whole_ref, sem_ref):
    count = table_ref.shape[0]
    rows = whole_ref.shape[0] // count
    copies = []
    for spot in range(count):
        source = low_ref if spot < count // 2 else high_ref
        where = pl.multiple_of(table_ref[spot] * rows, rows)
        copies.append(
            pltpu.make_async_copy(
                source.at[pl.ds((spot % (count // 2)) * rows, rows), :],
                whole_ref.at[pl.ds(where, rows), :],
                sem_ref.at[spot],
            )
        )
    for copy in copies:
        copy.start()
    for copy in copies:
        copy.wait()


def project_kernel(
    starts_ref,
    table_ref,
    own_ref,
    other_ref,
    spread_ref,
    low_ref,
    high_ref,
    proj_ref,
    step_ref,
    normed_ref,
    turned_ref,
    weights_ref,
    taps_ref,
    scale_ref,
    sem_ref,
    *,
    own_blocks,
    heads,
):
    step = pl.program_id(0)
    model_dim, columns = weights_ref.shape

    @pl.when(step == 0)
    def _():
        place_blocks(table_ref, low_ref, high_ref, weights_ref, sem_ref)
        extra = weights_ref[:, columns - LANES :].astype(f32).T
        scale_ref[...] = jnp.broadcast_to(extra[heads : heads + 1, :], scale_ref.shape)
        taps = extra[heads + 1 : heads + 5, :]
        taps = jnp.concatenate([taps, jnp.zeros_like(taps)], axis=0).astype(bf16)
        taps_ref[...] = dot_nn(taps, spread_ref[...])

    mine = (step >= starts_ref[0]) & (step < starts_ref[0] + own_blocks)
    tokens = jnp.where(mine, own_ref[...].astype(f32), other_ref[...].astype(f32))
    inv = lax.rsqrt(jnp.mean(tokens * tokens, axis=-1, keepdims=True) + epsilon)
    normed = (tokens * inv * scale_ref[:1, :]).astype(bf16)
    normed_ref[...] = normed
    turned_ref[...] = normed.T
    proj = dot_nn(normed, weights_ref[...])
    proj_ref[...] = proj[:, : columns - LANES].astype(bf16)
    step_ref[...] = proj[:, columns - LANES :]


def run_project(starts, table, own, other, spread, low, high, heads):
    own_rows, model_dim = own.shape
    columns = low.shape[1]
    own_blocks = own_rows // TOKEN_BLOCK
    blocks = own_blocks * (2 if other is not own else 1)
    length = blocks * TOKEN_BLOCK
    sds = jax.ShapeDtypeStruct
    return pl.pallas_call(
        partial(project_kernel, own_blocks=own_blocks, heads=heads),
        grid_spec=pltpu.PrefetchScalarGridSpec(
            num_scalar_prefetch=2,
            grid=(blocks,),
            in_specs=[
                pl.BlockSpec(
                    (TOKEN_BLOCK, model_dim), lambda i, s, t: (own_block(i, s, own_blocks), 0)
                ),
                pl.BlockSpec(
                    (TOKEN_BLOCK, model_dim), lambda i, s, t: (other_block(i, s, own_blocks), 0)
                ),
                pl.BlockSpec(spread.shape, lambda i, s, t: (0, 0)),
                pl.BlockSpec(memory_space=pl.ANY),
                pl.BlockSpec(memory_space=pl.ANY),
            ],
            out_specs=[
                pl.BlockSpec((TOKEN_BLOCK, columns - LANES), lambda i, s, t: (i, 0)),
                pl.BlockSpec((TOKEN_BLOCK, LANES), lambda i, s, t: (i, 0)),
                pl.BlockSpec((TOKEN_BLOCK, model_dim), lambda i, s, t: (i, 0)),
                pl.BlockSpec((model_dim, TOKEN_BLOCK), lambda i, s, t: (0, i)),
                pl.BlockSpec((model_dim, columns), lambda i, s, t: (0, 0)),
                pl.BlockSpec((8, spread.shape[1]), lambda i, s, t: (0, 0)),
                pl.BlockSpec((8, model_dim), lambda i, s, t: (0, 0)),
            ],
            scratch_shapes=[pltpu.SemaphoreType.DMA((table.shape[0],))],
        ),
        out_shape=(
            sds((length, columns - LANES), bf16),
            sds((length, LANES), f32),
            sds((length, model_dim), bf16),
            sds((model_dim, length), bf16),
            sds((model_dim, columns), bf16),
            sds((8, spread.shape[1]), f32),
            sds((8, model_dim), f32),
        ),
        name="norm_project",
        cost_estimate=cost(9),
    )(starts, table, own, other, spread, low, high)


def token_sum(values):
    total = values[:, :LANES]
    for at in range(LANES, values.shape[1], LANES):
        total = total + values[:, at : at + LANES]
    return jnp.sum(total.T, axis=0, keepdims=True)


def out_grad_kernel(
    starts_ref,
    table_ref,
    own_ref,
    other_ref,
    low_ref,
    high_ref,
    normed_ref,
    mixed_ref,
    gain_ref,
    gate_ref,
    nog_ref,
    turned_ref,
    sums_ref,
    weights_ref,
    sem_ref,
    *,
    own_blocks,
):
    step = pl.program_id(0)
    width = mixed_ref.shape[1]

    @pl.when(step == 0)
    def _():
        place_blocks(table_ref, low_ref, high_ref, weights_ref, sem_ref)

    mine = (step >= starts_ref[0]) & (step < starts_ref[0] + own_blocks)
    tokens = jnp.where(mine, own_ref[...].astype(f32), other_ref[...].astype(f32)).astype(bf16)
    turned_ref[...] = tokens.T
    gate = dot_nn(normed_ref[...], weights_ref[:, :width])
    gate_ref[...] = gate.astype(bf16)
    nog = dot_nn(tokens, weights_ref[:, width:])
    nog_ref[...] = nog.astype(bf16)
    gated = mixed_ref[...].astype(f32) * (gate * sigmoid(gate))
    sums_ref[...] = jnp.concatenate(
        [
            token_sum(gated * gated),
            token_sum(nog * gain_ref[...].astype(f32) * gated),
            jnp.zeros((6, TOKEN_BLOCK), f32),
        ],
        axis=0,
    )


def run_out_grad(starts, table, own, other, low, high, normed, mixed, gain):
    own_rows, model_dim = own.shape
    length, width = mixed.shape
    own_blocks = own_rows // TOKEN_BLOCK
    blocks = length // TOKEN_BLOCK
    sds = jax.ShapeDtypeStruct
    return pl.pallas_call(
        partial(out_grad_kernel, own_blocks=own_blocks),
        grid_spec=pltpu.PrefetchScalarGridSpec(
            num_scalar_prefetch=2,
            grid=(blocks,),
            in_specs=[
                pl.BlockSpec(
                    (TOKEN_BLOCK, model_dim), lambda i, s, t: (own_block(i, s, own_blocks), 0)
                ),
                pl.BlockSpec(
                    (TOKEN_BLOCK, model_dim), lambda i, s, t: (other_block(i, s, own_blocks), 0)
                ),
                pl.BlockSpec(memory_space=pl.ANY),
                pl.BlockSpec(memory_space=pl.ANY),
                pl.BlockSpec((TOKEN_BLOCK, model_dim), lambda i, s, t: (i, 0)),
                pl.BlockSpec((TOKEN_BLOCK, width), lambda i, s, t: (i, 0)),
                pl.BlockSpec((1, width), lambda i, s, t: (0, 0)),
            ],
            out_specs=[
                pl.BlockSpec((TOKEN_BLOCK, width), lambda i, s, t: (i, 0)),
                pl.BlockSpec((TOKEN_BLOCK, width), lambda i, s, t: (i, 0)),
                pl.BlockSpec((model_dim, TOKEN_BLOCK), lambda i, s, t: (0, i)),
                pl.BlockSpec((8, TOKEN_BLOCK), lambda i, s, t: (0, i)),
                pl.BlockSpec((model_dim, 2 * width), lambda i, s, t: (0, 0)),
            ],
            scratch_shapes=[pltpu.SemaphoreType.DMA((table.shape[0],))],
        ),
        out_shape=(
            sds((length, width), bf16),
            sds((length, width), bf16),
            sds((model_dim, length), bf16),
            sds((8, length), f32),
            sds((model_dim, 2 * width), bf16),
        ),
        name="out_grad",
        cost_estimate=cost(9),
    )(starts, table, own, other, low, high, normed, mixed, gain)


def store_blocks(table_ref, source_ref, keep_ref, send_ref):
    count = table_ref.shape[0]
    rows = source_ref.shape[0] // count
    half = count // 2
    for spot in range(half):
        where = pl.multiple_of(table_ref[spot] * rows, rows)
        keep_ref[spot * rows : (spot + 1) * rows, :] = source_ref[pl.ds(where, rows), :]
    for spot in range(half):
        where = pl.multiple_of(table_ref[half + spot] * rows, rows)
        send_ref[spot * rows : (spot + 1) * rows, :] = source_ref[pl.ds(where, rows), :].astype(
            bf16
        )


def gated_kernel(
    table_ref,
    gate_ref,
    nog_ref,
    mixed_ref,
    sums_ref,
    aux_ref,
    gain_ref,
    gturned_ref,
    nturned_ref,
    out_ref,
    dgate_ref,
    grad_ref,
    row_ref,
    keep_ref,
    send_ref,
    total_ref,
    *,
    full_inner,
):
    step = pl.program_id(0)
    width = gate_ref.shape[1]
    inv, mean = token_scales(sums_ref[...], full_inner)
    gain = gain_ref[...].astype(f32)
    gate = gate_ref[...].astype(f32)
    gate_sig = sigmoid(gate)
    gate_silu = gate * gate_sig
    mixed = mixed_ref[...].astype(f32)
    unit = mixed * gate_silu * inv
    nog = nog_ref[...].astype(f32)
    grad = inv * (nog * gain - unit * mean)
    dgate = (grad * mixed * silu_slope(gate, gate_sig)).astype(bf16)
    dgate_ref[...] = dgate
    grad_ref[...] = (grad * gate_silu * aux_ref[:, 7:8]).astype(bf16)
    normed_out = (unit * gain).astype(bf16)
    out_ref[...] = normed_out
    row = jnp.sum((nog * unit).reshape(-1, 8, width), axis=0)
    part_gate = dot_nn(nturned_ref[...], dgate)
    part_out = dot_nn(gturned_ref[...], normed_out)

    @pl.when(step == 0)
    def _():
        total_ref[:, :width] = part_gate
        total_ref[:, width:] = part_out
        row_ref[...] = row

    @pl.when(step > 0)
    def _():
        total_ref[:, :width] += part_gate
        total_ref[:, width:] += part_out
        row_ref[...] += row

    @pl.when(step == pl.num_programs(0) - 1)
    def _():
        store_blocks(table_ref, total_ref, keep_ref, send_ref)


def run_gated(table, gate, nog, mixed, sums, aux, gain, gturned, nturned, full_inner):
    length, width = gate.shape
    model_dim = gturned.shape[0]
    blocks = length // TOKEN_BLOCK
    sds = jax.ShapeDtypeStruct
    tokens = pl.BlockSpec((TOKEN_BLOCK, width), lambda i, t: (i, 0))
    turned = pl.BlockSpec((model_dim, TOKEN_BLOCK), lambda i, t: (0, i))
    halves_spec = pl.BlockSpec((model_dim // 2, 2 * width), lambda i, t: (0, 0))
    return pl.pallas_call(
        partial(gated_kernel, full_inner=float(full_inner)),
        grid_spec=pltpu.PrefetchScalarGridSpec(
            num_scalar_prefetch=1,
            grid=(blocks,),
            in_specs=[
                tokens,
                tokens,
                tokens,
                pl.BlockSpec((8, TOKEN_BLOCK), lambda i, t: (0, i)),
                pl.BlockSpec((TOKEN_BLOCK, aux.shape[1]), lambda i, t: (i, 0)),
                pl.BlockSpec((1, width), lambda i, t: (0, 0)),
                turned,
                turned,
            ],
            out_specs=[
                tokens,
                tokens,
                tokens,
                pl.BlockSpec((8, width), lambda i, t: (0, 0)),
                halves_spec,
                halves_spec,
            ],
            scratch_shapes=[pltpu.VMEM((model_dim, 2 * width), f32)],
        ),
        out_shape=(
            sds((length, width), bf16),
            sds((length, width), bf16),
            sds((length, width), bf16),
            sds((8, width), f32),
            sds((model_dim // 2, 2 * width), f32),
            sds((model_dim // 2, 2 * width), bf16),
        ),
        name="gated_grad",
        cost_estimate=cost(12),
    )(table, gate, nog, mixed, sums, aux, gain, gturned, nturned)


def out_kernel(starts_ref, rows_ref, weights_ref, send_ref, keep_ref):
    step = pl.program_id(0)
    half = pl.num_programs(0) // 2
    rows = dot_nt(rows_ref[...], weights_ref[...]).astype(bf16)

    @pl.when(step < half)
    def _():
        send_ref[...] = rows

    @pl.when(step >= half)
    def _():
        keep_ref[...] = rows


def run_out(starts, rows, weights):
    length, width = rows.shape
    model_dim = weights.shape[0]
    blocks = length // TOKEN_BLOCK
    half = blocks // 2
    sds = jax.ShapeDtypeStruct
    return pl.pallas_call(
        out_kernel,
        grid_spec=pltpu.PrefetchScalarGridSpec(
            num_scalar_prefetch=1,
            grid=(blocks,),
            in_specs=[
                pl.BlockSpec((TOKEN_BLOCK, width), lambda i, s: (lax.rem(i + s[0], blocks), 0)),
                pl.BlockSpec((model_dim, width), lambda i, s: (0, 1)),
            ],
            out_specs=[
                pl.BlockSpec((TOKEN_BLOCK, model_dim), lambda i, s: (jnp.minimum(i, half - 1), 0)),
                pl.BlockSpec((TOKEN_BLOCK, model_dim), lambda i, s: (jnp.maximum(i - half, 0), 0)),
            ],
        ),
        out_shape=(
            sds((length // 2, model_dim), bf16),
            sds((length // 2, model_dim), bf16),
        ),
        name="out_project",
        cost_estimate=cost(4),
    )(starts, rows, weights)


def norm_grad_kernel(
    starts_ref, dgate_ref, dproj_ref, gates_ref, weights_ref, normed_ref, grad_ref, total_ref
):
    grad = dot_nt(dgate_ref[...], gates_ref[...]) + dot_nt(dproj_ref[...], weights_ref[...])
    grad_ref[...] = grad.astype(grad_ref.dtype)
    part = jnp.sum(
        (grad * normed_ref[...].astype(f32)).reshape(-1, 8, grad.shape[1]), axis=0
    )

    @pl.when(pl.program_id(0) == 0)
    def _():
        total_ref[...] = part

    @pl.when(pl.program_id(0) > 0)
    def _():
        total_ref[...] += part


def run_norm_grad(starts, dgate, dproj, gates, weights, normed, kind):
    length, columns = dproj.shape
    width = dgate.shape[1]
    model_dim = weights.shape[0]
    blocks = length // TOKEN_BLOCK // 2
    sds = jax.ShapeDtypeStruct
    return pl.pallas_call(
        norm_grad_kernel,
        grid_spec=pltpu.PrefetchScalarGridSpec(
            num_scalar_prefetch=1,
            grid=(blocks,),
            in_specs=[
                pl.BlockSpec((TOKEN_BLOCK, width), lambda i, s: (i + s[0], 0)),
                pl.BlockSpec((TOKEN_BLOCK, columns), lambda i, s: (i + s[0], 0)),
                pl.BlockSpec((model_dim, width), lambda i, s: (0, 0)),
                pl.BlockSpec((model_dim, columns), lambda i, s: (0, 0)),
                pl.BlockSpec((TOKEN_BLOCK, model_dim), lambda i, s: (i + s[0], 0)),
            ],
            out_specs=[
                pl.BlockSpec((TOKEN_BLOCK, model_dim), lambda i, s: (i, 0)),
                pl.BlockSpec((8, model_dim), lambda i, s: (0, 0)),
            ],
        ),
        out_shape=(sds((length // 2, model_dim), kind), sds((8, model_dim), f32)),
        name="normed_grad",
        cost_estimate=cost(5),
    )(starts, dgate, dproj, gates, weights, normed)


def weight_grad_kernel(table_ref, turned_ref, dproj_ref, keep_ref, send_ref, total_ref):
    total_ref[...] = dot_nn(turned_ref[...], dproj_ref[...])
    store_blocks(table_ref, total_ref, keep_ref, send_ref)


def run_weight_grad(table, turned, dproj):
    model_dim, length = turned.shape
    columns = dproj.shape[1]
    tile = 3 * LANES if columns % (3 * LANES) == 0 else LANES
    sds = jax.ShapeDtypeStruct
    return pl.pallas_call(
        weight_grad_kernel,
        grid_spec=pltpu.PrefetchScalarGridSpec(
            num_scalar_prefetch=1,
            grid=(columns // tile,),
            in_specs=[
                pl.BlockSpec((model_dim, length), lambda i, t: (0, 0)),
                pl.BlockSpec((length, tile), lambda i, t: (0, i)),
            ],
            out_specs=[
                pl.BlockSpec((model_dim // 2, tile), lambda i, t: (0, i)),
                pl.BlockSpec((model_dim // 2, tile), lambda i, t: (0, i)),
            ],
            scratch_shapes=[pltpu.VMEM((model_dim, tile), f32)],
        ),
        out_shape=(
            sds((model_dim // 2, columns), f32),
            sds((model_dim // 2, columns), bf16),
        ),
        name="weight_grad",
        cost_estimate=cost(6),
    )(table, turned, dproj)


def after(value, *others):
    return lax.optimization_barrier((value,) + others)[0]


def cost(microseconds):
    return pl.CostEstimate(flops=int(microseconds * 1.1e9), transcendentals=0, bytes_accessed=0)


def pad_to(values, axis, size):
    pads = [(0, 0)] * values.ndim
    pads[axis] = (0, size - values.shape[axis])
    return jnp.pad(values, pads)


def body(
    hidden_in,
    segment_ids,
    norm_gain,
    proj_inner,
    proj_shared,
    proj_step,
    conv_inner,
    conv_shared,
    step_bias,
    log_decay,
    skip_gain,
    gate_gain,
    proj_out,
    out_grad,
):
    dp_count = lax.axis_size("dp")
    dp_index = lax.axis_index("dp")
    rows = proj_inner.shape[0]
    length = segment_ids.shape[0]
    model_dim = hidden_in.shape[1]
    local_inner = proj_inner.shape[2]
    heads = proj_step.shape[1]
    state_size = proj_shared.shape[2]
    kernel_len = conv_inner.shape[0]
    shared_size = 2 * state_size
    full_inner = local_inner * lax.axis_size("tensor")
    width = -(-local_inner // (2 * LANES)) * 2 * LANES
    tap_block = conv_shared.shape[2]
    tap_count = kernel_len * 2 * tap_block
    stages, core, table = block_plan()
    groups, core_table = core_groups()
    blocks = length // TOKEN_BLOCK
    starts = token_starts(blocks)
    two = lax.axis_size("tensor") == 2

    hidden_own, hidden_other = both_halves(hidden_in)
    tap_rows = conv_shared.transpose(1, 2, 0).reshape(2 * tap_block, kernel_len)
    tap_rows = pad_to(tap_rows, 0, rows)
    packed = jnp.concatenate(
        [
            pad_to(proj_inner[:, 1, :], 1, width),
            proj_shared.reshape(rows, shared_size),
            pad_to(jnp.concatenate([proj_step, norm_gain[:, None], tap_rows], axis=1), 1, LANES),
        ],
        axis=1,
    )
    later = jnp.concatenate(
        [pad_to(proj_inner[:, 0, :], 1, width), pad_to(proj_out.T, 1, width)], axis=1
    )
    at = jnp.arange(model_dim)
    block, inside = at // rows, at % rows
    side, spot = inside // tap_block, inside % tap_block
    spread = jnp.where(side < 2, side * state_size + block * tap_block + spot, -1)
    spread = (spread[:, None] == jnp.arange(shared_size)[None, :]).astype(bf16)
    aux, segr = token_facts(segment_ids)
    heads_block = jnp.stack([step_bias, log_decay, skip_gain])
    heads_block = pad_to(pad_to(heads_block, 1, LANES), 0, 8)
    tapi = pad_to(conv_inner, 1, width)
    gain = pad_to(gate_gain[None], 1, width)

    low = packed
    for number, stage in enumerate(stages):
        got = lax.ppermute(low, "dp", stage)
        if number == 0:
            got, spread, aux, segr, heads_block, tapi, gain, later = lax.optimization_barrier(
                (got, spread, aux, segr, heads_block, tapi, gain, later)
            )
        low = jnp.concatenate([low, got], axis=0)
    low, later = lax.optimization_barrier((low, later))
    high = lax.ppermute(low, "dp", core)
    later_low = exchange(jnp.concatenate([later] * (dp_count // 2), axis=0), groups)
    grad_own, grad_other = both_halves(after(out_grad, hidden_other))

    proj, praw, normed, normed_t, weights, taps, norm_scale = run_project(
        starts, table, hidden_own, hidden_other, spread, low, high, heads
    )
    norm_scale = norm_scale[:1]
    mixed, u, su, entry = run_forward(proj, praw, tapi, taps, heads_block, aux, segr)

    later_low, mixed, grad_other = lax.optimization_barrier((later_low, mixed, grad_other))
    later_high = lax.ppermute(later_low, "dp", core)
    gate, nog, grad_t, sums, later_rows = run_out_grad(
        starts, core_table, grad_own, grad_other, later_low, later_high, normed, mixed, gain
    )
    sums = total_over_tensor(sums)
    normed_out, dgate, mixed_grad, gain_rows, gkeep, gsend = run_gated(
        core_table, gate, nog, mixed, sums, aux, gain, grad_t, normed_t, full_inner
    )
    ggot = lax.ppermute(gsend, "dp", core)
    send_start = starts[1:] if two else jnp.zeros((1,), jnp.int32)
    keep_start = starts[:1] if two else jnp.full((1,), blocks // 2, jnp.int32)
    out_send, out_keep = run_out(send_start, normed_out, later_rows)
    ggot, out_send = lax.optimization_barrier((ggot, out_send))
    gsum = exchange((gkeep + ggot.astype(f32)).astype(bf16), groups)
    out_other = swap(out_send) if two else None

    dproj, wide, dtaps = run_backward(
        proj, praw, u, su, entry, mixed_grad, tapi, taps, heads_block, aux, segr
    )
    dproj, gsum = lax.optimization_barrier((dproj, gsum))
    if two:
        dproj, out_other = lax.optimization_barrier((dproj, out_other))
        out_half = out_keep.astype(f32) + out_other.astype(f32)
    else:
        out_half = add_halves(out_send, out_keep)
    hidden_out = (hidden_in.astype(f32) + out_half).astype(bf16)
    grad_send, norm_sum = run_norm_grad(
        send_start, dgate, dproj, later_rows, weights, normed, bf16
    )
    wkeep, wsend = run_weight_grad(core_table, normed_t, dproj)
    grad_keep, norm_more = run_norm_grad(
        keep_start, dgate, dproj, later_rows, weights, normed, f32
    )
    wgot = lax.ppermute(wsend, "dp", core)
    wgot, grad_keep = lax.optimization_barrier((wgot, grad_keep))
    wsum = exchange((wkeep + wgot.astype(f32)).astype(bf16), groups)
    if two:
        own_grad = grad_keep + swap(grad_send).astype(f32)
    else:
        own_grad = add_halves(grad_send, grad_keep)
    gsum = sum_blocks(gsum, rows)
    out_sum = gsum[:, width : width + local_inner].T
    wsum = sum_blocks(wsum, rows)
    ssum = wsum[:, width:]

    lanes = max(width, model_dim)
    norm_sum = jnp.sum(norm_sum + norm_more, axis=0, keepdims=True) / norm_scale
    small = jnp.concatenate(
        [
            pad_to(wide[:4], 1, lanes),
            pad_to(jnp.sum(gain_rows, axis=0, keepdims=True), 1, lanes),
            pad_to(wide[5:], 1, lanes),
            pad_to(dtaps[:kernel_len], 1, lanes),
            pad_to(norm_sum, 1, lanes),
            jnp.zeros((3, lanes), f32),
        ],
        axis=0,
    )
    small = total_over_dp(small)
    conv_total = small[:kernel_len, :local_inner]
    gain_total = small[4, :local_inner]
    skip_total = jnp.sum(small[5, :width].reshape(-1, HEAD_DIM), axis=1)[:heads]
    bias_total = small[6, :heads]
    decay_total = small[6, LANES : LANES + heads]
    small = total_over_tensor(small[8:16])
    norm_total = lax.dynamic_slice_in_dim(small[4, :model_dim], dp_index * rows, rows)
    taps_total = lax.dynamic_slice_in_dim(
        small[:kernel_len, :shared_size].reshape(kernel_len, 2, state_size),
        dp_index * tap_block,
        tap_block,
        axis=2,
    )
    inner_sum = jnp.stack([gsum[:, :local_inner], wsum[:, :local_inner]], axis=1)
    step_sum = ssum[:, shared_size : shared_size + heads]
    shared_total = total_over_tensor(ssum[:, :shared_size]).reshape(rows, 2, state_size)

    own = hidden_in.astype(f32)
    own_inv = lax.rsqrt(jnp.mean(own * own, axis=-1, keepdims=True) + epsilon)
    own_unit = own * own_inv
    scaled_in = own_grad * norm_scale
    hidden_grad = own_inv * (
        scaled_in - own_unit * jnp.mean(scaled_in * own_unit, axis=-1, keepdims=True)
    ) + out_grad.astype(f32)
    return (
        hidden_out,
        hidden_grad,
        norm_total,
        inner_sum,
        shared_total,
        step_sum,
        conv_total,
        taps_total,
        bias_total,
        decay_total,
        skip_total,
        gain_total,
        out_sum,
    )


def solution(mesh):
    in_specs = (
        P(("dp", "tensor"), None),
        P("dp"),
        P("dp"),
        P("dp", None, "tensor"),
        P("dp", None, None),
        P("dp", "tensor"),
        P(None, "tensor"),
        P(None, None, "dp"),
        P("tensor"),
        P("tensor"),
        P("tensor"),
        P("tensor"),
        P("tensor", "dp"),
        P(("dp", "tensor"), None),
    )
    out_specs = (
        P(("dp", "tensor"), None),
        P(("dp", "tensor"), None),
        P("dp"),
        P("dp", None, "tensor"),
        P("dp", None, None),
        P("dp", "tensor"),
        P(None, "tensor"),
        P(None, None, "dp"),
        P("tensor"),
        P("tensor"),
        P("tensor"),
        P("tensor"),
        P("tensor", "dp"),
    )
    return jax.shard_map(body, mesh=mesh, in_specs=in_specs, out_specs=out_specs, check_vma=False)
```

time: 264 us -> 216 us (0.82)
  Pallas kernels: 59.5 us -> 104 us
  waiting for transfers between devices: 68 us -> 28.6 us
  matrix products: 33.9 us -> 0 us
  other arithmetic: 31 us -> 15.4 us
  local copies, waits for them, and re-layouts: 36.1 us -> 26 us
  starting transfers between devices: 33.5 us -> 40.1 us
    pallas_call x2 -> x9, Pallas kernels: 59.5 us -> 104 us  [the longest x1 31.3 us: run_backward(): pl.pallas_call(backward_kernel, grid=(chunks,), in_specs=[chunk_spec(proj...]
    dot_general x6 -> x0, matrix products: 33.9 us -> none  [the longest x2 16.4 us: dot_nn(): lax.dot_general(a, b, (((1,), (0,)), ((), ())), preferred_element_type=f32)]
    ppermute x6 -> x7, waiting for transfers between devices: 33.3 us -> 5.23 us  [swap(): return lax.ppermute(values, 'tensor', [(0, 1), (1, 0)])]
    ppermute x16 -> x7, waiting for transfers between devices: 32.9 us -> 9.01 us  [the longest x3 6.84 us: body(): got = lax.ppermute(low, 'dp', stage)]
    all_to_all x0 -> x3, starting transfers between devices: none -> 15.7 us  [exchange(): lax.all_to_all(blocks, 'dp', 0, 0, axis_index_groups=groups, tiled=True)]
    ppermute x16 -> x7, starting transfers between devices: 20.4 us -> 7.61 us  [the longest x3 7.33 us: body(): got = lax.ppermute(low, 'dp', stage)]
    all_to_all x0 -> x3, waiting for transfers between devices: none -> 9.14 us  [exchange(): lax.all_to_all(blocks, 'dp', 0, 0, axis_index_groups=groups, tiled=True)]
    concatenate x2, local copies, waits for them, and re-layouts: 6.72 us -> 0.73 us  [the longest x1 0.68 us: body(): jnp.concatenate([later] * (dp_count // 2), axis=0)]
  transfers between devices with their start and end apart: 26 -> 21, of which waited for: 9 -> 12; matrix products, arithmetic and copies ran while one was open for 24% -> 15% of each run, Pallas kernels for 0% -> 29%
where the time goes in v2:
time: 216 us; the launch traced here: 215 us
  Pallas kernels  104 us (48%)
  starting transfers between devices  40.1 us (19%)
  waiting for transfers between devices  28.6 us (13%)
  local copies, waits for them, and re-layouts  26 us (12%)
  other arithmetic  15.4 us (7%)
    pallas_call x1, Pallas kernels, run_backward(): pl.pallas_call(backward_kernel, grid=(chunks,), in_specs=[chunk_spec(proj...  31.3 us
    pallas_call x1, Pallas kernels, run_forward(): pl.pallas_call(forward_kernel, grid=(chunks,), in_specs=[chunk_spec(proj....  17.1 us
    all_to_all x3, starting transfers between devices, exchange(): lax.all_to_all(blocks, 'dp', 0, 0, axis_index_groups=groups, tiled=True)  15.7 us
    pallas_call x1, Pallas kernels, run_gated(): pl.pallas_call(partial(gated_kernel, full_inner=float(full_inner)), grid_...  13.1 us
    pallas_call x2, Pallas kernels, run_norm_grad(): pl.pallas_call(norm_grad_kernel, grid_spec=pltpu.PrefetchScalarGridSpec(n...  10.7 us
    pallas_call x1, Pallas kernels, run_out_grad(): pl.pallas_call(partial(out_grad_kernel, own_blocks=own_blocks), grid_spec...  9.98 us
    ppermute x7, starting transfers between devices, swap(): return lax.ppermute(values, 'tensor', [(0, 1), (1, 0)])  9.77 us
    pallas_call x1, Pallas kernels, run_project(): pl.pallas_call(partial(project_kernel, own_blocks=own_blocks, heads=heads...  9.31 us
  transfers between devices with their start and end apart: 21, of which 12 were waited for; matrix products, arithmetic and copies ran while one was open for 15% of the time, Pallas kernels for 29%

profile of v2, /device:TPU:0, one launch (start us, length us, event | category | flops | bytes accessed | tf_op | source)
XLA Modules:
  0.0 214.8 jit_solution(18294180340774630029)
XLA Ops:
  5.2 4.1 %collective-permute-start.1 = (bf16[48,1152]{1,0:T(8,128)(2,1)S(1)}, bf16[48,1152]{1,0:T(8,128)(2,1)S(1)}, u32[]{:S(2)}, u32[]{:S(2)}) collective-permute-start(bf16[48,1152]{1,0:T(8,128)(2,1)S(1)} %pad_maximum_fusion.5), channel_id=1, source_target_pairs={{0,16},{2,18},{4,20},{6,22},{8,24},{10,26},{12,28},{14,30},{16,0},... | collective-permute-start | bytes 331784 | tf_op jit(solution)/shard_map/ppermute | solution.py:1080
  16.1 1.6 collective-permute-start.2
  17.8 4.4 %collective-permute-done.2 = bf16[96,1152]{1,0:T(8,128)(2,1)S(1)} collective-permute-done((bf16[96,1152]{1,0:T(8,128)(2,1)S(1)}, bf16[96,1152]{1,0:T(8,128)(2,1)S(1)}, u32[]{:S(2)}, u32[]{:S(2)}) %collective-permute-start.2) | collective-permute-done | bytes 221216 | tf_op jit(solution)/shard_map/ppermute | solution.py:1080
  22.2 1.6 collective-permute-start.3
  23.7 1.5 collective-permute-start
  28.1 2.5 %collective-permute-done.3 = bf16[192,1152]{1,0:T(8,128)(2,1)S(1)} collective-permute-done((bf16[192,1152]{1,0:T(8,128)(2,1)S(1)}, bf16[192,1152]{1,0:T(8,128)(2,1)S(1)}, u32[]{:S(2)}, u32[]{:S(2)}) %collective-permute-start.3) | collective-permute-done | bytes 442400 | tf_op jit(solution)/shard_map/ppermute | solution.py:1080
  36.1 4.4 %all-to-all-start = ((bf16[8,48,1536]{2,1,0:T(8,128)(2,1)}), bf16[8,48,1536]{2,1,0:T(8,128)(2,1)S(1)}, u32[]{:S(2)}, u32[]{:S(2)}) async-start(bf16[8,48,1536]{2,1,0:T(8,128)(2,1)} %bitcast.26), calls=%async_computation | async-start | bytes 2359296 | tf_op jit(solution)/shard_map/all_to_all | solution.py:498
  41.8 1.5 collective-permute-start.5
  43.3 9.3 %norm_project.1 = (bf16[1024,1024]{1,0:T(8,128)(2,1)}, f32[1024,128]{1,0:T(8,128)}, bf16[1024,768]{1,0:T(8,128)(2,1)}, bf16[768,1024]{1,0:T(8,128)(2,1)}, bf16[7...) custom-call(s32[2]{0:T(128)} %pad_add_fusion.1.starts_ref, s32[16]{0:T(128)} %fusion.36.table_ref, ...), custom_call_target="tpu_custom_call" | custom-call | flops 9900000256 | tf_op jit(solution)/shard_map/norm_project/pallas_call | solution.py:625
  52.6 17.1 %scan_forward.1 = (bf16[1024,768]{1,0:T(8,128)(2,1)}, bf16[1024,768]{1,0:T(8,128)(2,1)}, f32[1024,256]{1,0:T(8,128)}, bf16[8,128,768]{2,1,0:T(8,128)(2,1)}) custom-call(bf16[1024,1024]{1,0:T(8,128)(2,1)} %get-tuple-element.74.proj_ref, f32[1024,128]{1,0:T(8,128)} %get-tuple-element.75.step_ref.praw_ref, bf16[4,768]{1,0:T(4,128)(2,1)} %tapi_ref.1, ...), custom_call_target="tpu_custom_call" | custom-call | flops 19800000512 | tf_op jit(solution)/shard_map/scan_forward/pallas_call | solution.py:380
  70.5 2.2 %collective-permute-done.6.high_ref = bf16[384,1536]{1,0:T(8,128)(2,1)S(1)} collective-permute-done((bf16[384,1536]{1,0:T(8,128)(2,1)S(1)}, bf16[384,1536]{1,0:T(8,128)(2,1)S(1)}, u32[]{:S(2)}, u32[]{:S(2)}) %collective-permute-start.6) | collective-permute-done | bytes 1179680 | tf_op jit(solution)/shard_map/ppermute | solution.py:1098
  73.7 10.0 %out_grad.1 = (bf16[1024,768]{1,0:T(8,128)(2,1)}, bf16[1024,768]{1,0:T(8,128)(2,1)}, bf16[768,1024]{1,0:T(8,128)(2,1)}, f32[8,1024]{1,0:T(8,128)}, bf16[768,1536]{1,0:T(8,128)(2,1)}) custom-call(s32[2]{0:T(128)} %pad_add_fusion.1.starts_ref, s32[16]{0:T(128)} %fusion.35.table_ref, bf16[512,768]{1,0:T(8,128)(2,1)} %own_ref.2, bf16[512,768]{1,0:T(8,128)(2,1)} %copy-done.20, ...), custom_call_target="tpu_custom_call" | custom-call | flops 9900000256 | tf_op jit(solution)/shard_map/out_grad/pallas_call | solution.py:723
  85.1 2.8 %collective-permute-done.7 = f32[8,1024]{1,0:T(8,128)S(1)} collective-permute-done((f32[8,1024]{1,0:T(8,128)}, f32[8,1024]{1,0:T(8,128)S(1)}, u32[]{:S(2)}, u32[]{:S(2)}) %collective-permute-start.7) | collective-permute-done | bytes 32800 | tf_op jit(solution)/shard_map/ppermute | solution.py:517
  89.3 13.1 %gated_grad.1 = (bf16[1024,768]{1,0:T(8,128)(2,1)}, bf16[1024,768]{1,0:T(8,128)(2,1)}, bf16[1024,768]{1,0:T(8,128)(2,1)}, f32[8,768]{1,0:T(8,128)}, f32[384,1536]{1,0:T(8,128)}, /*index=5*/bf16[384,1536]{1,0:T(8,128)(2,1)}) custom-call(s32[16]{0:T(128)} %fusion.35.table_ref, bf16[1024,768]{1,0:T(8,128)(2,1)} %get-tuple-element.87.gate_ref, ...), custom_call_target="tpu_custom_call" | custom-call | flops 13200000000 | tf_op jit(solution)/shard_map/gated_grad/pallas_call | solution.py:841
  102.5 5.3 %out_project.1 = (bf16[512,768]{1,0:T(8,128)(2,1)}, bf16[512,768]{1,0:T(8,128)(2,1)}) custom-call(s32[1]{0:T(128)} %bitcast.starts_ref, bf16[1024,768]{1,0:T(8,128)(2,1)} %get-tuple-element.92.rows_ref, bf16[768,1536]{1,0:T(8,128)(2,1)} %get-tuple-element.93.weights_ref.gates_ref), custom_call_target="tpu_custom_call" | custom-call | flops 4400000000 | tf_op jit(solution)/shard_map/out_project/pallas_call | solution.py:899
  109.2 4.9 %all-to-all-start.1 = ((bf16[8,48,1536]{2,1,0:T(8,128)(2,1)}), bf16[8,48,1536]{2,1,0:T(8,128)(2,1)S(1)}, u32[]{:S(2)}, u32[]{:S(2)}) async-start(bf16[8,48,1536]{2,1,0:T(8,128)(2,1)} %bitcast.29), calls=%async_computation.1 | async-start | bytes 2359296 | tf_op jit(solution)/shard_map/all_to_all | solution.py:498
  114.6 31.3 %scan_backward.1 = (bf16[1024,1152]{1,0:T(8,128)(2,1)}, f32[8,768]{1,0:T(8,128)}, f32[8,256]{1,0:T(8,128)}) custom-call(bf16[1024,1024]{1,0:T(8,128)(2,1)} %get-tuple-element.74.proj_ref, f32[1024,128]{1,0:T(8,128)} %get-tuple-element.75.step_ref.praw_ref, bf16[1024,768]{1,0:T(8,128)(2,1)} %get-tuple-element.95.u_ref, f32[1024,256]{1,0:T(8,128)} %get-tuple-element.96.su_ref, ...), custom_call_target="tpu_custom_call" | custom-call | flops 35200000000 | tf_op jit(solution)/shard_map/scan_backward/pallas_call | solution.py:423
  148.2 6.8 %weight_grad.1 = (f32[384,1152]{1,0:T(8,128)}, bf16[384,1152]{1,0:T(8,128)(2,1)}) custom-call(s32[16]{0:T(128)} %fusion.35.table_ref, bf16[768,1024]{1,0:T(8,128)(2,1)} %get-tuple-element.91.nturned_ref.turned_ref, bf16[1024,1152]{1,0:T(8,128)(2,1)} %get-tuple-element.107.dproj_ref), custom_call_target="tpu_custom_call" | custom-call | flops 6600000000 | tf_op jit(solution)/shard_map/weight_grad/pallas_call | solution.py:979
  155.0 5.4 %normed_grad.2 = (f32[512,768]{1,0:T(8,128)}, f32[8,768]{1,0:T(8,128)}) custom-call(s32[1]{0:T(128)} %bitcast.2.starts_ref, bf16[1024,768]{1,0:T(8,128)(2,1)} %get-tuple-element.109.dgate_ref, bf16[1024,1152]{1,0:T(8,128)(2,1)} %get-tuple-element.107.dproj_ref, bf16[768,1536]{1,0:T(8,128)(2,1)} %get-tuple-element.93.weights_ref.gates_ref, ...), custom_call_target="tpu_custom_call" | custom-call | flops 5500000256 | tf_op jit(solution)/shard_map/normed_grad/pallas_call | solution.py:946
  160.4 5.3 %normed_grad.3 = (bf16[512,768]{1,0:T(8,128)(2,1)}, f32[8,768]{1,0:T(8,128)}) custom-call(s32[1]{0:T(128)} %bitcast.starts_ref, bf16[1024,768]{1,0:T(8,128)(2,1)} %get-tuple-element.109.dgate_ref, bf16[1024,1152]{1,0:T(8,128)(2,1)} %get-tuple-element.107.dproj_ref, bf16[768,1536]{1,0:T(8,128)(2,1)} %get-tuple-element.93.weights_ref.gates_ref, ...), custom_call_target="tpu_custom_call" | custom-call | flops 5500000256 | tf_op jit(solution)/shard_map/normed_grad/pallas_call | solution.py:946
  168.7 2.0 collective-permute-start.13
  170.7 1.6 collective-permute-start.11
  173.0 1.8 collective-permute-start.14
  175.0 2.2 %collective-permute-done.14 = f32[16,768]{1,0:T(8,128)S(1)} collective-permute-done((f32[16,768]{1,0:T(8,128)S(1)}, f32[16,768]{1,0:T(8,128)S(1)}, u32[]{:S(2)}, u32[]{:S(2)}) %collective-permute-start.14) | collective-permute-done | bytes 49184 | tf_op jit(solution)/shard_map/ppermute | solution.py:511
  177.2 2.7 %collective-permute-start.15 = (f32[16,768]{1,0:T(8,128)S(1)}, f32[16,768]{1,0:T(8,128)S(1)}, u32[]{:S(2)}, u32[]{:S(2)}) collective-permute-start(f32[16,768]{1,0:T(8,128)S(1)} %add.147), channel_id=1, source_target_pairs={{0,16},{2,18},{4,20},{6,22},{8,24},{10,26},{12,28},{14,30},{16,0},... | collective-permute-start | bytes 147464 | tf_op jit(solution)/shard_map/ppermute | solution.py:511
  180.6 1.6 collective-permute-done.15
  183.4 6.4 %all-to-all-start.2 = ((bf16[8,48,1152]{2,1,0:T(8,128)(2,1)}), bf16[8,48,1152]{2,1,0:T(8,128)(2,1)S(1)}, u32[]{:S(2)}, u32[]{:S(2)}) async-start(bf16[8,48,1152]{2,1,0:T(8,128)(2,1)} %bitcast.34), calls=%async_computation.2 | async-start | bytes 1769472 | tf_op jit(solution)/shard_map/all_to_all | solution.py:498
  190.3 1.6 collective-permute-start.16
  195.5 1.8 fusion.2
  197.3 3.4 %fusion.5 = (f32[512,768]{1,0:T(8,128)}, bf16[512,768]{1,0:T(8,128)(2,1)}) fusion(bf16[512,768]{1,0:T(8,128)(2,1)S(1)} %copy-done.1, bf16[512,768]{1,0:T(8,128)(2,1)S(1)} %copy-done.7, f32[512,768]{1,0:T(8,128)S(1)} %copy-done.2, bf16[512,768]{1,0:T(8,128)(2,1)} %collective-permute-done.11, f32[512]{0:T(512)S(1)} %broadcast_multiply_fusion, ...), kind=kLoop, calls=%fused_computation.12 | loop fusion | flops 5898240 | bytes 7871488 | tf_op jit(solution)/shard_map/add | solution.py:1178
  200.7 9.1 %all-to-all-done.2 = bf16[8,48,1152]{2,1,0:T(8,128)(2,1)S(1)} async-done(((bf16[8,48,1152]{2,1,0:T(8,128)(2,1)}), bf16[8,48,1152]{2,1,0:T(8,128)(2,1)S(1)}, u32[]{:S(2)}, u32[]{:S(2)}) %all-to-all-start.2) | async-done | bytes 884768 | tf_op jit(solution)/shard_map/all_to_all | solution.py:498
  210.0 1.6 collective-permute-start.17
  (153 shorter events, 42.9 us)
Async XLA Ops:
  0.6 13.5 %copy-start.11 = (s32[1024]{0:T(1024)S(1)}, s32[1024]{0:T(1024)}, u32[]{:S(2)}) copy-start(s32[1024]{0:T(1024)} %param.17) | copy-start | bytes 12292
  0.7 13.6 %copy-start.15 = (bf16[768]{0:T(1024)(128)(2,1)S(1)}, bf16[768]{0:T(1024)(128)(2,1)}, u32[]{:S(2)}) copy-start(bf16[768]{0:T(1024)(128)(2,1)} %param.27) | copy-start | bytes 4612
  0.7 14.3 %copy-start.16 = (f32[12]{0:T(128)S(1)}, f32[12]{0:T(128)}, u32[]{:S(2)}) copy-start(f32[12]{0:T(128)} %param.26) | copy-start | bytes 148
  0.7 14.3 %copy-start.17 = (f32[12]{0:T(128)S(1)}, f32[12]{0:T(128)}, u32[]{:S(2)}) copy-start(f32[12]{0:T(128)} %param.25) | copy-start | bytes 148
  0.7 14.3 %copy-start.18 = (f32[12]{0:T(128)S(1)}, f32[12]{0:T(128)}, u32[]{:S(2)}) copy-start(f32[12]{0:T(128)} %param.24) | copy-start | bytes 148
  0.7 14.9 %copy-start.12 = (bf16[768,48]{0,1:T(8,128)(2,1)S(1)}, bf16[768,48]{0,1:T(8,128)(2,1)}, u32[]{:S(2)}) copy-start(bf16[768,48]{0,1:T(8,128)(2,1)} %param.28) | copy-start | bytes 221188
  5.1 18.7 %copy-start = (bf16[512,768]{1,0:T(8,128)(2,1)S(1)}, bf16[512,768]{1,0:T(8,128)(2,1)}, u32[]{:S(2)}) copy-start(bf16[512,768]{1,0:T(8,128)(2,1)} %own_ref.1) | copy-start | bytes 2359300
  5.2 10.9 %collective-permute-start.1 = (bf16[48,1152]{1,0:T(8,128)(2,1)S(1)}, bf16[48,1152]{1,0:T(8,128)(2,1)S(1)}, u32[]{:S(2)}, u32[]{:S(2)}) collective-permute-start(bf16[48,1152]{1,0:T(8,128)(2,1)S(1)} %pad_maximum_fusion.5), channel_id=1, source_target_pairs={{0,16},{2,18},{4,20},{6,22},{8,24},{10,26},{12,28},{14,30},{16,0},... | collective-permute-start | bytes 331784 | tf_op jit(solution)/shard_map/ppermute | solution.py:1080
  16.1 6.0 %collective-permute-start.2 = (bf16[96,1152]{1,0:T(8,128)(2,1)S(1)}, bf16[96,1152]{1,0:T(8,128)(2,1)S(1)}, u32[]{:S(2)}, u32[]{:S(2)}) collective-permute-start(bf16[96,1152]{1,0:T(8,128)(2,1)S(1)} %pad_maximum_fusion.3), channel_id=1, source_target_pairs={{0,8},{2,6},{4,12},{6,2},{8,0},{10,14},{12,4},{14,10},{16,24},{18,... | collective-permute-start | bytes 663560 | tf_op jit(solution)/shard_map/ppermute | solution.py:1080
  22.2 8.4 %collective-permute-start.3 = (bf16[192,1152]{1,0:T(8,128)(2,1)S(1)}, bf16[192,1152]{1,0:T(8,128)(2,1)S(1)}, u32[]{:S(2)}, u32[]{:S(2)}) collective-permute-start(bf16[192,1152]{1,0:T(8,128)(2,1)S(1)} %pad_maximum_fusion.1), channel_id=1, source_target_pairs={{0,4},{2,10},{4,0},{6,14},{8,12},{10,2},{12,8},{14,6},{16,20},{18,... | collective-permute-start | bytes 1327112 | tf_op jit(solution)/shard_map/ppermute | solution.py:1080
  23.7 18.1 %collective-permute-start = (bf16[512,768]{1,0:T(8,128)(2,1)S(1)}, bf16[512,768]{1,0:T(8,128)(2,1)}, u32[]{:S(2)}, u32[]{:S(2)}) collective-permute-start(bf16[512,768]{1,0:T(8,128)(2,1)S(1)} %copy-done), channel_id=1, source_target_pairs={{0,1},{1,0},{2,3},{3,2},{4,5},{5,4},{6,7},{7,6},{8,9},{9,8},{10,11... | collective-permute-start | bytes 2359304 | tf_op jit(solution)/shard_map/ppermute | solution.py:517
  30.6 12.7 %collective-permute-start.4 = (bf16[384,1152]{1,0:T(8,128)(2,1)S(1)}, bf16[384,1152]{1,0:T(8,128)(2,1)}, u32[]{:S(2)}, u32[]{:S(2)}) collective-permute-start(bf16[384,1152]{1,0:T(8,128)(2,1)S(1)} %pad_maximum_fusion.low_ref), channel_id=1, source_target_pairs={{0,2},{2,0},{4,6},{6,4},{8,10},{10,8},{12,14},{14,12},{16,18},{18,... | collective-permute-start | bytes 2654216 | tf_op jit(solution)/shard_map/ppermute | solution.py:1087
  36.1 33.6 %all-to-all-start = ((bf16[8,48,1536]{2,1,0:T(8,128)(2,1)}), bf16[8,48,1536]{2,1,0:T(8,128)(2,1)S(1)}, u32[]{:S(2)}, u32[]{:S(2)}) async-start(bf16[8,48,1536]{2,1,0:T(8,128)(2,1)} %bitcast.26), calls=%async_computation | async-start | bytes 2359296 | tf_op jit(solution)/shard_map/all_to_all | solution.py:498
  41.8 27.9 %collective-permute-start.5 = (bf16[512,768]{1,0:T(8,128)(2,1)}, bf16[512,768]{1,0:T(8,128)(2,1)S(1)}, u32[]{:S(2)}, u32[]{:S(2)}) collective-permute-start(bf16[512,768]{1,0:T(8,128)(2,1)} %own_ref.2), channel_id=1, source_target_pairs={{0,1},{1,0},{2,3},{3,2},{4,5},{5,4},{6,7},{7,6},{8,9},{9,8},{10,11... | collective-permute-start | bytes 2359304 | tf_op jit(solution)/shard_map/ppermute | solution.py:517
  52.6 17.2 %copy-start.22 = (s32[2,16]{1,0:T(2,128)S(1)}, s32[2,16]{1,0:T(2,128)}, u32[]{:S(2)}) copy-start(s32[2,16]{1,0:T(2,128)} %constant.98.clone) | copy-start | bytes 388
  69.8 2.9 %collective-permute-start.6 = (bf16[384,1536]{1,0:T(8,128)(2,1)S(1)}, bf16[384,1536]{1,0:T(8,128)(2,1)S(1)}, u32[]{:S(2)}, u32[]{:S(2)}) collective-permute-start(bf16[384,1536]{1,0:T(8,128)(2,1)S(1)} %bitcast.67), channel_id=1, source_target_pairs={{0,2},{2,0},{4,6},{6,4},{8,10},{10,8},{12,14},{14,12},{16,18},{18,... | collective-permute-start | bytes 3538952 | tf_op jit(solution)/shard_map/ppermute | solution.py:1098
  83.7 4.2 %collective-permute-start.7 = (f32[8,1024]{1,0:T(8,128)}, f32[8,1024]{1,0:T(8,128)S(1)}, u32[]{:S(2)}, u32[]{:S(2)}) collective-permute-start(f32[8,1024]{1,0:T(8,128)} %get-tuple-element.89), channel_id=1, source_target_pairs={{0,1},{1,0},{2,3},{3,2},{4,5},{5,4},{6,7},{7,6},{8,9},{9,8},{10,11... | collective-permute-start | bytes 98312 | tf_op jit(solution)/shard_map/ppermute | solution.py:517
  102.4 5.4 %collective-permute-start.8 = (bf16[384,1536]{1,0:T(8,128)(2,1)}, bf16[384,1536]{1,0:T(8,128)(2,1)S(1)}, u32[]{:S(2)}, u32[]{:S(2)}) collective-permute-start(bf16[384,1536]{1,0:T(8,128)(2,1)} %get-tuple-element.101), channel_id=1, source_target_pairs={{0,2},{2,0},{4,6},{6,4},{8,10},{10,8},{12,14},{14,12},{16,18},{18,... | collective-permute-start | bytes 3538952 | tf_op jit(solution)/shard_map/ppermute | solution.py:1106
  109.2 39.0 %all-to-all-start.1 = ((bf16[8,48,1536]{2,1,0:T(8,128)(2,1)}), bf16[8,48,1536]{2,1,0:T(8,128)(2,1)S(1)}, u32[]{:S(2)}, u32[]{:S(2)}) async-start(bf16[8,48,1536]{2,1,0:T(8,128)(2,1)} %bitcast.29), calls=%async_computation.1 | async-start | bytes 2359296 | tf_op jit(solution)/shard_map/all_to_all | solution.py:498
  114.1 34.1 %collective-permute-start.9 = (bf16[512,768]{1,0:T(8,128)(2,1)S(1)}, bf16[512,768]{1,0:T(8,128)(2,1)S(1)}, u32[]{:S(2)}, u32[]{:S(2)}) collective-permute-start(bf16[512,768]{1,0:T(8,128)(2,1)S(1)} %copy-done.21), channel_id=1, source_target_pairs={{0,1},{1,0},{2,3},{3,2},{4,5},{5,4},{6,7},{7,6},{8,9},{9,8},{10,11... | collective-permute-start | bytes 2359304 | tf_op jit(solution)/shard_map/ppermute | solution.py:517
  114.6 32.8 %copy-start.13 = (f32[8,768]{1,0:T(8,128)S(1)}, f32[8,768]{1,0:T(8,128)}, u32[]{:S(2)}) copy-start(f32[8,768]{1,0:T(8,128)} %get-tuple-element.116) | copy-start | bytes 73732
  165.7 16.5 %collective-permute-start.10 = (bf16[384,1152]{1,0:T(8,128)(2,1)}, bf16[384,1152]{1,0:T(8,128)(2,1)S(1)}, u32[]{:S(2)}, u32[]{:S(2)}) collective-permute-start(bf16[384,1152]{1,0:T(8,128)(2,1)} %get-tuple-element.108), channel_id=1, source_target_pairs={{0,2},{2,0},{4,6},{6,4},{8,10},{10,8},{12,14},{14,12},{16,18},{18,... | collective-permute-start | bytes 2654216 | tf_op jit(solution)/shard_map/ppermute | solution.py:1131
  167.4 1.4 collective-permute-start.12
  168.7 4.3 %collective-permute-start.13 = (f32[16,768]{1,0:T(8,128)S(1)}, f32[16,768]{1,0:T(8,128)S(1)}, u32[]{:S(2)}, u32[]{:S(2)}) collective-permute-start(f32[16,768]{1,0:T(8,128)S(1)} %add.145), channel_id=1, source_target_pairs={{0,4},{2,6},{4,0},{6,2},{8,12},{10,14},{12,8},{14,10},{16,20},{18,... | collective-permute-start | bytes 147464 | tf_op jit(solution)/shard_map/ppermute | solution.py:511
  170.7 11.5 %copy-start.4 = (f32[384,1152]{1,0:T(8,128)S(1)}, f32[384,1152]{1,0:T(8,128)}, u32[]{:S(2)}) copy-start(f32[384,1152]{1,0:T(8,128)} %get-tuple-element.121) | copy-start | bytes 5308420
  170.7 24.8 %collective-permute-start.11 = (bf16[512,768]{1,0:T(8,128)(2,1)}, bf16[512,768]{1,0:T(8,128)(2,1)}, u32[]{:S(2)}, u32[]{:S(2)}) collective-permute-start(bf16[512,768]{1,0:T(8,128)(2,1)} %get-tuple-element.113), channel_id=1, source_target_pairs={{0,1},{1,0},{2,3},{3,2},{4,5},{5,4},{6,7},{7,6},{8,9},{9,8},{10,11... | collective-permute-start | bytes 2359304 | tf_op jit(solution)/shard_map/ppermute | solution.py:517
  173.0 4.2 %collective-permute-start.14 = (f32[16,768]{1,0:T(8,128)S(1)}, f32[16,768]{1,0:T(8,128)S(1)}, u32[]{:S(2)}, u32[]{:S(2)}) collective-permute-start(f32[16,768]{1,0:T(8,128)S(1)} %add.146), channel_id=1, source_target_pairs={{0,8},{2,10},{4,12},{6,14},{8,0},{10,2},{12,4},{14,6},{16,24},{18,... | collective-permute-start | bytes 147464 | tf_op jit(solution)/shard_map/ppermute | solution.py:511
  177.2 5.0 %collective-permute-start.15 = (f32[16,768]{1,0:T(8,128)S(1)}, f32[16,768]{1,0:T(8,128)S(1)}, u32[]{:S(2)}, u32[]{:S(2)}) collective-permute-start(f32[16,768]{1,0:T(8,128)S(1)} %add.147), channel_id=1, source_target_pairs={{0,16},{2,18},{4,20},{6,22},{8,24},{10,26},{12,28},{14,30},{16,0},... | collective-permute-start | bytes 147464 | tf_op jit(solution)/shard_map/ppermute | solution.py:511
  183.4 12.1 %copy-start.2 = (f32[512,768]{1,0:T(8,128)S(1)}, f32[512,768]{1,0:T(8,128)}, u32[]{:S(2)}) copy-start(f32[512,768]{1,0:T(8,128)} %get-tuple-element.112) | copy-start | bytes 4718596
  183.4 26.4 %all-to-all-start.2 = ((bf16[8,48,1152]{2,1,0:T(8,128)(2,1)}), bf16[8,48,1152]{2,1,0:T(8,128)(2,1)S(1)}, u32[]{:S(2)}, u32[]{:S(2)}) async-start(bf16[8,48,1152]{2,1,0:T(8,128)(2,1)} %bitcast.34), calls=%async_computation.2 | async-start | bytes 1769472 | tf_op jit(solution)/shard_map/all_to_all | solution.py:498
  190.3 3.8 %collective-permute-start.16 = (f32[8,768]{1,0:T(8,128)S(1)}, f32[8,768]{1,0:T(8,128)S(1)}, u32[]{:S(2)}, u32[]{:S(2)}) collective-permute-start(f32[8,768]{1,0:T(8,128)S(1)} %slice.112), channel_id=1, source_target_pairs={{0,1},{1,0},{2,3},{3,2},{4,5},{5,4},{6,7},{7,6},{8,9},{9,8},{10,11... | collective-permute-start | bytes 73736 | tf_op jit(solution)/shard_map/ppermute | solution.py:517
  210.0 4.2 %collective-permute-start.17 = (f32[48,256]{1,0:T(8,128)S(1)}, f32[48,256]{1,0:T(8,128)S(1)}, u32[]{:S(2)}, u32[]{:S(2)}) collective-permute-start(f32[48,256]{1,0:T(8,128)S(1)} %slice.116), channel_id=1, source_target_pairs={{0,1},{1,0},{2,3},{3,2},{4,5},{5,4},{6,7},{7,6},{8,9},{9,8},{10,11... | collective-permute-start | bytes 147464 | tf_op jit(solution)/shard_map/ppermute | solution.py:517
  (12 other events, 47.9 us)

commit v3 on v2

--- a/solution.py
+++ b/solution.py
@@ -187,7 +187,9 @@
     heads_ref,
     aux_ref,
     segr_ref,
+    gain_ref,
     dproj_ref,
+    small_ref,
     wide_ref,
     shared_ref,
     state_ref,
@@ -336,27 +338,63 @@
     wide_ref[6:7, :LANES] += jnp.sum(dstep, axis=0, keepdims=True)
     wide_ref[6:7, LANES : 2 * LANES] += jnp.sum(step * dlog, axis=0, keepdims=True) * rate
 
+    @pl.when(chunk == 0)
+    def _():
+        small_ref[...] = jnp.zeros_like(small_ref)
+        small_ref[:4, :width] = wide_ref[:4, :]
+        small_ref[:4, width : width + shared_size] = shared_ref[:4, :]
+        skip_row = dot_split(wide_ref[...], place)[5:6, :]
+        small_ref[0:1, step_cols] = skip_row
+        small_ref[1:2, step_cols] = wide_ref[6:7, :LANES]
+        small_ref[2:3, step_cols] = wide_ref[6:7, LANES : 2 * LANES]
+        small_ref[4:5, :width] = jnp.sum(gain_ref[...], axis=0, keepdims=True)
+
+
+def facts_kernel(seg_ref, aux_ref, segr_ref):
+    seg = seg_ref[...].astype(f32)
+    chunks = seg.shape[0]
+    segr_ref[...] = seg
+    none = jnp.full((1, CHUNK), -1.0, f32)
+    before = jnp.concatenate([none, seg[: chunks - 1]], axis=0) if chunks > 1 else none
+    behind = jnp.concatenate([seg[1:], none], axis=0) if chunks > 1 else none
+    lane = lax.broadcasted_iota(jnp.int32, seg.shape, 1)
+    facts = [seg]
+    for offset in range(1, 4):
+        earlier = jnp.where(
+            lane >= offset, pltpu.roll(seg, offset, 1), pltpu.roll(before, offset, 1)
+        )
+        facts.append((earlier == seg).astype(f32))
+    for offset in range(1, 4):
+        later = jnp.where(
+            lane < CHUNK - offset,
+            pltpu.roll(seg, CHUNK - offset, 1),
+            pltpu.roll(behind, CHUNK - offset, 1),
+        )
+        facts.append((later == seg).astype(f32))
+    last = jnp.broadcast_to(seg[:, CHUNK - 1 :], seg.shape)
+    prior = jnp.broadcast_to(before[:, CHUNK - 1 :], seg.shape)
+    facts.append((seg != 0.0).astype(f32))
+    facts.append((seg == prior).astype(f32))
+    facts.append((seg == last).astype(f32))
+    facts.append((last == prior).astype(f32))
+    empty = jnp.zeros((LANES - len(facts), CHUNK), f32)
+    for chunk in range(chunks):
+        rows = jnp.concatenate([f[chunk : chunk + 1, :] for f in facts] + [empty], axis=0)
+        aux_ref[chunk * CHUNK : (chunk + 1) * CHUNK, :] = rows.T[:, : aux_ref.shape[1]]
+
 
 def token_facts(segments):
     length = segments.shape[0]
     chunks = length // CHUNK
-    columns = [segments]
-    for offset in range(1, 4):
-        earlier = jnp.concatenate([jnp.full((offset,), -1, jnp.int32), segments[: length - offset]])
-        columns.append(earlier == segments)
-    for offset in range(1, 4):
-        later = jnp.concatenate([segments[offset:], jnp.full((offset,), -1, jnp.int32)])
-        columns.append(later == segments)
-    columns.append(segments != 0)
-    blocks = segments.reshape(chunks, CHUNK)
-    last = blocks[:, CHUNK - 1 :]
-    prior = jnp.concatenate([jnp.full((1, 1), -1, jnp.int32), last[: chunks - 1]], axis=0)
-    columns.append((blocks == prior).reshape(length))
-    columns.append((blocks == last).reshape(length))
-    columns.append(jnp.broadcast_to(last == prior, blocks.shape).reshape(length))
-    columns += [jnp.zeros_like(segments)] * 5
-    aux = jnp.stack([c.astype(f32) for c in columns], axis=1)
-    return aux, blocks.astype(f32)
+    return pl.pallas_call(
+        facts_kernel,
+        out_shape=(
+            jax.ShapeDtypeStruct((length, 16), f32),
+            jax.ShapeDtypeStruct((chunks, CHUNK), f32),
+        ),
+        name="token_facts",
+        cost_estimate=cost(2),
+    )(segments.reshape(chunks, CHUNK))
 
 
 def chunk_spec(columns, last):
@@ -412,7 +450,7 @@
     )(proj, praw, tapi, taps, heads, aux, segr)
 
 
-def run_backward(proj, praw, u, su, entry, grad, tapi, taps, heads, aux, segr):
+def run_backward(proj, praw, u, su, entry, grad, tapi, taps, heads, aux, segr, gain_rows):
     length, width = u.shape
     shared_size = su.shape[1]
     state_size = shared_size // 2
@@ -435,18 +473,19 @@
             fixed_spec(heads),
             chunk_spec(aux.shape[1], last),
             fixed_spec(segr),
+            fixed_spec(gain_rows),
         ],
         out_specs=[
             chunk_spec(columns, last),
-            pl.BlockSpec((8, width), lambda i: (0, 0)),
-            pl.BlockSpec((8, shared_size), lambda i: (0, 0)),
+            pl.BlockSpec((8, columns), lambda i: (0, 0)),
         ],
         out_shape=(
             sds((length, columns), bf16),
-            sds((8, width), f32),
-            sds((8, shared_size), f32),
+            sds((8, columns), f32),
         ),
         scratch_shapes=[
+            pltpu.VMEM((8, width), f32),
+            pltpu.VMEM((8, shared_size), f32),
             pltpu.VMEM((state_size, width), f32),
             pltpu.VMEM((8, width), f32),
             pltpu.VMEM((8, shared_size), f32),
@@ -458,7 +497,7 @@
         ],
         name="scan_backward",
         cost_estimate=cost(32),
-    )(proj, praw, u, su, entry, grad, tapi, taps, heads, aux, segr)
+    )(proj, praw, u, su, entry, grad, tapi, taps, heads, aux, segr, gain_rows)
 
 
 def block_plan():
@@ -504,15 +543,6 @@
     return jnp.sum(blocks.reshape(-1, rows, blocks.shape[1]).astype(f32), axis=0)
 
 
-def total_over_dp(values):
-    count = lax.axis_size("dp")
-    bit = 1
-    while bit < count:
-        values = values + lax.ppermute(values, "dp", [(i, i ^ bit) for i in range(count)])
-        bit *= 2
-    return values
-
-
 def swap(values):
     return lax.ppermute(values, "tensor", [(0, 1), (1, 0)])
 
@@ -619,7 +649,7 @@
     own_rows, model_dim = own.shape
     columns = low.shape[1]
     own_blocks = own_rows // TOKEN_BLOCK
-    blocks = own_blocks * (2 if other is not own else 1)
+    blocks = own_blocks * (2 if lax.axis_size("tensor") == 2 else 1)
     length = blocks * TOKEN_BLOCK
     sds = jax.ShapeDtypeStruct
     return pl.pallas_call(
@@ -779,6 +809,7 @@
     nog_ref,
     mixed_ref,
     sums_ref,
+    more_ref,
     aux_ref,
     gain_ref,
     gturned_ref,
@@ -795,7 +826,7 @@
 ):
     step = pl.program_id(0)
     width = gate_ref.shape[1]
-    inv, mean = token_scales(sums_ref[...], full_inner)
+    inv, mean = token_scales(sums_ref[...] + more_ref[...], full_inner)
     gain = gain_ref[...].astype(f32)
     gate = gate_ref[...].astype(f32)
     gate_sig = sigmoid(gate)
@@ -830,7 +861,7 @@
         store_blocks(table_ref, total_ref, keep_ref, send_ref)
 
 
-def run_gated(table, gate, nog, mixed, sums, aux, gain, gturned, nturned, full_inner):
+def run_gated(table, gate, nog, mixed, sums, more, aux, gain, gturned, nturned, full_inner):
     length, width = gate.shape
     model_dim = gturned.shape[0]
     blocks = length // TOKEN_BLOCK
@@ -847,6 +878,7 @@
                 tokens,
                 tokens,
                 tokens,
+                pl.BlockSpec((8, TOKEN_BLOCK), lambda i, t: (0, i)),
                 pl.BlockSpec((8, TOKEN_BLOCK), lambda i, t: (0, i)),
                 pl.BlockSpec((TOKEN_BLOCK, aux.shape[1]), lambda i, t: (i, 0)),
                 pl.BlockSpec((1, width), lambda i, t: (0, 0)),
@@ -873,7 +905,7 @@
         ),
         name="gated_grad",
         cost_estimate=cost(12),
-    )(table, gate, nog, mixed, sums, aux, gain, gturned, nturned)
+    )(table, gate, nog, mixed, sums, more, aux, gain, gturned, nturned)
 
 
 def out_kernel(starts_ref, rows_ref, weights_ref, send_ref, keep_ref):
@@ -919,30 +951,16 @@
     )(starts, rows, weights)
 
 
-def norm_grad_kernel(
-    starts_ref, dgate_ref, dproj_ref, gates_ref, weights_ref, normed_ref, grad_ref, total_ref
-):
+def norm_grad_kernel(starts_ref, dgate_ref, dproj_ref, gates_ref, weights_ref, grad_ref):
     grad = dot_nt(dgate_ref[...], gates_ref[...]) + dot_nt(dproj_ref[...], weights_ref[...])
     grad_ref[...] = grad.astype(grad_ref.dtype)
-    part = jnp.sum(
-        (grad * normed_ref[...].astype(f32)).reshape(-1, 8, grad.shape[1]), axis=0
-    )
-
-    @pl.when(pl.program_id(0) == 0)
-    def _():
-        total_ref[...] = part
-
-    @pl.when(pl.program_id(0) > 0)
-    def _():
-        total_ref[...] += part
-
-
-def run_norm_grad(starts, dgate, dproj, gates, weights, normed, kind):
+
+
+def run_norm_grad(starts, dgate, dproj, gates, weights, kind):
     length, columns = dproj.shape
     width = dgate.shape[1]
     model_dim = weights.shape[0]
     blocks = length // TOKEN_BLOCK // 2
-    sds = jax.ShapeDtypeStruct
     return pl.pallas_call(
         norm_grad_kernel,
         grid_spec=pltpu.PrefetchScalarGridSpec(
@@ -953,28 +971,30 @@
                 pl.BlockSpec((TOKEN_BLOCK, columns), lambda i, s: (i + s[0], 0)),
                 pl.BlockSpec((model_dim, width), lambda i, s: (0, 0)),
                 pl.BlockSpec((model_dim, columns), lambda i, s: (0, 0)),
-                pl.BlockSpec((TOKEN_BLOCK, model_dim), lambda i, s: (i + s[0], 0)),
             ],
-            out_specs=[
-                pl.BlockSpec((TOKEN_BLOCK, model_dim), lambda i, s: (i, 0)),
-                pl.BlockSpec((8, model_dim), lambda i, s: (0, 0)),
-            ],
+            out_specs=pl.BlockSpec((TOKEN_BLOCK, model_dim), lambda i, s: (i, 0)),
         ),
-        out_shape=(sds((length // 2, model_dim), kind), sds((8, model_dim), f32)),
+        out_shape=jax.ShapeDtypeStruct((length // 2, model_dim), kind),
         name="normed_grad",
         cost_estimate=cost(5),
-    )(starts, dgate, dproj, gates, weights, normed)
-
-
-def weight_grad_kernel(table_ref, turned_ref, dproj_ref, keep_ref, send_ref, total_ref):
+    )(starts, dgate, dproj, gates, weights)
+
+
+def weight_grad_kernel(
+    table_ref, turned_ref, dproj_ref, small_ref, keep_ref, send_ref, total_ref
+):
     total_ref[...] = dot_nn(turned_ref[...], dproj_ref[...])
+    half = keep_ref.shape[0] - 8
     store_blocks(table_ref, total_ref, keep_ref, send_ref)
-
-
-def run_weight_grad(table, turned, dproj):
+    keep_ref[half:, :] = small_ref[...]
+    send_ref[half:, :] = small_ref[...].astype(bf16)
+
+
+def run_weight_grad(table, turned, dproj, small):
     model_dim, length = turned.shape
     columns = dproj.shape[1]
     tile = 3 * LANES if columns % (3 * LANES) == 0 else LANES
+    held = model_dim // 2 + 8
     sds = jax.ShapeDtypeStruct
     return pl.pallas_call(
         weight_grad_kernel,
@@ -984,20 +1004,18 @@
             in_specs=[
                 pl.BlockSpec((model_dim, length), lambda i, t: (0, 0)),
                 pl.BlockSpec((length, tile), lambda i, t: (0, i)),
+                pl.BlockSpec((8, tile), lambda i, t: (0, i)),
             ],
             out_specs=[
-                pl.BlockSpec((model_dim // 2, tile), lambda i, t: (0, i)),
-                pl.BlockSpec((model_dim // 2, tile), lambda i, t: (0, i)),
+                pl.BlockSpec((held, tile), lambda i, t: (0, i)),
+                pl.BlockSpec((held, tile), lambda i, t: (0, i)),
             ],
             scratch_shapes=[pltpu.VMEM((model_dim, tile), f32)],
         ),
-        out_shape=(
-            sds((model_dim // 2, columns), f32),
-            sds((model_dim // 2, columns), bf16),
-        ),
+        out_shape=(sds((held, columns), f32), sds((held, columns), bf16)),
         name="weight_grad",
         cost_estimate=cost(6),
-    )(table, turned, dproj)
+    )(table, turned, dproj, small)
 
 
 def after(value, *others):
@@ -1050,6 +1068,7 @@
     starts = token_starts(blocks)
     two = lax.axis_size("tensor") == 2
 
+    chips = dp_count // 2
     hidden_own, hidden_other = both_halves(hidden_in)
     tap_rows = conv_shared.transpose(1, 2, 0).reshape(2 * tap_block, kernel_len)
     tap_rows = pad_to(tap_rows, 0, rows)
@@ -1079,13 +1098,19 @@
     for number, stage in enumerate(stages):
         got = lax.ppermute(low, "dp", stage)
         if number == 0:
-            got, spread, aux, segr, heads_block, tapi, gain, later = lax.optimization_barrier(
-                (got, spread, aux, segr, heads_block, tapi, gain, later)
+            got, aux, segr = lax.optimization_barrier((got, aux, segr))
+        if number == 1:
+            got, heads_block, tapi, spread, table, core_table = lax.optimization_barrier(
+                (got, heads_block, tapi, spread, table, core_table)
             )
+        if number == len(stages) - 1:
+            later_all = jnp.broadcast_to(later[None], (chips,) + later.shape)
+            later_all = later_all.reshape(chips * rows, 2 * width)
+            got, later_all, gain = lax.optimization_barrier((got, later_all, gain))
         low = jnp.concatenate([low, got], axis=0)
-    low, later = lax.optimization_barrier((low, later))
+    low, later_all, hidden_other = lax.optimization_barrier((low, later_all, hidden_other))
     high = lax.ppermute(low, "dp", core)
-    later_low = exchange(jnp.concatenate([later] * (dp_count // 2), axis=0), groups)
+    later_low = exchange(later_all, groups)
     grad_own, grad_other = both_halves(after(out_grad, hidden_other))
 
     proj, praw, normed, normed_t, weights, taps, norm_scale = run_project(
@@ -1099,9 +1124,13 @@
     gate, nog, grad_t, sums, later_rows = run_out_grad(
         starts, core_table, grad_own, grad_other, later_low, later_high, normed, mixed, gain
     )
-    sums = total_over_tensor(sums)
+    if two:
+        more = swap(sums)
+    else:
+        sums = lax.psum(sums, "tensor")
+        more = jnp.zeros_like(sums)
     normed_out, dgate, mixed_grad, gain_rows, gkeep, gsend = run_gated(
-        core_table, gate, nog, mixed, sums, aux, gain, grad_t, normed_t, full_inner
+        core_table, gate, nog, mixed, sums, more, aux, gain, grad_t, normed_t, full_inner
     )
     ggot = lax.ppermute(gsend, "dp", core)
     send_start = starts[1:] if two else jnp.zeros((1,), jnp.int32)
@@ -1111,65 +1140,68 @@
     gsum = exchange((gkeep + ggot.astype(f32)).astype(bf16), groups)
     out_other = swap(out_send) if two else None
 
-    dproj, wide, dtaps = run_backward(
-        proj, praw, u, su, entry, mixed_grad, tapi, taps, heads_block, aux, segr
+    dproj, small = run_backward(
+        proj, praw, u, su, entry, mixed_grad, tapi, taps, heads_block, aux, segr, gain_rows
     )
     dproj, gsum = lax.optimization_barrier((dproj, gsum))
+    wkeep, wsend = run_weight_grad(core_table, normed_t, dproj, small)
+    wgot = lax.ppermute(wsend, "dp", core)
+    grad_send = run_norm_grad(send_start, dgate, dproj, later_rows, weights, bf16)
+    wgot, grad_send = lax.optimization_barrier((wgot, grad_send))
+    held = rows * chips
+    wtotal = (wkeep + wgot.astype(f32)).astype(bf16)
+    wtotal = jnp.concatenate(
+        [
+            wtotal[:held].reshape(chips, rows, -1),
+            jnp.broadcast_to(wtotal[None, held:], (chips, 8, wtotal.shape[1])),
+        ],
+        axis=1,
+    ).reshape(chips * (rows + 8), -1)
+    wtotal, dproj, gsum, out_keep = lax.optimization_barrier((wtotal, dproj, gsum, out_keep))
+    wsum = exchange(wtotal, groups)
+    grad_keep = run_norm_grad(keep_start, dgate, dproj, later_rows, weights, f32)
     if two:
-        dproj, out_other = lax.optimization_barrier((dproj, out_other))
         out_half = out_keep.astype(f32) + out_other.astype(f32)
+        own_grad = grad_keep + swap(grad_send).astype(f32)
     else:
         out_half = add_halves(out_send, out_keep)
+        own_grad = add_halves(grad_send, grad_keep)
     hidden_out = (hidden_in.astype(f32) + out_half).astype(bf16)
-    grad_send, norm_sum = run_norm_grad(
-        send_start, dgate, dproj, later_rows, weights, normed, bf16
-    )
-    wkeep, wsend = run_weight_grad(core_table, normed_t, dproj)
-    grad_keep, norm_more = run_norm_grad(
-        keep_start, dgate, dproj, later_rows, weights, normed, f32
-    )
-    wgot = lax.ppermute(wsend, "dp", core)
-    wgot, grad_keep = lax.optimization_barrier((wgot, grad_keep))
-    wsum = exchange((wkeep + wgot.astype(f32)).astype(bf16), groups)
-    if two:
-        own_grad = grad_keep + swap(grad_send).astype(f32)
-    else:
-        own_grad = add_halves(grad_send, grad_keep)
     gsum = sum_blocks(gsum, rows)
     out_sum = gsum[:, width : width + local_inner].T
-    wsum = sum_blocks(wsum, rows)
-    ssum = wsum[:, width:]
-
-    lanes = max(width, model_dim)
-    norm_sum = jnp.sum(norm_sum + norm_more, axis=0, keepdims=True) / norm_scale
-    small = jnp.concatenate(
+    gate_sum = gsum[:, :local_inner]
+
+    wsum = sum_blocks(wsum, rows + 8)
+    small = wsum[rows:]
+    wsum = wsum[:rows]
+    conv_total = small[:kernel_len, :local_inner]
+    gain_total = small[4, :local_inner]
+    skip_total = small[0, width + shared_size : width + shared_size + heads]
+    bias_total = small[1, width + shared_size : width + shared_size + heads]
+    decay_total = small[2, width + shared_size : width + shared_size + heads]
+    norm_row = jnp.sum(gate_sum * proj_inner[:, 0, :].astype(f32), axis=1) + jnp.sum(
+        wsum * packed.astype(f32) * (jnp.arange(packed.shape[1]) < width + shared_size + heads),
+        axis=1,
+    )
+    final = jnp.concatenate(
         [
-            pad_to(wide[:4], 1, lanes),
-            pad_to(jnp.sum(gain_rows, axis=0, keepdims=True), 1, lanes),
-            pad_to(wide[5:], 1, lanes),
-            pad_to(dtaps[:kernel_len], 1, lanes),
-            pad_to(norm_sum, 1, lanes),
-            jnp.zeros((3, lanes), f32),
+            wsum[:, width : width + shared_size],
+            small[:kernel_len, width : width + shared_size],
+            pad_to(norm_row[None], 1, shared_size),
         ],
         axis=0,
     )
-    small = total_over_dp(small)
-    conv_total = small[:kernel_len, :local_inner]
-    gain_total = small[4, :local_inner]
-    skip_total = jnp.sum(small[5, :width].reshape(-1, HEAD_DIM), axis=1)[:heads]
-    bias_total = small[6, :heads]
-    decay_total = small[6, LANES : LANES + heads]
-    small = total_over_tensor(small[8:16])
-    norm_total = lax.dynamic_slice_in_dim(small[4, :model_dim], dp_index * rows, rows)
+    final = total_over_tensor(pad_to(final, 0, rows + 8))
+    shared_total = final[:rows].reshape(rows, 2, state_size)
     taps_total = lax.dynamic_slice_in_dim(
-        small[:kernel_len, :shared_size].reshape(kernel_len, 2, state_size),
+        final[rows : rows + kernel_len].reshape(kernel_len, 2, state_size),
         dp_index * tap_block,
         tap_block,
         axis=2,
     )
-    inner_sum = jnp.stack([gsum[:, :local_inner], wsum[:, :local_inner]], axis=1)
-    step_sum = ssum[:, shared_size : shared_size + heads]
-    shared_total = total_over_tensor(ssum[:, :shared_size]).reshape(rows, 2, state_size)
+    norm_total = final[rows + kernel_len, :rows] / norm_gain.astype(f32)
+    inner_sum = jnp.stack([gate_sum, wsum[:, :local_inner]], axis=1)
+    step_sum = wsum[:, width + shared_size : width + shared_size + heads]
 
     own = hidden_in.astype(f32)
     own_inv = lax.rsqrt(jnp.mean(own * own, axis=-1, keepdims=True) + epsilon)

time: 216 us -> 202 us (0.935)
  local copies, waits for them, and re-layouts: 26 us -> 15.1 us
  starting transfers between devices: 40.1 us -> 31.3 us
  waiting for transfers between devices: 28.6 us -> 33.9 us
    ppermute x7 -> x6, waiting for transfers between devices: 5.23 us -> 20 us  [swap(): return lax.ppermute(values, 'tensor', [(0, 1), (1, 0)])]
    all_to_all x3, waiting for transfers between devices: 9.14 us -> 1.23 us  [exchange(): lax.all_to_all(blocks, 'dp', 0, 0, axis_index_groups=groups, tiled=True)]
    ppermute x4 -> x0, starting transfers between devices: 7.02 us -> none  [total_over_dp(): lax.ppermute(values, 'dp', [(i, i ^ bit) for i in range(count)])]
    ppermute x4 -> x0, waiting for transfers between devices: 5.18 us -> none  [total_over_dp(): lax.ppermute(values, 'dp', [(i, i ^ bit) for i in range(count)])]
    unnamed x59 -> x40, local copies, waits for them, and re-layouts: 9.05 us -> 4.87 us
    slice x12 -> x7, local copies, waits for them, and re-layouts: 4.77 us -> 0.84 us  [the longest x1 0.75 us: body(): norm_scale = norm_scale[:1]]
    ppermute x3, waiting for transfers between devices: 6.84 us -> 9.85 us  [body(): got = lax.ppermute(low, 'dp', stage)]
    ppermute x7 -> x6, starting transfers between devices: 9.77 us -> 7.61 us  [swap(): return lax.ppermute(values, 'tensor', [(0, 1), (1, 0)])]
  transfers between devices with their start and end apart: 21 -> 16, of which waited for: 12 -> 8; matrix products, arithmetic and copies ran while one was open for 15% -> 8% of each run, Pallas kernels for 29% -> 37%
where the time goes in v3:
time: 202 us; the launch traced here: 201 us
  Pallas kernels  105 us (52%)
  waiting for transfers between devices  33.9 us (17%)
  starting transfers between devices  31.3 us (15%)
  local copies, waits for them, and re-layouts  15.1 us (7%)
  other arithmetic  14.6 us (7%)
    pallas_call x1, Pallas kernels, run_backward(): pl.pallas_call(backward_kernel, grid=(chunks,), in_specs=[chunk_spec(proj...  31.7 us
    ppermute x6, waiting for transfers between devices, swap(): return lax.ppermute(values, 'tensor', [(0, 1), (1, 0)])  20 us
    pallas_call x1, Pallas kernels, run_forward(): pl.pallas_call(forward_kernel, grid=(chunks,), in_specs=[chunk_spec(proj....  17.1 us
    all_to_all x3, starting transfers between devices, exchange(): lax.all_to_all(blocks, 'dp', 0, 0, axis_index_groups=groups, tiled=True)  16.1 us
    pallas_call x1, Pallas kernels, run_gated(): pl.pallas_call(partial(gated_kernel, full_inner=float(full_inner)), grid_...  13.2 us
    pallas_call x1, Pallas kernels, run_out_grad(): pl.pallas_call(partial(out_grad_kernel, own_blocks=own_blocks), grid_spec...  10 us
    pallas_call x2, Pallas kernels, run_norm_grad(): pl.pallas_call(norm_grad_kernel, grid_spec=pltpu.PrefetchScalarGridSpec(n...  9.99 us
    ppermute x3, waiting for transfers between devices, body(): got = lax.ppermute(low, 'dp', stage)  9.85 us
  transfers between devices with their start and end apart: 16, of which 8 were waited for; matrix products, arithmetic and copies ran while one was open for 8% of the time, Pallas kernels for 37%

profile of v3, /device:TPU:0, one launch (start us, length us, event | category | flops | bytes accessed | tf_op | source)
XLA Modules:
  0.0 201.0 jit_solution(13356562199464517184)
XLA Ops:
  3.7 1.2 fusion.32
  5.1 4.1 %collective-permute-start = (bf16[48,1152]{1,0:T(8,128)(2,1)S(1)}, bf16[48,1152]{1,0:T(8,128)(2,1)S(1)}, u32[]{:S(2)}, u32[]{:S(2)}) collective-permute-start(bf16[48,1152]{1,0:T(8,128)(2,1)S(1)} %pad_maximum_fusion.6), channel_id=1, source_target_pairs={{0,16},{2,18},{4,20},{6,22},{8,24},{10,26},{12,28},{14,30},{16,0},... | collective-permute-start | bytes 331784 | tf_op jit(solution)/shard_map/ppermute | solution.py:1099
  9.2 1.5 collective-permute-start.3
  10.8 1.8 token_facts.1
  14.7 1.5 collective-permute-start.1
  17.1 3.6 %collective-permute-done.1 = bf16[96,1152]{1,0:T(8,128)(2,1)S(1)} collective-permute-done((bf16[96,1152]{1,0:T(8,128)(2,1)S(1)}, bf16[96,1152]{1,0:T(8,128)(2,1)S(1)}, u32[]{:S(2)}, u32[]{:S(2)}) %collective-permute-start.1) | collective-permute-done | bytes 221216 | tf_op jit(solution)/shard_map/ppermute | solution.py:1099
  20.7 1.6 collective-permute-start.2
  22.9 6.1 %collective-permute-done.2 = bf16[192,1152]{1,0:T(8,128)(2,1)S(1)} collective-permute-done((bf16[192,1152]{1,0:T(8,128)(2,1)S(1)}, bf16[192,1152]{1,0:T(8,128)(2,1)S(1)}, u32[]{:S(2)}, u32[]{:S(2)}) %collective-permute-start.2) | collective-permute-done | bytes 442400 | tf_op jit(solution)/shard_map/ppermute | solution.py:1099
  31.0 5.7 %all-to-all-start = ((bf16[8,48,1536]{2,1,0:T(8,128)(2,1)}), bf16[8,48,1536]{2,1,0:T(8,128)(2,1)S(1)}, u32[]{:S(2)}, u32[]{:S(2)}) async-start(bf16[8,48,1536]{2,1,0:T(8,128)(2,1)} %bitcast.15), calls=%async_computation | async-start | bytes 2359296 | tf_op jit(solution)/shard_map/all_to_all | solution.py:537
  36.7 1.6 collective-permute-start.5
  38.3 9.3 %norm_project.1 = (bf16[1024,1024]{1,0:T(8,128)(2,1)}, f32[1024,128]{1,0:T(8,128)}, bf16[1024,768]{1,0:T(8,128)(2,1)}, bf16[768,1024]{1,0:T(8,128)(2,1)}, bf16[7...) custom-call(s32[2]{0:T(128)} %pad_add_fusion.starts_ref, s32[16]{0:T(128)} %get-tuple-element.76.table_ref, ...), custom_call_target="tpu_custom_call" | custom-call | flops 9900000256 | tf_op jit(solution)/shard_map/norm_project/pallas_call | solution.py:655
  47.6 17.1 %scan_forward.1 = (bf16[1024,768]{1,0:T(8,128)(2,1)}, bf16[1024,768]{1,0:T(8,128)(2,1)}, f32[1024,256]{1,0:T(8,128)}, bf16[8,128,768]{2,1,0:T(8,128)(2,1)}) custom-call(bf16[1024,1024]{1,0:T(8,128)(2,1)} %get-tuple-element.84.proj_ref, f32[1024,128]{1,0:T(8,128)} %get-tuple-element.85.step_ref.praw_ref, bf16[4,768]{1,0:T(4,128)(2,1)} %tapi_ref.1, ...), custom_call_target="tpu_custom_call" | custom-call | flops 19800000512 | tf_op jit(solution)/shard_map/scan_forward/pallas_call | solution.py:418
  64.7 1.2 all-to-all-done
  66.0 2.8 %collective-permute-done.6.high_ref = bf16[384,1536]{1,0:T(8,128)(2,1)S(1)} collective-permute-done((bf16[384,1536]{1,0:T(8,128)(2,1)S(1)}, bf16[384,1536]{1,0:T(8,128)(2,1)S(1)}, u32[]{:S(2)}, u32[]{:S(2)}) %collective-permute-start.6) | collective-permute-done | bytes 1179680 | tf_op jit(solution)/shard_map/ppermute | solution.py:1123
  69.8 10.0 %out_grad.1 = (bf16[1024,768]{1,0:T(8,128)(2,1)}, bf16[1024,768]{1,0:T(8,128)(2,1)}, bf16[768,1024]{1,0:T(8,128)(2,1)}, f32[8,1024]{1,0:T(8,128)}, bf16[768,1536]{1,0:T(8,128)(2,1)}) custom-call(s32[2]{0:T(128)} %pad_add_fusion.starts_ref, s32[16]{0:T(128)} %get-tuple-element.75.table_ref, bf16[512,768]{1,0:T(8,128)(2,1)} %own_ref.2, ...), custom_call_target="tpu_custom_call" | custom-call | flops 9900000256 | tf_op jit(solution)/shard_map/out_grad/pallas_call | solution.py:753
  79.8 1.6 collective-permute-start.7
  81.4 2.6 %collective-permute-done.7.more_ref = f32[8,1024]{1,0:T(8,128)S(1)} collective-permute-done((f32[8,1024]{1,0:T(8,128)}, f32[8,1024]{1,0:T(8,128)S(1)}, u32[]{:S(2)}, u32[]{:S(2)}) %collective-permute-start.7) | collective-permute-done | bytes 32800 | tf_op jit(solution)/shard_map/ppermute | solution.py:547
  84.6 13.2 %gated_grad.1 = (bf16[1024,768]{1,0:T(8,128)(2,1)}, bf16[1024,768]{1,0:T(8,128)(2,1)}, bf16[1024,768]{1,0:T(8,128)(2,1)}, f32[8,768]{1,0:T(8,128)}, f32[384,1536]{1,0:T(8,128)}, /*index=5*/bf16[384,1536]{1,0:T(8,128)(2,1)}) custom-call(s32[16]{0:T(128)} %get-tuple-element.75.table_ref, bf16[1024,768]{1,0:T(8,128)(2,1)} %get-tuple-element.102.gate_ref, ...), custom_call_target="tpu_custom_call" | custom-call | flops 13200000000 | tf_op jit(solution)/shard_map/gated_grad/pallas_call | solution.py:872
  98.2 5.3 %out_project.1 = (bf16[512,768]{1,0:T(8,128)(2,1)}, bf16[512,768]{1,0:T(8,128)(2,1)}) custom-call(s32[1]{0:T(128)} %bitcast.11.starts_ref, bf16[1024,768]{1,0:T(8,128)(2,1)} %get-tuple-element.111.rows_ref, bf16[768,1536]{1,0:T(8,128)(2,1)} %get-tuple-element.112.weights_ref.gates_ref), custom_call_target="tpu_custom_call" | custom-call | flops 4400000000 | tf_op jit(solution)/shard_map/out_project/pallas_call | solution.py:931
  103.5 2.7 %add_convert_fusion = bf16[384,1536]{1,0:T(8,128)(2,1)} fusion(f32[384,1536]{1,0:T(8,128)S(1)} %copy-done.2, bf16[384,1536]{1,0:T(8,128)(2,1)} %collective-permute-done.8), kind=kLoop, calls=%fused_computation.4 | loop fusion | flops 1769472 | bytes 4718592 | tf_op jit(solution)/shard_map/convert_element_type | solution.py:1140
  106.2 4.8 %all-to-all-start.1 = ((bf16[8,48,1536]{2,1,0:T(8,128)(2,1)}), bf16[8,48,1536]{2,1,0:T(8,128)(2,1)S(1)}, u32[]{:S(2)}, u32[]{:S(2)}) async-start(bf16[8,48,1536]{2,1,0:T(8,128)(2,1)} %bitcast.17), calls=%async_computation.1 | async-start | bytes 2359296 | tf_op jit(solution)/shard_map/all_to_all | solution.py:537
  111.0 31.7 %scan_backward.1 = (bf16[1024,1152]{1,0:T(8,128)(2,1)}, f32[8,1152]{1,0:T(8,128)}) custom-call(bf16[1024,1024]{1,0:T(8,128)(2,1)} %get-tuple-element.84.proj_ref, f32[1024,128]{1,0:T(8,128)} %get-tuple-element.85.step_ref.praw_ref, bf16[1024,768]{1,0:T(8,128)(2,1)} %get-tuple-element.91.u_ref, f32[1024,256]{1,0:T(8,128)} %get-tuple-element.92.su_ref, ...), custom_call_target="tpu_custom_call" | custom-call | flops 35200000000 | tf_op jit(solution)/shard_map/scan_backward/pallas_call | solution.py:461
  142.7 6.8 %weight_grad.1 = (f32[392,1152]{1,0:T(8,128)}, bf16[392,1152]{1,0:T(8,128)(2,1)}) custom-call(s32[16]{0:T(128)} %get-tuple-element.75.table_ref, bf16[768,1024]{1,0:T(8,128)(2,1)} %get-tuple-element.83.nturned_ref.turned_ref, bf16[1024,1152]{1,0:T(8,128)(2,1)} %get-tuple-element.126.dproj_ref, f32[8,1152]{1,0:T(8,128)} %get-tuple-element.116.small_ref), custom_call_target="tpu_custom_call" | custom-call | flops 6600000000 | tf_op jit(solution)/shard_map/weight_grad/pallas_call | solution.py:999
  151.3 4.9 %normed_grad.2 = bf16[512,768]{1,0:T(8,128)(2,1)} custom-call(s32[1]{0:T(128)} %bitcast.11.starts_ref, bf16[1024,768]{1,0:T(8,128)(2,1)} %get-tuple-element.119.dgate_ref, bf16[1024,1152]{1,0:T(8,128)(2,1)} %get-tuple-element.126.dproj_ref, bf16[768,1536]{1,0:T(8,128)(2,1)} %get-tuple-element.112.weights_ref.gates_ref, ...), custom_call_target="tpu_custom_call" | custom-call | flops 5500000256 | tf_op jit(solution)/shard_map/normed_grad/pallas_call | solution.py:964
  156.2 1.7 add_convert_fusion.1
  159.1 5.5 %all-to-all-start.2 = ((bf16[8,56,1152]{2,1,0:T(8,128)(2,1)}), bf16[8,56,1152]{2,1,0:T(8,128)(2,1)S(1)}, u32[]{:S(2)}, u32[]{:S(2)}) async-start(bf16[8,56,1152]{2,1,0:T(8,128)(2,1)} %pad_maximum_fusion), calls=%async_computation.2 | async-start | bytes 2064384 | tf_op jit(solution)/shard_map/all_to_all | solution.py:537
  164.6 1.5 collective-permute-start.11
  166.1 5.1 %normed_grad.3 = f32[512,768]{1,0:T(8,128)} custom-call(s32[1]{0:T(128)} %bitcast.10.starts_ref, bf16[1024,768]{1,0:T(8,128)(2,1)} %get-tuple-element.119.dgate_ref, bf16[1024,1152]{1,0:T(8,128)(2,1)} %get-tuple-element.126.dproj_ref, bf16[768,1536]{1,0:T(8,128)(2,1)} %get-tuple-element.112.weights_ref.gates_ref, ...), custom_call_target="tpu_custom_call" | custom-call | flops 5500000256 | tf_op jit(solution)/shard_map/normed_grad/pallas_call | solution.py:964
  172.2 15.2 %collective-permute-done.11 = bf16[512,768]{1,0:T(8,128)(2,1)} collective-permute-done((bf16[512,768]{1,0:T(8,128)(2,1)}, bf16[512,768]{1,0:T(8,128)(2,1)}, u32[]{:S(2)}, u32[]{:S(2)}) %collective-permute-start.11) | collective-permute-done | bytes 786464 | tf_op jit(solution)/shard_map/ppermute | solution.py:547
  187.4 1.7 fusion.2
  189.1 3.6 %fusion.5 = (f32[512,768]{1,0:T(8,128)}, bf16[512,768]{1,0:T(8,128)(2,1)}) fusion(bf16[512,768]{1,0:T(8,128)(2,1)S(1)} %copy-done, bf16[512,768]{1,0:T(8,128)(2,1)S(1)} %copy-done.6, f32[512,768]{1,0:T(8,128)S(1)} %copy-done.1, bf16[512,768]{1,0:T(8,128)(2,1)} %collective-permute-done.11, f32[512]{0:T(512)S(1)} %broadcast_multiply_fusion, ...), kind=kLoop, calls=%fused_computation.12 | loop fusion | flops 5898240 | bytes 7871488 | tf_op jit(solution)/shard_map/add | solution.py:1210
  197.0 2.1 %collective-permute-done.12 = f32[56,256]{1,0:T(8,128)S(1)} collective-permute-done((f32[56,256]{1,0:T(8,128)S(1)}, f32[56,256]{1,0:T(8,128)S(1)}, u32[]{:S(2)}, u32[]{:S(2)}) %collective-permute-start.12) | collective-permute-done | bytes 57376 | tf_op jit(solution)/shard_map/ppermute | solution.py:547
  (102 shorter events, 20.7 us)
Async XLA Ops:
  5.1 9.6 %collective-permute-start = (bf16[48,1152]{1,0:T(8,128)(2,1)S(1)}, bf16[48,1152]{1,0:T(8,128)(2,1)S(1)}, u32[]{:S(2)}, u32[]{:S(2)}) collective-permute-start(bf16[48,1152]{1,0:T(8,128)(2,1)S(1)} %pad_maximum_fusion.6), channel_id=1, source_target_pairs={{0,16},{2,18},{4,20},{6,22},{8,24},{10,26},{12,28},{14,30},{16,0},... | collective-permute-start | bytes 331784 | tf_op jit(solution)/shard_map/ppermute | solution.py:1099
  9.2 21.1 %collective-permute-start.3 = (bf16[512,768]{1,0:T(8,128)(2,1)}, bf16[512,768]{1,0:T(8,128)(2,1)}, u32[]{:S(2)}, u32[]{:S(2)}) collective-permute-start(bf16[512,768]{1,0:T(8,128)(2,1)} %own_ref.1), channel_id=1, source_target_pairs={{0,1},{1,0},{2,3},{3,2},{4,5},{5,4},{6,7},{7,6},{8,9},{9,8},{10,11... | collective-permute-start | bytes 2359304 | tf_op jit(solution)/shard_map/ppermute | solution.py:547
  10.8 1.9 copy-start.10
  10.8 1.9 copy-start.11
  10.8 1.9 copy-start.12
  10.8 2.5 %copy-start.14 = (s32[2,16]{1,0:T(2,128)S(1)}, s32[2,16]{1,0:T(2,128)}, u32[]{:S(2)}) copy-start(s32[2,16]{1,0:T(2,128)} %constant.87.clone) | copy-start | bytes 388
  12.6 9.7 %copy-start.9 = (bf16[768]{0:T(1024)(128)(2,1)S(1)}, bf16[768]{0:T(1024)(128)(2,1)}, u32[]{:S(2)}) copy-start(bf16[768]{0:T(1024)(128)(2,1)} %param.27) | copy-start | bytes 4612
  12.6 10.3 %copy-start.8 = (bf16[768,48]{0,1:T(8,128)(2,1)S(1)}, bf16[768,48]{0,1:T(8,128)(2,1)}, u32[]{:S(2)}) copy-start(bf16[768,48]{0,1:T(8,128)(2,1)} %param.28) | copy-start | bytes 221188
  14.7 6.0 %collective-permute-start.1 = (bf16[96,1152]{1,0:T(8,128)(2,1)S(1)}, bf16[96,1152]{1,0:T(8,128)(2,1)S(1)}, u32[]{:S(2)}, u32[]{:S(2)}) collective-permute-start(bf16[96,1152]{1,0:T(8,128)(2,1)S(1)} %pad_maximum_fusion.4), channel_id=1, source_target_pairs={{0,8},{2,6},{4,12},{6,2},{8,0},{10,14},{12,4},{14,10},{16,24},{18,... | collective-permute-start | bytes 663560 | tf_op jit(solution)/shard_map/ppermute | solution.py:1099
  20.7 8.4 %collective-permute-start.2 = (bf16[192,1152]{1,0:T(8,128)(2,1)S(1)}, bf16[192,1152]{1,0:T(8,128)(2,1)S(1)}, u32[]{:S(2)}, u32[]{:S(2)}) collective-permute-start(bf16[192,1152]{1,0:T(8,128)(2,1)S(1)} %pad_maximum_fusion.2), channel_id=1, source_target_pairs={{0,4},{2,10},{4,0},{6,14},{8,12},{10,2},{12,8},{14,6},{16,20},{18,... | collective-permute-start | bytes 1327112 | tf_op jit(solution)/shard_map/ppermute | solution.py:1099
  30.3 8.0 %copy-start.4 = (bf16[384,1152]{1,0:T(8,128)(2,1)}, bf16[384,1152]{1,0:T(8,128)(2,1)S(1)}, u32[]{:S(2)}) copy-start(bf16[384,1152]{1,0:T(8,128)(2,1)S(1)} %pad_maximum_fusion.1.low_ref) | copy-start | bytes 2654212
  30.3 6.4 %copy-start.5 = (bf16[512,768]{1,0:T(8,128)(2,1)S(1)}, bf16[512,768]{1,0:T(8,128)(2,1)}, u32[]{:S(2)}) copy-start(bf16[512,768]{1,0:T(8,128)(2,1)} %own_ref.2) | copy-start | bytes 2359300
  30.3 8.0 %collective-permute-start.4 = (bf16[384,1152]{1,0:T(8,128)(2,1)S(1)}, bf16[384,1152]{1,0:T(8,128)(2,1)}, u32[]{:S(2)}, u32[]{:S(2)}) collective-permute-start(bf16[384,1152]{1,0:T(8,128)(2,1)S(1)} %pad_maximum_fusion.1.low_ref), channel_id=1, source_target_pairs={{0,2},{2,0},{4,6},{6,4},{8,10},{10,8},{12,14},{14,12},{16,18},{18,... | collective-permute-start | bytes 2654216 | tf_op jit(solution)/shard_map/ppermute | solution.py:1112
  31.0 35.0 %all-to-all-start = ((bf16[8,48,1536]{2,1,0:T(8,128)(2,1)}), bf16[8,48,1536]{2,1,0:T(8,128)(2,1)S(1)}, u32[]{:S(2)}, u32[]{:S(2)}) async-start(bf16[8,48,1536]{2,1,0:T(8,128)(2,1)} %bitcast.15), calls=%async_computation | async-start | bytes 2359296 | tf_op jit(solution)/shard_map/all_to_all | solution.py:537
  36.7 28.0 %collective-permute-start.5 = (bf16[512,768]{1,0:T(8,128)(2,1)S(1)}, bf16[512,768]{1,0:T(8,128)(2,1)}, u32[]{:S(2)}, u32[]{:S(2)}) collective-permute-start(bf16[512,768]{1,0:T(8,128)(2,1)S(1)} %copy-done.5), channel_id=1, source_target_pairs={{0,1},{1,0},{2,3},{3,2},{4,5},{5,4},{6,7},{7,6},{8,9},{9,8},{10,11... | collective-permute-start | bytes 2359304 | tf_op jit(solution)/shard_map/ppermute | solution.py:547
  65.9 2.9 %copy-start.3 = (bf16[8,48,1536]{2,1,0:T(8,128)(2,1)}, bf16[8,48,1536]{2,1,0:T(8,128)(2,1)S(1)}, u32[]{:S(2)}) copy-start(bf16[8,48,1536]{2,1,0:T(8,128)(2,1)S(1)} %all-to-all-done) | copy-start | bytes 3538948
  66.0 2.8 %collective-permute-start.6 = (bf16[384,1536]{1,0:T(8,128)(2,1)S(1)}, bf16[384,1536]{1,0:T(8,128)(2,1)S(1)}, u32[]{:S(2)}, u32[]{:S(2)}) collective-permute-start(bf16[384,1536]{1,0:T(8,128)(2,1)S(1)} %bitcast.60), channel_id=1, source_target_pairs={{0,2},{2,0},{4,6},{6,4},{8,10},{10,8},{12,14},{14,12},{16,18},{18,... | collective-permute-start | bytes 3538952 | tf_op jit(solution)/shard_map/ppermute | solution.py:1123
  68.8 1.0 copy-start.15
  79.8 4.2 %collective-permute-start.7 = (f32[8,1024]{1,0:T(8,128)}, f32[8,1024]{1,0:T(8,128)S(1)}, u32[]{:S(2)}, u32[]{:S(2)}) collective-permute-start(f32[8,1024]{1,0:T(8,128)} %get-tuple-element.104.sums_ref), channel_id=1, source_target_pairs={{0,1},{1,0},{2,3},{3,2},{4,5},{5,4},{6,7},{7,6},{8,9},{9,8},{10,11... | collective-permute-start | bytes 98312 | tf_op jit(solution)/shard_map/ppermute | solution.py:547
  84.6 13.3 %copy-start = (bf16[512,768]{1,0:T(8,128)(2,1)S(1)}, bf16[512,768]{1,0:T(8,128)(2,1)}, u32[]{:S(2)}) copy-start(bf16[512,768]{1,0:T(8,128)(2,1)} %own_ref.1) | copy-start | bytes 2359300
  97.8 5.7 %collective-permute-start.8 = (bf16[384,1536]{1,0:T(8,128)(2,1)}, bf16[384,1536]{1,0:T(8,128)(2,1)}, u32[]{:S(2)}, u32[]{:S(2)}) collective-permute-start(bf16[384,1536]{1,0:T(8,128)(2,1)} %get-tuple-element.110), channel_id=1, source_target_pairs={{0,2},{2,0},{4,6},{6,4},{8,10},{10,8},{12,14},{14,12},{16,18},{18,... | collective-permute-start | bytes 3538952 | tf_op jit(solution)/shard_map/ppermute | solution.py:1135
  98.2 5.4 %copy-start.2 = (f32[384,1536]{1,0:T(8,128)S(1)}, f32[384,1536]{1,0:T(8,128)}, u32[]{:S(2)}) copy-start(f32[384,1536]{1,0:T(8,128)} %get-tuple-element.109) | copy-start | bytes 7077892
  106.2 36.5 %all-to-all-start.1 = ((bf16[8,48,1536]{2,1,0:T(8,128)(2,1)}), bf16[8,48,1536]{2,1,0:T(8,128)(2,1)S(1)}, u32[]{:S(2)}, u32[]{:S(2)}) async-start(bf16[8,48,1536]{2,1,0:T(8,128)(2,1)} %bitcast.17), calls=%async_computation.1 | async-start | bytes 2359296 | tf_op jit(solution)/shard_map/all_to_all | solution.py:537
  149.5 6.7 %collective-permute-start.9 = (bf16[392,1152]{1,0:T(8,128)(2,1)}, bf16[392,1152]{1,0:T(8,128)(2,1)S(1)}, u32[]{:S(2)}, u32[]{:S(2)}) collective-permute-start(bf16[392,1152]{1,0:T(8,128)(2,1)} %get-tuple-element.118), channel_id=1, source_target_pairs={{0,2},{2,0},{4,6},{6,4},{8,10},{10,8},{12,14},{14,12},{16,18},{18,... | collective-permute-start | bytes 2709512 | tf_op jit(solution)/shard_map/ppermute | solution.py:1148
  150.4 38.7 %collective-permute-start.10 = (bf16[512,768]{1,0:T(8,128)(2,1)}, bf16[512,768]{1,0:T(8,128)(2,1)}, u32[]{:S(2)}, u32[]{:S(2)}) collective-permute-start(bf16[512,768]{1,0:T(8,128)(2,1)} %get-tuple-element.125), channel_id=1, source_target_pairs={{0,1},{1,0},{2,3},{3,2},{4,5},{5,4},{6,7},{7,6},{8,9},{9,8},{10,11... | collective-permute-start | bytes 2359304 | tf_op jit(solution)/shard_map/ppermute | solution.py:547
  159.1 33.7 %all-to-all-start.2 = ((bf16[8,56,1152]{2,1,0:T(8,128)(2,1)}), bf16[8,56,1152]{2,1,0:T(8,128)(2,1)S(1)}, u32[]{:S(2)}, u32[]{:S(2)}) async-start(bf16[8,56,1152]{2,1,0:T(8,128)(2,1)} %pad_maximum_fusion), calls=%async_computation.2 | async-start | bytes 2064384 | tf_op jit(solution)/shard_map/all_to_all | solution.py:537
  164.6 22.8 %collective-permute-start.11 = (bf16[512,768]{1,0:T(8,128)(2,1)}, bf16[512,768]{1,0:T(8,128)(2,1)}, u32[]{:S(2)}, u32[]{:S(2)}) collective-permute-start(bf16[512,768]{1,0:T(8,128)(2,1)} %normed_grad.2), channel_id=1, source_target_pairs={{0,1},{1,0},{2,3},{3,2},{4,5},{5,4},{6,7},{7,6},{8,9},{9,8},{10,11... | collective-permute-start | bytes 2359304 | tf_op jit(solution)/shard_map/ppermute | solution.py:547
  171.2 16.2 %copy-start.1 = (f32[512,768]{1,0:T(8,128)S(1)}, f32[512,768]{1,0:T(8,128)}, u32[]{:S(2)}) copy-start(f32[512,768]{1,0:T(8,128)} %normed_grad.3) | copy-start | bytes 4718596
  172.2 16.9 %copy-start.6 = (bf16[512,768]{1,0:T(8,128)(2,1)S(1)}, bf16[512,768]{1,0:T(8,128)(2,1)}, u32[]{:S(2)}) copy-start(bf16[512,768]{1,0:T(8,128)(2,1)} %own_ref.2) | copy-start | bytes 2359300
  172.2 16.9 %copy-start.7 = (bf16[512,768]{1,0:T(8,128)(2,1)S(1)}, bf16[512,768]{1,0:T(8,128)(2,1)}, u32[]{:S(2)}) copy-start(bf16[512,768]{1,0:T(8,128)(2,1)} %get-tuple-element.124) | copy-start | bytes 2359300
  192.8 6.4 %copy-start.13 = (bf16[48]{0:T(256)(128)(2,1)S(1)}, bf16[48]{0:T(256)(128)(2,1)}, u32[]{:S(2)}) copy-start(bf16[48]{0:T(256)(128)(2,1)} %param.18) | copy-start | bytes 292
  194.9 4.2 %collective-permute-start.12 = (f32[56,256]{1,0:T(8,128)S(1)}, f32[56,256]{1,0:T(8,128)S(1)}, u32[]{:S(2)}, u32[]{:S(2)}) collective-permute-start(f32[56,256]{1,0:T(8,128)S(1)} %pad.29), channel_id=1, source_target_pairs={{0,1},{1,0},{2,3},{3,2},{4,5},{5,4},{6,7},{7,6},{8,9},{9,8},{10,11... | collective-permute-start | bytes 172040 | tf_op jit(solution)/shard_map/ppermute | solution.py:547
  (1 other events, 0.6 us)

commit v4 on v3

--- a/solution.py
+++ b/solution.py
@@ -12,6 +12,7 @@
 CHUNK = 128
 LANES = 128
 TOKEN_BLOCK = 256
+VMEM_BASE = 16
 epsilon = 1e-05
 f32 = jnp.float32
 bf16 = jnp.bfloat16
@@ -176,6 +177,7 @@
 
 
 def backward_kernel(
+    table_ref,
     proj_ref,
     praw_ref,
     u_ref,
@@ -188,10 +190,17 @@
     aux_ref,
     segr_ref,
     gain_ref,
+    turned_ref,
     dproj_ref,
-    small_ref,
+    keep_ref,
+    send_ref,
     wide_ref,
     shared_ref,
+    small_ref,
+    total_ref,
+    grads_ref,
+    held_ref,
+    sem_ref,
     state_ref,
     ahead_ref,
     sahead_ref,
@@ -209,9 +218,11 @@
     shared_cols = slice(width, width + shared_size)
     step_cols = slice(width + shared_size, width + shared_size + LANES)
     chunk = chunks - 1 - pl.program_id(0)
+    copy = pltpu.make_async_copy(turned_ref, held_ref, sem_ref.at[0])
 
     @pl.when(pl.program_id(0) == 0)
     def _():
+        copy.start()
         for ref in (state_ref, ahead_ref, sahead_ref, row_ref, wide_ref, shared_ref):
             ref[...] = jnp.zeros_like(ref)
 
@@ -253,6 +264,7 @@
     dstate_low = dstate.astype(bf16)
     past = dot_nn(c_rows, entry)
     bds = dot_nn(b_rows, dstate_low)
+    here = pl.ds(pl.multiple_of(chunk * CHUNK, CHUNK), CHUNK)
     score_grad = jnp.zeros((CHUNK, CHUNK), f32)
     col_part = jnp.zeros((CHUNK, LANES), f32)
     for pair in range(pairs):
@@ -312,7 +324,9 @@
             wide_ref[3 - offset : 4 - offset, lanes] += jnp.sum(
                 cin * moved, axis=0, keepdims=True
             )
-        dproj_ref[:, lanes] = dcin.astype(bf16)
+        dcin = dcin.astype(bf16)
+        dproj_ref[:, lanes] = dcin
+        grads_ref[here, lanes] = dcin
         wide_ref[5:6, lanes] += jnp.sum(g * x, axis=0, keepdims=True)
     score_low = jnp.where(same, score_grad, 0.0).astype(bf16)
     ge_all = ge_ref[...]
@@ -330,11 +344,14 @@
         moved = ahead_shift(window, offset) * aux[:, 3 + offset : 4 + offset]
         dsin = dsin + taps[3 - offset : 4 - offset, :] * moved
         shared_ref[3 - offset : 4 - offset, :] += jnp.sum(sin * moved, axis=0, keepdims=True)
-    dproj_ref[:, shared_cols] = dsin.astype(bf16)
+    dsin = dsin.astype(bf16)
+    dproj_ref[:, shared_cols] = dsin
+    grads_ref[here, shared_cols] = dsin
     ddecay = row_ref[...].T - col_part + dot_split(prodb_ref[...], place)
     dlog = dot_exact(unsumming, ddecay)
     dstep = (dot_split(proda_ref[...], place) + rate * dlog) * live * sigmoid(pre)
     dproj_ref[:, step_cols] = dstep.astype(bf16)
+    grads_ref[here, step_cols] = dstep.astype(bf16)
     wide_ref[6:7, :LANES] += jnp.sum(dstep, axis=0, keepdims=True)
     wide_ref[6:7, LANES : 2 * LANES] += jnp.sum(step * dlog, axis=0, keepdims=True) * rate
 
@@ -348,6 +365,14 @@
         small_ref[1:2, step_cols] = wide_ref[6:7, :LANES]
         small_ref[2:3, step_cols] = wide_ref[6:7, LANES : 2 * LANES]
         small_ref[4:5, :width] = jnp.sum(gain_ref[...], axis=0, keepdims=True)
+        copy.wait()
+        held = keep_ref.shape[0] - 8
+        keep_ref[held:, :] = small_ref[...].astype(bf16)
+        send_ref[held:, :] = small_ref[...].astype(bf16)
+        tile = total_ref.shape[1]
+        for at in range(0, width + shared_size + LANES, tile):
+            total_ref[...] = dot_nn(held_ref[...], grads_ref[:, at : at + tile])
+            store_blocks(table_ref, total_ref, keep_ref, send_ref, slice(at, at + tile))
 
 
 def facts_kernel(seg_ref, aux_ref, segr_ref):
@@ -394,6 +419,7 @@
         ),
         name="token_facts",
         cost_estimate=cost(2),
+        compiler_params=vmem_limit(length),
     )(segments.reshape(chunks, CHUNK))
 
 
@@ -414,7 +440,7 @@
     shared_size = taps.shape[1]
     state_size = shared_size // 2
     chunks = length // CHUNK
-    sds = jax.ShapeDtypeStruct
+    proj, praw = from_store(proj, praw)
     return pl.pallas_call(
         forward_kernel,
         grid=(chunks,),
@@ -434,10 +460,10 @@
             pl.BlockSpec((1, state_size, width), lambda i: (i, 0, 0)),
         ],
         out_shape=(
-            sds((length, width), bf16),
-            sds((length, width), bf16),
-            sds((length, shared_size), f32),
-            sds((chunks, state_size, width), bf16),
+            stored((length, width), bf16),
+            stored((length, width), bf16),
+            stored((length, shared_size), f32),
+            stored((chunks, state_size, width), bf16),
         ),
         scratch_shapes=[
             pltpu.VMEM((state_size, width), f32),
@@ -447,57 +473,82 @@
         ],
         name="scan_forward",
         cost_estimate=cost(18),
+        compiler_params=vmem_limit(length),
     )(proj, praw, tapi, taps, heads, aux, segr)
 
 
-def run_backward(proj, praw, u, su, entry, grad, tapi, taps, heads, aux, segr, gain_rows):
+def run_backward(
+    table, proj, praw, u, su, entry, grad, tapi, taps, heads, aux, segr, gain_rows, turned
+):
     length, width = u.shape
     shared_size = su.shape[1]
     state_size = shared_size // 2
+    model_dim = turned.shape[0]
     chunks = length // CHUNK
     last = chunks - 1
     columns = width + shared_size + LANES
+    kept = model_dim // 2 + 8
     sds = jax.ShapeDtypeStruct
+    proj, praw, u, su, entry, grad, turned = from_store(proj, praw, u, su, entry, grad, turned)
+
+    def back(size):
+        return pl.BlockSpec((CHUNK, size), lambda i, t: (last - i, 0))
+
+    def fixed(shape):
+        return pl.BlockSpec(shape, lambda i, t: (0, 0))
+
     return pl.pallas_call(
         backward_kernel,
-        grid=(chunks,),
-        in_specs=[
-            chunk_spec(proj.shape[1], last),
-            chunk_spec(LANES, last),
-            chunk_spec(width, last),
-            chunk_spec(shared_size, last),
-            pl.BlockSpec((1, state_size, width), lambda i: (last - i, 0, 0)),
-            chunk_spec(width, last),
-            fixed_spec(tapi),
-            fixed_spec(taps),
-            fixed_spec(heads),
-            chunk_spec(aux.shape[1], last),
-            fixed_spec(segr),
-            fixed_spec(gain_rows),
-        ],
-        out_specs=[
-            chunk_spec(columns, last),
-            pl.BlockSpec((8, columns), lambda i: (0, 0)),
-        ],
+        grid_spec=pltpu.PrefetchScalarGridSpec(
+            num_scalar_prefetch=1,
+            grid=(chunks,),
+            in_specs=[
+                back(proj.shape[1]),
+                back(LANES),
+                back(width),
+                back(shared_size),
+                pl.BlockSpec((1, state_size, width), lambda i, t: (last - i, 0, 0)),
+                back(width),
+                fixed(tapi.shape),
+                fixed(taps.shape),
+                fixed(heads.shape),
+                back(aux.shape[1]),
+                fixed(segr.shape),
+                fixed(gain_rows.shape),
+                pl.BlockSpec(memory_space=pl.ANY),
+            ],
+            out_specs=[
+                back(columns),
+                fixed((kept, columns)),
+                fixed((kept, columns)),
+            ],
+            scratch_shapes=[
+                pltpu.VMEM((8, width), f32),
+                pltpu.VMEM((8, shared_size), f32),
+                pltpu.VMEM((8, columns), f32),
+                pltpu.VMEM((model_dim, column_tile(columns)), f32),
+                pltpu.VMEM((length, columns), bf16),
+                pltpu.VMEM((model_dim, length), bf16),
+                pltpu.SemaphoreType.DMA((1,)),
+                pltpu.VMEM((state_size, width), f32),
+                pltpu.VMEM((8, width), f32),
+                pltpu.VMEM((8, shared_size), f32),
+                pltpu.VMEM((CHUNK, width), bf16),
+                pltpu.VMEM((CHUNK, width), bf16),
+                pltpu.VMEM((LANES, CHUNK), f32),
+                pltpu.VMEM((CHUNK, width), f32),
+                pltpu.VMEM((CHUNK, width), f32),
+            ],
+        ),
         out_shape=(
-            sds((length, columns), bf16),
-            sds((8, columns), f32),
+            stored((length, columns), bf16),
+            stored((kept, columns), bf16),
+            stored((kept, columns), bf16),
         ),
-        scratch_shapes=[
-            pltpu.VMEM((8, width), f32),
-            pltpu.VMEM((8, shared_size), f32),
-            pltpu.VMEM((state_size, width), f32),
-            pltpu.VMEM((8, width), f32),
-            pltpu.VMEM((8, shared_size), f32),
-            pltpu.VMEM((CHUNK, width), bf16),
-            pltpu.VMEM((CHUNK, width), bf16),
-            pltpu.VMEM((LANES, CHUNK), f32),
-            pltpu.VMEM((CHUNK, width), f32),
-            pltpu.VMEM((CHUNK, width), f32),
-        ],
         name="scan_backward",
-        cost_estimate=cost(32),
-    )(proj, praw, u, su, entry, grad, tapi, taps, heads, aux, segr, gain_rows)
+        cost_estimate=cost(36),
+        compiler_params=vmem_limit(length),
+    )(table, proj, praw, u, su, entry, grad, tapi, taps, heads, aux, segr, gain_rows, turned)
 
 
 def block_plan():
@@ -652,6 +703,7 @@
     blocks = own_blocks * (2 if lax.axis_size("tensor") == 2 else 1)
     length = blocks * TOKEN_BLOCK
     sds = jax.ShapeDtypeStruct
+    own, other, low, high = from_store(own, other, low, high)
     return pl.pallas_call(
         partial(project_kernel, own_blocks=own_blocks, heads=heads),
         grid_spec=pltpu.PrefetchScalarGridSpec(
@@ -680,16 +732,17 @@
             scratch_shapes=[pltpu.SemaphoreType.DMA((table.shape[0],))],
         ),
         out_shape=(
-            sds((length, columns - LANES), bf16),
-            sds((length, LANES), f32),
-            sds((length, model_dim), bf16),
-            sds((model_dim, length), bf16),
-            sds((model_dim, columns), bf16),
+            stored((length, columns - LANES), bf16),
+            stored((length, LANES), f32),
+            stored((length, model_dim), bf16),
+            stored((model_dim, length), bf16),
+            stored((model_dim, columns), bf16),
             sds((8, spread.shape[1]), f32),
             sds((8, model_dim), f32),
         ),
         name="norm_project",
         cost_estimate=cost(9),
+        compiler_params=vmem_limit(length),
     )(starts, table, own, other, spread, low, high)
 
 
@@ -750,6 +803,7 @@
     own_blocks = own_rows // TOKEN_BLOCK
     blocks = length // TOKEN_BLOCK
     sds = jax.ShapeDtypeStruct
+    own, other, normed, mixed = from_store(own, other, normed, mixed)
     return pl.pallas_call(
         partial(out_grad_kernel, own_blocks=own_blocks),
         grid_spec=pltpu.PrefetchScalarGridSpec(
@@ -782,25 +836,27 @@
             sds((length, width), bf16),
             sds((model_dim, length), bf16),
             sds((8, length), f32),
-            sds((model_dim, 2 * width), bf16),
+            stored((model_dim, 2 * width), bf16),
         ),
         name="out_grad",
         cost_estimate=cost(9),
+        compiler_params=vmem_limit(length),
     )(starts, table, own, other, low, high, normed, mixed, gain)
 
 
-def store_blocks(table_ref, source_ref, keep_ref, send_ref):
+def column_tile(columns):
+    return 3 * LANES if columns % (3 * LANES) == 0 else LANES
+
+
+def store_blocks(table_ref, source_ref, keep_ref, send_ref, columns):
     count = table_ref.shape[0]
     rows = source_ref.shape[0] // count
     half = count // 2
-    for spot in range(half):
+    for spot in range(count):
+        target = keep_ref if spot < half else send_ref
+        at = (spot % half) * rows
         where = pl.multiple_of(table_ref[spot] * rows, rows)
-        keep_ref[spot * rows : (spot + 1) * rows, :] = source_ref[pl.ds(where, rows), :]
-    for spot in range(half):
-        where = pl.multiple_of(table_ref[half + spot] * rows, rows)
-        send_ref[spot * rows : (spot + 1) * rows, :] = source_ref[pl.ds(where, rows), :].astype(
-            bf16
-        )
+        target[at : at + rows, columns] = source_ref[pl.ds(where, rows), :].astype(bf16)
 
 
 def gated_kernel(
@@ -821,53 +877,66 @@
     keep_ref,
     send_ref,
     total_ref,
+    both_ref,
+    gheld_ref,
+    nheld_ref,
+    sem_ref,
     *,
     full_inner,
 ):
     step = pl.program_id(0)
     width = gate_ref.shape[1]
+    tile = total_ref.shape[1]
+    copies = [
+        pltpu.make_async_copy(nturned_ref, nheld_ref, sem_ref.at[0]),
+        pltpu.make_async_copy(gturned_ref, gheld_ref, sem_ref.at[1]),
+    ]
+
+    @pl.when(step == 0)
+    def _():
+        for copy in copies:
+            copy.start()
+
     inv, mean = token_scales(sums_ref[...] + more_ref[...], full_inner)
     gain = gain_ref[...].astype(f32)
-    gate = gate_ref[...].astype(f32)
-    gate_sig = sigmoid(gate)
-    gate_silu = gate * gate_sig
-    mixed = mixed_ref[...].astype(f32)
-    unit = mixed * gate_silu * inv
-    nog = nog_ref[...].astype(f32)
-    grad = inv * (nog * gain - unit * mean)
-    dgate = (grad * mixed * silu_slope(gate, gate_sig)).astype(bf16)
-    dgate_ref[...] = dgate
-    grad_ref[...] = (grad * gate_silu * aux_ref[:, 7:8]).astype(bf16)
-    normed_out = (unit * gain).astype(bf16)
-    out_ref[...] = normed_out
-    row = jnp.sum((nog * unit).reshape(-1, 8, width), axis=0)
-    part_gate = dot_nn(nturned_ref[...], dgate)
-    part_out = dot_nn(gturned_ref[...], normed_out)
-
-    @pl.when(step == 0)
-    def _():
-        total_ref[:, :width] = part_gate
-        total_ref[:, width:] = part_out
-        row_ref[...] = row
-
-    @pl.when(step > 0)
-    def _():
-        total_ref[:, :width] += part_gate
-        total_ref[:, width:] += part_out
-        row_ref[...] += row
+    here = pl.ds(pl.multiple_of(step * TOKEN_BLOCK, TOKEN_BLOCK), TOKEN_BLOCK)
+    live = aux_ref[:, 7:8]
+    for at in range(0, width, LANES):
+        lanes = slice(at, at + LANES)
+        gate = gate_ref[:, lanes].astype(f32)
+        gate_sig = sigmoid(gate)
+        gate_silu = gate * gate_sig
+        mixed = mixed_ref[:, lanes].astype(f32)
+        unit = mixed * gate_silu * inv
+        nog = nog_ref[:, lanes].astype(f32)
+        grad = inv * (nog * gain[:, lanes] - unit * mean)
+        dgate = (grad * mixed * silu_slope(gate, gate_sig)).astype(bf16)
+        dgate_ref[:, lanes] = dgate
+        both_ref[here, lanes] = dgate
+        grad_ref[:, lanes] = (grad * gate_silu * live).astype(bf16)
+        normed_out = (unit * gain[:, lanes]).astype(bf16)
+        out_ref[:, lanes] = normed_out
+        both_ref[here, slice(width + at, width + at + LANES)] = normed_out
+        row_ref[pl.ds(step * 8, 8), lanes] = jnp.sum((nog * unit).reshape(-1, 8, LANES), axis=0)
 
     @pl.when(step == pl.num_programs(0) - 1)
     def _():
-        store_blocks(table_ref, total_ref, keep_ref, send_ref)
+        for copy in copies:
+            copy.wait()
+        for at in range(0, 2 * width, tile):
+            turned = nheld_ref if at < width else gheld_ref
+            total_ref[...] = dot_nn(turned[...], both_ref[:, at : at + tile])
+            store_blocks(table_ref, total_ref, keep_ref, send_ref, slice(at, at + tile))
 
 
 def run_gated(table, gate, nog, mixed, sums, more, aux, gain, gturned, nturned, full_inner):
     length, width = gate.shape
     model_dim = gturned.shape[0]
     blocks = length // TOKEN_BLOCK
+    tile = column_tile(width)
     sds = jax.ShapeDtypeStruct
+    mixed, nturned = from_store(mixed, nturned)
     tokens = pl.BlockSpec((TOKEN_BLOCK, width), lambda i, t: (i, 0))
-    turned = pl.BlockSpec((model_dim, TOKEN_BLOCK), lambda i, t: (0, i))
     halves_spec = pl.BlockSpec((model_dim // 2, 2 * width), lambda i, t: (0, 0))
     return pl.pallas_call(
         partial(gated_kernel, full_inner=float(full_inner)),
@@ -882,29 +951,36 @@
                 pl.BlockSpec((8, TOKEN_BLOCK), lambda i, t: (0, i)),
                 pl.BlockSpec((TOKEN_BLOCK, aux.shape[1]), lambda i, t: (i, 0)),
                 pl.BlockSpec((1, width), lambda i, t: (0, 0)),
-                turned,
-                turned,
+                pl.BlockSpec(memory_space=pl.ANY),
+                pl.BlockSpec(memory_space=pl.ANY),
             ],
             out_specs=[
                 tokens,
                 tokens,
                 tokens,
-                pl.BlockSpec((8, width), lambda i, t: (0, 0)),
+                pl.BlockSpec((8 * blocks, width), lambda i, t: (0, 0)),
                 halves_spec,
                 halves_spec,
             ],
-            scratch_shapes=[pltpu.VMEM((model_dim, 2 * width), f32)],
+            scratch_shapes=[
+                pltpu.VMEM((model_dim, tile), f32),
+                pltpu.VMEM((length, 2 * width), bf16),
+                pltpu.VMEM((model_dim, length), bf16),
+                pltpu.VMEM((model_dim, length), bf16),
+                pltpu.SemaphoreType.DMA((2,)),
+            ],
         ),
         out_shape=(
             sds((length, width), bf16),
-            sds((length, width), bf16),
-            sds((length, width), bf16),
-            sds((8, width), f32),
-            sds((model_dim // 2, 2 * width), f32),
+            stored((length, width), bf16),
+            stored((length, width), bf16),
+            sds((8 * blocks, width), f32),
+            sds((model_dim // 2, 2 * width), bf16),
             sds((model_dim // 2, 2 * width), bf16),
         ),
         name="gated_grad",
-        cost_estimate=cost(12),
+        cost_estimate=cost(9),
+        compiler_params=vmem_limit(length),
     )(table, gate, nog, mixed, sums, more, aux, gain, gturned, nturned)
 
 
@@ -928,6 +1004,7 @@
     blocks = length // TOKEN_BLOCK
     half = blocks // 2
     sds = jax.ShapeDtypeStruct
+    (weights,) = from_store(weights)
     return pl.pallas_call(
         out_kernel,
         grid_spec=pltpu.PrefetchScalarGridSpec(
@@ -948,6 +1025,7 @@
         ),
         name="out_project",
         cost_estimate=cost(4),
+        compiler_params=vmem_limit(length),
     )(starts, rows, weights)
 
 
@@ -961,6 +1039,7 @@
     width = dgate.shape[1]
     model_dim = weights.shape[0]
     blocks = length // TOKEN_BLOCK // 2
+    dgate, dproj, gates, weights = from_store(dgate, dproj, gates, weights)
     return pl.pallas_call(
         norm_grad_kernel,
         grid_spec=pltpu.PrefetchScalarGridSpec(
@@ -977,45 +1056,8 @@
         out_shape=jax.ShapeDtypeStruct((length // 2, model_dim), kind),
         name="normed_grad",
         cost_estimate=cost(5),
+        compiler_params=vmem_limit(length),
     )(starts, dgate, dproj, gates, weights)
-
-
-def weight_grad_kernel(
-    table_ref, turned_ref, dproj_ref, small_ref, keep_ref, send_ref, total_ref
-):
-    total_ref[...] = dot_nn(turned_ref[...], dproj_ref[...])
-    half = keep_ref.shape[0] - 8
-    store_blocks(table_ref, total_ref, keep_ref, send_ref)
-    keep_ref[half:, :] = small_ref[...]
-    send_ref[half:, :] = small_ref[...].astype(bf16)
-
-
-def run_weight_grad(table, turned, dproj, small):
-    model_dim, length = turned.shape
-    columns = dproj.shape[1]
-    tile = 3 * LANES if columns % (3 * LANES) == 0 else LANES
-    held = model_dim // 2 + 8
-    sds = jax.ShapeDtypeStruct
-    return pl.pallas_call(
-        weight_grad_kernel,
-        grid_spec=pltpu.PrefetchScalarGridSpec(
-            num_scalar_prefetch=1,
-            grid=(columns // tile,),
-            in_specs=[
-                pl.BlockSpec((model_dim, length), lambda i, t: (0, 0)),
-                pl.BlockSpec((length, tile), lambda i, t: (0, i)),
-                pl.BlockSpec((8, tile), lambda i, t: (0, i)),
-            ],
-            out_specs=[
-                pl.BlockSpec((held, tile), lambda i, t: (0, i)),
-                pl.BlockSpec((held, tile), lambda i, t: (0, i)),
-            ],
-            scratch_shapes=[pltpu.VMEM((model_dim, tile), f32)],
-        ),
-        out_shape=(sds((held, columns), f32), sds((held, columns), bf16)),
-        name="weight_grad",
-        cost_estimate=cost(6),
-    )(table, turned, dproj, small)
 
 
 def after(value, *others):
@@ -1024,6 +1066,18 @@
 
 def cost(microseconds):
     return pl.CostEstimate(flops=int(microseconds * 1.1e9), transcendentals=0, bytes_accessed=0)
+
+
+def stored(shape, kind):
+    return pltpu.HBM(shape, kind)
+
+
+def from_store(*values):
+    return tuple(pltpu.with_memory_space_constraint(v, pltpu.HBM) for v in values)
+
+
+def vmem_limit(length):
+    return pltpu.CompilerParams(vmem_limit_bytes=min(60, VMEM_BASE + length // 128) << 20)
 
 
 def pad_to(values, axis, size):
@@ -1134,22 +1188,37 @@
     )
     ggot = lax.ppermute(gsend, "dp", core)
     send_start = starts[1:] if two else jnp.zeros((1,), jnp.int32)
-    keep_start = starts[:1] if two else jnp.full((1,), blocks // 2, jnp.int32)
     out_send, out_keep = run_out(send_start, normed_out, later_rows)
     ggot, out_send = lax.optimization_barrier((ggot, out_send))
-    gsum = exchange((gkeep + ggot.astype(f32)).astype(bf16), groups)
+    gsum = exchange((gkeep.astype(f32) + ggot.astype(f32)).astype(bf16), groups)
     out_other = swap(out_send) if two else None
 
-    dproj, small = run_backward(
-        proj, praw, u, su, entry, mixed_grad, tapi, taps, heads_block, aux, segr, gain_rows
-    )
-    dproj, gsum = lax.optimization_barrier((dproj, gsum))
-    wkeep, wsend = run_weight_grad(core_table, normed_t, dproj, small)
+    dproj, wkeep, wsend = run_backward(
+        core_table,
+        proj,
+        praw,
+        u,
+        su,
+        entry,
+        mixed_grad,
+        tapi,
+        taps,
+        heads_block,
+        aux,
+        segr,
+        gain_rows,
+        normed_t,
+    )
+    if two:
+        wsend, gsum, out_other = lax.optimization_barrier((wsend, gsum, out_other))
+    else:
+        wsend, gsum = lax.optimization_barrier((wsend, gsum))
     wgot = lax.ppermute(wsend, "dp", core)
     grad_send = run_norm_grad(send_start, dgate, dproj, later_rows, weights, bf16)
     wgot, grad_send = lax.optimization_barrier((wgot, grad_send))
+    grad_other = swap(grad_send) if two else None
     held = rows * chips
-    wtotal = (wkeep + wgot.astype(f32)).astype(bf16)
+    wtotal = (wkeep.astype(f32) + wgot.astype(f32)).astype(bf16)
     wtotal = jnp.concatenate(
         [
             wtotal[:held].reshape(chips, rows, -1),
@@ -1157,12 +1226,13 @@
         ],
         axis=1,
     ).reshape(chips * (rows + 8), -1)
-    wtotal, dproj, gsum, out_keep = lax.optimization_barrier((wtotal, dproj, gsum, out_keep))
+    wtotal, dproj = lax.optimization_barrier((wtotal, dproj))
     wsum = exchange(wtotal, groups)
+    keep_start = starts[:1] if two else jnp.full((1,), blocks // 2, jnp.int32)
     grad_keep = run_norm_grad(keep_start, dgate, dproj, later_rows, weights, f32)
     if two:
         out_half = out_keep.astype(f32) + out_other.astype(f32)
-        own_grad = grad_keep + swap(grad_send).astype(f32)
+        own_grad = grad_keep + grad_other.astype(f32)
     else:
         out_half = add_halves(out_send, out_keep)
         own_grad = add_halves(grad_send, grad_keep)

time: 202 us -> 192 us (0.950)
  Pallas kernels: 105 us -> 95.5 us
  waiting for transfers between devices: 33.9 us -> 38 us
  local copies, waits for them, and re-layouts: 15.1 us -> 12.1 us
    ppermute x3, waiting for transfers between devices: 9.85 us -> 13.5 us  [body(): got = lax.ppermute(low, 'dp', stage)]
    pallas_call x2 -> x1, Pallas kernels: 38.5 us -> 35.4 us  [run_backward(): pl.pallas_call(backward_kernel, grid_spec=pltpu.PrefetchScalarGridSpec(nu...]
    all_to_all x3, waiting for transfers between devices: 1.23 us -> 4.15 us  [exchange(): lax.all_to_all(blocks, 'dp', 0, 0, axis_index_groups=groups, tiled=True)]
    pallas_call x1, Pallas kernels: 13.2 us -> 10.5 us  [run_gated(): pl.pallas_call(partial(gated_kernel, full_inner=float(full_inner)), grid_...]
    reduce_sum x2, other arithmetic: 0.29 us -> 2.85 us  [sum_blocks(): jnp.sum(blocks.reshape(-1, rows, blocks.shape[1]).astype(f32), axis=0)]
    ppermute x6, waiting for transfers between devices: 20 us -> 17.5 us  [swap(): return lax.ppermute(values, 'tensor', [(0, 1), (1, 0)])]
  transfers between devices with their start and end apart: 16 -> 16, of which waited for: 8 -> 9; matrix products, arithmetic and copies ran while one was open for 8% -> 5% of each run, Pallas kernels for 37% -> 39%
where the time goes in v4:
time: 192 us; the launch traced here: 191 us
  Pallas kernels  95.5 us (50%)
  waiting for transfers between devices  38 us (20%)
  starting transfers between devices  30.7 us (16%)
  other arithmetic  13.7 us (7%)
  local copies, waits for them, and re-layouts  12.1 us (6%)
    pallas_call x1, Pallas kernels, run_backward(): pl.pallas_call(backward_kernel, grid_spec=pltpu.PrefetchScalarGridSpec(nu...  35.4 us
    ppermute x6, waiting for transfers between devices, swap(): return lax.ppermute(values, 'tensor', [(0, 1), (1, 0)])  17.5 us
    pallas_call x1, Pallas kernels, run_forward(): pl.pallas_call(forward_kernel, grid=(chunks,), in_specs=[chunk_spec(proj....  16.9 us
    all_to_all x3, starting transfers between devices, exchange(): lax.all_to_all(blocks, 'dp', 0, 0, axis_index_groups=groups, tiled=True)  15.9 us
    ppermute x3, waiting for transfers between devices, body(): got = lax.ppermute(low, 'dp', stage)  13.5 us
    pallas_call x1, Pallas kernels, run_out_grad(): pl.pallas_call(partial(out_grad_kernel, own_blocks=own_blocks), grid_spec...  11.4 us
    pallas_call x1, Pallas kernels, run_gated(): pl.pallas_call(partial(gated_kernel, full_inner=float(full_inner)), grid_...  10.5 us
    pallas_call x1, Pallas kernels, run_project(): pl.pallas_call(partial(project_kernel, own_blocks=own_blocks, heads=heads...  9.04 us
  transfers between devices with their start and end apart: 16, of which 9 were waited for; matrix products, arithmetic and copies ran while one was open for 5% of the time, Pallas kernels for 39%

profile of v4, /device:TPU:0, one launch (start us, length us, event | category | flops | bytes accessed | tf_op | source)
XLA Modules:
  0.0 191.0 jit_solution(6561428542146858049)
XLA Ops:
  3.7 1.3 fusion.32
  5.1 4.1 %collective-permute-start = (bf16[48,1152]{1,0:T(8,128)(2,1)S(1)}, bf16[48,1152]{1,0:T(8,128)(2,1)S(1)}, u32[]{:S(2)}, u32[]{:S(2)}) collective-permute-start(bf16[48,1152]{1,0:T(8,128)(2,1)S(1)} %pad_maximum_fusion.6), channel_id=1, source_target_pairs={{0,16},{2,18},{4,20},{6,22},{8,24},{10,26},{12,28},{14,30},{16,0},... | collective-permute-start | bytes 331784 | tf_op jit(solution)/shard_map/ppermute | solution.py:1153
  9.2 1.5 collective-permute-start.3
  12.9 1.8 collective-permute-done
  15.6 5.0 %collective-permute-done.1 = bf16[96,1152]{1,0:T(8,128)(2,1)S(1)} collective-permute-done((bf16[96,1152]{1,0:T(8,128)(2,1)S(1)}, bf16[96,1152]{1,0:T(8,128)(2,1)S(1)}, u32[]{:S(2)}, u32[]{:S(2)}) %collective-permute-start.1) | collective-permute-done | bytes 221216 | tf_op jit(solution)/shard_map/ppermute | solution.py:1153
  20.7 1.6 collective-permute-start.2
  22.4 6.7 %collective-permute-done.2 = bf16[192,1152]{1,0:T(8,128)(2,1)S(1)} collective-permute-done((bf16[192,1152]{1,0:T(8,128)(2,1)S(1)}, bf16[192,1152]{1,0:T(8,128)(2,1)S(1)}, u32[]{:S(2)}, u32[]{:S(2)}) %collective-permute-start.2) | collective-permute-done | bytes 442400 | tf_op jit(solution)/shard_map/ppermute | solution.py:1153
  31.4 5.9 %all-to-all-start = ((bf16[8,48,1536]{2,1,0:T(8,128)(2,1)}), bf16[8,48,1536]{2,1,0:T(8,128)(2,1)S(1)}, u32[]{:S(2)}, u32[]{:S(2)}) async-start(bf16[8,48,1536]{2,1,0:T(8,128)(2,1)} %broadcast_in_dim.11), calls=%async_computation | async-start | bytes 2359296 | tf_op jit(solution)/shard_map/all_to_all | solution.py:588
  37.3 1.6 collective-permute-start.5
  38.9 9.0 %norm_project.1 = (bf16[1024,1024]{1,0:T(8,128)(2,1)}, f32[1024,128]{1,0:T(8,128)}, bf16[1024,768]{1,0:T(8,128)(2,1)}, bf16[768,1024]{1,0:T(8,128)(2,1)}, bf16[7...) custom-call(s32[2]{0:T(128)S(1)} %pad_add_fusion.starts_ref, s32[16]{0:T(128)S(1)} %get-tuple-element.80.table_ref, ...), custom_call_target="tpu_custom_call" | custom-call | flops 9900000256 | tf_op jit(solution)/shard_map/norm_project/pallas_call | solution.py:707
  47.9 16.9 %scan_forward.1 = (bf16[1024,768]{1,0:T(8,128)(2,1)}, bf16[1024,768]{1,0:T(8,128)(2,1)}, f32[1024,256]{1,0:T(8,128)}, bf16[8,128,768]{2,1,0:T(8,128)(2,1)}) custom-call(bf16[1024,1024]{1,0:T(8,128)(2,1)} %get-tuple-element.83.proj_ref, f32[1024,128]{1,0:T(8,128)} %get-tuple-element.84.step_ref.praw_ref, bf16[4,768]{1,0:T(4,128)(2,1)S(1)} %copy-done, ...), custom_call_target="tpu_custom_call" | custom-call | flops 19800000512 | tf_op jit(solution)/shard_map/scan_forward/pallas_call | solution.py:444
  64.8 1.5 all-to-all-done
  66.4 2.8 %collective-permute-done.6.high_ref = bf16[384,1536]{1,0:T(8,128)(2,1)S(1)} collective-permute-done((bf16[384,1536]{1,0:T(8,128)(2,1)S(1)}, bf16[384,1536]{1,0:T(8,128)(2,1)S(1)}, u32[]{:S(2)}, u32[]{:S(2)}) %collective-permute-start.6) | collective-permute-done | bytes 1179680 | tf_op jit(solution)/shard_map/ppermute | solution.py:1177
  69.2 11.4 %out_grad.1 = (bf16[1024,768]{1,0:T(8,128)(2,1)S(1)}, bf16[1024,768]{1,0:T(8,128)(2,1)S(1)}, bf16[768,1024]{1,0:T(8,128)(2,1)S(1)}, f32[8,1024]{1,0:T(8,128)S(1)}, bf16[768,1536]{1,0:T(8,128)(2,1)}) custom-call(s32[2]{0:T(128)S(1)} %pad_add_fusion.starts_ref, s32[16]{0:T(128)S(1)} %get-tuple-element.73.table_ref, bf16[512,768]{1,0:T(8,128)(2,1)} %own_ref.2, ...), custom_call_target="tpu_custom_call" | custom-call | flops 9900000256 | tf_op jit(solution)/shard_map/out_grad/pallas_call | solution.py:807
  80.6 1.6 collective-permute-start.7
  82.2 2.4 %collective-permute-done.7.more_ref = f32[8,1024]{1,0:T(8,128)S(1)} collective-permute-done((f32[8,1024]{1,0:T(8,128)S(1)}, f32[8,1024]{1,0:T(8,128)S(1)}, u32[]{:S(2)}, u32[]{:S(2)}) %collective-permute-start.7) | collective-permute-done | bytes 32800 | tf_op jit(solution)/shard_map/ppermute | solution.py:598
  84.6 10.5 %gated_grad.1 = (bf16[1024,768]{1,0:T(8,128)(2,1)S(1)}, bf16[1024,768]{1,0:T(8,128)(2,1)}, bf16[1024,768]{1,0:T(8,128)(2,1)}, f32[32,768]{1,0:T(8,128)S(1)}, bf1...) custom-call(s32[16]{0:T(128)S(1)} %get-tuple-element.73.table_ref, ...), custom_call_target="tpu_custom_call" | custom-call | flops 9900000256 | tf_op jit(solution)/shard_map/gated_grad/pallas_call | solution.py:941
  95.4 3.5 %out_project.1 = (bf16[512,768]{1,0:T(8,128)(2,1)S(1)}, bf16[512,768]{1,0:T(8,128)(2,1)S(1)}) custom-call(s32[1]{0:T(128)} %bitcast.starts_ref, bf16[1024,768]{1,0:T(8,128)(2,1)S(1)} %get-tuple-element.101.rows_ref, bf16[768,1536]{1,0:T(8,128)(2,1)} %get-tuple-element.102.weights_ref.gates_ref), custom_call_target="tpu_custom_call" | custom-call | flops 4400000000 | tf_op jit(solution)/shard_map/out_project/pallas_call | solution.py:1008
  98.9 1.3 add_convert_fusion
  100.2 4.5 %all-to-all-start.1 = ((bf16[8,48,1536]{2,1,0:T(8,128)(2,1)}), bf16[8,48,1536]{2,1,0:T(8,128)(2,1)}, u32[]{:S(2)}, u32[]{:S(2)}) async-start(bf16[8,48,1536]{2,1,0:T(8,128)(2,1)} %bitcast.57), calls=%async_computation.1 | async-start | bytes 2359296 | tf_op jit(solution)/shard_map/all_to_all | solution.py:588
  104.7 1.5 collective-permute-start.9
  106.3 35.4 %scan_backward.1 = (bf16[1024,1152]{1,0:T(8,128)(2,1)}, bf16[392,1152]{1,0:T(8,128)(2,1)}, bf16[392,1152]{1,0:T(8,128)(2,1)}) custom-call(s32[16]{0:T(128)S(1)} %get-tuple-element.73.table_ref, bf16[1024,1024]{1,0:T(8,128)(2,1)} %get-tuple-element.83.proj_ref, f32[1024,128]{1,0:T(8,128)} %get-tuple-element.84.step_ref.praw_ref, ...), custom_call_target="tpu_custom_call" | custom-call | flops 39600001024 | tf_op jit(solution)/shard_map/scan_backward/pallas_call | solution.py:500
  142.0 4.3 %normed_grad.2 = bf16[512,768]{1,0:T(8,128)(2,1)S(1)} custom-call(s32[1]{0:T(128)} %bitcast.starts_ref, bf16[1024,768]{1,0:T(8,128)(2,1)} %get-tuple-element.116.dgate_ref, bf16[1024,1152]{1,0:T(8,128)(2,1)} %get-tuple-element.122.dproj_ref, bf16[768,1536]{1,0:T(8,128)(2,1)} %get-tuple-element.102.weights_ref.gates_ref, ...), custom_call_target="tpu_custom_call" | custom-call | flops 5500000256 | tf_op jit(solution)/shard_map/normed_grad/pallas_call | solution.py:1043
  146.3 1.4 add_convert_fusion.1
  148.9 5.5 %all-to-all-start.2 = ((bf16[8,56,1152]{2,1,0:T(8,128)(2,1)}), bf16[8,56,1152]{2,1,0:T(8,128)(2,1)}, u32[]{:S(2)}, u32[]{:S(2)}) async-start(bf16[8,56,1152]{2,1,0:T(8,128)(2,1)} %pad_maximum_fusion), calls=%async_computation.2 | async-start | bytes 2064384 | tf_op jit(solution)/shard_map/all_to_all | solution.py:588
  155.2 1.5 convert_reduce_fusion
  157.5 4.2 %normed_grad.3 = f32[512,768]{1,0:T(8,128)S(1)} custom-call(s32[1]{0:T(128)} %bitcast.11.starts_ref, bf16[1024,768]{1,0:T(8,128)(2,1)} %get-tuple-element.116.dgate_ref, bf16[1024,1152]{1,0:T(8,128)(2,1)} %get-tuple-element.122.dproj_ref, bf16[768,1536]{1,0:T(8,128)(2,1)} %get-tuple-element.102.weights_ref.gates_ref, ...), custom_call_target="tpu_custom_call" | custom-call | flops 5500000256 | tf_op jit(solution)/shard_map/normed_grad/pallas_call | solution.py:1043
  161.7 12.3 %collective-permute-done.11 = bf16[512,768]{1,0:T(8,128)(2,1)S(1)} collective-permute-done((bf16[512,768]{1,0:T(8,128)(2,1)S(1)}, bf16[512,768]{1,0:T(8,128)(2,1)S(1)}, u32[]{:S(2)}, u32[]{:S(2)}) %collective-permute-start.11) | collective-permute-done | bytes 786464 | tf_op jit(solution)/shard_map/ppermute | solution.py:598
  174.6 3.4 %fusion.5 = (f32[512,768]{1,0:T(8,128)}, bf16[512,768]{1,0:T(8,128)(2,1)}) fusion(bf16[512,768]{1,0:T(8,128)(2,1)S(1)} %copy-done.2, bf16[512,768]{1,0:T(8,128)(2,1)S(1)} %copy-done.7, f32[512,768]{1,0:T(8,128)S(1)} %normed_grad.3, bf16[512,768]{1,0:T(8,128)(2,1)S(1)} %collective-permute-done.11, f32[512]{0:T(512)S(1)} %broadcast_multiply_fusion, ...), kind=kLoop, calls=%fused_computation.12 | loop fusion | flops 5898240 | bytes 7871488 | tf_op jit(solution)/shard_map/add | solution.py:1280
  177.9 2.6 %all-to-all-done.2 = bf16[8,56,1152]{2,1,0:T(8,128)(2,1)} async-done(((bf16[8,56,1152]{2,1,0:T(8,128)(2,1)}), bf16[8,56,1152]{2,1,0:T(8,128)(2,1)}, u32[]{:S(2)}, u32[]{:S(2)}) %all-to-all-start.2) | async-done | bytes 1032224 | tf_op jit(solution)/shard_map/all_to_all | solution.py:588
  180.5 1.4 convert_reduce_fusion.1
  186.4 2.7 %collective-permute-done.12 = f32[56,256]{1,0:T(8,128)S(1)} collective-permute-done((f32[56,256]{1,0:T(8,128)S(1)}, f32[56,256]{1,0:T(8,128)S(1)}, u32[]{:S(2)}, u32[]{:S(2)}) %collective-permute-start.12) | collective-permute-done | bytes 57376 | tf_op jit(solution)/shard_map/ppermute | solution.py:598
  (101 shorter events, 18.9 us)
Async XLA Ops:
  3.7 26.5 %copy-start.4 = (bf16[6,8,2,128]{3,1,2,0:T(8,128)(2,1)}, bf16[6,8,2,128]{3,1,2,0:T(8,128)(2,1)S(1)}, u32[]{:S(2)}) copy-start(bf16[6,8,2,128]{3,1,2,0:T(8,128)(2,1)S(1)} %copy.47) | copy-start | bytes 73732
  5.1 25.2 %copy-start.8 = (bf16[48,128]{1,0:T(8,128)(2,1)}, bf16[48,128]{1,0:T(8,128)(2,1)S(1)}, u32[]{:S(2)}) copy-start(bf16[48,128]{1,0:T(8,128)(2,1)S(1)} %pad.25) | copy-start | bytes 36868
  5.1 9.6 %collective-permute-start = (bf16[48,1152]{1,0:T(8,128)(2,1)S(1)}, bf16[48,1152]{1,0:T(8,128)(2,1)S(1)}, u32[]{:S(2)}, u32[]{:S(2)}) collective-permute-start(bf16[48,1152]{1,0:T(8,128)(2,1)S(1)} %pad_maximum_fusion.6), channel_id=1, source_target_pairs={{0,16},{2,18},{4,20},{6,22},{8,24},{10,26},{12,28},{14,30},{16,0},... | collective-permute-start | bytes 331784 | tf_op jit(solution)/shard_map/ppermute | solution.py:1153
  9.2 22.0 %collective-permute-start.3 = (bf16[512,768]{1,0:T(8,128)(2,1)}, bf16[512,768]{1,0:T(8,128)(2,1)}, u32[]{:S(2)}, u32[]{:S(2)}) collective-permute-start(bf16[512,768]{1,0:T(8,128)(2,1)} %own_ref.1), channel_id=1, source_target_pairs={{0,1},{1,0},{2,3},{3,2},{4,5},{5,4},{6,7},{7,6},{8,9},{9,8},{10,11... | collective-permute-start | bytes 2359304 | tf_op jit(solution)/shard_map/ppermute | solution.py:598
  10.8 0.7 copy-start.1
  11.5 0.7 copy-start.13
  11.5 0.7 copy-start.14
  11.5 0.7 copy-start.16
  11.8 10.6 %copy-start.11 = (bf16[768]{0:T(1024)(128)(2,1)S(1)}, bf16[768]{0:T(1024)(128)(2,1)}, u32[]{:S(2)}) copy-start(bf16[768]{0:T(1024)(128)(2,1)} %param.27) | copy-start | bytes 4612
  11.8 10.6 %copy-start.10 = (bf16[768,48]{0,1:T(8,128)(2,1)S(1)}, bf16[768,48]{0,1:T(8,128)(2,1)}, u32[]{:S(2)}) copy-start(bf16[768,48]{0,1:T(8,128)(2,1)} %param.28) | copy-start | bytes 221188
  14.7 6.0 %collective-permute-start.1 = (bf16[96,1152]{1,0:T(8,128)(2,1)S(1)}, bf16[96,1152]{1,0:T(8,128)(2,1)S(1)}, u32[]{:S(2)}, u32[]{:S(2)}) collective-permute-start(bf16[96,1152]{1,0:T(8,128)(2,1)S(1)} %pad_maximum_fusion.4), channel_id=1, source_target_pairs={{0,8},{2,6},{4,12},{6,2},{8,0},{10,14},{12,4},{14,10},{16,24},{18,... | collective-permute-start | bytes 663560 | tf_op jit(solution)/shard_map/ppermute | solution.py:1153
  20.7 8.4 %collective-permute-start.2 = (bf16[192,1152]{1,0:T(8,128)(2,1)S(1)}, bf16[192,1152]{1,0:T(8,128)(2,1)S(1)}, u32[]{:S(2)}, u32[]{:S(2)}) collective-permute-start(bf16[192,1152]{1,0:T(8,128)(2,1)S(1)} %pad_maximum_fusion.2), channel_id=1, source_target_pairs={{0,4},{2,10},{4,0},{6,14},{8,12},{10,2},{12,8},{14,6},{16,20},{18,... | collective-permute-start | bytes 1327112 | tf_op jit(solution)/shard_map/ppermute | solution.py:1153
  31.3 6.0 %copy-start.6 = (bf16[512,768]{1,0:T(8,128)(2,1)S(1)}, bf16[512,768]{1,0:T(8,128)(2,1)}, u32[]{:S(2)}) copy-start(bf16[512,768]{1,0:T(8,128)(2,1)} %own_ref.2) | copy-start | bytes 2359300
  31.3 7.6 %collective-permute-start.4 = (bf16[384,1152]{1,0:T(8,128)(2,1)}, bf16[384,1152]{1,0:T(8,128)(2,1)}, u32[]{:S(2)}, u32[]{:S(2)}) collective-permute-start(bf16[384,1152]{1,0:T(8,128)(2,1)} %pad_maximum_fusion.1.low_ref), channel_id=1, source_target_pairs={{0,2},{2,0},{4,6},{6,4},{8,10},{10,8},{12,14},{14,12},{16,18},{18,... | collective-permute-start | bytes 2654216 | tf_op jit(solution)/shard_map/ppermute | solution.py:1166
  31.4 35.0 %all-to-all-start = ((bf16[8,48,1536]{2,1,0:T(8,128)(2,1)}), bf16[8,48,1536]{2,1,0:T(8,128)(2,1)S(1)}, u32[]{:S(2)}, u32[]{:S(2)}) async-start(bf16[8,48,1536]{2,1,0:T(8,128)(2,1)} %broadcast_in_dim.11), calls=%async_computation | async-start | bytes 2359296 | tf_op jit(solution)/shard_map/all_to_all | solution.py:588
  37.3 10.6 %copy-start = (bf16[4,768]{1,0:T(4,128)(2,1)S(1)}, bf16[4,768]{1,0:T(4,128)(2,1)}, u32[]{:S(2)}) copy-start(bf16[4,768]{1,0:T(4,128)(2,1)} %tapi_ref.1) | copy-start | bytes 18436
  37.3 27.6 %collective-permute-start.5 = (bf16[512,768]{1,0:T(8,128)(2,1)S(1)}, bf16[512,768]{1,0:T(8,128)(2,1)}, u32[]{:S(2)}, u32[]{:S(2)}) collective-permute-start(bf16[512,768]{1,0:T(8,128)(2,1)S(1)} %copy-done.6), channel_id=1, source_target_pairs={{0,1},{1,0},{2,3},{3,2},{4,5},{5,4},{6,7},{7,6},{8,9},{9,8},{10,11... | collective-permute-start | bytes 2359304 | tf_op jit(solution)/shard_map/ppermute | solution.py:598
  66.4 2.8 %collective-permute-start.6 = (bf16[384,1536]{1,0:T(8,128)(2,1)S(1)}, bf16[384,1536]{1,0:T(8,128)(2,1)S(1)}, u32[]{:S(2)}, u32[]{:S(2)}) collective-permute-start(bf16[384,1536]{1,0:T(8,128)(2,1)S(1)} %bitcast.54), channel_id=1, source_target_pairs={{0,2},{2,0},{4,6},{6,4},{8,10},{10,8},{12,14},{14,12},{16,18},{18,... | collective-permute-start | bytes 3538952 | tf_op jit(solution)/shard_map/ppermute | solution.py:1177
  80.6 4.0 %collective-permute-start.7 = (f32[8,1024]{1,0:T(8,128)S(1)}, f32[8,1024]{1,0:T(8,128)S(1)}, u32[]{:S(2)}, u32[]{:S(2)}) collective-permute-start(f32[8,1024]{1,0:T(8,128)S(1)} %get-tuple-element.98.sums_ref), channel_id=1, source_target_pairs={{0,1},{1,0},{2,3},{3,2},{4,5},{5,4},{6,7},{7,6},{8,9},{9,8},{10,11... | collective-permute-start | bytes 98312 | tf_op jit(solution)/shard_map/ppermute | solution.py:598
  84.6 10.6 %copy-start.2 = (bf16[512,768]{1,0:T(8,128)(2,1)S(1)}, bf16[512,768]{1,0:T(8,128)(2,1)}, u32[]{:S(2)}) copy-start(bf16[512,768]{1,0:T(8,128)(2,1)} %own_ref.1) | copy-start | bytes 2359300
  95.1 3.8 %collective-permute-start.8 = (bf16[384,1536]{1,0:T(8,128)(2,1)S(1)}, bf16[384,1536]{1,0:T(8,128)(2,1)S(1)}, u32[]{:S(2)}, u32[]{:S(2)}) collective-permute-start(bf16[384,1536]{1,0:T(8,128)(2,1)S(1)} %get-tuple-element.111), channel_id=1, source_target_pairs={{0,2},{2,0},{4,6},{6,4},{8,10},{10,8},{12,14},{14,12},{16,18},{18,... | collective-permute-start | bytes 3538952 | tf_op jit(solution)/shard_map/ppermute | solution.py:1189
  100.2 41.5 %all-to-all-start.1 = ((bf16[8,48,1536]{2,1,0:T(8,128)(2,1)}), bf16[8,48,1536]{2,1,0:T(8,128)(2,1)}, u32[]{:S(2)}, u32[]{:S(2)}) async-start(bf16[8,48,1536]{2,1,0:T(8,128)(2,1)} %bitcast.57), calls=%async_computation.1 | async-start | bytes 2359296 | tf_op jit(solution)/shard_map/all_to_all | solution.py:588
  104.7 36.9 %collective-permute-start.9 = (bf16[512,768]{1,0:T(8,128)(2,1)S(1)}, bf16[512,768]{1,0:T(8,128)(2,1)}, u32[]{:S(2)}, u32[]{:S(2)}) collective-permute-start(bf16[512,768]{1,0:T(8,128)(2,1)S(1)} %get-tuple-element.114), channel_id=1, source_target_pairs={{0,1},{1,0},{2,3},{3,2},{4,5},{5,4},{6,7},{7,6},{8,9},{9,8},{10,11... | collective-permute-start | bytes 2359304 | tf_op jit(solution)/shard_map/ppermute | solution.py:598
  141.7 4.6 %collective-permute-start.10 = (bf16[392,1152]{1,0:T(8,128)(2,1)}, bf16[392,1152]{1,0:T(8,128)(2,1)}, u32[]{:S(2)}, u32[]{:S(2)}) collective-permute-start(bf16[392,1152]{1,0:T(8,128)(2,1)} %get-tuple-element.118), channel_id=1, source_target_pairs={{0,2},{2,0},{4,6},{6,4},{8,10},{10,8},{12,14},{14,12},{16,18},{18,... | collective-permute-start | bytes 2709512 | tf_op jit(solution)/shard_map/ppermute | solution.py:1216
  142.0 4.3 %copy-start.3 = (bf16[392,1152]{1,0:T(8,128)(2,1)S(1)}, bf16[392,1152]{1,0:T(8,128)(2,1)}, u32[]{:S(2)}) copy-start(bf16[392,1152]{1,0:T(8,128)(2,1)} %get-tuple-element.117) | copy-start | bytes 2709508
  148.9 31.7 %all-to-all-start.2 = ((bf16[8,56,1152]{2,1,0:T(8,128)(2,1)}), bf16[8,56,1152]{2,1,0:T(8,128)(2,1)}, u32[]{:S(2)}, u32[]{:S(2)}) async-start(bf16[8,56,1152]{2,1,0:T(8,128)(2,1)} %pad_maximum_fusion), calls=%async_computation.2 | async-start | bytes 2064384 | tf_op jit(solution)/shard_map/all_to_all | solution.py:588
  154.4 19.7 %collective-permute-start.11 = (bf16[512,768]{1,0:T(8,128)(2,1)S(1)}, bf16[512,768]{1,0:T(8,128)(2,1)S(1)}, u32[]{:S(2)}, u32[]{:S(2)}) collective-permute-start(bf16[512,768]{1,0:T(8,128)(2,1)S(1)} %normed_grad.2), channel_id=1, source_target_pairs={{0,1},{1,0},{2,3},{3,2},{4,5},{5,4},{6,7},{7,6},{8,9},{9,8},{10,11... | collective-permute-start | bytes 2359304 | tf_op jit(solution)/shard_map/ppermute | solution.py:598
  161.7 12.9 %copy-start.7 = (bf16[512,768]{1,0:T(8,128)(2,1)S(1)}, bf16[512,768]{1,0:T(8,128)(2,1)}, u32[]{:S(2)}) copy-start(bf16[512,768]{1,0:T(8,128)(2,1)} %own_ref.2) | copy-start | bytes 2359300
  177.9 5.2 %copy-start.5 = (bf16[6,8,2,128]{3,1,2,0:T(8,128)(2,1)S(1)}, bf16[6,8,2,128]{3,1,2,0:T(8,128)(2,1)}, u32[]{:S(2)}) copy-start(bf16[6,8,2,128]{3,1,2,0:T(8,128)(2,1)} %copy-done.4) | copy-start | bytes 73732
  177.9 5.2 %copy-start.9 = (bf16[48,128]{1,0:T(8,128)(2,1)S(1)}, bf16[48,128]{1,0:T(8,128)(2,1)}, u32[]{:S(2)}) copy-start(bf16[48,128]{1,0:T(8,128)(2,1)} %copy-done.8) | copy-start | bytes 36868
  177.9 11.3 %copy-start.15 = (bf16[48]{0:T(256)(128)(2,1)S(1)}, bf16[48]{0:T(256)(128)(2,1)}, u32[]{:S(2)}) copy-start(bf16[48]{0:T(256)(128)(2,1)} %param.18) | copy-start | bytes 292
  184.9 4.2 %collective-permute-start.12 = (f32[56,256]{1,0:T(8,128)S(1)}, f32[56,256]{1,0:T(8,128)S(1)}, u32[]{:S(2)}, u32[]{:S(2)}) collective-permute-start(f32[56,256]{1,0:T(8,128)S(1)} %pad.29), channel_id=1, source_target_pairs={{0,1},{1,0},{2,3},{3,2},{4,5},{5,4},{6,7},{7,6},{8,9},{9,8},{10,11... | collective-permute-start | bytes 172040 | tf_op jit(solution)/shard_map/ppermute | solution.py:598
  (1 other events, 0.7 us)

commit v5 on v4

--- a/solution.py
+++ b/solution.py
@@ -13,6 +13,7 @@
 LANES = 128
 TOKEN_BLOCK = 256
 VMEM_BASE = 16
+ROW_TILE = 64
 epsilon = 1e-05
 f32 = jnp.float32
 bf16 = jnp.bfloat16
@@ -41,6 +42,17 @@
     high = a.astype(bf16)
     rest = (a - high.astype(f32)).astype(bf16)
     return dot_nn(high, b) + dot_nn(rest, b)
+
+
+def two_parts(values):
+    high = values.astype(bf16)
+    rest = (values - high.astype(f32)).astype(bf16)
+    return jnp.concatenate([high, rest], axis=1)
+
+
+def spread_matrix(shape, size):
+    rows = lax.rem(lax.broadcasted_iota(jnp.int32, shape, 0), LANES)
+    return (rows == lax.broadcasted_iota(jnp.int32, shape, 1) // size).astype(bf16)
 
 
 def sigmoid(v):
@@ -89,6 +101,8 @@
     carry_ref,
     scarry_ref,
     xw_ref,
+    channels_ref,
+    columns_ref,
 ):
     width = mixed_ref.shape[1]
     pairs = width // LANES
@@ -100,6 +114,8 @@
     def _():
         for ref in (state_ref, carry_ref, scarry_ref):
             ref[...] = jnp.zeros_like(ref)
+        channels_ref[...] = spread_matrix(channels_ref.shape, HEAD_DIM)
+        columns_ref[...] = spread_matrix(columns_ref.shape, CHUNK)
 
     rows = lax.broadcasted_iota(jnp.int32, (CHUNK, CHUNK), 0)
     cols = lax.broadcasted_iota(jnp.int32, (CHUNK, CHUNK), 1)
@@ -122,11 +138,17 @@
     scores = jnp.where(same, dot_nt(c_rows, b_rows), 0.0)
     step = softplus(step_ref[...] + bias) * live
     decay = dot_exact(summing, step * rate)
+    decay_parts = two_parts(decay)
+    decay = decay_parts[:, :LANES].astype(f32) + decay_parts[:, LANES:].astype(f32)
+    decay_wide = dot_nn(decay_parts, columns_ref[...])
     decay_t = decay.T
     last = decay[CHUNK - 1 :, :]
     entry_scale = jnp.exp(decay) * aux[:, 8:9]
     end_scale = jnp.exp(last - decay) * aux[:, 9:10]
     keep = jnp.exp(last) * aux[:1, 10:11]
+    step_wide = dot_nn(two_parts(step), channels_ref[...])
+    entry_wide = dot_nn(two_parts(entry_scale), channels_ref[...])
+    end_wide = dot_nn(two_parts(end_scale), channels_ref[...])
     state = state_ref[...]
     state_low = state.astype(bf16)
     entry_ref[...] = state_low[None]
@@ -140,12 +162,12 @@
         u = conv_rows(window, tapi_ref[:, lanes].astype(f32), aux)
         u_ref[:, lanes] = u.astype(bf16)
         x = u * sigmoid(u)
-        scaled = x * halves(lane_low, step, head)
+        scaled = x * step_wide[:, lanes]
         mixing = jnp.concatenate(
             [
                 (
                     scores
-                    * jnp.exp(jnp.minimum(decay[:, h : h + 1] - decay_t[h : h + 1, :], 0.0))
+                    * jnp.exp(jnp.minimum(decay_wide[:, h * CHUNK : (h + 1) * CHUNK] - decay_t[h : h + 1, :], 0.0))
                 ).astype(bf16)
                 for h in (head, head + 1)
             ],
@@ -155,10 +177,10 @@
             [jnp.where(lane_low, scaled, 0.0), jnp.where(lane_low, 0.0, scaled)], axis=0
         ).astype(bf16)
         inside = dot_nn(mixing, stacked)
-        xw_ref[:, lanes] = (scaled * halves(lane_low, end_scale, head)).astype(bf16)
+        xw_ref[:, lanes] = (scaled * end_wide[:, lanes]).astype(bf16)
         mixed = (
             inside
-            + past[:, lanes] * halves(lane_low, entry_scale, head)
+            + past[:, lanes] * entry_wide[:, lanes]
             + halves(lane_low[:1], skips, head) * x
         ) * live
         mixed_ref[:, lanes] = mixed.astype(bf16)
@@ -209,6 +231,8 @@
     row_ref,
     proda_ref,
     prodb_ref,
+    channels_ref,
+    columns_ref,
 ):
     width = u_ref.shape[1]
     chunks = pl.num_programs(0)
@@ -223,6 +247,8 @@
     @pl.when(pl.program_id(0) == 0)
     def _():
         copy.start()
+        channels_ref[...] = spread_matrix(channels_ref.shape, HEAD_DIM)
+        columns_ref[...] = spread_matrix(columns_ref.shape, CHUNK)
         for ref in (state_ref, ahead_ref, sahead_ref, row_ref, wide_ref, shared_ref):
             ref[...] = jnp.zeros_like(ref)
 
@@ -254,11 +280,17 @@
     pre = praw_ref[...] + bias
     step = softplus(pre) * live
     decay = dot_exact(summing, step * rate)
+    decay_parts = two_parts(decay)
+    decay = decay_parts[:, :LANES].astype(f32) + decay_parts[:, LANES:].astype(f32)
+    decay_wide = dot_nn(decay_parts, columns_ref[...])
     decay_t = decay.T
     last = decay[CHUNK - 1 :, :]
     entry_scale = jnp.exp(decay) * aux[:, 8:9]
     end_scale = jnp.exp(last - decay) * aux[:, 9:10]
     keep = jnp.exp(last) * aux[:1, 10:11]
+    step_wide = dot_nn(two_parts(step), channels_ref[...])
+    entry_wide = dot_nn(two_parts(entry_scale), channels_ref[...])
+    end_wide = dot_nn(two_parts(end_scale), channels_ref[...])
     entry = entry_ref[0]
     dstate = state_ref[...]
     dstate_low = dstate.astype(bf16)
@@ -275,7 +307,7 @@
         u = u_ref[:, lanes].astype(f32)
         u_sig = sigmoid(u)
         x = u * u_sig
-        step_c = halves(lane_low, step, head)
+        step_c = step_wide[:, lanes]
         scaled = x * step_c
         stacked = jnp.concatenate(
             [jnp.where(lane_low, scaled, 0.0), jnp.where(lane_low, 0.0, scaled)], axis=0
@@ -283,7 +315,7 @@
         dmix = dot_nt(stacked, g_low)
         mixing = []
         for k, h in enumerate((head, head + 1)):
-            decays = jnp.exp(jnp.minimum(decay_t[h : h + 1, :] - decay[:, h : h + 1], 0.0))
+            decays = jnp.exp(jnp.minimum(decay_t[h : h + 1, :] - decay_wide[:, h * CHUNK : (h + 1) * CHUNK], 0.0))
             dmix_h = dmix[k * CHUNK : (k + 1) * CHUNK, :]
             score_grad = score_grad + dmix_h * decays
             mixing_h = scores * decays
@@ -294,8 +326,8 @@
         g_stacked = jnp.concatenate(
             [jnp.where(lane_low, g, 0.0), jnp.where(lane_low, 0.0, g)], axis=0
         ).astype(bf16)
-        end_c = halves(lane_low, end_scale, head)
-        entry_c = halves(lane_low, entry_scale, head)
+        end_c = end_wide[:, lanes]
+        entry_c = entry_wide[:, lanes]
         keep_c = halves(lane_low[:1], keep, head)
         from_state = end_c * bds[:, lanes]
         dscaled = dot_nn(jnp.concatenate(mixing, axis=1), g_stacked) + from_state
@@ -470,9 +502,11 @@
             pltpu.VMEM((8, width), f32),
             pltpu.VMEM((8, shared_size), f32),
             pltpu.VMEM((CHUNK, width), bf16),
+            pltpu.VMEM((2 * LANES, width), bf16),
+            pltpu.VMEM((2 * LANES, width // HEAD_DIM * CHUNK), bf16),
         ],
         name="scan_forward",
-        cost_estimate=cost(18),
+        cost_estimate=cost(3),
         compiler_params=vmem_limit(length),
     )(proj, praw, tapi, taps, heads, aux, segr)
 
@@ -538,6 +572,8 @@
                 pltpu.VMEM((LANES, CHUNK), f32),
                 pltpu.VMEM((CHUNK, width), f32),
                 pltpu.VMEM((CHUNK, width), f32),
+                pltpu.VMEM((2 * LANES, width), bf16),
+                pltpu.VMEM((2 * LANES, width // HEAD_DIM * CHUNK), bf16),
             ],
         ),
         out_shape=(
@@ -665,9 +701,10 @@
     step_ref,
     normed_ref,
     turned_ref,
-    weights_ref,
+    whole_ref,
     taps_ref,
     scale_ref,
+    weights_ref,
     sem_ref,
     *,
     own_blocks,
@@ -675,10 +712,16 @@
 ):
     step = pl.program_id(0)
     model_dim, columns = weights_ref.shape
+    store = pltpu.make_async_copy(weights_ref, whole_ref, sem_ref.at[table_ref.shape[0]])
+
+    @pl.when(step == pl.num_programs(0) - 1)
+    def _():
+        store.wait()
 
     @pl.when(step == 0)
     def _():
         place_blocks(table_ref, low_ref, high_ref, weights_ref, sem_ref)
+        store.start()
         extra = weights_ref[:, columns - LANES :].astype(f32).T
         scale_ref[...] = jnp.broadcast_to(extra[heads : heads + 1, :], scale_ref.shape)
         taps = extra[heads + 1 : heads + 5, :]
@@ -725,11 +768,14 @@
                 pl.BlockSpec((TOKEN_BLOCK, LANES), lambda i, s, t: (i, 0)),
                 pl.BlockSpec((TOKEN_BLOCK, model_dim), lambda i, s, t: (i, 0)),
                 pl.BlockSpec((model_dim, TOKEN_BLOCK), lambda i, s, t: (0, i)),
-                pl.BlockSpec((model_dim, columns), lambda i, s, t: (0, 0)),
+                pl.BlockSpec(memory_space=pl.ANY),
                 pl.BlockSpec((8, spread.shape[1]), lambda i, s, t: (0, 0)),
                 pl.BlockSpec((8, model_dim), lambda i, s, t: (0, 0)),
             ],
-            scratch_shapes=[pltpu.SemaphoreType.DMA((table.shape[0],))],
+            scratch_shapes=[
+                pltpu.VMEM((model_dim, columns), bf16),
+                pltpu.SemaphoreType.DMA((table.shape[0] + 1,)),
+            ],
         ),
         out_shape=(
             stored((length, columns - LANES), bf16),
@@ -741,7 +787,7 @@
             sds((8, model_dim), f32),
         ),
         name="norm_project",
-        cost_estimate=cost(9),
+        cost_estimate=cost(2),
         compiler_params=vmem_limit(length),
     )(starts, table, own, other, spread, low, high)
 
@@ -767,6 +813,7 @@
     nog_ref,
     turned_ref,
     sums_ref,
+    whole_ref,
     weights_ref,
     sem_ref,
     *,
@@ -774,10 +821,16 @@
 ):
     step = pl.program_id(0)
     width = mixed_ref.shape[1]
+    store = pltpu.make_async_copy(weights_ref, whole_ref, sem_ref.at[table_ref.shape[0]])
 
     @pl.when(step == 0)
     def _():
         place_blocks(table_ref, low_ref, high_ref, weights_ref, sem_ref)
+        store.start()
+
+    @pl.when(step == pl.num_programs(0) - 1)
+    def _():
+        store.wait()
 
     mine = (step >= starts_ref[0]) & (step < starts_ref[0] + own_blocks)
     tokens = jnp.where(mine, own_ref[...].astype(f32), other_ref[...].astype(f32)).astype(bf16)
@@ -827,9 +880,12 @@
                 pl.BlockSpec((TOKEN_BLOCK, width), lambda i, s, t: (i, 0)),
                 pl.BlockSpec((model_dim, TOKEN_BLOCK), lambda i, s, t: (0, i)),
                 pl.BlockSpec((8, TOKEN_BLOCK), lambda i, s, t: (0, i)),
-                pl.BlockSpec((model_dim, 2 * width), lambda i, s, t: (0, 0)),
-            ],
-            scratch_shapes=[pltpu.SemaphoreType.DMA((table.shape[0],))],
+                pl.BlockSpec(memory_space=pl.ANY),
+            ],
+            scratch_shapes=[
+                pltpu.VMEM((model_dim, 2 * width), bf16),
+                pltpu.SemaphoreType.DMA((table.shape[0] + 1,)),
+            ],
         ),
         out_shape=(
             sds((length, width), bf16),
@@ -899,25 +955,34 @@
 
     inv, mean = token_scales(sums_ref[...] + more_ref[...], full_inner)
     gain = gain_ref[...].astype(f32)
-    here = pl.ds(pl.multiple_of(step * TOKEN_BLOCK, TOKEN_BLOCK), TOKEN_BLOCK)
-    live = aux_ref[:, 7:8]
+    start = pl.multiple_of(step * TOKEN_BLOCK, TOKEN_BLOCK)
+    sums = {}
+    for top in range(0, TOKEN_BLOCK, ROW_TILE):
+        part = slice(top, top + ROW_TILE)
+        here = pl.ds(start + top, ROW_TILE)
+        live = aux_ref[part, 7:8]
+        inv_part = inv[part]
+        mean_part = mean[part]
+        for at in range(0, width, LANES):
+            lanes = slice(at, at + LANES)
+            gate = gate_ref[part, lanes].astype(f32)
+            gate_sig = sigmoid(gate)
+            gate_silu = gate * gate_sig
+            mixed = mixed_ref[part, lanes].astype(f32)
+            unit = mixed * gate_silu * inv_part
+            nog = nog_ref[part, lanes].astype(f32)
+            grad = inv_part * (nog * gain[:, lanes] - unit * mean_part)
+            dgate = (grad * mixed * silu_slope(gate, gate_sig)).astype(bf16)
+            dgate_ref[part, lanes] = dgate
+            both_ref[here, lanes] = dgate
+            grad_ref[part, lanes] = (grad * gate_silu * live).astype(bf16)
+            normed_out = (unit * gain[:, lanes]).astype(bf16)
+            out_ref[part, lanes] = normed_out
+            both_ref[here, slice(width + at, width + at + LANES)] = normed_out
+            row = jnp.sum((nog * unit).reshape(-1, 8, LANES), axis=0)
+            sums[at] = row if top == 0 else sums[at] + row
     for at in range(0, width, LANES):
-        lanes = slice(at, at + LANES)
-        gate = gate_ref[:, lanes].astype(f32)
-        gate_sig = sigmoid(gate)
-        gate_silu = gate * gate_sig
-        mixed = mixed_ref[:, lanes].astype(f32)
-        unit = mixed * gate_silu * inv
-        nog = nog_ref[:, lanes].astype(f32)
-        grad = inv * (nog * gain[:, lanes] - unit * mean)
-        dgate = (grad * mixed * silu_slope(gate, gate_sig)).astype(bf16)
-        dgate_ref[:, lanes] = dgate
-        both_ref[here, lanes] = dgate
-        grad_ref[:, lanes] = (grad * gate_silu * live).astype(bf16)
-        normed_out = (unit * gain[:, lanes]).astype(bf16)
-        out_ref[:, lanes] = normed_out
-        both_ref[here, slice(width + at, width + at + LANES)] = normed_out
-        row_ref[pl.ds(step * 8, 8), lanes] = jnp.sum((nog * unit).reshape(-1, 8, LANES), axis=0)
+        row_ref[pl.ds(step * 8, 8), slice(at, at + LANES)] = sums[at]
 
     @pl.when(step == pl.num_programs(0) - 1)
     def _():
@@ -1148,8 +1213,12 @@
     tapi = pad_to(conv_inner, 1, width)
     gain = pad_to(gate_gain[None], 1, width)
 
+    later_all = jnp.broadcast_to(later[None], (chips,) + later.shape)
+    later_all = later_all.reshape(chips * rows, 2 * width)
     low = packed
     for number, stage in enumerate(stages):
+        if number == len(stages) - 1:
+            low, later_all = lax.optimization_barrier((low, later_all))
         got = lax.ppermute(low, "dp", stage)
         if number == 0:
             got, aux, segr = lax.optimization_barrier((got, aux, segr))
@@ -1158,13 +1227,11 @@
                 (got, heads_block, tapi, spread, table, core_table)
             )
         if number == len(stages) - 1:
-            later_all = jnp.broadcast_to(later[None], (chips,) + later.shape)
-            later_all = later_all.reshape(chips * rows, 2 * width)
-            got, later_all, gain = lax.optimization_barrier((got, later_all, gain))
+            got, gain = lax.optimization_barrier((got, gain))
         low = jnp.concatenate([low, got], axis=0)
-    low, later_all, hidden_other = lax.optimization_barrier((low, later_all, hidden_other))
+    later_low = exchange(later_all, groups)
+    low, hidden_other = lax.optimization_barrier((low, hidden_other))
     high = lax.ppermute(low, "dp", core)
-    later_low = exchange(later_all, groups)
     grad_own, grad_other = both_halves(after(out_grad, hidden_other))
 
     proj, praw, normed, normed_t, weights, taps, norm_scale = run_project(

time: 192 us -> 182 us (0.948)
  Pallas kernels: 95.5 us -> 81 us
  starting transfers between devices: 30.7 us -> 33.1 us
    pallas_call x1, Pallas kernels: 35.4 us -> 28.1 us  [run_backward(): pl.pallas_call(backward_kernel, grid_spec=pltpu.PrefetchScalarGridSpec(nu...]
    pallas_call x1, Pallas kernels: 16.9 us -> 11.4 us  [run_forward(): pl.pallas_call(forward_kernel, grid=(chunks,), in_specs=[chunk_spec(proj....]
    all_to_all x3, starting transfers between devices: 15.9 us -> 19.1 us  [exchange(): lax.all_to_all(blocks, 'dp', 0, 0, axis_index_groups=groups, tiled=True)]
    unnamed x40 -> x36, local copies, waits for them, and re-layouts: 4.28 us -> 3.58 us
  transfers between devices with their start and end apart: 16 -> 16, of which waited for: 9 -> 9; matrix products, arithmetic and copies ran while one was open for 5% -> 6% of each run, Pallas kernels for 39% -> 33%
where the time goes in v5:
time: 182 us; the launch traced here: 181 us
  Pallas kernels  81 us (45%)
  waiting for transfers between devices  39.3 us (22%)
  starting transfers between devices  33.1 us (18%)
  other arithmetic  15 us (8%)
  local copies, waits for them, and re-layouts  11.4 us (6%)
    pallas_call x1, Pallas kernels, run_backward(): pl.pallas_call(backward_kernel, grid_spec=pltpu.PrefetchScalarGridSpec(nu...  28.1 us
    all_to_all x3, starting transfers between devices, exchange(): lax.all_to_all(blocks, 'dp', 0, 0, axis_index_groups=groups, tiled=True)  19.1 us
    ppermute x6, waiting for transfers between devices, swap(): return lax.ppermute(values, 'tensor', [(0, 1), (1, 0)])  18.2 us
    ppermute x3, waiting for transfers between devices, body(): got = lax.ppermute(low, 'dp', stage)  14.8 us
    pallas_call x1, Pallas kernels, run_forward(): pl.pallas_call(forward_kernel, grid=(chunks,), in_specs=[chunk_spec(proj....  11.4 us
    pallas_call x1, Pallas kernels, run_gated(): pl.pallas_call(partial(gated_kernel, full_inner=float(full_inner)), grid_...  10.7 us
    pallas_call x1, Pallas kernels, run_out_grad(): pl.pallas_call(partial(out_grad_kernel, own_blocks=own_blocks), grid_spec...  10.1 us
    pallas_call x2, Pallas kernels, run_norm_grad(): pl.pallas_call(norm_grad_kernel, grid_spec=pltpu.PrefetchScalarGridSpec(n...  8.48 us
  transfers between devices with their start and end apart: 16, of which 9 were waited for; matrix products, arithmetic and copies ran while one was open for 6% of the time, Pallas kernels for 33%

profile of v5, /device:TPU:0, one launch (start us, length us, event | category | flops | bytes accessed | tf_op | source)
XLA Modules:
  0.0 180.9 jit_solution(12792641839426928663)
XLA Ops:
  3.7 1.3 fusion.32
  5.1 4.1 %collective-permute-start = (bf16[48,1152]{1,0:T(8,128)(2,1)S(1)}, bf16[48,1152]{1,0:T(8,128)(2,1)S(1)}, u32[]{:S(2)}, u32[]{:S(2)}) collective-permute-start(bf16[48,1152]{1,0:T(8,128)(2,1)S(1)} %pad_maximum_fusion.6), channel_id=1, source_target_pairs={{0,16},{2,18},{4,20},{6,22},{8,24},{10,26},{12,28},{14,30},{16,0},... | collective-permute-start | bytes 331784 | tf_op jit(solution)/shard_map/ppermute | solution.py:1222
  9.3 1.5 collective-permute-start.3
  12.4 2.3 %collective-permute-done = bf16[48,1152]{1,0:T(8,128)(2,1)S(1)} collective-permute-done((bf16[48,1152]{1,0:T(8,128)(2,1)S(1)}, bf16[48,1152]{1,0:T(8,128)(2,1)S(1)}, u32[]{:S(2)}, u32[]{:S(2)}) %collective-permute-start) | collective-permute-done | bytes 110624 | tf_op jit(solution)/shard_map/ppermute | solution.py:1222
  15.5 5.2 %collective-permute-done.1 = bf16[96,1152]{1,0:T(8,128)(2,1)S(1)} collective-permute-done((bf16[96,1152]{1,0:T(8,128)(2,1)S(1)}, bf16[96,1152]{1,0:T(8,128)(2,1)S(1)}, u32[]{:S(2)}, u32[]{:S(2)}) %collective-permute-start.1) | collective-permute-done | bytes 221216 | tf_op jit(solution)/shard_map/ppermute | solution.py:1222
  21.9 1.5 collective-permute-start.2
  23.4 4.8 %all-to-all-start = ((bf16[8,48,1536]{2,1,0:T(8,128)(2,1)}), bf16[8,48,1536]{2,1,0:T(8,128)(2,1)S(1)}, u32[]{:S(2)}, u32[]{:S(2)}) async-start(bf16[8,48,1536]{2,1,0:T(8,128)(2,1)} %bitcast.15), calls=%async_computation | async-start | bytes 2359296 | tf_op jit(solution)/shard_map/all_to_all | solution.py:624
  28.2 7.4 %collective-permute-done.2 = bf16[192,1152]{1,0:T(8,128)(2,1)} collective-permute-done((bf16[192,1152]{1,0:T(8,128)(2,1)S(1)}, bf16[192,1152]{1,0:T(8,128)(2,1)}, u32[]{:S(2)}, u32[]{:S(2)}) %collective-permute-start.2) | collective-permute-done | bytes 442400 | tf_op jit(solution)/shard_map/ppermute | solution.py:1222
  35.6 2.0 %pad_maximum_fusion.1.low_ref = bf16[384,1152]{1,0:T(8,128)(2,1)} fusion(bf16[192,1152]{1,0:T(8,128)(2,1)} %collective-permute-done.2, bf16[192,1152]{1,0:T(8,128)(2,1)S(1)} %pad_maximum_fusion.2), kind=kLoop, calls=%fused_computation.17 | loop fusion | flops 1769472 | bytes 1769472 | tf_op jit(solution)/shard_map/concatenate | solution.py:1231
  37.6 1.5 collective-permute-start.5
  40.4 8.4 %norm_project.1 = (bf16[1024,1024]{1,0:T(8,128)(2,1)}, f32[1024,128]{1,0:T(8,128)}, bf16[1024,768]{1,0:T(8,128)(2,1)}, bf16[768,1024]{1,0:T(8,128)(2,1)}, bf16[7...) custom-call(s32[2]{0:T(128)S(1)} %pad_add_fusion.starts_ref, s32[16]{0:T(128)S(1)} %get-tuple-element.80.table_ref, ...), custom_call_target="tpu_custom_call" | custom-call | flops 2200000000 | tf_op jit(solution)/shard_map/norm_project/pallas_call | solution.py:750
  48.9 11.4 %scan_forward.1 = (bf16[1024,768]{1,0:T(8,128)(2,1)}, bf16[1024,768]{1,0:T(8,128)(2,1)}, f32[1024,256]{1,0:T(8,128)}, bf16[8,128,768]{2,1,0:T(8,128)(2,1)}) custom-call(bf16[1024,1024]{1,0:T(8,128)(2,1)} %get-tuple-element.83.proj_ref, f32[1024,128]{1,0:T(8,128)} %get-tuple-element.84.step_ref.praw_ref, bf16[4,768]{1,0:T(4,128)(2,1)S(1)} %copy-done, ...), custom_call_target="tpu_custom_call" | custom-call | flops 3300000000 | tf_op jit(solution)/shard_map/scan_forward/pallas_call | solution.py:476
  60.5 2.7 %collective-permute-done.6.high_ref = bf16[384,1536]{1,0:T(8,128)(2,1)S(1)} collective-permute-done((bf16[384,1536]{1,0:T(8,128)(2,1)S(1)}, bf16[384,1536]{1,0:T(8,128)(2,1)S(1)}, u32[]{:S(2)}, u32[]{:S(2)}) %collective-permute-start.6) | collective-permute-done | bytes 1179680 | tf_op jit(solution)/shard_map/ppermute | solution.py:1244
  63.2 10.1 %out_grad.1 = (bf16[1024,768]{1,0:T(8,128)(2,1)S(1)}, bf16[1024,768]{1,0:T(8,128)(2,1)S(1)}, bf16[768,1024]{1,0:T(8,128)(2,1)S(1)}, f32[8,1024]{1,0:T(8,128)S(1)}, bf16[768,1536]{1,0:T(8,128)(2,1)}) custom-call(s32[2]{0:T(128)S(1)} %pad_add_fusion.starts_ref, s32[16]{0:T(128)S(1)} %get-tuple-element.73.table_ref, bf16[512,768]{1,0:T(8,128)(2,1)} %own_ref.2, ...), custom_call_target="tpu_custom_call" | custom-call | flops 9900000256 | tf_op jit(solution)/shard_map/out_grad/pallas_call | solution.py:860
  73.4 1.6 collective-permute-start.7
  74.9 2.4 %collective-permute-done.7.more_ref = f32[8,1024]{1,0:T(8,128)S(1)} collective-permute-done((f32[8,1024]{1,0:T(8,128)S(1)}, f32[8,1024]{1,0:T(8,128)S(1)}, u32[]{:S(2)}, u32[]{:S(2)}) %collective-permute-start.7) | collective-permute-done | bytes 32800 | tf_op jit(solution)/shard_map/ppermute | solution.py:634
  77.3 10.7 %gated_grad.1 = (bf16[1024,768]{1,0:T(8,128)(2,1)S(1)}, bf16[1024,768]{1,0:T(8,128)(2,1)}, bf16[1024,768]{1,0:T(8,128)(2,1)}, f32[32,768]{1,0:T(8,128)S(1)}, bf1...) custom-call(s32[16]{0:T(128)S(1)} %get-tuple-element.73.table_ref, ...), custom_call_target="tpu_custom_call" | custom-call | flops 9900000256 | tf_op jit(solution)/shard_map/gated_grad/pallas_call | solution.py:1006
  88.3 3.5 %out_project.1 = (bf16[512,768]{1,0:T(8,128)(2,1)S(1)}, bf16[512,768]{1,0:T(8,128)(2,1)S(1)}) custom-call(s32[1]{0:T(128)} %bitcast.starts_ref, bf16[1024,768]{1,0:T(8,128)(2,1)S(1)} %get-tuple-element.101.rows_ref, bf16[768,1536]{1,0:T(8,128)(2,1)} %get-tuple-element.102.weights_ref.gates_ref), custom_call_target="tpu_custom_call" | custom-call | flops 4400000000 | tf_op jit(solution)/shard_map/out_project/pallas_call | solution.py:1073
  91.9 1.3 add_convert_fusion
  93.2 8.3 %all-to-all-start.1 = ((bf16[8,48,1536]{2,1,0:T(8,128)(2,1)}), bf16[8,48,1536]{2,1,0:T(8,128)(2,1)}, u32[]{:S(2)}, u32[]{:S(2)}) async-start(bf16[8,48,1536]{2,1,0:T(8,128)(2,1)} %bitcast.57), calls=%async_computation.1 | async-start | bytes 2359296 | tf_op jit(solution)/shard_map/all_to_all | solution.py:624
  101.5 1.5 collective-permute-start.9
  103.0 28.1 %scan_backward.1 = (bf16[1024,1152]{1,0:T(8,128)(2,1)}, bf16[392,1152]{1,0:T(8,128)(2,1)}, bf16[392,1152]{1,0:T(8,128)(2,1)}) custom-call(s32[16]{0:T(128)S(1)} %get-tuple-element.73.table_ref, bf16[1024,1024]{1,0:T(8,128)(2,1)} %get-tuple-element.83.proj_ref, f32[1024,128]{1,0:T(8,128)} %get-tuple-element.84.step_ref.praw_ref, ...), custom_call_target="tpu_custom_call" | custom-call | flops 39600001024 | tf_op jit(solution)/shard_map/scan_backward/pallas_call | solution.py:534
  131.2 4.3 %normed_grad.2 = bf16[512,768]{1,0:T(8,128)(2,1)S(1)} custom-call(s32[1]{0:T(128)} %bitcast.starts_ref, bf16[1024,768]{1,0:T(8,128)(2,1)} %get-tuple-element.116.dgate_ref, bf16[1024,1152]{1,0:T(8,128)(2,1)} %get-tuple-element.122.dproj_ref, bf16[768,1536]{1,0:T(8,128)(2,1)} %get-tuple-element.102.weights_ref.gates_ref, ...), custom_call_target="tpu_custom_call" | custom-call | flops 5500000256 | tf_op jit(solution)/shard_map/normed_grad/pallas_call | solution.py:1108
  135.5 1.4 add_convert_fusion.1
  138.2 6.0 %all-to-all-start.2 = ((bf16[8,56,1152]{2,1,0:T(8,128)(2,1)}), bf16[8,56,1152]{2,1,0:T(8,128)(2,1)}, u32[]{:S(2)}, u32[]{:S(2)}) async-start(bf16[8,56,1152]{2,1,0:T(8,128)(2,1)} %pad_maximum_fusion), calls=%async_computation.2 | async-start | bytes 2064384 | tf_op jit(solution)/shard_map/all_to_all | solution.py:624
  144.7 1.5 convert_reduce_fusion
  146.9 4.2 %normed_grad.3 = f32[512,768]{1,0:T(8,128)S(1)} custom-call(s32[1]{0:T(128)} %bitcast.11.starts_ref, bf16[1024,768]{1,0:T(8,128)(2,1)} %get-tuple-element.116.dgate_ref, bf16[1024,1152]{1,0:T(8,128)(2,1)} %get-tuple-element.122.dproj_ref, bf16[768,1536]{1,0:T(8,128)(2,1)} %get-tuple-element.102.weights_ref.gates_ref, ...), custom_call_target="tpu_custom_call" | custom-call | flops 5500000256 | tf_op jit(solution)/shard_map/normed_grad/pallas_call | solution.py:1108
  151.1 12.7 %collective-permute-done.11 = bf16[512,768]{1,0:T(8,128)(2,1)S(1)} collective-permute-done((bf16[512,768]{1,0:T(8,128)(2,1)S(1)}, bf16[512,768]{1,0:T(8,128)(2,1)S(1)}, u32[]{:S(2)}, u32[]{:S(2)}) %collective-permute-start.11) | collective-permute-done | bytes 786464 | tf_op jit(solution)/shard_map/ppermute | solution.py:634
  164.4 3.6 %fusion.5 = (f32[512,768]{1,0:T(8,128)}, bf16[512,768]{1,0:T(8,128)(2,1)}) fusion(bf16[512,768]{1,0:T(8,128)(2,1)S(1)} %copy-done.2, bf16[512,768]{1,0:T(8,128)(2,1)} %own_ref.2, f32[512,768]{1,0:T(8,128)S(1)} %normed_grad.3, bf16[512,768]{1,0:T(8,128)(2,1)S(1)} %collective-permute-done.11, f32[512]{0:T(512)S(1)} %broadcast_multiply_fusion, ...), kind=kLoop, calls=%fused_computation.12 | loop fusion | flops 5898240 | bytes 7871488 | tf_op jit(solution)/shard_map/add | solution.py:1347
  168.0 2.4 %all-to-all-done.2 = bf16[8,56,1152]{2,1,0:T(8,128)(2,1)} async-done(((bf16[8,56,1152]{2,1,0:T(8,128)(2,1)}), bf16[8,56,1152]{2,1,0:T(8,128)(2,1)}, u32[]{:S(2)}, u32[]{:S(2)}) %all-to-all-start.2) | async-done | bytes 1032224 | tf_op jit(solution)/shard_map/all_to_all | solution.py:624
  170.3 1.4 convert_reduce_fusion.1
  175.9 3.1 %collective-permute-done.12 = f32[56,256]{1,0:T(8,128)S(1)} collective-permute-done((f32[56,256]{1,0:T(8,128)S(1)}, f32[56,256]{1,0:T(8,128)S(1)}, u32[]{:S(2)}, u32[]{:S(2)}) %collective-permute-start.12) | collective-permute-done | bytes 57376 | tf_op jit(solution)/shard_map/ppermute | solution.py:634
  (97 shorter events, 17.6 us)
Async XLA Ops:
  0.6 10.3 %copy-start.1 = (s32[1024]{0:T(1024)S(1)}, s32[1024]{0:T(1024)}, u32[]{:S(2)}) copy-start(s32[1024]{0:T(1024)} %param.17) | copy-start | bytes 12292
  3.7 17.0 %copy-start.4 = (bf16[6,8,2,128]{3,1,2,0:T(8,128)(2,1)}, bf16[6,8,2,128]{3,1,2,0:T(8,128)(2,1)S(1)}, u32[]{:S(2)}) copy-start(bf16[6,8,2,128]{3,1,2,0:T(8,128)(2,1)S(1)} %copy.47) | copy-start | bytes 73732
  5.1 15.6 %copy-start.6 = (bf16[48,128]{1,0:T(8,128)(2,1)}, bf16[48,128]{1,0:T(8,128)(2,1)S(1)}, u32[]{:S(2)}) copy-start(bf16[48,128]{1,0:T(8,128)(2,1)S(1)} %pad.25) | copy-start | bytes 36868
  5.1 9.6 %collective-permute-start = (bf16[48,1152]{1,0:T(8,128)(2,1)S(1)}, bf16[48,1152]{1,0:T(8,128)(2,1)S(1)}, u32[]{:S(2)}, u32[]{:S(2)}) collective-permute-start(bf16[48,1152]{1,0:T(8,128)(2,1)S(1)} %pad_maximum_fusion.6), channel_id=1, source_target_pairs={{0,16},{2,18},{4,20},{6,22},{8,24},{10,26},{12,28},{14,30},{16,0},... | collective-permute-start | bytes 331784 | tf_op jit(solution)/shard_map/ppermute | solution.py:1222
  9.3 28.4 %collective-permute-start.3 = (bf16[512,768]{1,0:T(8,128)(2,1)}, bf16[512,768]{1,0:T(8,128)(2,1)}, u32[]{:S(2)}, u32[]{:S(2)}) collective-permute-start(bf16[512,768]{1,0:T(8,128)(2,1)} %own_ref.1), channel_id=1, source_target_pairs={{0,1},{1,0},{2,3},{3,2},{4,5},{5,4},{6,7},{7,6},{8,9},{9,8},{10,11... | collective-permute-start | bytes 2359304 | tf_op jit(solution)/shard_map/ppermute | solution.py:634
  11.0 0.7 copy-start.10
  11.0 0.7 copy-start.11
  11.0 0.7 copy-start.12
  11.0 0.7 copy-start.14
  11.1 4.4 %copy-start.8 = (bf16[768,48]{0,1:T(8,128)(2,1)S(1)}, bf16[768,48]{0,1:T(8,128)(2,1)}, u32[]{:S(2)}) copy-start(bf16[768,48]{0,1:T(8,128)(2,1)} %param.28) | copy-start | bytes 221188
  14.7 6.0 %collective-permute-start.1 = (bf16[96,1152]{1,0:T(8,128)(2,1)S(1)}, bf16[96,1152]{1,0:T(8,128)(2,1)S(1)}, u32[]{:S(2)}, u32[]{:S(2)}) collective-permute-start(bf16[96,1152]{1,0:T(8,128)(2,1)S(1)} %pad_maximum_fusion.4), channel_id=1, source_target_pairs={{0,8},{2,6},{4,12},{6,2},{8,0},{10,14},{12,4},{14,10},{16,24},{18,... | collective-permute-start | bytes 663560 | tf_op jit(solution)/shard_map/ppermute | solution.py:1222
  20.7 7.5 %copy-start.9 = (bf16[768]{0:T(1024)(128)(2,1)S(1)}, bf16[768]{0:T(1024)(128)(2,1)}, u32[]{:S(2)}) copy-start(bf16[768]{0:T(1024)(128)(2,1)} %param.27) | copy-start | bytes 4612
  21.9 13.7 %collective-permute-start.2 = (bf16[192,1152]{1,0:T(8,128)(2,1)S(1)}, bf16[192,1152]{1,0:T(8,128)(2,1)}, u32[]{:S(2)}, u32[]{:S(2)}) collective-permute-start(bf16[192,1152]{1,0:T(8,128)(2,1)S(1)} %pad_maximum_fusion.2), channel_id=1, source_target_pairs={{0,4},{2,10},{4,0},{6,14},{8,12},{10,2},{12,8},{14,6},{16,20},{18,... | collective-permute-start | bytes 1327112 | tf_op jit(solution)/shard_map/ppermute | solution.py:1222
  23.4 36.9 %all-to-all-start = ((bf16[8,48,1536]{2,1,0:T(8,128)(2,1)}), bf16[8,48,1536]{2,1,0:T(8,128)(2,1)S(1)}, u32[]{:S(2)}, u32[]{:S(2)}) async-start(bf16[8,48,1536]{2,1,0:T(8,128)(2,1)} %bitcast.15), calls=%async_computation | async-start | bytes 2359296 | tf_op jit(solution)/shard_map/all_to_all | solution.py:624
  37.6 2.8 %collective-permute-start.4 = (bf16[384,1152]{1,0:T(8,128)(2,1)}, bf16[384,1152]{1,0:T(8,128)(2,1)}, u32[]{:S(2)}, u32[]{:S(2)}) collective-permute-start(bf16[384,1152]{1,0:T(8,128)(2,1)} %pad_maximum_fusion.1.low_ref), channel_id=1, source_target_pairs={{0,2},{2,0},{4,6},{6,4},{8,10},{10,8},{12,14},{14,12},{16,18},{18,... | collective-permute-start | bytes 2654216 | tf_op jit(solution)/shard_map/ppermute | solution.py:1234
  37.6 22.7 %collective-permute-start.5 = (bf16[512,768]{1,0:T(8,128)(2,1)}, bf16[512,768]{1,0:T(8,128)(2,1)}, u32[]{:S(2)}, u32[]{:S(2)}) collective-permute-start(bf16[512,768]{1,0:T(8,128)(2,1)} %own_ref.2), channel_id=1, source_target_pairs={{0,1},{1,0},{2,3},{3,2},{4,5},{5,4},{6,7},{7,6},{8,9},{9,8},{10,11... | collective-permute-start | bytes 2359304 | tf_op jit(solution)/shard_map/ppermute | solution.py:634
  39.2 9.6 %copy-start = (bf16[4,768]{1,0:T(4,128)(2,1)S(1)}, bf16[4,768]{1,0:T(4,128)(2,1)}, u32[]{:S(2)}) copy-start(bf16[4,768]{1,0:T(4,128)(2,1)} %tapi_ref.1) | copy-start | bytes 18436
  60.3 2.9 %collective-permute-start.6 = (bf16[384,1536]{1,0:T(8,128)(2,1)S(1)}, bf16[384,1536]{1,0:T(8,128)(2,1)S(1)}, u32[]{:S(2)}, u32[]{:S(2)}) collective-permute-start(bf16[384,1536]{1,0:T(8,128)(2,1)S(1)} %bitcast.54), channel_id=1, source_target_pairs={{0,2},{2,0},{4,6},{6,4},{8,10},{10,8},{12,14},{14,12},{16,18},{18,... | collective-permute-start | bytes 3538952 | tf_op jit(solution)/shard_map/ppermute | solution.py:1244
  73.4 4.0 %collective-permute-start.7 = (f32[8,1024]{1,0:T(8,128)S(1)}, f32[8,1024]{1,0:T(8,128)S(1)}, u32[]{:S(2)}, u32[]{:S(2)}) collective-permute-start(f32[8,1024]{1,0:T(8,128)S(1)} %get-tuple-element.98.sums_ref), channel_id=1, source_target_pairs={{0,1},{1,0},{2,3},{3,2},{4,5},{5,4},{6,7},{7,6},{8,9},{9,8},{10,11... | collective-permute-start | bytes 98312 | tf_op jit(solution)/shard_map/ppermute | solution.py:634
  77.3 10.7 %copy-start.2 = (bf16[512,768]{1,0:T(8,128)(2,1)S(1)}, bf16[512,768]{1,0:T(8,128)(2,1)}, u32[]{:S(2)}) copy-start(bf16[512,768]{1,0:T(8,128)(2,1)} %own_ref.1) | copy-start | bytes 2359300
  88.0 3.8 %collective-permute-start.8 = (bf16[384,1536]{1,0:T(8,128)(2,1)S(1)}, bf16[384,1536]{1,0:T(8,128)(2,1)S(1)}, u32[]{:S(2)}, u32[]{:S(2)}) collective-permute-start(bf16[384,1536]{1,0:T(8,128)(2,1)S(1)} %get-tuple-element.111), channel_id=1, source_target_pairs={{0,2},{2,0},{4,6},{6,4},{8,10},{10,8},{12,14},{14,12},{16,18},{18,... | collective-permute-start | bytes 3538952 | tf_op jit(solution)/shard_map/ppermute | solution.py:1256
  93.2 37.9 %all-to-all-start.1 = ((bf16[8,48,1536]{2,1,0:T(8,128)(2,1)}), bf16[8,48,1536]{2,1,0:T(8,128)(2,1)}, u32[]{:S(2)}, u32[]{:S(2)}) async-start(bf16[8,48,1536]{2,1,0:T(8,128)(2,1)} %bitcast.57), calls=%async_computation.1 | async-start | bytes 2359296 | tf_op jit(solution)/shard_map/all_to_all | solution.py:624
  101.5 29.6 %collective-permute-start.9 = (bf16[512,768]{1,0:T(8,128)(2,1)S(1)}, bf16[512,768]{1,0:T(8,128)(2,1)}, u32[]{:S(2)}, u32[]{:S(2)}) collective-permute-start(bf16[512,768]{1,0:T(8,128)(2,1)S(1)} %get-tuple-element.114), channel_id=1, source_target_pairs={{0,1},{1,0},{2,3},{3,2},{4,5},{5,4},{6,7},{7,6},{8,9},{9,8},{10,11... | collective-permute-start | bytes 2359304 | tf_op jit(solution)/shard_map/ppermute | solution.py:634
  131.1 4.4 %collective-permute-start.10 = (bf16[392,1152]{1,0:T(8,128)(2,1)}, bf16[392,1152]{1,0:T(8,128)(2,1)}, u32[]{:S(2)}, u32[]{:S(2)}) collective-permute-start(bf16[392,1152]{1,0:T(8,128)(2,1)} %get-tuple-element.118), channel_id=1, source_target_pairs={{0,2},{2,0},{4,6},{6,4},{8,10},{10,8},{12,14},{14,12},{16,18},{18,... | collective-permute-start | bytes 2709512 | tf_op jit(solution)/shard_map/ppermute | solution.py:1283
  131.2 4.3 %copy-start.3 = (bf16[392,1152]{1,0:T(8,128)(2,1)S(1)}, bf16[392,1152]{1,0:T(8,128)(2,1)}, u32[]{:S(2)}) copy-start(bf16[392,1152]{1,0:T(8,128)(2,1)} %get-tuple-element.117) | copy-start | bytes 2709508
  138.2 32.2 %all-to-all-start.2 = ((bf16[8,56,1152]{2,1,0:T(8,128)(2,1)}), bf16[8,56,1152]{2,1,0:T(8,128)(2,1)}, u32[]{:S(2)}, u32[]{:S(2)}) async-start(bf16[8,56,1152]{2,1,0:T(8,128)(2,1)} %pad_maximum_fusion), calls=%async_computation.2 | async-start | bytes 2064384 | tf_op jit(solution)/shard_map/all_to_all | solution.py:624
  144.2 19.6 %collective-permute-start.11 = (bf16[512,768]{1,0:T(8,128)(2,1)S(1)}, bf16[512,768]{1,0:T(8,128)(2,1)S(1)}, u32[]{:S(2)}, u32[]{:S(2)}) collective-permute-start(bf16[512,768]{1,0:T(8,128)(2,1)S(1)} %normed_grad.2), channel_id=1, source_target_pairs={{0,1},{1,0},{2,3},{3,2},{4,5},{5,4},{6,7},{7,6},{8,9},{9,8},{10,11... | collective-permute-start | bytes 2359304 | tf_op jit(solution)/shard_map/ppermute | solution.py:634
  168.0 4.9 %copy-start.5 = (bf16[6,8,2,128]{3,1,2,0:T(8,128)(2,1)S(1)}, bf16[6,8,2,128]{3,1,2,0:T(8,128)(2,1)}, u32[]{:S(2)}) copy-start(bf16[6,8,2,128]{3,1,2,0:T(8,128)(2,1)} %copy-done.4) | copy-start | bytes 73732
  168.0 4.9 %copy-start.7 = (bf16[48,128]{1,0:T(8,128)(2,1)S(1)}, bf16[48,128]{1,0:T(8,128)(2,1)}, u32[]{:S(2)}) copy-start(bf16[48,128]{1,0:T(8,128)(2,1)} %copy-done.6) | copy-start | bytes 36868
  168.0 11.0 %copy-start.13 = (bf16[48]{0:T(256)(128)(2,1)S(1)}, bf16[48]{0:T(256)(128)(2,1)}, u32[]{:S(2)}) copy-start(bf16[48]{0:T(256)(128)(2,1)} %param.18) | copy-start | bytes 292
  174.7 4.2 %collective-permute-start.12 = (f32[56,256]{1,0:T(8,128)S(1)}, f32[56,256]{1,0:T(8,128)S(1)}, u32[]{:S(2)}, u32[]{:S(2)}) collective-permute-start(f32[56,256]{1,0:T(8,128)S(1)} %pad.29), channel_id=1, source_target_pairs={{0,1},{1,0},{2,3},{3,2},{4,5},{5,4},{6,7},{7,6},{8,9},{9,8},{10,11... | collective-permute-start | bytes 172040 | tf_op jit(solution)/shard_map/ppermute | solution.py:634

commit v6 on v5

--- a/solution.py
+++ b/solution.py
@@ -65,6 +65,15 @@
 
 def halves(lane_low, values, head):
     return jnp.where(lane_low, values[:, head : head + 1], values[:, head + 1 : head + 2])
+
+
+def head_sides():
+    low = (lax.broadcasted_iota(jnp.int32, (CHUNK, LANES), 1) < HEAD_DIM).astype(f32)
+    return low.astype(bf16), (1.0 - low).astype(bf16)
+
+
+def by_head(values, sides):
+    return jnp.concatenate([values * sides[0], values * sides[1]], axis=0)
 
 
 def back_shift(window, offset):
@@ -122,6 +131,7 @@
     lower = rows >= cols
     summing = lower.astype(f32)
     lane_low = lax.broadcasted_iota(jnp.int32, (CHUNK, LANES), 1) < HEAD_DIM
+    sides = head_sides()
     bias = heads_ref[0:1, :]
     rate = -jnp.exp(heads_ref[1:2, :])
     skips = heads_ref[2:3, :]
@@ -173,9 +183,7 @@
             ],
             axis=1,
         )
-        stacked = jnp.concatenate(
-            [jnp.where(lane_low, scaled, 0.0), jnp.where(lane_low, 0.0, scaled)], axis=0
-        ).astype(bf16)
+        stacked = by_head(scaled.astype(bf16), sides)
         inside = dot_nn(mixing, stacked)
         xw_ref[:, lanes] = (scaled * end_wide[:, lanes]).astype(bf16)
         mixed = (
@@ -260,6 +268,7 @@
     last_row = (lax.broadcasted_iota(jnp.int32, (CHUNK, LANES), 0) == CHUNK - 1).astype(f32)
     lane_ids = lax.broadcasted_iota(jnp.int32, (CHUNK, LANES), 1)
     lane_low = lane_ids < HEAD_DIM
+    sides = head_sides()
     bias = heads_ref[0:1, :]
     rate = -jnp.exp(heads_ref[1:2, :])
     skips = heads_ref[2:3, :]
@@ -309,9 +318,7 @@
         x = u * u_sig
         step_c = step_wide[:, lanes]
         scaled = x * step_c
-        stacked = jnp.concatenate(
-            [jnp.where(lane_low, scaled, 0.0), jnp.where(lane_low, 0.0, scaled)], axis=0
-        ).astype(bf16)
+        stacked = by_head(scaled.astype(bf16), sides)
         dmix = dot_nt(stacked, g_low)
         mixing = []
         for k, h in enumerate((head, head + 1)):
@@ -323,9 +330,7 @@
             both = mixing_h * dmix_h
             col_part = jnp.where(lane_ids == h, jnp.sum(both, axis=1, keepdims=True), col_part)
             row_ref[h : h + 1, :] = jnp.sum(both, axis=0, keepdims=True)
-        g_stacked = jnp.concatenate(
-            [jnp.where(lane_low, g, 0.0), jnp.where(lane_low, 0.0, g)], axis=0
-        ).astype(bf16)
+        g_stacked = by_head(g_low, sides)
         end_c = end_wide[:, lanes]
         entry_c = entry_wide[:, lanes]
         keep_c = halves(lane_low[:1], keep, head)
@@ -339,7 +344,7 @@
         tail = jnp.sum(q, axis=0, keepdims=True) + keep_c * jnp.sum(
             dstate_p * entry[:, lanes].astype(f32), axis=0, keepdims=True
         )
-        proda_ref[:, lanes] = x * dscaled
+        proda_ref[:, lanes] = (x * dscaled).astype(bf16)
         prodb_ref[:, lanes] = ge * past[:, lanes] - q + last_row * tail
         state_ref[:, lanes] = dstate_p * keep_c
         dx = step_c * dscaled + halves(lane_low[:1], skips, head) * g
@@ -381,7 +386,7 @@
     grads_ref[here, shared_cols] = dsin
     ddecay = row_ref[...].T - col_part + dot_split(prodb_ref[...], place)
     dlog = dot_exact(unsumming, ddecay)
-    dstep = (dot_split(proda_ref[...], place) + rate * dlog) * live * sigmoid(pre)
+    dstep = (dot_nn(proda_ref[...], place) + rate * dlog) * live * sigmoid(pre)
     dproj_ref[:, step_cols] = dstep.astype(bf16)
     grads_ref[here, step_cols] = dstep.astype(bf16)
     wide_ref[6:7, :LANES] += jnp.sum(dstep, axis=0, keepdims=True)
@@ -570,7 +575,7 @@
                 pltpu.VMEM((CHUNK, width), bf16),
                 pltpu.VMEM((CHUNK, width), bf16),
                 pltpu.VMEM((LANES, CHUNK), f32),
-                pltpu.VMEM((CHUNK, width), f32),
+                pltpu.VMEM((CHUNK, width), bf16),
                 pltpu.VMEM((CHUNK, width), f32),
                 pltpu.VMEM((2 * LANES, width), bf16),
                 pltpu.VMEM((2 * LANES, width // HEAD_DIM * CHUNK), bf16),
@@ -856,7 +861,7 @@
     own_blocks = own_rows // TOKEN_BLOCK
     blocks = length // TOKEN_BLOCK
     sds = jax.ShapeDtypeStruct
-    own, other, normed, mixed = from_store(own, other, normed, mixed)
+    own, other, normed, mixed, low, high = from_store(own, other, normed, mixed, low, high)
     return pl.pallas_call(
         partial(out_grad_kernel, own_blocks=own_blocks),
         grid_spec=pltpu.PrefetchScalarGridSpec(
@@ -1123,6 +1128,66 @@
         cost_estimate=cost(5),
         compiler_params=vmem_limit(length),
     )(starts, dgate, dproj, gates, weights)
+
+
+def finish_kernel(
+    got_ref, gate_ref, later_ref, packed_ref, inner_ref, step_ref, small_ref, final_ref, *, heads
+):
+    rows, width = gate_ref.shape
+    columns = packed_ref.shape[1]
+    shared_cols = slice(width, columns - LANES)
+    group = rows + 8
+    total = got_ref[:group, :].astype(f32)
+    for chip in range(1, got_ref.shape[0] // group):
+        total = total + got_ref[chip * group : (chip + 1) * group, :].astype(f32)
+    weights = total[:rows]
+    small = total[rows:]
+    gate = gate_ref[...]
+    inner_ref[:, 0, :] = gate
+    inner_ref[:, 1, :] = weights[:, :width]
+    step_ref[...] = weights[:, columns - LANES :]
+    small_ref[...] = small
+    real = lax.broadcasted_iota(jnp.int32, (rows, columns), 1) < columns - LANES + heads
+    scaled = jnp.where(real, weights * packed_ref[...].astype(f32), 0.0)
+    norm = jnp.sum(scaled, axis=1, keepdims=True) + jnp.sum(
+        gate * later_ref[...].astype(f32), axis=1, keepdims=True
+    )
+    final_ref[...] = jnp.zeros_like(final_ref)
+    shared_size = columns - LANES - width
+    final_ref[:rows, :shared_size] = weights[:, shared_cols]
+    final_ref[rows:, :shared_size] = small[:, shared_cols]
+    final_ref[:rows, shared_size:] = jnp.broadcast_to(norm, (rows, LANES))
+
+
+def run_finish(got, gate, later, packed, heads):
+    rows, width = gate.shape
+    columns = packed.shape[1]
+    sds = jax.ShapeDtypeStruct
+    return pl.pallas_call(
+        partial(finish_kernel, heads=heads),
+        grid=(1,),
+        in_specs=[
+            fixed_spec(got),
+            fixed_spec(gate),
+            pl.BlockSpec((rows, width), lambda i: (0, 0)),
+            fixed_spec(packed),
+        ],
+        out_specs=[
+            pl.BlockSpec((rows, 2, width), lambda i: (0, 0, 0)),
+            pl.BlockSpec((rows, LANES), lambda i: (0, 0)),
+            pl.BlockSpec((8, columns), lambda i: (0, 0)),
+            pl.BlockSpec((rows + 8, columns - width), lambda i: (0, 0)),
+        ],
+        out_shape=(
+            sds((rows, 2, width), f32),
+            sds((rows, LANES), f32),
+            sds((8, columns), f32),
+            sds((rows + 8, columns - width), f32),
+        ),
+        name="finish",
+        cost_estimate=cost(2),
+        compiler_params=vmem_limit(1024),
+    )(got, gate, later, packed)
 
 
 def after(value, *others):
@@ -1306,39 +1371,23 @@
     hidden_out = (hidden_in.astype(f32) + out_half).astype(bf16)
     gsum = sum_blocks(gsum, rows)
     out_sum = gsum[:, width : width + local_inner].T
-    gate_sum = gsum[:, :local_inner]
-
-    wsum = sum_blocks(wsum, rows + 8)
-    small = wsum[rows:]
-    wsum = wsum[:rows]
+    inner_sum, step_sum, small, final = run_finish(wsum, gsum[:, :width], later, packed, heads)
     conv_total = small[:kernel_len, :local_inner]
     gain_total = small[4, :local_inner]
     skip_total = small[0, width + shared_size : width + shared_size + heads]
     bias_total = small[1, width + shared_size : width + shared_size + heads]
     decay_total = small[2, width + shared_size : width + shared_size + heads]
-    norm_row = jnp.sum(gate_sum * proj_inner[:, 0, :].astype(f32), axis=1) + jnp.sum(
-        wsum * packed.astype(f32) * (jnp.arange(packed.shape[1]) < width + shared_size + heads),
-        axis=1,
-    )
-    final = jnp.concatenate(
-        [
-            wsum[:, width : width + shared_size],
-            small[:kernel_len, width : width + shared_size],
-            pad_to(norm_row[None], 1, shared_size),
-        ],
-        axis=0,
-    )
-    final = total_over_tensor(pad_to(final, 0, rows + 8))
-    shared_total = final[:rows].reshape(rows, 2, state_size)
+    final = total_over_tensor(final)
+    shared_total = final[:rows, :shared_size].reshape(rows, 2, state_size)
     taps_total = lax.dynamic_slice_in_dim(
-        final[rows : rows + kernel_len].reshape(kernel_len, 2, state_size),
+        final[rows : rows + kernel_len, :shared_size].reshape(kernel_len, 2, state_size),
         dp_index * tap_block,
         tap_block,
         axis=2,
     )
-    norm_total = final[rows + kernel_len, :rows] / norm_gain.astype(f32)
-    inner_sum = jnp.stack([gate_sum, wsum[:, :local_inner]], axis=1)
-    step_sum = wsum[:, width + shared_size : width + shared_size + heads]
+    norm_total = final[:rows, shared_size] / norm_gain.astype(f32)
+    inner_sum = inner_sum[:, :, :local_inner]
+    step_sum = step_sum[:, :heads]
 
     own = hidden_in.astype(f32)
     own_inv = lax.rsqrt(jnp.mean(own * own, axis=-1, keepdims=True) + epsilon)

time: 182 us -> 177 us (0.973)
  other arithmetic: 15 us -> 11.6 us
  Pallas kernels: 81 us -> 78.9 us
    pallas_call x1, Pallas kernels: 10.1 us -> 8.09 us  [run_out_grad(): pl.pallas_call(partial(out_grad_kernel, own_blocks=own_blocks), grid_spec...]
    unnamed x36 -> x33, local copies, waits for them, and re-layouts: 3.58 us -> 3.64 us
  transfers between devices with their start and end apart: 16 -> 16, of which waited for: 9 -> 10; matrix products, arithmetic and copies ran while one was open for 6% -> 6% of each run, Pallas kernels for 33% -> 34%
where the time goes in v6:
time: 177 us; the launch traced here: 176 us
  Pallas kernels  78.9 us (45%)
  waiting for transfers between devices  40.4 us (23%)
  starting transfers between devices  32.2 us (18%)
  local copies, waits for them, and re-layouts  12.2 us (7%)
  other arithmetic  11.6 us (7%)
    pallas_call x1, Pallas kernels, run_backward(): pl.pallas_call(backward_kernel, grid_spec=pltpu.PrefetchScalarGridSpec(nu...  26.9 us
    ppermute x6, waiting for transfers between devices, swap(): return lax.ppermute(values, 'tensor', [(0, 1), (1, 0)])  18.5 us
    all_to_all x3, starting transfers between devices, exchange(): lax.all_to_all(blocks, 'dp', 0, 0, axis_index_groups=groups, tiled=True)  18.3 us
    ppermute x3, waiting for transfers between devices, body(): got = lax.ppermute(low, 'dp', stage)  14.8 us
    pallas_call x1, Pallas kernels, run_forward(): pl.pallas_call(forward_kernel, grid=(chunks,), in_specs=[chunk_spec(proj....  11.5 us
    pallas_call x1, Pallas kernels, run_gated(): pl.pallas_call(partial(gated_kernel, full_inner=float(full_inner)), grid_...  10.7 us
    pallas_call x2, Pallas kernels, run_norm_grad(): pl.pallas_call(norm_grad_kernel, grid_spec=pltpu.PrefetchScalarGridSpec(n...  8.51 us
    pallas_call x1, Pallas kernels, run_project(): pl.pallas_call(partial(project_kernel, own_blocks=own_blocks, heads=heads...  8.44 us
  transfers between devices with their start and end apart: 16, of which 10 were waited for; matrix products, arithmetic and copies ran while one was open for 6% of the time, Pallas kernels for 34%

profile of v6, /device:TPU:0, one launch (start us, length us, event | category | flops | bytes accessed | tf_op | source)
XLA Modules:
  0.0 176.2 jit_solution(4611416383374340978)
XLA Ops:
  3.7 1.2 fusion.28
  5.1 4.1 %collective-permute-start = (bf16[48,1152]{1,0:T(8,128)(2,1)S(1)}, bf16[48,1152]{1,0:T(8,128)(2,1)S(1)}, u32[]{:S(2)}, u32[]{:S(2)}) collective-permute-start(bf16[48,1152]{1,0:T(8,128)(2,1)S(1)} %pad_maximum_fusion.5.packed_ref), channel_id=1, source_target_pairs={{0,16},{2,18},{4,20},{6,22},{8,24},{10,26},{12,28},{14,30},{16,0},... | collective-permute-start | bytes 331784 | tf_op jit(solution)/shard_map/ppermute | solution.py:1287
  9.2 1.5 collective-permute-start.3
  12.4 2.3 %collective-permute-done = bf16[48,1152]{1,0:T(8,128)(2,1)S(1)} collective-permute-done((bf16[48,1152]{1,0:T(8,128)(2,1)S(1)}, bf16[48,1152]{1,0:T(8,128)(2,1)S(1)}, u32[]{:S(2)}, u32[]{:S(2)}) %collective-permute-start) | collective-permute-done | bytes 110624 | tf_op jit(solution)/shard_map/ppermute | solution.py:1287
  15.5 5.2 %collective-permute-done.1 = bf16[96,1152]{1,0:T(8,128)(2,1)S(1)} collective-permute-done((bf16[96,1152]{1,0:T(8,128)(2,1)S(1)}, bf16[96,1152]{1,0:T(8,128)(2,1)S(1)}, u32[]{:S(2)}, u32[]{:S(2)}) %collective-permute-start.1) | collective-permute-done | bytes 221216 | tf_op jit(solution)/shard_map/ppermute | solution.py:1287
  20.7 1.1 broadcast_in_dim.11
  21.9 1.5 collective-permute-start.2
  23.4 4.8 %all-to-all-start = ((bf16[8,48,1536]{2,1,0:T(8,128)(2,1)}), bf16[8,48,1536]{2,1,0:T(8,128)(2,1)S(1)}, u32[]{:S(2)}, u32[]{:S(2)}) async-start(bf16[8,48,1536]{2,1,0:T(8,128)(2,1)} %bitcast.15), calls=%async_computation | async-start | bytes 2359296 | tf_op jit(solution)/shard_map/all_to_all | solution.py:629
  28.2 7.4 %collective-permute-done.2 = bf16[192,1152]{1,0:T(8,128)(2,1)S(1)} collective-permute-done((bf16[192,1152]{1,0:T(8,128)(2,1)S(1)}, bf16[192,1152]{1,0:T(8,128)(2,1)S(1)}, u32[]{:S(2)}, u32[]{:S(2)}) %collective-permute-start.2) | collective-permute-done | bytes 442400 | tf_op jit(solution)/shard_map/ppermute | solution.py:1287
  36.6 1.5 collective-permute-start.5
  38.2 1.2 collective-permute-done.4.high_ref
  39.4 8.4 %norm_project.1 = (bf16[1024,1024]{1,0:T(8,128)(2,1)}, f32[1024,128]{1,0:T(8,128)}, bf16[1024,768]{1,0:T(8,128)(2,1)}, bf16[768,1024]{1,0:T(8,128)(2,1)}, bf16[7...) custom-call(s32[2]{0:T(128)S(1)} %pad_add_fusion.starts_ref, s32[16]{0:T(128)S(1)} %get-tuple-element.84.table_ref, ...), custom_call_target="tpu_custom_call" | custom-call | flops 2200000000 | tf_op jit(solution)/shard_map/norm_project/pallas_call | solution.py:755
  47.8 11.5 %scan_forward.1 = (bf16[1024,768]{1,0:T(8,128)(2,1)}, bf16[1024,768]{1,0:T(8,128)(2,1)}, f32[1024,256]{1,0:T(8,128)}, bf16[8,128,768]{2,1,0:T(8,128)(2,1)}) custom-call(bf16[1024,1024]{1,0:T(8,128)(2,1)} %get-tuple-element.87.proj_ref, f32[1024,128]{1,0:T(8,128)} %get-tuple-element.88.step_ref.praw_ref, bf16[4,768]{1,0:T(4,128)(2,1)S(1)} %copy-done, ...), custom_call_target="tpu_custom_call" | custom-call | flops 3300000000 | tf_op jit(solution)/shard_map/scan_forward/pallas_call | solution.py:481
  59.5 2.7 %collective-permute-done.6.high_ref = bf16[384,1536]{1,0:T(8,128)(2,1)S(1)} collective-permute-done((bf16[384,1536]{1,0:T(8,128)(2,1)S(1)}, bf16[384,1536]{1,0:T(8,128)(2,1)S(1)}, u32[]{:S(2)}, u32[]{:S(2)}) %collective-permute-start.6) | collective-permute-done | bytes 1179680 | tf_op jit(solution)/shard_map/ppermute | solution.py:1309
  63.3 8.1 %out_grad.1 = (bf16[1024,768]{1,0:T(8,128)(2,1)S(1)}, bf16[1024,768]{1,0:T(8,128)(2,1)S(1)}, bf16[768,1024]{1,0:T(8,128)(2,1)S(1)}, f32[8,1024]{1,0:T(8,128)S(1)}, bf16[768,1536]{1,0:T(8,128)(2,1)}) custom-call(s32[2]{0:T(128)S(1)} %pad_add_fusion.starts_ref, s32[16]{0:T(128)S(1)} %get-tuple-element.77.table_ref, bf16[512,768]{1,0:T(8,128)(2,1)} %own_ref.2, ...), custom_call_target="tpu_custom_call" | custom-call | flops 9900000256 | tf_op jit(solution)/shard_map/out_grad/pallas_call | solution.py:865
  71.4 1.6 collective-permute-start.7
  73.0 2.4 %collective-permute-done.7.more_ref = f32[8,1024]{1,0:T(8,128)S(1)} collective-permute-done((f32[8,1024]{1,0:T(8,128)S(1)}, f32[8,1024]{1,0:T(8,128)S(1)}, u32[]{:S(2)}, u32[]{:S(2)}) %collective-permute-start.7) | collective-permute-done | bytes 32800 | tf_op jit(solution)/shard_map/ppermute | solution.py:639
  75.3 10.7 %gated_grad.1 = (bf16[1024,768]{1,0:T(8,128)(2,1)S(1)}, bf16[1024,768]{1,0:T(8,128)(2,1)}, bf16[1024,768]{1,0:T(8,128)(2,1)}, f32[32,768]{1,0:T(8,128)S(1)}, bf1...) custom-call(s32[16]{0:T(128)S(1)} %get-tuple-element.77.table_ref, ...), custom_call_target="tpu_custom_call" | custom-call | flops 9900000256 | tf_op jit(solution)/shard_map/gated_grad/pallas_call | solution.py:1011
  86.1 3.5 %out_project.1 = (bf16[512,768]{1,0:T(8,128)(2,1)S(1)}, bf16[512,768]{1,0:T(8,128)(2,1)S(1)}) custom-call(s32[1]{0:T(128)} %bitcast.starts_ref, bf16[1024,768]{1,0:T(8,128)(2,1)S(1)} %get-tuple-element.105.rows_ref, bf16[768,1536]{1,0:T(8,128)(2,1)} %get-tuple-element.106.weights_ref.gates_ref), custom_call_target="tpu_custom_call" | custom-call | flops 4400000000 | tf_op jit(solution)/shard_map/out_project/pallas_call | solution.py:1078
  89.6 1.3 add_convert_fusion
  90.9 8.2 %all-to-all-start.1 = ((bf16[8,48,1536]{2,1,0:T(8,128)(2,1)}), bf16[8,48,1536]{2,1,0:T(8,128)(2,1)}, u32[]{:S(2)}, u32[]{:S(2)}) async-start(bf16[8,48,1536]{2,1,0:T(8,128)(2,1)} %bitcast.47), calls=%async_computation.1 | async-start | bytes 2359296 | tf_op jit(solution)/shard_map/all_to_all | solution.py:629
  99.1 1.5 collective-permute-start.9
  100.7 26.9 %scan_backward.1 = (bf16[1024,1152]{1,0:T(8,128)(2,1)}, bf16[392,1152]{1,0:T(8,128)(2,1)}, bf16[392,1152]{1,0:T(8,128)(2,1)}) custom-call(s32[16]{0:T(128)S(1)} %get-tuple-element.77.table_ref, bf16[1024,1024]{1,0:T(8,128)(2,1)} %get-tuple-element.87.proj_ref, f32[1024,128]{1,0:T(8,128)} %get-tuple-element.88.step_ref.praw_ref, ...), custom_call_target="tpu_custom_call" | custom-call | flops 39600001024 | tf_op jit(solution)/shard_map/scan_backward/pallas_call | solution.py:539
  128.7 4.3 %normed_grad.2 = bf16[512,768]{1,0:T(8,128)(2,1)S(1)} custom-call(s32[1]{0:T(128)} %bitcast.starts_ref, bf16[1024,768]{1,0:T(8,128)(2,1)} %get-tuple-element.120.dgate_ref, bf16[1024,1152]{1,0:T(8,128)(2,1)} %get-tuple-element.126.dproj_ref, bf16[768,1536]{1,0:T(8,128)(2,1)} %get-tuple-element.106.weights_ref.gates_ref, ...), custom_call_target="tpu_custom_call" | custom-call | flops 5500000256 | tf_op jit(solution)/shard_map/normed_grad/pallas_call | solution.py:1113
  133.0 1.4 add_convert_fusion.1
  135.6 5.3 %all-to-all-start.2 = ((bf16[8,56,1152]{2,1,0:T(8,128)(2,1)}), bf16[8,56,1152]{2,1,0:T(8,128)(2,1)S(1)}, u32[]{:S(2)}, u32[]{:S(2)}) async-start(bf16[8,56,1152]{2,1,0:T(8,128)(2,1)} %pad_maximum_fusion), calls=%async_computation.2 | async-start | bytes 2064384 | tf_op jit(solution)/shard_map/all_to_all | solution.py:629
  141.4 1.5 convert_reduce_fusion
  143.5 4.2 %normed_grad.3 = f32[512,768]{1,0:T(8,128)S(1)} custom-call(s32[1]{0:T(128)} %bitcast.11.starts_ref, bf16[1024,768]{1,0:T(8,128)(2,1)} %get-tuple-element.120.dgate_ref, bf16[1024,1152]{1,0:T(8,128)(2,1)} %get-tuple-element.126.dproj_ref, bf16[768,1536]{1,0:T(8,128)(2,1)} %get-tuple-element.106.weights_ref.gates_ref, ...), custom_call_target="tpu_custom_call" | custom-call | flops 5500000256 | tf_op jit(solution)/shard_map/normed_grad/pallas_call | solution.py:1113
  147.8 12.8 %collective-permute-done.11 = bf16[512,768]{1,0:T(8,128)(2,1)S(1)} collective-permute-done((bf16[512,768]{1,0:T(8,128)(2,1)S(1)}, bf16[512,768]{1,0:T(8,128)(2,1)S(1)}, u32[]{:S(2)}, u32[]{:S(2)}) %collective-permute-start.11) | collective-permute-done | bytes 786464 | tf_op jit(solution)/shard_map/ppermute | solution.py:639
  161.0 3.6 %fusion.5 = (f32[512,768]{1,0:T(8,128)}, bf16[512,768]{1,0:T(8,128)(2,1)}) fusion(bf16[512,768]{1,0:T(8,128)(2,1)S(1)} %copy-done.3, bf16[512,768]{1,0:T(8,128)(2,1)} %own_ref.2, f32[512,768]{1,0:T(8,128)S(1)} %normed_grad.3, bf16[512,768]{1,0:T(8,128)(2,1)S(1)} %collective-permute-done.11, f32[512]{0:T(512)S(1)} %broadcast_multiply_fusion, ...), kind=kLoop, calls=%fused_computation.11 | loop fusion | flops 5898240 | bytes 7871488 | tf_op jit(solution)/shard_map/add | solution.py:1396
  164.7 2.3 %all-to-all-done.2 = bf16[8,56,1152]{2,1,0:T(8,128)(2,1)S(1)} async-done(((bf16[8,56,1152]{2,1,0:T(8,128)(2,1)}), bf16[8,56,1152]{2,1,0:T(8,128)(2,1)S(1)}, u32[]{:S(2)}, u32[]{:S(2)}) %all-to-all-start.2) | async-done | bytes 1032224 | tf_op jit(solution)/shard_map/all_to_all | solution.py:629
  170.8 3.4 %collective-permute-done.12 = f32[56,384]{1,0:T(8,128)S(1)} collective-permute-done((f32[56,384]{1,0:T(8,128)S(1)}, f32[56,384]{1,0:T(8,128)S(1)}, u32[]{:S(2)}, u32[]{:S(2)}) %collective-permute-start.12) | collective-permute-done | bytes 86048 | tf_op jit(solution)/shard_map/ppermute | solution.py:639
  (86 shorter events, 17.8 us)
Async XLA Ops:
  0.6 10.3 %copy-start.1 = (s32[1024]{0:T(1024)S(1)}, s32[1024]{0:T(1024)}, u32[]{:S(2)}) copy-start(s32[1024]{0:T(1024)} %param.17) | copy-start | bytes 12292
  5.1 9.6 %collective-permute-start = (bf16[48,1152]{1,0:T(8,128)(2,1)S(1)}, bf16[48,1152]{1,0:T(8,128)(2,1)S(1)}, u32[]{:S(2)}, u32[]{:S(2)}) collective-permute-start(bf16[48,1152]{1,0:T(8,128)(2,1)S(1)} %pad_maximum_fusion.5.packed_ref), channel_id=1, source_target_pairs={{0,16},{2,18},{4,20},{6,22},{8,24},{10,26},{12,28},{14,30},{16,0},... | collective-permute-start | bytes 331784 | tf_op jit(solution)/shard_map/ppermute | solution.py:1287
  9.2 27.4 %collective-permute-start.3 = (bf16[512,768]{1,0:T(8,128)(2,1)}, bf16[512,768]{1,0:T(8,128)(2,1)}, u32[]{:S(2)}, u32[]{:S(2)}) collective-permute-start(bf16[512,768]{1,0:T(8,128)(2,1)} %own_ref.1), channel_id=1, source_target_pairs={{0,1},{1,0},{2,3},{3,2},{4,5},{5,4},{6,7},{7,6},{8,9},{9,8},{10,11... | collective-permute-start | bytes 2359304 | tf_op jit(solution)/shard_map/ppermute | solution.py:639
  11.0 0.7 copy-start.8
  11.0 0.7 copy-start.9
  11.0 0.7 copy-start.10
  11.0 0.7 copy-start.12
  11.0 4.4 %copy-start.6 = (bf16[768,48]{0,1:T(8,128)(2,1)S(1)}, bf16[768,48]{0,1:T(8,128)(2,1)}, u32[]{:S(2)}) copy-start(bf16[768,48]{0,1:T(8,128)(2,1)} %param.28) | copy-start | bytes 221188
  14.7 6.0 %collective-permute-start.1 = (bf16[96,1152]{1,0:T(8,128)(2,1)S(1)}, bf16[96,1152]{1,0:T(8,128)(2,1)S(1)}, u32[]{:S(2)}, u32[]{:S(2)}) collective-permute-start(bf16[96,1152]{1,0:T(8,128)(2,1)S(1)} %pad_maximum_fusion.3), channel_id=1, source_target_pairs={{0,8},{2,6},{4,12},{6,2},{8,0},{10,14},{12,4},{14,10},{16,24},{18,... | collective-permute-start | bytes 663560 | tf_op jit(solution)/shard_map/ppermute | solution.py:1287
  20.7 7.4 %copy-start.7 = (bf16[768]{0:T(1024)(128)(2,1)S(1)}, bf16[768]{0:T(1024)(128)(2,1)}, u32[]{:S(2)}) copy-start(bf16[768]{0:T(1024)(128)(2,1)} %param.27) | copy-start | bytes 4612
  21.9 13.7 %collective-permute-start.2 = (bf16[192,1152]{1,0:T(8,128)(2,1)S(1)}, bf16[192,1152]{1,0:T(8,128)(2,1)S(1)}, u32[]{:S(2)}, u32[]{:S(2)}) collective-permute-start(bf16[192,1152]{1,0:T(8,128)(2,1)S(1)} %pad_maximum_fusion.2), channel_id=1, source_target_pairs={{0,4},{2,10},{4,0},{6,14},{8,12},{10,2},{12,8},{14,6},{16,20},{18,... | collective-permute-start | bytes 1327112 | tf_op jit(solution)/shard_map/ppermute | solution.py:1287
  23.4 35.9 %all-to-all-start = ((bf16[8,48,1536]{2,1,0:T(8,128)(2,1)}), bf16[8,48,1536]{2,1,0:T(8,128)(2,1)S(1)}, u32[]{:S(2)}, u32[]{:S(2)}) async-start(bf16[8,48,1536]{2,1,0:T(8,128)(2,1)} %bitcast.15), calls=%async_computation | async-start | bytes 2359296 | tf_op jit(solution)/shard_map/all_to_all | solution.py:629
  36.6 2.8 %collective-permute-start.4 = (bf16[384,1152]{1,0:T(8,128)(2,1)}, bf16[384,1152]{1,0:T(8,128)(2,1)}, u32[]{:S(2)}, u32[]{:S(2)}) collective-permute-start(bf16[384,1152]{1,0:T(8,128)(2,1)} %pad_maximum_fusion.1.low_ref), channel_id=1, source_target_pairs={{0,2},{2,0},{4,6},{6,4},{8,10},{10,8},{12,14},{14,12},{16,18},{18,... | collective-permute-start | bytes 2654216 | tf_op jit(solution)/shard_map/ppermute | solution.py:1299
  36.6 22.7 %collective-permute-start.5 = (bf16[512,768]{1,0:T(8,128)(2,1)}, bf16[512,768]{1,0:T(8,128)(2,1)}, u32[]{:S(2)}, u32[]{:S(2)}) collective-permute-start(bf16[512,768]{1,0:T(8,128)(2,1)} %own_ref.2), channel_id=1, source_target_pairs={{0,1},{1,0},{2,3},{3,2},{4,5},{5,4},{6,7},{7,6},{8,9},{9,8},{10,11... | collective-permute-start | bytes 2359304 | tf_op jit(solution)/shard_map/ppermute | solution.py:639
  38.2 9.6 %copy-start = (bf16[4,768]{1,0:T(4,128)(2,1)S(1)}, bf16[4,768]{1,0:T(4,128)(2,1)}, u32[]{:S(2)}) copy-start(bf16[4,768]{1,0:T(4,128)(2,1)} %tapi_ref.1) | copy-start | bytes 18436
  59.3 2.9 %copy-start.4 = (bf16[8,48,1536]{2,1,0:T(8,128)(2,1)}, bf16[8,48,1536]{2,1,0:T(8,128)(2,1)S(1)}, u32[]{:S(2)}) copy-start(bf16[8,48,1536]{2,1,0:T(8,128)(2,1)S(1)} %all-to-all-done) | copy-start | bytes 3538948
  59.3 2.9 %collective-permute-start.6 = (bf16[384,1536]{1,0:T(8,128)(2,1)S(1)}, bf16[384,1536]{1,0:T(8,128)(2,1)S(1)}, u32[]{:S(2)}, u32[]{:S(2)}) collective-permute-start(bf16[384,1536]{1,0:T(8,128)(2,1)S(1)} %bitcast.52), channel_id=1, source_target_pairs={{0,2},{2,0},{4,6},{6,4},{8,10},{10,8},{12,14},{14,12},{16,18},{18,... | collective-permute-start | bytes 3538952 | tf_op jit(solution)/shard_map/ppermute | solution.py:1309
  62.2 1.0 copy-start.13
  71.4 4.0 %collective-permute-start.7 = (f32[8,1024]{1,0:T(8,128)S(1)}, f32[8,1024]{1,0:T(8,128)S(1)}, u32[]{:S(2)}, u32[]{:S(2)}) collective-permute-start(f32[8,1024]{1,0:T(8,128)S(1)} %get-tuple-element.102.sums_ref), channel_id=1, source_target_pairs={{0,1},{1,0},{2,3},{3,2},{4,5},{5,4},{6,7},{7,6},{8,9},{9,8},{10,11... | collective-permute-start | bytes 98312 | tf_op jit(solution)/shard_map/ppermute | solution.py:639
  86.0 3.6 %collective-permute-start.8 = (bf16[384,1536]{1,0:T(8,128)(2,1)S(1)}, bf16[384,1536]{1,0:T(8,128)(2,1)S(1)}, u32[]{:S(2)}, u32[]{:S(2)}) collective-permute-start(bf16[384,1536]{1,0:T(8,128)(2,1)S(1)} %get-tuple-element.115), channel_id=1, source_target_pairs={{0,2},{2,0},{4,6},{6,4},{8,10},{10,8},{12,14},{14,12},{16,18},{18,... | collective-permute-start | bytes 3538952 | tf_op jit(solution)/shard_map/ppermute | solution.py:1321
  90.9 37.6 %all-to-all-start.1 = ((bf16[8,48,1536]{2,1,0:T(8,128)(2,1)}), bf16[8,48,1536]{2,1,0:T(8,128)(2,1)}, u32[]{:S(2)}, u32[]{:S(2)}) async-start(bf16[8,48,1536]{2,1,0:T(8,128)(2,1)} %bitcast.47), calls=%async_computation.1 | async-start | bytes 2359296 | tf_op jit(solution)/shard_map/all_to_all | solution.py:629
  99.1 28.5 %collective-permute-start.9 = (bf16[512,768]{1,0:T(8,128)(2,1)S(1)}, bf16[512,768]{1,0:T(8,128)(2,1)}, u32[]{:S(2)}, u32[]{:S(2)}) collective-permute-start(bf16[512,768]{1,0:T(8,128)(2,1)S(1)} %get-tuple-element.118), channel_id=1, source_target_pairs={{0,1},{1,0},{2,3},{3,2},{4,5},{5,4},{6,7},{7,6},{8,9},{9,8},{10,11... | collective-permute-start | bytes 2359304 | tf_op jit(solution)/shard_map/ppermute | solution.py:639
  100.7 27.8 %copy-start.2 = (bf16[512,768]{1,0:T(8,128)(2,1)S(1)}, bf16[512,768]{1,0:T(8,128)(2,1)}, u32[]{:S(2)}) copy-start(bf16[512,768]{1,0:T(8,128)(2,1)} %own_ref.1) | copy-start | bytes 2359300
  128.5 4.6 %collective-permute-start.10 = (bf16[392,1152]{1,0:T(8,128)(2,1)}, bf16[392,1152]{1,0:T(8,128)(2,1)}, u32[]{:S(2)}, u32[]{:S(2)}) collective-permute-start(bf16[392,1152]{1,0:T(8,128)(2,1)} %get-tuple-element.122), channel_id=1, source_target_pairs={{0,2},{2,0},{4,6},{6,4},{8,10},{10,8},{12,14},{14,12},{16,18},{18,... | collective-permute-start | bytes 2709512 | tf_op jit(solution)/shard_map/ppermute | solution.py:1348
  128.7 4.3 %copy-start.5 = (bf16[392,1152]{1,0:T(8,128)(2,1)S(1)}, bf16[392,1152]{1,0:T(8,128)(2,1)}, u32[]{:S(2)}) copy-start(bf16[392,1152]{1,0:T(8,128)(2,1)} %get-tuple-element.121) | copy-start | bytes 2709508
  135.6 31.3 %all-to-all-start.2 = ((bf16[8,56,1152]{2,1,0:T(8,128)(2,1)}), bf16[8,56,1152]{2,1,0:T(8,128)(2,1)S(1)}, u32[]{:S(2)}, u32[]{:S(2)}) async-start(bf16[8,56,1152]{2,1,0:T(8,128)(2,1)} %pad_maximum_fusion), calls=%async_computation.2 | async-start | bytes 2064384 | tf_op jit(solution)/shard_map/all_to_all | solution.py:629
  140.9 19.7 %collective-permute-start.11 = (bf16[512,768]{1,0:T(8,128)(2,1)S(1)}, bf16[512,768]{1,0:T(8,128)(2,1)S(1)}, u32[]{:S(2)}, u32[]{:S(2)}) collective-permute-start(bf16[512,768]{1,0:T(8,128)(2,1)S(1)} %normed_grad.2), channel_id=1, source_target_pairs={{0,1},{1,0},{2,3},{3,2},{4,5},{5,4},{6,7},{7,6},{8,9},{9,8},{10,11... | collective-permute-start | bytes 2359304 | tf_op jit(solution)/shard_map/ppermute | solution.py:639
  143.5 17.0 %copy-start.3 = (bf16[512,768]{1,0:T(8,128)(2,1)S(1)}, bf16[512,768]{1,0:T(8,128)(2,1)}, u32[]{:S(2)}) copy-start(bf16[512,768]{1,0:T(8,128)(2,1)} %own_ref.1) | copy-start | bytes 2359300
  166.9 7.4 %copy-start.11 = (bf16[48]{0:T(256)(128)(2,1)S(1)}, bf16[48]{0:T(256)(128)(2,1)}, u32[]{:S(2)}) copy-start(bf16[48]{0:T(256)(128)(2,1)} %param.18) | copy-start | bytes 292
  169.7 4.5 %collective-permute-start.12 = (f32[56,384]{1,0:T(8,128)S(1)}, f32[56,384]{1,0:T(8,128)S(1)}, u32[]{:S(2)}, u32[]{:S(2)}) collective-permute-start(f32[56,384]{1,0:T(8,128)S(1)} %get-tuple-element.131), channel_id=1, source_target_pairs={{0,1},{1,0},{2,3},{3,2},{4,5},{5,4},{6,7},{7,6},{8,9},{9,8},{10,11... | collective-permute-start | bytes 258056 | tf_op jit(solution)/shard_map/ppermute | solution.py:639

commit v7 on v6

--- a/solution.py
+++ b/solution.py
@@ -861,7 +861,7 @@
     own_blocks = own_rows // TOKEN_BLOCK
     blocks = length // TOKEN_BLOCK
     sds = jax.ShapeDtypeStruct
-    own, other, normed, mixed, low, high = from_store(own, other, normed, mixed, low, high)
+    own, other, normed, mixed, low, high = from_store(own, other, normed, mixed, low) + (high,)
     return pl.pallas_call(
         partial(out_grad_kernel, own_blocks=own_blocks),
         grid_spec=pltpu.PrefetchScalarGridSpec(

time: 177 us -> 176 us (level)
    unnamed x33 -> x31, local copies, waits for them, and re-layouts: 3.64 us -> 2.63 us
where the time goes in v7:
time: 176 us; the launch traced here: 175 us
  Pallas kernels  79.1 us (45%)
  waiting for transfers between devices  40.4 us (23%)
  starting transfers between devices  32.1 us (18%)
  other arithmetic  11.6 us (7%)
  local copies, waits for them, and re-layouts  11.2 us (6%)
    pallas_call x1, Pallas kernels, run_backward(): pl.pallas_call(backward_kernel, grid_spec=pltpu.PrefetchScalarGridSpec(nu...  26.9 us
    ppermute x6, waiting for transfers between devices, swap(): return lax.ppermute(values, 'tensor', [(0, 1), (1, 0)])  18.5 us
    all_to_all x3, starting transfers between devices, exchange(): lax.all_to_all(blocks, 'dp', 0, 0, axis_index_groups=groups, tiled=True)  18.3 us
    ppermute x3, waiting for transfers between devices, body(): got = lax.ppermute(low, 'dp', stage)  14.8 us
    pallas_call x1, Pallas kernels, run_forward(): pl.pallas_call(forward_kernel, grid=(chunks,), in_specs=[chunk_spec(proj....  11.5 us
    pallas_call x1, Pallas kernels, run_gated(): pl.pallas_call(partial(gated_kernel, full_inner=float(full_inner)), grid_...  10.7 us
    pallas_call x2, Pallas kernels, run_norm_grad(): pl.pallas_call(norm_grad_kernel, grid_spec=pltpu.PrefetchScalarGridSpec(n...  8.52 us
    pallas_call x1, Pallas kernels, run_project(): pl.pallas_call(partial(project_kernel, own_blocks=own_blocks, heads=heads...  8.45 us
  transfers between devices with their start and end apart: 16, of which 10 were waited for; matrix products, arithmetic and copies ran while one was open for 6% of the time, Pallas kernels for 34%

profile of v7, /device:TPU:0, one launch (start us, length us, event | category | flops | bytes accessed | tf_op | source)
XLA Modules:
  0.0 175.4 jit_solution(13994618505401006704)
XLA Ops:
  3.7 1.2 fusion.28
  5.1 4.1 %collective-permute-start = (bf16[48,1152]{1,0:T(8,128)(2,1)S(1)}, bf16[48,1152]{1,0:T(8,128)(2,1)S(1)}, u32[]{:S(2)}, u32[]{:S(2)}) collective-permute-start(bf16[48,1152]{1,0:T(8,128)(2,1)S(1)} %pad_maximum_fusion.5.packed_ref), channel_id=1, source_target_pairs={{0,16},{2,18},{4,20},{6,22},{8,24},{10,26},{12,28},{14,30},{16,0},... | collective-permute-start | bytes 331784 | tf_op jit(solution)/shard_map/ppermute | solution.py:1287
  9.2 1.5 collective-permute-start.3
  12.4 2.3 %collective-permute-done = bf16[48,1152]{1,0:T(8,128)(2,1)S(1)} collective-permute-done((bf16[48,1152]{1,0:T(8,128)(2,1)S(1)}, bf16[48,1152]{1,0:T(8,128)(2,1)S(1)}, u32[]{:S(2)}, u32[]{:S(2)}) %collective-permute-start) | collective-permute-done | bytes 110624 | tf_op jit(solution)/shard_map/ppermute | solution.py:1287
  15.5 5.2 %collective-permute-done.1 = bf16[96,1152]{1,0:T(8,128)(2,1)S(1)} collective-permute-done((bf16[96,1152]{1,0:T(8,128)(2,1)S(1)}, bf16[96,1152]{1,0:T(8,128)(2,1)S(1)}, u32[]{:S(2)}, u32[]{:S(2)}) %collective-permute-start.1) | collective-permute-done | bytes 221216 | tf_op jit(solution)/shard_map/ppermute | solution.py:1287
  20.7 1.1 broadcast_in_dim.11
  21.8 1.5 collective-permute-start.2
  23.4 4.8 %all-to-all-start = ((bf16[8,48,1536]{2,1,0:T(8,128)(2,1)}), bf16[8,48,1536]{2,1,0:T(8,128)(2,1)S(1)}, u32[]{:S(2)}, u32[]{:S(2)}) async-start(bf16[8,48,1536]{2,1,0:T(8,128)(2,1)} %bitcast.15), calls=%async_computation | async-start | bytes 2359296 | tf_op jit(solution)/shard_map/all_to_all | solution.py:629
  28.2 7.4 %collective-permute-done.2 = bf16[192,1152]{1,0:T(8,128)(2,1)S(1)} collective-permute-done((bf16[192,1152]{1,0:T(8,128)(2,1)S(1)}, bf16[192,1152]{1,0:T(8,128)(2,1)S(1)}, u32[]{:S(2)}, u32[]{:S(2)}) %collective-permute-start.2) | collective-permute-done | bytes 442400 | tf_op jit(solution)/shard_map/ppermute | solution.py:1287
  36.6 1.5 collective-permute-start.5
  38.2 1.2 collective-permute-done.4.high_ref
  39.3 8.4 %norm_project.1 = (bf16[1024,1024]{1,0:T(8,128)(2,1)}, f32[1024,128]{1,0:T(8,128)}, bf16[1024,768]{1,0:T(8,128)(2,1)}, bf16[768,1024]{1,0:T(8,128)(2,1)}, bf16[7...) custom-call(s32[2]{0:T(128)S(1)} %pad_add_fusion.starts_ref, s32[16]{0:T(128)S(1)} %get-tuple-element.84.table_ref, ...), custom_call_target="tpu_custom_call" | custom-call | flops 2200000000 | tf_op jit(solution)/shard_map/norm_project/pallas_call | solution.py:755
  47.8 11.5 %scan_forward.1 = (bf16[1024,768]{1,0:T(8,128)(2,1)}, bf16[1024,768]{1,0:T(8,128)(2,1)}, f32[1024,256]{1,0:T(8,128)}, bf16[8,128,768]{2,1,0:T(8,128)(2,1)}) custom-call(bf16[1024,1024]{1,0:T(8,128)(2,1)} %get-tuple-element.87.proj_ref, f32[1024,128]{1,0:T(8,128)} %get-tuple-element.88.step_ref.praw_ref, bf16[4,768]{1,0:T(4,128)(2,1)S(1)} %copy-done, ...), custom_call_target="tpu_custom_call" | custom-call | flops 3300000000 | tf_op jit(solution)/shard_map/scan_forward/pallas_call | solution.py:481
  59.5 2.7 %collective-permute-done.6.high_ref = bf16[384,1536]{1,0:T(8,128)(2,1)S(1)} collective-permute-done((bf16[384,1536]{1,0:T(8,128)(2,1)S(1)}, bf16[384,1536]{1,0:T(8,128)(2,1)S(1)}, u32[]{:S(2)}, u32[]{:S(2)}) %collective-permute-start.6) | collective-permute-done | bytes 1179680 | tf_op jit(solution)/shard_map/ppermute | solution.py:1309
  62.2 8.3 %out_grad.1 = (bf16[1024,768]{1,0:T(8,128)(2,1)S(1)}, bf16[1024,768]{1,0:T(8,128)(2,1)S(1)}, bf16[768,1024]{1,0:T(8,128)(2,1)S(1)}, f32[8,1024]{1,0:T(8,128)S(1)}, bf16[768,1536]{1,0:T(8,128)(2,1)}) custom-call(s32[2]{0:T(128)S(1)} %pad_add_fusion.starts_ref, s32[16]{0:T(128)S(1)} %get-tuple-element.77.table_ref, bf16[512,768]{1,0:T(8,128)(2,1)} %own_ref.2, ...), custom_call_target="tpu_custom_call" | custom-call | flops 9900000256 | tf_op jit(solution)/shard_map/out_grad/pallas_call | solution.py:865
  70.6 1.6 collective-permute-start.7
  72.2 2.4 %collective-permute-done.7.more_ref = f32[8,1024]{1,0:T(8,128)S(1)} collective-permute-done((f32[8,1024]{1,0:T(8,128)S(1)}, f32[8,1024]{1,0:T(8,128)S(1)}, u32[]{:S(2)}, u32[]{:S(2)}) %collective-permute-start.7) | collective-permute-done | bytes 32800 | tf_op jit(solution)/shard_map/ppermute | solution.py:639
  74.6 10.7 %gated_grad.1 = (bf16[1024,768]{1,0:T(8,128)(2,1)S(1)}, bf16[1024,768]{1,0:T(8,128)(2,1)}, bf16[1024,768]{1,0:T(8,128)(2,1)}, f32[32,768]{1,0:T(8,128)S(1)}, bf1...) custom-call(s32[16]{0:T(128)S(1)} %get-tuple-element.77.table_ref, ...), custom_call_target="tpu_custom_call" | custom-call | flops 9900000256 | tf_op jit(solution)/shard_map/gated_grad/pallas_call | solution.py:1011
  85.3 3.5 %out_project.1 = (bf16[512,768]{1,0:T(8,128)(2,1)S(1)}, bf16[512,768]{1,0:T(8,128)(2,1)S(1)}) custom-call(s32[1]{0:T(128)} %bitcast.starts_ref, bf16[1024,768]{1,0:T(8,128)(2,1)S(1)} %get-tuple-element.105.rows_ref, bf16[768,1536]{1,0:T(8,128)(2,1)} %get-tuple-element.106.weights_ref.gates_ref), custom_call_target="tpu_custom_call" | custom-call | flops 4400000000 | tf_op jit(solution)/shard_map/out_project/pallas_call | solution.py:1078
  88.8 1.3 add_convert_fusion
  90.1 8.2 %all-to-all-start.1 = ((bf16[8,48,1536]{2,1,0:T(8,128)(2,1)}), bf16[8,48,1536]{2,1,0:T(8,128)(2,1)}, u32[]{:S(2)}, u32[]{:S(2)}) async-start(bf16[8,48,1536]{2,1,0:T(8,128)(2,1)} %bitcast.47), calls=%async_computation.1 | async-start | bytes 2359296 | tf_op jit(solution)/shard_map/all_to_all | solution.py:629
  98.4 1.5 collective-permute-start.9
  99.9 26.9 %scan_backward.1 = (bf16[1024,1152]{1,0:T(8,128)(2,1)}, bf16[392,1152]{1,0:T(8,128)(2,1)}, bf16[392,1152]{1,0:T(8,128)(2,1)}) custom-call(s32[16]{0:T(128)S(1)} %get-tuple-element.77.table_ref, bf16[1024,1024]{1,0:T(8,128)(2,1)} %get-tuple-element.87.proj_ref, f32[1024,128]{1,0:T(8,128)} %get-tuple-element.88.step_ref.praw_ref, ...), custom_call_target="tpu_custom_call" | custom-call | flops 39600001024 | tf_op jit(solution)/shard_map/scan_backward/pallas_call | solution.py:539
  128.0 4.3 %normed_grad.2 = bf16[512,768]{1,0:T(8,128)(2,1)S(1)} custom-call(s32[1]{0:T(128)} %bitcast.starts_ref, bf16[1024,768]{1,0:T(8,128)(2,1)} %get-tuple-element.120.dgate_ref, bf16[1024,1152]{1,0:T(8,128)(2,1)} %get-tuple-element.126.dproj_ref, bf16[768,1536]{1,0:T(8,128)(2,1)} %get-tuple-element.106.weights_ref.gates_ref, ...), custom_call_target="tpu_custom_call" | custom-call | flops 5500000256 | tf_op jit(solution)/shard_map/normed_grad/pallas_call | solution.py:1113
  132.3 1.4 add_convert_fusion.1
  134.8 5.3 %all-to-all-start.2 = ((bf16[8,56,1152]{2,1,0:T(8,128)(2,1)}), bf16[8,56,1152]{2,1,0:T(8,128)(2,1)S(1)}, u32[]{:S(2)}, u32[]{:S(2)}) async-start(bf16[8,56,1152]{2,1,0:T(8,128)(2,1)} %pad_maximum_fusion), calls=%async_computation.2 | async-start | bytes 2064384 | tf_op jit(solution)/shard_map/all_to_all | solution.py:629
  140.6 1.5 convert_reduce_fusion
  142.7 4.2 %normed_grad.3 = f32[512,768]{1,0:T(8,128)S(1)} custom-call(s32[1]{0:T(128)} %bitcast.11.starts_ref, bf16[1024,768]{1,0:T(8,128)(2,1)} %get-tuple-element.120.dgate_ref, bf16[1024,1152]{1,0:T(8,128)(2,1)} %get-tuple-element.126.dproj_ref, bf16[768,1536]{1,0:T(8,128)(2,1)} %get-tuple-element.106.weights_ref.gates_ref, ...), custom_call_target="tpu_custom_call" | custom-call | flops 5500000256 | tf_op jit(solution)/shard_map/normed_grad/pallas_call | solution.py:1113
  147.0 12.8 %collective-permute-done.11 = bf16[512,768]{1,0:T(8,128)(2,1)S(1)} collective-permute-done((bf16[512,768]{1,0:T(8,128)(2,1)S(1)}, bf16[512,768]{1,0:T(8,128)(2,1)S(1)}, u32[]{:S(2)}, u32[]{:S(2)}) %collective-permute-start.11) | collective-permute-done | bytes 786464 | tf_op jit(solution)/shard_map/ppermute | solution.py:639
  160.3 3.6 %fusion.5 = (f32[512,768]{1,0:T(8,128)}, bf16[512,768]{1,0:T(8,128)(2,1)}) fusion(bf16[512,768]{1,0:T(8,128)(2,1)S(1)} %copy-done.3, bf16[512,768]{1,0:T(8,128)(2,1)} %own_ref.2, f32[512,768]{1,0:T(8,128)S(1)} %normed_grad.3, bf16[512,768]{1,0:T(8,128)(2,1)S(1)} %collective-permute-done.11, f32[512]{0:T(512)S(1)} %broadcast_multiply_fusion, ...), kind=kLoop, calls=%fused_computation.11 | loop fusion | flops 5898240 | bytes 7871488 | tf_op jit(solution)/shard_map/add | solution.py:1396
  163.9 2.3 %all-to-all-done.2 = bf16[8,56,1152]{2,1,0:T(8,128)(2,1)S(1)} async-done(((bf16[8,56,1152]{2,1,0:T(8,128)(2,1)}), bf16[8,56,1152]{2,1,0:T(8,128)(2,1)S(1)}, u32[]{:S(2)}, u32[]{:S(2)}) %all-to-all-start.2) | async-done | bytes 1032224 | tf_op jit(solution)/shard_map/all_to_all | solution.py:629
  170.0 3.4 %collective-permute-done.12 = f32[56,384]{1,0:T(8,128)S(1)} collective-permute-done((f32[56,384]{1,0:T(8,128)S(1)}, f32[56,384]{1,0:T(8,128)S(1)}, u32[]{:S(2)}, u32[]{:S(2)}) %collective-permute-start.12) | collective-permute-done | bytes 86048 | tf_op jit(solution)/shard_map/ppermute | solution.py:639
  (84 shorter events, 16.8 us)
Async XLA Ops:
  0.6 10.3 %copy-start.1 = (s32[1024]{0:T(1024)S(1)}, s32[1024]{0:T(1024)}, u32[]{:S(2)}) copy-start(s32[1024]{0:T(1024)} %param.17) | copy-start | bytes 12292
  5.1 9.6 %collective-permute-start = (bf16[48,1152]{1,0:T(8,128)(2,1)S(1)}, bf16[48,1152]{1,0:T(8,128)(2,1)S(1)}, u32[]{:S(2)}, u32[]{:S(2)}) collective-permute-start(bf16[48,1152]{1,0:T(8,128)(2,1)S(1)} %pad_maximum_fusion.5.packed_ref), channel_id=1, source_target_pairs={{0,16},{2,18},{4,20},{6,22},{8,24},{10,26},{12,28},{14,30},{16,0},... | collective-permute-start | bytes 331784 | tf_op jit(solution)/shard_map/ppermute | solution.py:1287
  9.2 27.3 %collective-permute-start.3 = (bf16[512,768]{1,0:T(8,128)(2,1)}, bf16[512,768]{1,0:T(8,128)(2,1)}, u32[]{:S(2)}, u32[]{:S(2)}) collective-permute-start(bf16[512,768]{1,0:T(8,128)(2,1)} %own_ref.1), channel_id=1, source_target_pairs={{0,1},{1,0},{2,3},{3,2},{4,5},{5,4},{6,7},{7,6},{8,9},{9,8},{10,11... | collective-permute-start | bytes 2359304 | tf_op jit(solution)/shard_map/ppermute | solution.py:639
  11.0 0.7 copy-start.8
  11.0 0.7 copy-start.9
  11.0 0.7 copy-start.10
  11.0 0.7 copy-start.12
  11.0 4.4 %copy-start.6 = (bf16[768,48]{0,1:T(8,128)(2,1)S(1)}, bf16[768,48]{0,1:T(8,128)(2,1)}, u32[]{:S(2)}) copy-start(bf16[768,48]{0,1:T(8,128)(2,1)} %param.28) | copy-start | bytes 221188
  14.7 6.0 %collective-permute-start.1 = (bf16[96,1152]{1,0:T(8,128)(2,1)S(1)}, bf16[96,1152]{1,0:T(8,128)(2,1)S(1)}, u32[]{:S(2)}, u32[]{:S(2)}) collective-permute-start(bf16[96,1152]{1,0:T(8,128)(2,1)S(1)} %pad_maximum_fusion.3), channel_id=1, source_target_pairs={{0,8},{2,6},{4,12},{6,2},{8,0},{10,14},{12,4},{14,10},{16,24},{18,... | collective-permute-start | bytes 663560 | tf_op jit(solution)/shard_map/ppermute | solution.py:1287
  20.7 7.4 %copy-start.7 = (bf16[768]{0:T(1024)(128)(2,1)S(1)}, bf16[768]{0:T(1024)(128)(2,1)}, u32[]{:S(2)}) copy-start(bf16[768]{0:T(1024)(128)(2,1)} %param.27) | copy-start | bytes 4612
  21.8 13.7 %collective-permute-start.2 = (bf16[192,1152]{1,0:T(8,128)(2,1)S(1)}, bf16[192,1152]{1,0:T(8,128)(2,1)S(1)}, u32[]{:S(2)}, u32[]{:S(2)}) collective-permute-start(bf16[192,1152]{1,0:T(8,128)(2,1)S(1)} %pad_maximum_fusion.2), channel_id=1, source_target_pairs={{0,4},{2,10},{4,0},{6,14},{8,12},{10,2},{12,8},{14,6},{16,20},{18,... | collective-permute-start | bytes 1327112 | tf_op jit(solution)/shard_map/ppermute | solution.py:1287
  23.4 35.9 %all-to-all-start = ((bf16[8,48,1536]{2,1,0:T(8,128)(2,1)}), bf16[8,48,1536]{2,1,0:T(8,128)(2,1)S(1)}, u32[]{:S(2)}, u32[]{:S(2)}) async-start(bf16[8,48,1536]{2,1,0:T(8,128)(2,1)} %bitcast.15), calls=%async_computation | async-start | bytes 2359296 | tf_op jit(solution)/shard_map/all_to_all | solution.py:629
  36.6 2.8 %collective-permute-start.4 = (bf16[384,1152]{1,0:T(8,128)(2,1)}, bf16[384,1152]{1,0:T(8,128)(2,1)}, u32[]{:S(2)}, u32[]{:S(2)}) collective-permute-start(bf16[384,1152]{1,0:T(8,128)(2,1)} %pad_maximum_fusion.1.low_ref), channel_id=1, source_target_pairs={{0,2},{2,0},{4,6},{6,4},{8,10},{10,8},{12,14},{14,12},{16,18},{18,... | collective-permute-start | bytes 2654216 | tf_op jit(solution)/shard_map/ppermute | solution.py:1299
  36.6 22.7 %collective-permute-start.5 = (bf16[512,768]{1,0:T(8,128)(2,1)}, bf16[512,768]{1,0:T(8,128)(2,1)}, u32[]{:S(2)}, u32[]{:S(2)}) collective-permute-start(bf16[512,768]{1,0:T(8,128)(2,1)} %own_ref.2), channel_id=1, source_target_pairs={{0,1},{1,0},{2,3},{3,2},{4,5},{5,4},{6,7},{7,6},{8,9},{9,8},{10,11... | collective-permute-start | bytes 2359304 | tf_op jit(solution)/shard_map/ppermute | solution.py:639
  38.2 9.6 %copy-start = (bf16[4,768]{1,0:T(4,128)(2,1)S(1)}, bf16[4,768]{1,0:T(4,128)(2,1)}, u32[]{:S(2)}) copy-start(bf16[4,768]{1,0:T(4,128)(2,1)} %tapi_ref.1) | copy-start | bytes 18436
  59.3 2.9 %copy-start.4 = (bf16[8,48,1536]{2,1,0:T(8,128)(2,1)}, bf16[8,48,1536]{2,1,0:T(8,128)(2,1)S(1)}, u32[]{:S(2)}) copy-start(bf16[8,48,1536]{2,1,0:T(8,128)(2,1)S(1)} %all-to-all-done) | copy-start | bytes 3538948
  59.3 2.9 %collective-permute-start.6 = (bf16[384,1536]{1,0:T(8,128)(2,1)S(1)}, bf16[384,1536]{1,0:T(8,128)(2,1)S(1)}, u32[]{:S(2)}, u32[]{:S(2)}) collective-permute-start(bf16[384,1536]{1,0:T(8,128)(2,1)S(1)} %bitcast.52), channel_id=1, source_target_pairs={{0,2},{2,0},{4,6},{6,4},{8,10},{10,8},{12,14},{14,12},{16,18},{18,... | collective-permute-start | bytes 3538952 | tf_op jit(solution)/shard_map/ppermute | solution.py:1309
  70.6 4.0 %collective-permute-start.7 = (f32[8,1024]{1,0:T(8,128)S(1)}, f32[8,1024]{1,0:T(8,128)S(1)}, u32[]{:S(2)}, u32[]{:S(2)}) collective-permute-start(f32[8,1024]{1,0:T(8,128)S(1)} %get-tuple-element.102.sums_ref), channel_id=1, source_target_pairs={{0,1},{1,0},{2,3},{3,2},{4,5},{5,4},{6,7},{7,6},{8,9},{9,8},{10,11... | collective-permute-start | bytes 98312 | tf_op jit(solution)/shard_map/ppermute | solution.py:639
  85.3 3.6 %collective-permute-start.8 = (bf16[384,1536]{1,0:T(8,128)(2,1)S(1)}, bf16[384,1536]{1,0:T(8,128)(2,1)S(1)}, u32[]{:S(2)}, u32[]{:S(2)}) collective-permute-start(bf16[384,1536]{1,0:T(8,128)(2,1)S(1)} %get-tuple-element.115), channel_id=1, source_target_pairs={{0,2},{2,0},{4,6},{6,4},{8,10},{10,8},{12,14},{14,12},{16,18},{18,... | collective-permute-start | bytes 3538952 | tf_op jit(solution)/shard_map/ppermute | solution.py:1321
  90.1 37.6 %all-to-all-start.1 = ((bf16[8,48,1536]{2,1,0:T(8,128)(2,1)}), bf16[8,48,1536]{2,1,0:T(8,128)(2,1)}, u32[]{:S(2)}, u32[]{:S(2)}) async-start(bf16[8,48,1536]{2,1,0:T(8,128)(2,1)} %bitcast.47), calls=%async_computation.1 | async-start | bytes 2359296 | tf_op jit(solution)/shard_map/all_to_all | solution.py:629
  98.4 28.5 %collective-permute-start.9 = (bf16[512,768]{1,0:T(8,128)(2,1)S(1)}, bf16[512,768]{1,0:T(8,128)(2,1)}, u32[]{:S(2)}, u32[]{:S(2)}) collective-permute-start(bf16[512,768]{1,0:T(8,128)(2,1)S(1)} %get-tuple-element.118), channel_id=1, source_target_pairs={{0,1},{1,0},{2,3},{3,2},{4,5},{5,4},{6,7},{7,6},{8,9},{9,8},{10,11... | collective-permute-start | bytes 2359304 | tf_op jit(solution)/shard_map/ppermute | solution.py:639
  99.9 27.8 %copy-start.2 = (bf16[512,768]{1,0:T(8,128)(2,1)S(1)}, bf16[512,768]{1,0:T(8,128)(2,1)}, u32[]{:S(2)}) copy-start(bf16[512,768]{1,0:T(8,128)(2,1)} %own_ref.1) | copy-start | bytes 2359300
  127.7 4.6 %collective-permute-start.10 = (bf16[392,1152]{1,0:T(8,128)(2,1)}, bf16[392,1152]{1,0:T(8,128)(2,1)}, u32[]{:S(2)}, u32[]{:S(2)}) collective-permute-start(bf16[392,1152]{1,0:T(8,128)(2,1)} %get-tuple-element.122), channel_id=1, source_target_pairs={{0,2},{2,0},{4,6},{6,4},{8,10},{10,8},{12,14},{14,12},{16,18},{18,... | collective-permute-start | bytes 2709512 | tf_op jit(solution)/shard_map/ppermute | solution.py:1348
  128.0 4.3 %copy-start.5 = (bf16[392,1152]{1,0:T(8,128)(2,1)S(1)}, bf16[392,1152]{1,0:T(8,128)(2,1)}, u32[]{:S(2)}) copy-start(bf16[392,1152]{1,0:T(8,128)(2,1)} %get-tuple-element.121) | copy-start | bytes 2709508
  134.8 31.3 %all-to-all-start.2 = ((bf16[8,56,1152]{2,1,0:T(8,128)(2,1)}), bf16[8,56,1152]{2,1,0:T(8,128)(2,1)S(1)}, u32[]{:S(2)}, u32[]{:S(2)}) async-start(bf16[8,56,1152]{2,1,0:T(8,128)(2,1)} %pad_maximum_fusion), calls=%async_computation.2 | async-start | bytes 2064384 | tf_op jit(solution)/shard_map/all_to_all | solution.py:629
  140.1 19.7 %collective-permute-start.11 = (bf16[512,768]{1,0:T(8,128)(2,1)S(1)}, bf16[512,768]{1,0:T(8,128)(2,1)S(1)}, u32[]{:S(2)}, u32[]{:S(2)}) collective-permute-start(bf16[512,768]{1,0:T(8,128)(2,1)S(1)} %normed_grad.2), channel_id=1, source_target_pairs={{0,1},{1,0},{2,3},{3,2},{4,5},{5,4},{6,7},{7,6},{8,9},{9,8},{10,11... | collective-permute-start | bytes 2359304 | tf_op jit(solution)/shard_map/ppermute | solution.py:639
  142.7 17.0 %copy-start.3 = (bf16[512,768]{1,0:T(8,128)(2,1)S(1)}, bf16[512,768]{1,0:T(8,128)(2,1)}, u32[]{:S(2)}) copy-start(bf16[512,768]{1,0:T(8,128)(2,1)} %own_ref.1) | copy-start | bytes 2359300
  166.2 7.4 %copy-start.11 = (bf16[48]{0:T(256)(128)(2,1)S(1)}, bf16[48]{0:T(256)(128)(2,1)}, u32[]{:S(2)}) copy-start(bf16[48]{0:T(256)(128)(2,1)} %param.18) | copy-start | bytes 292
  168.9 4.5 %collective-permute-start.12 = (f32[56,384]{1,0:T(8,128)S(1)}, f32[56,384]{1,0:T(8,128)S(1)}, u32[]{:S(2)}, u32[]{:S(2)}) collective-permute-start(f32[56,384]{1,0:T(8,128)S(1)} %get-tuple-element.131), channel_id=1, source_target_pairs={{0,1},{1,0},{2,3},{3,2},{4,5},{5,4},{6,7},{7,6},{8,9},{9,8},{10,11... | collective-permute-start | bytes 258056 | tf_op jit(solution)/shard_map/ppermute | solution.py:639

commit v8 on v7

--- a/solution.py
+++ b/solution.py
@@ -751,7 +751,7 @@
     blocks = own_blocks * (2 if lax.axis_size("tensor") == 2 else 1)
     length = blocks * TOKEN_BLOCK
     sds = jax.ShapeDtypeStruct
-    own, other, low, high = from_store(own, other, low, high)
+    own, other, low = from_store(own, other, low)
     return pl.pallas_call(
         partial(project_kernel, own_blocks=own_blocks, heads=heads),
         grid_spec=pltpu.PrefetchScalarGridSpec(

time: 176 us -> 175 us (level)
  transfers between devices with their start and end apart: 16 -> 16, of which waited for: 10 -> 10; matrix products, arithmetic and copies ran while one was open for 6% -> 5% of each run, Pallas kernels for 34% -> 34%
where the time goes in v8:
time: 175 us; the launch traced here: 174 us
  Pallas kernels  78.9 us (45%)
  waiting for transfers between devices  40.2 us (23%)
  starting transfers between devices  32.3 us (18%)
  local copies, waits for them, and re-layouts  11.2 us (6%)
  other arithmetic  10.6 us (6%)
    pallas_call x1, Pallas kernels, run_backward(): pl.pallas_call(backward_kernel, grid_spec=pltpu.PrefetchScalarGridSpec(nu...  26.9 us
    ppermute x6, waiting for transfers between devices, swap(): return lax.ppermute(values, 'tensor', [(0, 1), (1, 0)])  18.5 us
    all_to_all x3, starting transfers between devices, exchange(): lax.all_to_all(blocks, 'dp', 0, 0, axis_index_groups=groups, tiled=True)  18.3 us
    ppermute x3, waiting for transfers between devices, body(): got = lax.ppermute(low, 'dp', stage)  14.8 us
    pallas_call x1, Pallas kernels, run_forward(): pl.pallas_call(forward_kernel, grid=(chunks,), in_specs=[chunk_spec(proj....  11.5 us
    pallas_call x1, Pallas kernels, run_gated(): pl.pallas_call(partial(gated_kernel, full_inner=float(full_inner)), grid_...  10.7 us
    pallas_call x2, Pallas kernels, run_norm_grad(): pl.pallas_call(norm_grad_kernel, grid_spec=pltpu.PrefetchScalarGridSpec(n...  8.52 us
    pallas_call x1, Pallas kernels, run_out_grad(): pl.pallas_call(partial(out_grad_kernel, own_blocks=own_blocks), grid_spec...  8.34 us
  transfers between devices with their start and end apart: 16, of which 10 were waited for; matrix products, arithmetic and copies ran while one was open for 5% of the time, Pallas kernels for 34%

profile of v8, /device:TPU:0, one launch (start us, length us, event | category | flops | bytes accessed | tf_op | source)
XLA Modules:
  0.0 174.2 jit_solution(10298410813921825432)
XLA Ops:
  3.7 1.2 fusion.28
  5.1 4.1 %collective-permute-start = (bf16[48,1152]{1,0:T(8,128)(2,1)S(1)}, bf16[48,1152]{1,0:T(8,128)(2,1)S(1)}, u32[]{:S(2)}, u32[]{:S(2)}) collective-permute-start(bf16[48,1152]{1,0:T(8,128)(2,1)S(1)} %pad_maximum_fusion.5.packed_ref), channel_id=1, source_target_pairs={{0,16},{2,18},{4,20},{6,22},{8,24},{10,26},{12,28},{14,30},{16,0},... | collective-permute-start | bytes 331784 | tf_op jit(solution)/shard_map/ppermute | solution.py:1287
  9.2 1.5 collective-permute-start.3
  12.4 2.3 %collective-permute-done = bf16[48,1152]{1,0:T(8,128)(2,1)S(1)} collective-permute-done((bf16[48,1152]{1,0:T(8,128)(2,1)S(1)}, bf16[48,1152]{1,0:T(8,128)(2,1)S(1)}, u32[]{:S(2)}, u32[]{:S(2)}) %collective-permute-start) | collective-permute-done | bytes 110624 | tf_op jit(solution)/shard_map/ppermute | solution.py:1287
  15.5 5.2 %collective-permute-done.1 = bf16[96,1152]{1,0:T(8,128)(2,1)S(1)} collective-permute-done((bf16[96,1152]{1,0:T(8,128)(2,1)S(1)}, bf16[96,1152]{1,0:T(8,128)(2,1)S(1)}, u32[]{:S(2)}, u32[]{:S(2)}) %collective-permute-start.1) | collective-permute-done | bytes 221216 | tf_op jit(solution)/shard_map/ppermute | solution.py:1287
  20.7 1.1 broadcast_in_dim.11
  21.8 1.5 collective-permute-start.2
  23.4 4.8 %all-to-all-start = ((bf16[8,48,1536]{2,1,0:T(8,128)(2,1)}), bf16[8,48,1536]{2,1,0:T(8,128)(2,1)}, u32[]{:S(2)}, u32[]{:S(2)}) async-start(bf16[8,48,1536]{2,1,0:T(8,128)(2,1)} %bitcast.15), calls=%async_computation | async-start | bytes 2359296 | tf_op jit(solution)/shard_map/all_to_all | solution.py:629
  28.2 7.4 %collective-permute-done.2 = bf16[192,1152]{1,0:T(8,128)(2,1)S(1)} collective-permute-done((bf16[192,1152]{1,0:T(8,128)(2,1)S(1)}, bf16[192,1152]{1,0:T(8,128)(2,1)S(1)}, u32[]{:S(2)}, u32[]{:S(2)}) %collective-permute-start.2) | collective-permute-done | bytes 442400 | tf_op jit(solution)/shard_map/ppermute | solution.py:1287
  35.7 1.6 collective-permute-start.5
  38.1 8.2 %norm_project.1 = (bf16[1024,1024]{1,0:T(8,128)(2,1)}, f32[1024,128]{1,0:T(8,128)}, bf16[1024,768]{1,0:T(8,128)(2,1)}, bf16[768,1024]{1,0:T(8,128)(2,1)}, bf16[7...) custom-call(s32[2]{0:T(128)S(1)} %pad_add_fusion.starts_ref, s32[16]{0:T(128)S(1)} %get-tuple-element.84.table_ref, ...), custom_call_target="tpu_custom_call" | custom-call | flops 2200000000 | tf_op jit(solution)/shard_map/norm_project/pallas_call | solution.py:755
  46.4 11.5 %scan_forward.1 = (bf16[1024,768]{1,0:T(8,128)(2,1)}, bf16[1024,768]{1,0:T(8,128)(2,1)}, f32[1024,256]{1,0:T(8,128)}, bf16[8,128,768]{2,1,0:T(8,128)(2,1)}) custom-call(bf16[1024,1024]{1,0:T(8,128)(2,1)} %get-tuple-element.87.proj_ref, f32[1024,128]{1,0:T(8,128)} %get-tuple-element.88.step_ref.praw_ref, bf16[4,768]{1,0:T(4,128)(2,1)S(1)} %copy-done, ...), custom_call_target="tpu_custom_call" | custom-call | flops 3300000000 | tf_op jit(solution)/shard_map/scan_forward/pallas_call | solution.py:481
  58.1 2.9 %collective-permute-done.6.high_ref = bf16[384,1536]{1,0:T(8,128)(2,1)S(1)} collective-permute-done((bf16[384,1536]{1,0:T(8,128)(2,1)}, bf16[384,1536]{1,0:T(8,128)(2,1)S(1)}, u32[]{:S(2)}, u32[]{:S(2)}) %collective-permute-start.6) | collective-permute-done | bytes 1179680 | tf_op jit(solution)/shard_map/ppermute | solution.py:1309
  61.0 8.3 %out_grad.1 = (bf16[1024,768]{1,0:T(8,128)(2,1)S(1)}, bf16[1024,768]{1,0:T(8,128)(2,1)S(1)}, bf16[768,1024]{1,0:T(8,128)(2,1)S(1)}, f32[8,1024]{1,0:T(8,128)S(1)}, bf16[768,1536]{1,0:T(8,128)(2,1)}) custom-call(s32[2]{0:T(128)S(1)} %pad_add_fusion.starts_ref, s32[16]{0:T(128)S(1)} %get-tuple-element.77.table_ref, bf16[512,768]{1,0:T(8,128)(2,1)} %own_ref.2, ...), custom_call_target="tpu_custom_call" | custom-call | flops 9900000256 | tf_op jit(solution)/shard_map/out_grad/pallas_call | solution.py:865
  69.3 1.6 collective-permute-start.7
  70.9 2.4 %collective-permute-done.7.more_ref = f32[8,1024]{1,0:T(8,128)S(1)} collective-permute-done((f32[8,1024]{1,0:T(8,128)S(1)}, f32[8,1024]{1,0:T(8,128)S(1)}, u32[]{:S(2)}, u32[]{:S(2)}) %collective-permute-start.7) | collective-permute-done | bytes 32800 | tf_op jit(solution)/shard_map/ppermute | solution.py:639
  73.3 10.7 %gated_grad.1 = (bf16[1024,768]{1,0:T(8,128)(2,1)S(1)}, bf16[1024,768]{1,0:T(8,128)(2,1)}, bf16[1024,768]{1,0:T(8,128)(2,1)}, f32[32,768]{1,0:T(8,128)S(1)}, bf1...) custom-call(s32[16]{0:T(128)S(1)} %get-tuple-element.77.table_ref, ...), custom_call_target="tpu_custom_call" | custom-call | flops 9900000256 | tf_op jit(solution)/shard_map/gated_grad/pallas_call | solution.py:1011
  84.1 3.5 %out_project.1 = (bf16[512,768]{1,0:T(8,128)(2,1)S(1)}, bf16[512,768]{1,0:T(8,128)(2,1)S(1)}) custom-call(s32[1]{0:T(128)} %bitcast.starts_ref, bf16[1024,768]{1,0:T(8,128)(2,1)S(1)} %get-tuple-element.105.rows_ref, bf16[768,1536]{1,0:T(8,128)(2,1)} %get-tuple-element.106.weights_ref.gates_ref), custom_call_target="tpu_custom_call" | custom-call | flops 4400000000 | tf_op jit(solution)/shard_map/out_project/pallas_call | solution.py:1078
  87.6 1.3 add_convert_fusion
  88.9 8.2 %all-to-all-start.1 = ((bf16[8,48,1536]{2,1,0:T(8,128)(2,1)}), bf16[8,48,1536]{2,1,0:T(8,128)(2,1)}, u32[]{:S(2)}, u32[]{:S(2)}) async-start(bf16[8,48,1536]{2,1,0:T(8,128)(2,1)} %bitcast.47), calls=%async_computation.1 | async-start | bytes 2359296 | tf_op jit(solution)/shard_map/all_to_all | solution.py:629
  97.1 1.5 collective-permute-start.9
  98.7 26.9 %scan_backward.1 = (bf16[1024,1152]{1,0:T(8,128)(2,1)}, bf16[392,1152]{1,0:T(8,128)(2,1)}, bf16[392,1152]{1,0:T(8,128)(2,1)}) custom-call(s32[16]{0:T(128)S(1)} %get-tuple-element.77.table_ref, bf16[1024,1024]{1,0:T(8,128)(2,1)} %get-tuple-element.87.proj_ref, f32[1024,128]{1,0:T(8,128)} %get-tuple-element.88.step_ref.praw_ref, ...), custom_call_target="tpu_custom_call" | custom-call | flops 39600001024 | tf_op jit(solution)/shard_map/scan_backward/pallas_call | solution.py:539
  126.7 4.3 %normed_grad.2 = bf16[512,768]{1,0:T(8,128)(2,1)S(1)} custom-call(s32[1]{0:T(128)} %bitcast.starts_ref, bf16[1024,768]{1,0:T(8,128)(2,1)} %get-tuple-element.120.dgate_ref, bf16[1024,1152]{1,0:T(8,128)(2,1)} %get-tuple-element.126.dproj_ref, bf16[768,1536]{1,0:T(8,128)(2,1)} %get-tuple-element.106.weights_ref.gates_ref, ...), custom_call_target="tpu_custom_call" | custom-call | flops 5500000256 | tf_op jit(solution)/shard_map/normed_grad/pallas_call | solution.py:1113
  131.0 1.4 add_convert_fusion.1
  132.6 1.1 pad_maximum_fusion
  133.6 5.3 %all-to-all-start.2 = ((bf16[8,56,1152]{2,1,0:T(8,128)(2,1)}), bf16[8,56,1152]{2,1,0:T(8,128)(2,1)S(1)}, u32[]{:S(2)}, u32[]{:S(2)}) async-start(bf16[8,56,1152]{2,1,0:T(8,128)(2,1)} %pad_maximum_fusion), calls=%async_computation.2 | async-start | bytes 2064384 | tf_op jit(solution)/shard_map/all_to_all | solution.py:629
  139.4 1.5 convert_reduce_fusion
  141.5 4.2 %normed_grad.3 = f32[512,768]{1,0:T(8,128)S(1)} custom-call(s32[1]{0:T(128)} %bitcast.11.starts_ref, bf16[1024,768]{1,0:T(8,128)(2,1)} %get-tuple-element.120.dgate_ref, bf16[1024,1152]{1,0:T(8,128)(2,1)} %get-tuple-element.126.dproj_ref, bf16[768,1536]{1,0:T(8,128)(2,1)} %get-tuple-element.106.weights_ref.gates_ref, ...), custom_call_target="tpu_custom_call" | custom-call | flops 5500000256 | tf_op jit(solution)/shard_map/normed_grad/pallas_call | solution.py:1113
  145.8 12.8 %collective-permute-done.11 = bf16[512,768]{1,0:T(8,128)(2,1)S(1)} collective-permute-done((bf16[512,768]{1,0:T(8,128)(2,1)S(1)}, bf16[512,768]{1,0:T(8,128)(2,1)S(1)}, u32[]{:S(2)}, u32[]{:S(2)}) %collective-permute-start.11) | collective-permute-done | bytes 786464 | tf_op jit(solution)/shard_map/ppermute | solution.py:639
  159.1 3.6 %fusion.5 = (f32[512,768]{1,0:T(8,128)}, bf16[512,768]{1,0:T(8,128)(2,1)}) fusion(bf16[512,768]{1,0:T(8,128)(2,1)S(1)} %copy-done.3, bf16[512,768]{1,0:T(8,128)(2,1)} %own_ref.2, f32[512,768]{1,0:T(8,128)S(1)} %normed_grad.3, bf16[512,768]{1,0:T(8,128)(2,1)S(1)} %collective-permute-done.11, f32[512]{0:T(512)S(1)} %broadcast_multiply_fusion, ...), kind=kLoop, calls=%fused_computation.11 | loop fusion | flops 5898240 | bytes 7871488 | tf_op jit(solution)/shard_map/add | solution.py:1396
  162.7 2.3 %all-to-all-done.2 = bf16[8,56,1152]{2,1,0:T(8,128)(2,1)S(1)} async-done(((bf16[8,56,1152]{2,1,0:T(8,128)(2,1)}), bf16[8,56,1152]{2,1,0:T(8,128)(2,1)S(1)}, u32[]{:S(2)}, u32[]{:S(2)}) %all-to-all-start.2) | async-done | bytes 1032224 | tf_op jit(solution)/shard_map/all_to_all | solution.py:629
  168.8 3.4 %collective-permute-done.12 = f32[56,384]{1,0:T(8,128)S(1)} collective-permute-done((f32[56,384]{1,0:T(8,128)S(1)}, f32[56,384]{1,0:T(8,128)S(1)}, u32[]{:S(2)}, u32[]{:S(2)}) %collective-permute-start.12) | collective-permute-done | bytes 86048 | tf_op jit(solution)/shard_map/ppermute | solution.py:639
  (84 shorter events, 15.5 us)
Async XLA Ops:
  0.6 10.3 %copy-start.1 = (s32[1024]{0:T(1024)S(1)}, s32[1024]{0:T(1024)}, u32[]{:S(2)}) copy-start(s32[1024]{0:T(1024)} %param.17) | copy-start | bytes 12292
  5.1 9.6 %collective-permute-start = (bf16[48,1152]{1,0:T(8,128)(2,1)S(1)}, bf16[48,1152]{1,0:T(8,128)(2,1)S(1)}, u32[]{:S(2)}, u32[]{:S(2)}) collective-permute-start(bf16[48,1152]{1,0:T(8,128)(2,1)S(1)} %pad_maximum_fusion.5.packed_ref), channel_id=1, source_target_pairs={{0,16},{2,18},{4,20},{6,22},{8,24},{10,26},{12,28},{14,30},{16,0},... | collective-permute-start | bytes 331784 | tf_op jit(solution)/shard_map/ppermute | solution.py:1287
  9.2 26.4 %collective-permute-start.3 = (bf16[512,768]{1,0:T(8,128)(2,1)}, bf16[512,768]{1,0:T(8,128)(2,1)}, u32[]{:S(2)}, u32[]{:S(2)}) collective-permute-start(bf16[512,768]{1,0:T(8,128)(2,1)} %own_ref.1), channel_id=1, source_target_pairs={{0,1},{1,0},{2,3},{3,2},{4,5},{5,4},{6,7},{7,6},{8,9},{9,8},{10,11... | collective-permute-start | bytes 2359304 | tf_op jit(solution)/shard_map/ppermute | solution.py:639
  11.0 0.7 copy-start.8
  11.0 0.7 copy-start.9
  11.0 0.7 copy-start.10
  11.0 0.7 copy-start.12
  11.0 4.4 %copy-start.6 = (bf16[768,48]{0,1:T(8,128)(2,1)S(1)}, bf16[768,48]{0,1:T(8,128)(2,1)}, u32[]{:S(2)}) copy-start(bf16[768,48]{0,1:T(8,128)(2,1)} %param.28) | copy-start | bytes 221188
  14.7 6.0 %collective-permute-start.1 = (bf16[96,1152]{1,0:T(8,128)(2,1)S(1)}, bf16[96,1152]{1,0:T(8,128)(2,1)S(1)}, u32[]{:S(2)}, u32[]{:S(2)}) collective-permute-start(bf16[96,1152]{1,0:T(8,128)(2,1)S(1)} %pad_maximum_fusion.3), channel_id=1, source_target_pairs={{0,8},{2,6},{4,12},{6,2},{8,0},{10,14},{12,4},{14,10},{16,24},{18,... | collective-permute-start | bytes 663560 | tf_op jit(solution)/shard_map/ppermute | solution.py:1287
  20.7 7.4 %copy-start.7 = (bf16[768]{0:T(1024)(128)(2,1)S(1)}, bf16[768]{0:T(1024)(128)(2,1)}, u32[]{:S(2)}) copy-start(bf16[768]{0:T(1024)(128)(2,1)} %param.27) | copy-start | bytes 4612
  21.8 13.7 %collective-permute-start.2 = (bf16[192,1152]{1,0:T(8,128)(2,1)S(1)}, bf16[192,1152]{1,0:T(8,128)(2,1)S(1)}, u32[]{:S(2)}, u32[]{:S(2)}) collective-permute-start(bf16[192,1152]{1,0:T(8,128)(2,1)S(1)} %pad_maximum_fusion.2), channel_id=1, source_target_pairs={{0,4},{2,10},{4,0},{6,14},{8,12},{10,2},{12,8},{14,6},{16,20},{18,... | collective-permute-start | bytes 1327112 | tf_op jit(solution)/shard_map/ppermute | solution.py:1287
  23.4 34.5 %all-to-all-start = ((bf16[8,48,1536]{2,1,0:T(8,128)(2,1)}), bf16[8,48,1536]{2,1,0:T(8,128)(2,1)}, u32[]{:S(2)}, u32[]{:S(2)}) async-start(bf16[8,48,1536]{2,1,0:T(8,128)(2,1)} %bitcast.15), calls=%async_computation | async-start | bytes 2359296 | tf_op jit(solution)/shard_map/all_to_all | solution.py:629
  35.6 2.5 %copy-start.5 = (bf16[384,1152]{1,0:T(8,128)(2,1)}, bf16[384,1152]{1,0:T(8,128)(2,1)S(1)}, u32[]{:S(2)}) copy-start(bf16[384,1152]{1,0:T(8,128)(2,1)S(1)} %pad_maximum_fusion.1.low_ref) | copy-start | bytes 2654212
  35.6 2.5 %collective-permute-start.4 = (bf16[384,1152]{1,0:T(8,128)(2,1)S(1)}, bf16[384,1152]{1,0:T(8,128)(2,1)S(1)}, u32[]{:S(2)}, u32[]{:S(2)}) collective-permute-start(bf16[384,1152]{1,0:T(8,128)(2,1)S(1)} %pad_maximum_fusion.1.low_ref), channel_id=1, source_target_pairs={{0,2},{2,0},{4,6},{6,4},{8,10},{10,8},{12,14},{14,12},{16,18},{18,... | collective-permute-start | bytes 2654216 | tf_op jit(solution)/shard_map/ppermute | solution.py:1299
  35.7 22.1 %collective-permute-start.5 = (bf16[512,768]{1,0:T(8,128)(2,1)}, bf16[512,768]{1,0:T(8,128)(2,1)}, u32[]{:S(2)}, u32[]{:S(2)}) collective-permute-start(bf16[512,768]{1,0:T(8,128)(2,1)} %own_ref.2), channel_id=1, source_target_pairs={{0,1},{1,0},{2,3},{3,2},{4,5},{5,4},{6,7},{7,6},{8,9},{9,8},{10,11... | collective-permute-start | bytes 2359304 | tf_op jit(solution)/shard_map/ppermute | solution.py:639
  37.4 9.0 %copy-start = (bf16[4,768]{1,0:T(4,128)(2,1)S(1)}, bf16[4,768]{1,0:T(4,128)(2,1)}, u32[]{:S(2)}) copy-start(bf16[4,768]{1,0:T(4,128)(2,1)} %tapi_ref.1) | copy-start | bytes 18436
  57.9 3.1 %collective-permute-start.6 = (bf16[384,1536]{1,0:T(8,128)(2,1)}, bf16[384,1536]{1,0:T(8,128)(2,1)S(1)}, u32[]{:S(2)}, u32[]{:S(2)}) collective-permute-start(bf16[384,1536]{1,0:T(8,128)(2,1)} %bitcast.16.low_ref), channel_id=1, source_target_pairs={{0,2},{2,0},{4,6},{6,4},{8,10},{10,8},{12,14},{14,12},{16,18},{18,... | collective-permute-start | bytes 3538952 | tf_op jit(solution)/shard_map/ppermute | solution.py:1309
  69.3 4.0 %collective-permute-start.7 = (f32[8,1024]{1,0:T(8,128)S(1)}, f32[8,1024]{1,0:T(8,128)S(1)}, u32[]{:S(2)}, u32[]{:S(2)}) collective-permute-start(f32[8,1024]{1,0:T(8,128)S(1)} %get-tuple-element.102.sums_ref), channel_id=1, source_target_pairs={{0,1},{1,0},{2,3},{3,2},{4,5},{5,4},{6,7},{7,6},{8,9},{9,8},{10,11... | collective-permute-start | bytes 98312 | tf_op jit(solution)/shard_map/ppermute | solution.py:639
  84.0 3.6 %collective-permute-start.8 = (bf16[384,1536]{1,0:T(8,128)(2,1)S(1)}, bf16[384,1536]{1,0:T(8,128)(2,1)S(1)}, u32[]{:S(2)}, u32[]{:S(2)}) collective-permute-start(bf16[384,1536]{1,0:T(8,128)(2,1)S(1)} %get-tuple-element.115), channel_id=1, source_target_pairs={{0,2},{2,0},{4,6},{6,4},{8,10},{10,8},{12,14},{14,12},{16,18},{18,... | collective-permute-start | bytes 3538952 | tf_op jit(solution)/shard_map/ppermute | solution.py:1321
  88.9 37.6 %all-to-all-start.1 = ((bf16[8,48,1536]{2,1,0:T(8,128)(2,1)}), bf16[8,48,1536]{2,1,0:T(8,128)(2,1)}, u32[]{:S(2)}, u32[]{:S(2)}) async-start(bf16[8,48,1536]{2,1,0:T(8,128)(2,1)} %bitcast.47), calls=%async_computation.1 | async-start | bytes 2359296 | tf_op jit(solution)/shard_map/all_to_all | solution.py:629
  97.1 28.5 %collective-permute-start.9 = (bf16[512,768]{1,0:T(8,128)(2,1)S(1)}, bf16[512,768]{1,0:T(8,128)(2,1)}, u32[]{:S(2)}, u32[]{:S(2)}) collective-permute-start(bf16[512,768]{1,0:T(8,128)(2,1)S(1)} %get-tuple-element.118), channel_id=1, source_target_pairs={{0,1},{1,0},{2,3},{3,2},{4,5},{5,4},{6,7},{7,6},{8,9},{9,8},{10,11... | collective-permute-start | bytes 2359304 | tf_op jit(solution)/shard_map/ppermute | solution.py:639
  98.7 27.8 %copy-start.2 = (bf16[512,768]{1,0:T(8,128)(2,1)S(1)}, bf16[512,768]{1,0:T(8,128)(2,1)}, u32[]{:S(2)}) copy-start(bf16[512,768]{1,0:T(8,128)(2,1)} %own_ref.1) | copy-start | bytes 2359300
  126.5 4.6 %collective-permute-start.10 = (bf16[392,1152]{1,0:T(8,128)(2,1)}, bf16[392,1152]{1,0:T(8,128)(2,1)}, u32[]{:S(2)}, u32[]{:S(2)}) collective-permute-start(bf16[392,1152]{1,0:T(8,128)(2,1)} %get-tuple-element.122), channel_id=1, source_target_pairs={{0,2},{2,0},{4,6},{6,4},{8,10},{10,8},{12,14},{14,12},{16,18},{18,... | collective-permute-start | bytes 2709512 | tf_op jit(solution)/shard_map/ppermute | solution.py:1348
  126.7 4.3 %copy-start.4 = (bf16[392,1152]{1,0:T(8,128)(2,1)S(1)}, bf16[392,1152]{1,0:T(8,128)(2,1)}, u32[]{:S(2)}) copy-start(bf16[392,1152]{1,0:T(8,128)(2,1)} %get-tuple-element.121) | copy-start | bytes 2709508
  133.6 31.3 %all-to-all-start.2 = ((bf16[8,56,1152]{2,1,0:T(8,128)(2,1)}), bf16[8,56,1152]{2,1,0:T(8,128)(2,1)S(1)}, u32[]{:S(2)}, u32[]{:S(2)}) async-start(bf16[8,56,1152]{2,1,0:T(8,128)(2,1)} %pad_maximum_fusion), calls=%async_computation.2 | async-start | bytes 2064384 | tf_op jit(solution)/shard_map/all_to_all | solution.py:629
  138.9 19.7 %collective-permute-start.11 = (bf16[512,768]{1,0:T(8,128)(2,1)S(1)}, bf16[512,768]{1,0:T(8,128)(2,1)S(1)}, u32[]{:S(2)}, u32[]{:S(2)}) collective-permute-start(bf16[512,768]{1,0:T(8,128)(2,1)S(1)} %normed_grad.2), channel_id=1, source_target_pairs={{0,1},{1,0},{2,3},{3,2},{4,5},{5,4},{6,7},{7,6},{8,9},{9,8},{10,11... | collective-permute-start | bytes 2359304 | tf_op jit(solution)/shard_map/ppermute | solution.py:639
  141.5 17.0 %copy-start.3 = (bf16[512,768]{1,0:T(8,128)(2,1)S(1)}, bf16[512,768]{1,0:T(8,128)(2,1)}, u32[]{:S(2)}) copy-start(bf16[512,768]{1,0:T(8,128)(2,1)} %own_ref.1) | copy-start | bytes 2359300
  165.0 7.4 %copy-start.11 = (bf16[48]{0:T(256)(128)(2,1)S(1)}, bf16[48]{0:T(256)(128)(2,1)}, u32[]{:S(2)}) copy-start(bf16[48]{0:T(256)(128)(2,1)} %param.18) | copy-start | bytes 292
  167.7 4.5 %collective-permute-start.12 = (f32[56,384]{1,0:T(8,128)S(1)}, f32[56,384]{1,0:T(8,128)S(1)}, u32[]{:S(2)}, u32[]{:S(2)}) collective-permute-start(f32[56,384]{1,0:T(8,128)S(1)} %get-tuple-element.131), channel_id=1, source_target_pairs={{0,1},{1,0},{2,3},{3,2},{4,5},{5,4},{6,7},{7,6},{8,9},{9,8},{10,11... | collective-permute-start | bytes 258056 | tf_op jit(solution)/shard_map/ppermute | solution.py:639
